TPU v7x, 32 devices: a whole 2x2x4 slice. The times are simulated.
32 devices in a mesh: tm: 2 (over y), clip: 4 (over x, core), mp: 4 (over z).
Axes of the slice: x: 2, y: 2, z: 4, core: 2. Of those that a mesh axis runs over, the one named last changes fastest.
Arguments:
- tokens: bfloat16 [8, 16, 128, 1024], P('clip', 'tm', None, 'mp'), may hold values from -6 to 6
- cotangent: bfloat16 [8, 16, 128, 1024], P('clip', 'tm', None, 'mp'), may hold values from -6 to 6
- ratio: int32 [8], P('clip'), may hold values from 50 to 100
- priority: int32 [8, 16, 128], P('clip', 'tm'), may hold values from 0 to 99
- frame_order: int32 [8, 16], P('clip'), may hold values from 0 to 15, each once within a row
- mask_embed: bfloat16 [1024], P('mp'), may hold values from -6 to 6
- gains: bfloat16 [3, 1024], P(None, 'mp'), may hold values from 0.099609375 to 1.8984375
- qkv_space: bfloat16 [1024, 3, 1024], P(None, None, 'mp'), may hold values from -0.1875 to 0.1875
- out_space: bfloat16 [1024, 1024], P('mp'), may hold values from -0.75 to 0.75
- qkv_time: bfloat16 [1024, 3, 1024], P(None, None, 'mp'), may hold values from -0.1875 to 0.1875
- out_time: bfloat16 [1024, 1024], P('mp'), may hold values from -0.375 to 0.375
- w_in: bfloat16 [1024, 4096], P(None, 'mp'), may hold values from -0.1875 to 0.1875
- w_out: bfloat16 [4096, 1024], P('mp'), may hold values from -0.09375 to 0.09375
Outputs:
- block_out: bfloat16 [8, 16, 128, 1024], P('clip', 'tm', None, 'mp')
- grad_tokens: float32 [8, 16, 128, 1024], P('clip', 'tm', None, 'mp')
- grad_mask_embed: float32 [1024], P('mp')
- grad_gains: float32 [3, 1024], P(None, 'mp')
- grad_qkv_space: float32 [1024, 3, 1024], P(('tm', 'clip'), None, 'mp')
- grad_out_space: float32 [1024, 1024], P('mp', ('tm', 'clip'))
- grad_qkv_time: float32 [1024, 3, 1024], P(('tm', 'clip'), None, 'mp')
- grad_out_time: float32 [1024, 1024], P('mp', ('tm', 'clip'))
- grad_w_in: float32 [1024, 4096], P(('tm', 'clip'), 'mp')
- grad_w_out: float32 [4096, 1024], P('mp', ('tm', 'clip'))
Inputs may be any that keep to these rules, and one draw needn't show every extreme that they name: Each row of frame_order holds each of 0 to 15 once.
All inputs are finite; a program needn't handle non-finite values.
Results may differ from a plain program's by a relative error of at most 0.02.
Values may be sent and summed in bfloat16 or wider, within the bound.
A program may use at most 192 MiB of HBM per device.

v0:
```python
import math

import jax
import jax.numpy as jnp
from jax import lax
from jax.sharding import PartitionSpec as P

HEAD_DIM = 64
MICRO = 2


eps_norm = 1e-05


def gelu_tanh(values):
    return jax.nn.gelu(values, approximate=True)


def norm_forward_pass(residual_stream, gain_coefficients, complete_width):
    reduced_totals = lax.psum(
        (jnp.sum(residual_stream, axis=-1), jnp.sum(residual_stream * residual_stream, axis=-1)),
        "mp",
    )
    centered_rows = reduced_totals[0] / complete_width
    spread = reduced_totals[1] / complete_width - centered_rows * centered_rows
    inverse_scale = lax.rsqrt(spread + eps_norm)
    standardized_rows = (residual_stream - centered_rows[:, None]) * inverse_scale[:, None]
    shard_rows = (standardized_rows * gain_coefficients).astype(jnp.bfloat16)
    normalized_rows = lax.all_gather(shard_rows, "mp", axis=1, tiled=True)
    return (normalized_rows, standardized_rows, inverse_scale)


def norm_reverse_pass(
    normalized_gradient, standardized_rows, inverse_scale, gain_coefficients, complete_width
):
    gain_gradient = jnp.sum(normalized_gradient * standardized_rows, axis=0)
    standardized_gradient = normalized_gradient * gain_coefficients
    reduced_totals = lax.psum(
        (
            jnp.sum(standardized_gradient, axis=-1),
            jnp.sum(standardized_gradient * standardized_rows, axis=-1),
        ),
        "mp",
    )
    grad_resid = (
        standardized_gradient
        - reduced_totals[0][:, None] / complete_width
        - standardized_rows * (reduced_totals[1][:, None] / complete_width)
    ) * inverse_scale[:, None]
    return (grad_resid, gain_gradient)


def sum_features(grad_full):
    return lax.psum_scatter(
        grad_full.astype(jnp.bfloat16), "mp", scatter_dimension=1, tiled=True
    ).astype(jnp.float32)


def branch_out(hidden, weight):
    partial_rows = jnp.dot(hidden, weight, preferred_element_type=jnp.float32)
    return lax.psum_scatter(partial_rows, "mp", scatter_dimension=1, tiled=True)


def branch_back(grad_resid, hidden, weight):
    grad_rows = lax.all_gather(grad_resid.astype(jnp.bfloat16), "mp", axis=1, tiled=True)
    weight_grad = jnp.einsum("rk,rd->kd", hidden, grad_rows, preferred_element_type=jnp.float32)
    grad_hidden = jnp.einsum("rd,kd->rk", grad_rows, weight, preferred_element_type=jnp.float32)
    return (grad_hidden, weight_grad)


def qkv_back(normalized_rows, grad_joined, weight):
    weight_grad = jnp.einsum(
        "rd,trk->dtk", normalized_rows, grad_joined, preferred_element_type=jnp.float32
    )
    grad_full = jnp.einsum("trk,dtk->rd", grad_joined, weight, preferred_element_type=jnp.float32)
    return (weight_grad, sum_features(grad_full))


def reduce_grads(local_grads, small_grads):
    reduced = (
        lax.psum_scatter(local_grads[0], ("tm", "clip"), scatter_dimension=0, tiled=True),
        lax.psum_scatter(local_grads[1], ("tm", "clip"), scatter_dimension=1, tiled=True),
        lax.psum_scatter(local_grads[2], ("tm", "clip"), scatter_dimension=0, tiled=True),
        lax.psum_scatter(local_grads[3], ("tm", "clip"), scatter_dimension=1, tiled=True),
        lax.psum_scatter(local_grads[4], ("tm", "clip"), scatter_dimension=0, tiled=True),
        lax.psum_scatter(local_grads[5], ("tm", "clip"), scatter_dimension=1, tiled=True),
    )
    reduced_small = lax.psum((small_grads[0], small_grads[1]), ("tm", "clip"))
    return (reduced, reduced_small)


def space_forward(normalized_rows, weight, frame_count, patches, heads_local, scale):
    joined = jnp.einsum(
        "rd,dtk->trk", normalized_rows, weight, preferred_element_type=jnp.float32
    ).astype(jnp.bfloat16)
    shape_heads = (frame_count, patches, heads_local, HEAD_DIM)
    scores = (
        jnp.einsum(
            "bshd,bthd->bhst",
            joined[0].reshape(shape_heads),
            joined[1].reshape(shape_heads),
            preferred_element_type=jnp.float32,
        )
        * scale
    )
    highest = jnp.max(scores, axis=-1, keepdims=True)
    exponent = jnp.exp(scores - highest)
    reduced_totals = jnp.sum(exponent, axis=-1, keepdims=True)
    log_total = highest + jnp.log(reduced_totals)
    attention = (exponent / reduced_totals).astype(jnp.bfloat16)
    mixed = jnp.einsum(
        "bhst,bthd->bshd",
        attention,
        joined[2].reshape(shape_heads),
        preferred_element_type=jnp.float32,
    )
    return (
        joined,
        log_total,
        mixed.astype(jnp.bfloat16).reshape(frame_count * patches, heads_local * HEAD_DIM),
    )


def space_backward(grad_mixed, joined, log_total, frame_count, patches, heads_local, scale):
    shape_heads = (frame_count, patches, heads_local, HEAD_DIM)
    queries = joined[0].reshape(shape_heads)
    key_rows = joined[1].reshape(shape_heads)
    values = joined[2].reshape(shape_heads)
    grad_out = grad_mixed.reshape(shape_heads)
    scores = (
        jnp.einsum("bshd,bthd->bhst", queries, key_rows, preferred_element_type=jnp.float32) * scale
    )
    attention = jnp.exp(scores - log_total)
    grad_values = jnp.einsum(
        "bhst,bshd->bthd",
        attention.astype(jnp.bfloat16),
        grad_out,
        preferred_element_type=jnp.float32,
    )
    grad_att = jnp.einsum("bshd,bthd->bhst", grad_out, values, preferred_element_type=jnp.float32)
    grad_scores = (
        attention * (grad_att - jnp.sum(attention * grad_att, axis=-1, keepdims=True))
    ).astype(jnp.bfloat16)
    grad_queries = (
        jnp.einsum("bhst,bthd->bshd", grad_scores, key_rows, preferred_element_type=jnp.float32)
        * scale
    )
    grad_keys = (
        jnp.einsum("bhst,bshd->bthd", grad_scores, queries, preferred_element_type=jnp.float32)
        * scale
    )
    row_count = frame_count * patches
    stacked = jnp.stack(
        [
            grad_queries.reshape(row_count, -1),
            grad_keys.reshape(row_count, -1),
            grad_values.reshape(row_count, -1),
        ]
    )
    return stacked.astype(jnp.bfloat16)


def time_scores(queries, keys_all, visible, scale):
    scores = (
        jnp.einsum("cfshd,cgshd->chfgs", queries, keys_all, preferred_element_type=jnp.float32)
        * scale
    )
    return jnp.where(visible, scores, -1e30)


def time_forward(queries, keys_all, values_all, visible, scale):
    scores = time_scores(queries, keys_all, visible, scale)
    highest = jnp.max(scores, axis=3, keepdims=True)
    exponent = jnp.exp(scores - highest)
    reduced_totals = jnp.sum(exponent, axis=3, keepdims=True)
    log_total = highest + jnp.log(reduced_totals)
    attention = (exponent / reduced_totals).astype(jnp.bfloat16)
    mixed = jnp.einsum(
        "chfgs,cgshd->cfshd", attention, values_all, preferred_element_type=jnp.float32
    )
    return (log_total, mixed.astype(jnp.bfloat16))


def time_backward(grad_mixed, queries, keys_all, values_all, visible, log_total, scale):
    grad_out = grad_mixed.reshape(queries.shape)
    scores = time_scores(queries, keys_all, visible, scale)
    attention = jnp.exp(scores - log_total)
    grad_values = jnp.einsum(
        "chfgs,cfshd->cgshd",
        attention.astype(jnp.bfloat16),
        grad_out,
        preferred_element_type=jnp.float32,
    )
    grad_att = jnp.einsum(
        "cfshd,cgshd->chfgs", grad_out, values_all, preferred_element_type=jnp.float32
    )
    grad_scores = (
        attention * (grad_att - jnp.sum(attention * grad_att, axis=3, keepdims=True))
    ).astype(jnp.bfloat16)
    grad_queries = (
        jnp.einsum("chfgs,cgshd->cfshd", grad_scores, keys_all, preferred_element_type=jnp.float32)
        * scale
    )
    grad_keys = (
        jnp.einsum("chfgs,cfshd->cgshd", grad_scores, queries, preferred_element_type=jnp.float32)
        * scale
    )
    return (grad_queries, grad_keys, grad_values)


def shards(
    tokens,
    cotangent,
    ratio,
    priority,
    frame_order,
    mask_embed,
    gains,
    qkv_space,
    out_space,
    qkv_time,
    out_time,
    w_in,
    w_out,
):
    scale = 1.0 / math.sqrt(HEAD_DIM)
    clips_local = tokens.shape[0] // MICRO
    frames_local = tokens.shape[1]
    patches = tokens.shape[2]
    cols_local = tokens.shape[3]
    frames_all = frame_order.shape[1]
    hidden_width = qkv_space.shape[0]
    joined_local = qkv_space.shape[2]
    heads_local = joined_local // HEAD_DIM
    row_count = clips_local * frames_local * patches
    gain_broadcast = gains.astype(jnp.float32)
    embed_row = mask_embed.astype(jnp.float32)
    first_frame = lax.axis_index("tm") * frames_local
    shape_local = (clips_local, frames_local, patches, joined_local)
    shape_heads = (clips_local, frames_local, patches, heads_local, HEAD_DIM)
    shape_all = (clips_local, frames_all, patches, heads_local, HEAD_DIM)
    outputs = []
    input_grads = []
    weight_total = None
    small_total = None
    for batch_index in range(MICRO):
        lower = batch_index * clips_local
        upper = lower + clips_local
        source = tokens[lower:upper].reshape(row_count, cols_local).astype(jnp.float32)
        upstream = cotangent[lower:upper].reshape(row_count, cols_local).astype(jnp.float32)
        masked = (priority[lower:upper] < ratio[lower:upper][:, None, None]).reshape(row_count)
        order_rows = frame_order[lower:upper]
        residual_stream0 = jnp.where(masked[:, None], embed_row[None, :], source)
        normalized_rows0, standardized_rows0, inverse_deviation0 = norm_forward_pass(
            residual_stream0, gain_broadcast[0], hidden_width
        )
        joined0, total0, mixed0 = space_forward(
            normalized_rows0, qkv_space, clips_local * frames_local, patches, heads_local, scale
        )
        residual_stream1 = residual_stream0 + branch_out(mixed0, out_space)
        normalized_rows1, standardized_rows1, inverse_deviation1 = norm_forward_pass(
            residual_stream1, gain_broadcast[1], hidden_width
        )
        joined1 = jnp.einsum(
            "rd,dtk->trk", normalized_rows1, qkv_time, preferred_element_type=jnp.float32
        ).astype(jnp.bfloat16)
        queries_local = joined1[0].reshape(shape_local)
        keys_local = joined1[1].reshape(shape_local)
        values_local = joined1[2].reshape(shape_local)
        keys_all, values_all = (
            lax.all_gather(keys_local, "tm", axis=1, tiled=True),
            lax.all_gather(values_local, "tm", axis=1, tiled=True),
        )
        query_order = lax.dynamic_slice_in_dim(order_rows, first_frame, frames_local, axis=1)
        time_visible = (order_rows[:, None, :] <= query_order[:, :, None])[:, None, :, :, None]
        time_q = queries_local.reshape(shape_heads)
        time_k = keys_all.reshape(shape_all)
        time_v = values_all.reshape(shape_all)
        total1, mixed_frames = time_forward(time_q, time_k, time_v, time_visible, scale)
        mixed1 = mixed_frames.reshape(row_count, joined_local)
        residual_stream2 = residual_stream1 + branch_out(mixed1, out_time)
        normalized_rows2, standardized_rows2, inverse_deviation2 = norm_forward_pass(
            residual_stream2, gain_broadcast[2], hidden_width
        )
        projected = jnp.dot(normalized_rows2, w_in, preferred_element_type=jnp.float32)
        activated, gelu_pull = jax.vjp(gelu_tanh, projected)
        hidden = activated.astype(jnp.bfloat16)
        resid3 = residual_stream2 + branch_out(hidden, w_out)
        outputs.append(
            resid3.astype(jnp.bfloat16).reshape(clips_local, frames_local, patches, cols_local)
        )
        grad3 = jnp.where(masked[:, None], upstream, 0.0)
        grad_hidden, grad_w_out = branch_back(grad3, hidden, w_out)
        grad_inner = gelu_pull(grad_hidden)[0].astype(jnp.bfloat16)
        grad_w_in = jnp.einsum(
            "rd,rk->dk", normalized_rows2, grad_inner, preferred_element_type=jnp.float32
        )
        normalized_gradient2 = sum_features(
            jnp.einsum("rk,dk->rd", grad_inner, w_in, preferred_element_type=jnp.float32)
        )
        backward_third, gain_gradient2 = norm_reverse_pass(
            normalized_gradient2,
            standardized_rows2,
            inverse_deviation2,
            gain_broadcast[2],
            hidden_width,
        )
        grad2 = grad3 + backward_third
        grad_mixed1, grad_out_time = branch_back(grad2, mixed1, out_time)
        grad_mixed_low = grad_mixed1.astype(jnp.bfloat16).reshape(shape_local)
        grad_queries, grad_keys, grad_values = time_backward(
            grad_mixed_low, time_q, time_k, time_v, time_visible, total1, scale
        )
        key_part, value_part = (
            lax.psum_scatter(
                grad_keys.reshape(clips_local, frames_all, patches, joined_local).astype(
                    jnp.bfloat16
                ),
                "tm",
                scatter_dimension=1,
                tiled=True,
            ).astype(jnp.float32),
            lax.psum_scatter(
                grad_values.reshape(clips_local, frames_all, patches, joined_local).astype(
                    jnp.bfloat16
                ),
                "tm",
                scatter_dimension=1,
                tiled=True,
            ).astype(jnp.float32),
        )
        grad_joined1 = jnp.stack(
            [
                grad_queries.reshape(row_count, joined_local),
                key_part.reshape(row_count, joined_local),
                value_part.reshape(row_count, joined_local),
            ]
        ).astype(jnp.bfloat16)
        grad_qkv_time, normalized_gradient1 = qkv_back(normalized_rows1, grad_joined1, qkv_time)
        backward_second, gain_gradient1 = norm_reverse_pass(
            normalized_gradient1,
            standardized_rows1,
            inverse_deviation1,
            gain_broadcast[1],
            hidden_width,
        )
        grad1 = grad2 + backward_second
        grad_mixed0, grad_out_space = branch_back(grad1, mixed0, out_space)
        grad_joined0 = space_backward(
            grad_mixed0.astype(jnp.bfloat16),
            joined0,
            total0,
            clips_local * frames_local,
            patches,
            heads_local,
            scale,
        )
        grad_qkv_space, normalized_gradient0 = qkv_back(normalized_rows0, grad_joined0, qkv_space)
        backward_first, gain_gradient0 = norm_reverse_pass(
            normalized_gradient0,
            standardized_rows0,
            inverse_deviation0,
            gain_broadcast[0],
            hidden_width,
        )
        grad0 = grad1 + backward_first
        input_grads.append(
            jnp.where(masked[:, None], 0.0, grad0).reshape(
                clips_local, frames_local, patches, cols_local
            )
        )
        grad_embed = jnp.sum(jnp.where(masked[:, None], grad0, 0.0), axis=0)
        gain_grads = jnp.stack([gain_gradient0, gain_gradient1, gain_gradient2])
        local_grads = (
            grad_qkv_space,
            grad_out_space,
            grad_qkv_time,
            grad_out_time,
            grad_w_in,
            grad_w_out,
        )
        small_grads = (gain_grads, grad_embed)
        reduced, reduced_small = reduce_grads(local_grads, small_grads)
        if weight_total is None:
            weight_total = reduced
            small_total = reduced_small
        else:
            weight_total = tuple((total + grad for total, grad in zip(weight_total, reduced)))
            small_total = tuple((total + grad for total, grad in zip(small_total, reduced_small)))
    return (
        jnp.concatenate(outputs, axis=0),
        jnp.concatenate(input_grads, axis=0),
        small_total[1],
        small_total[0],
        weight_total[0],
        weight_total[1],
        weight_total[2],
        weight_total[3],
        weight_total[4],
        weight_total[5],
    )


def solution(mesh):
    return jax.shard_map(
        shards,
        mesh=mesh,
        in_specs=(
            P("clip", "tm", None, "mp"),
            P("clip", "tm", None, "mp"),
            P("clip"),
            P("clip", "tm", None),
            P("clip", None),
            P("mp"),
            P(None, "mp"),
            P(None, None, "mp"),
            P("mp", None),
            P(None, None, "mp"),
            P("mp", None),
            P(None, "mp"),
            P("mp", None),
        ),
        out_specs=(
            P("clip", "tm", None, "mp"),
            P("clip", "tm", None, "mp"),
            P("mp"),
            P(None, "mp"),
            P(("tm", "clip"), None, "mp"),
            P("mp", ("tm", "clip")),
            P(("tm", "clip"), None, "mp"),
            P("mp", ("tm", "clip")),
            P(("tm", "clip"), "mp"),
            P("mp", ("tm", "clip")),
        ),
        check_vma=False,
    )
```

profile of v0, /device:TPU:9, one launch (start us, length us, event | category | flops | bytes accessed | tf_op | source)
XLA Modules:
  0.0 1890.0 jit_solution(4307672605485570398)
XLA Ops:
  14.2 11.9 all-reduce.6
  30.5 49.3 %all-gather.27.cloned.1.call-done = bf16[1024,1024]{1,0:T(8,128)(2,1)} async-done(((bf16[1024,256]{1,0:T(8,128)(2,1)}), bf16[1024,1024]{1,0:T(8,128)(2,1)}) %all-gather.27.cloned.1.call-update) | async-done | bytes 2097168 | tf_op jit(solution)/shard_map/all_gather | solution.py:29
  102.0 24.5 %all-gather.17.cloned.1.call-done = bf16[1024,1024]{1,0:T(8,128)(2,1)} async-done(((bf16[1024,256]{1,0:T(8,128)(2,1)}), bf16[1024,1024]{1,0:T(8,128)(2,1)}) %all-gather.17.cloned.1.call-update) | async-done | bytes 2097168 | tf_op jit(solution)/shard_map/all_gather | solution.py:29
  150.5 54.9 %reduce-scatter.29.cloned.1.call-done = f32[1024,256]{1,0:T(8,128)} async-done(((f32[1024,1024]{1,0:T(8,128)}), f32[1024,256]{1,0:T(8,128)}) %reduce-scatter.29.cloned.1.call-update) | async-done | bytes 1048592 | tf_op jit(solution)/shard_map/reduce_scatter | solution.py:61
  205.3 79.6 %reduce-scatter.23.cloned.1.call-done = f32[1024,256]{1,0:T(8,128)} async-done(((f32[1024,1024]{1,0:T(8,128)}), f32[1024,256]{1,0:T(8,128)}) %reduce-scatter.23.cloned.1.call-update) | async-done | bytes 1048592 | tf_op jit(solution)/shard_map/reduce_scatter | solution.py:61
  288.7 11.4 all-reduce.5
  303.6 49.2 %all-gather.29.cloned.1.call-done = bf16[1024,1024]{1,0:T(8,128)(2,1)} async-done(((bf16[1024,256]{1,0:T(8,128)(2,1)}), bf16[1024,1024]{1,0:T(8,128)(2,1)}) %all-gather.29.cloned.1.call-update) | async-done | bytes 2097168 | tf_op jit(solution)/shard_map/all_gather | solution.py:29
  358.5 40.7 %all-gather.19.cloned.1.call-done = bf16[1024,1024]{1,0:T(8,128)(2,1)} async-done(((bf16[1024,256]{1,0:T(8,128)(2,1)}), bf16[1024,1024]{1,0:T(8,128)(2,1)}) %all-gather.19.cloned.1.call-update) | async-done | bytes 2097168 | tf_op jit(solution)/shard_map/all_gather | solution.py:29
  406.8 15.0 all-gather.33.cloned.1.call-done
  426.0 18.7 all-gather.31.cloned.1.call-done
  472.3 18.0 all-gather.21.cloned.1.call-done
  511.5 58.0 %reduce-scatter.31.cloned.1.call-done = f32[1024,256]{1,0:T(8,128)} async-done(((f32[1024,1024]{1,0:T(8,128)}), f32[1024,256]{1,0:T(8,128)}) %reduce-scatter.31.cloned.1.call-update) | async-done | bytes 1048592 | tf_op jit(solution)/shard_map/reduce_scatter | solution.py:61
  572.2 76.9 %reduce-scatter.25.cloned.1.call-done = f32[1024,256]{1,0:T(8,128)} async-done(((f32[1024,1024]{1,0:T(8,128)}), f32[1024,256]{1,0:T(8,128)}) %reduce-scatter.25.cloned.1.call-update) | async-done | bytes 1048592 | tf_op jit(solution)/shard_map/reduce_scatter | solution.py:61
  651.4 11.4 all-reduce.4
  665.5 30.6 %all-gather.37.cloned.1.call-done = bf16[1024,1024]{1,0:T(8,128)(2,1)} async-done(((bf16[1024,256]{1,0:T(8,128)(2,1)}), bf16[1024,1024]{1,0:T(8,128)(2,1)}) %all-gather.37.cloned.1.call-update) | async-done | bytes 2097168 | tf_op jit(solution)/shard_map/all_gather | solution.py:65
  696.1 6.5 fusion.225
  702.6 39.9 %all-gather.25.cloned.1.call-done = bf16[1024,1024]{1,0:T(8,128)(2,1)} async-done(((bf16[1024,256]{1,0:T(8,128)(2,1)}), bf16[1024,1024]{1,0:T(8,128)(2,1)}) %all-gather.25.cloned.1.call-update) | async-done | bytes 2097168 | tf_op jit(solution)/shard_map/all_gather | solution.py:29
  742.5 8.3 fusion.6
  756.5 40.7 %reduce-scatter.35.cloned.1.call-done = bf16[1024,256]{1,0:T(8,128)(2,1)} async-done(((bf16[1024,1024]{1,0:T(8,128)(2,1)}), bf16[1024,256]{1,0:T(8,128)(2,1)}) %reduce-scatter.35.cloned.1.call-update) | async-done | bytes 524304 | tf_op jit(solution)/shard_map/reduce_scatter | solution.py:54
  801.3 44.0 %all-gather.43.cloned.1.call-done = bf16[1024,1024]{1,0:T(8,128)(2,1)} async-done(((bf16[1024,256]{1,0:T(8,128)(2,1)}), bf16[1024,1024]{1,0:T(8,128)(2,1)}) %all-gather.43.cloned.1.call-update) | async-done | bytes 2097168 | tf_op jit(solution)/shard_map/all_gather | solution.py:65
  845.2 6.7 fusion.226
  851.9 39.9 %all-gather.35.cloned.1.call-done = bf16[1024,1024]{1,0:T(8,128)(2,1)} async-done(((bf16[1024,256]{1,0:T(8,128)(2,1)}), bf16[1024,1024]{1,0:T(8,128)(2,1)}) %all-gather.35.cloned.1.call-update) | async-done | bytes 2097168 | tf_op jit(solution)/shard_map/all_gather | solution.py:29
  891.8 8.3 fusion.13
  906.8 6.8 fusion.197
  913.6 6.8 fusion.198
  920.6 25.9 %reduce-scatter.45.cloned.1.call-done = bf16[1024,256]{1,0:T(8,128)(2,1)} async-done(((bf16[1024,1024]{1,0:T(8,128)(2,1)}), bf16[1024,256]{1,0:T(8,128)(2,1)}) %reduce-scatter.45.cloned.1.call-update) | async-done | bytes 524304 | tf_op jit(solution)/shard_map/reduce_scatter | solution.py:54
  948.2 14.6 all-reduce.3
  962.8 64.9 %reduce-scatter.27.cloned.1.call-done = f32[1024,256]{1,0:T(8,128)} async-done(((f32[1024,1024]{1,0:T(8,128)}), f32[1024,256]{1,0:T(8,128)}) %reduce-scatter.27.cloned.1.call-update) | async-done | bytes 1048592 | tf_op jit(solution)/shard_map/reduce_scatter | solution.py:61
  1027.7 79.4 %reduce-scatter.33.cloned.1.call-done = f32[1024,256]{1,0:T(8,128)} async-done(((f32[1024,1024]{1,0:T(8,128)}), f32[1024,256]{1,0:T(8,128)}) %reduce-scatter.33.cloned.1.call-update) | async-done | bytes 1048592 | tf_op jit(solution)/shard_map/reduce_scatter | solution.py:61
  1120.6 37.5 %all-gather.45.cloned.1.call-done = bf16[1024,1024]{1,0:T(8,128)(2,1)} async-done(((bf16[1024,256]{1,0:T(8,128)(2,1)}), bf16[1024,1024]{1,0:T(8,128)(2,1)}) %all-gather.45.cloned.1.call-update) | async-done | bytes 2097168 | tf_op jit(solution)/shard_map/all_gather | solution.py:65
  1195.6 8.5 all-gather.39.cloned.1.call-done
  1243.1 5.8 reduce-scatter.49.cloned.1.call-done
  1263.8 7.7 reduce-scatter.37.cloned.1.call-done
  1272.8 21.3 %reduce-scatter.39.cloned.1.call-done = bf16[1,8,128,256]{2,3,1,0:T(8,128)(2,1)} async-done(((bf16[1,16,128,256]{2,3,1,0:T(8,128)(2,1)}), bf16[1,8,128,256]{2,3,1,0:T(8,128)(2,1)}) %reduce-scatter.39.cloned.1.call-update) | async-done | bytes 524304 | tf_op jit(solution)/shard_map/reduce_scatter | solution.py:323
  1300.7 36.9 %reduce-scatter.51.cloned.1.call-done = bf16[1024,256]{1,0:T(8,128)(2,1)} async-done(((bf16[1024,1024]{1,0:T(8,128)(2,1)}), bf16[1024,256]{1,0:T(8,128)(2,1)}) %reduce-scatter.51.cloned.1.call-update) | async-done | bytes 524304 | tf_op jit(solution)/shard_map/reduce_scatter | solution.py:54
  1337.7 46.2 %reduce-scatter.41.cloned.1.call-done = bf16[1024,256]{1,0:T(8,128)(2,1)} async-done(((bf16[1024,1024]{1,0:T(8,128)(2,1)}), bf16[1024,256]{1,0:T(8,128)(2,1)}) %reduce-scatter.41.cloned.1.call-update) | async-done | bytes 524304 | tf_op jit(solution)/shard_map/reduce_scatter | solution.py:54
  1386.4 12.8 all-reduce.2
  1405.0 48.8 %all-gather.47.cloned.1.call-done = bf16[1024,1024]{1,0:T(8,128)(2,1)} async-done(((bf16[1024,256]{1,0:T(8,128)(2,1)}), bf16[1024,1024]{1,0:T(8,128)(2,1)}) %all-gather.47.cloned.1.call-update) | async-done | bytes 2097168 | tf_op jit(solution)/shard_map/all_gather | solution.py:65
  1477.3 23.0 %all-gather.41.cloned.1.call-done = bf16[1024,1024]{1,0:T(8,128)(2,1)} async-done(((bf16[1024,256]{1,0:T(8,128)(2,1)}), bf16[1024,1024]{1,0:T(8,128)(2,1)}) %all-gather.41.cloned.1.call-update) | async-done | bytes 2097168 | tf_op jit(solution)/shard_map/all_gather | solution.py:65
  1573.3 16.7 reduce-scatter.43.cloned.1.call-done
  1593.5 12.8 all-reduce.1
  1610.9 16.7 all-reduce
  1630.7 16.5 reduce-scatter.65.cloned.1.call-done
  1647.1 55.7 %reduce-scatter.63.cloned.1.call-done = f32[128,1024]{1,0:T(8,128)} async-done(((f32[1024,1024]{1,0:T(8,128)}), f32[128,1024]{1,0:T(8,128)}) %reduce-scatter.63.cloned.1.call-update) | async-done | bytes 524304 | tf_op jit(solution)/shard_map/reduce_scatter | solution.py:85
  1702.8 39.7 %reduce-scatter.61.cloned.1.call-done = f32[256,128]{1,0:T(8,128)} async-done(((f32[256,1024]{1,0:T(8,128)}), f32[256,128]{1,0:T(8,128)}) %reduce-scatter.61.cloned.1.call-update) | async-done | bytes 131088 | tf_op jit(solution)/shard_map/reduce_scatter | solution.py:84
  1742.5 50.1 %reduce-scatter.59.cloned.1.call-done = f32[128,3,256]{2,0,1:T(8,128)} async-done(((f32[1024,3,256]{2,0,1:T(8,128)}), f32[128,3,256]{2,0,1:T(8,128)}) %reduce-scatter.59.cloned.1.call-update) | async-done | bytes 393232 | tf_op jit(solution)/shard_map/reduce_scatter | solution.py:83
  1792.6 39.9 %reduce-scatter.57.cloned.1.call-done = f32[256,128]{1,0:T(8,128)} async-done(((f32[256,1024]{1,0:T(8,128)}), f32[256,128]{1,0:T(8,128)}) %reduce-scatter.57.cloned.1.call-update) | async-done | bytes 131088 | tf_op jit(solution)/shard_map/reduce_scatter | solution.py:82
  1832.5 50.7 %reduce-scatter.55.cloned.1.call-done = f32[128,3,256]{2,0,1:T(8,128)} async-done(((f32[1024,3,256]{2,0,1:T(8,128)}), f32[128,3,256]{2,0,1:T(8,128)}) %reduce-scatter.55.cloned.1.call-update) | async-done | bytes 393232 | tf_op jit(solution)/shard_map/reduce_scatter | solution.py:81
  (531 shorter events, 383.7 us)
Async XLA Ops:
  7.2 735.3 %copy-start = (bf16[1024,1024]{1,0:T(8,128)(2,1)S(1)}, bf16[1024,1024]{1,0:T(8,128)(2,1)}, u32[]{:S(2)}) copy-start(bf16[1024,1024]{1,0:T(8,128)(2,1)} %param.24) | copy-start | bytes 6291460
  7.2 72.7 %all-gather.27.cloned.1.call-start = ((), (), s32[]{:S(2)}) async-start(), calls=%async_computation.30 | async-start | bytes 2621440 | tf_op jit(solution)/shard_map/all_gather | solution.py:29
  9.3 275.6 %copy-start.110 = (f32[256]{0:T(256)}, f32[256]{0:T(256)S(1)}, u32[]{:S(2)}) copy-start(f32[256]{0:T(256)S(1)} %convert_element_type.318) | copy-start | bytes 3076
  29.7 96.8 %all-gather.17.cloned.1.call-start = ((), (), s32[]{:S(2)}) async-start(), calls=%async_computation.22 | async-start | bytes 2621440 | tf_op jit(solution)/shard_map/all_gather | solution.py:29
  30.5 174.8 %reduce-scatter.29.cloned.1.call-start = ((), (), s32[]{:S(2)}) async-start(), calls=%async_computation.31 | async-start | bytes 5242880 | tf_op jit(solution)/shard_map/reduce_scatter | solution.py:61
  101.5 183.4 %reduce-scatter.23.cloned.1.call-start = ((), (), s32[]{:S(2)}) async-start(), calls=%async_computation.23 | async-start | bytes 5242880 | tf_op jit(solution)/shard_map/reduce_scatter | solution.py:61
  148.0 136.9 %copy-start.10 = (bf16[2,8,128,256]{3,2,1,0:T(8,128)(2,1)S(1)}, bf16[2,8,128,256]{3,2,1,0:T(8,128)(2,1)}, u32[]{:S(2)}) copy-start(bf16[2,8,128,256]{3,2,1,0:T(8,128)(2,1)} %param.13) | copy-start | bytes 3145732
  148.1 204.7 %all-gather.29.cloned.1.call-start = ((), (), s32[]{:S(2)}) async-start(), calls=%async_computation.32 | async-start | bytes 2621440 | tf_op jit(solution)/shard_map/all_gather | solution.py:29
  303.0 96.3 %all-gather.19.cloned.1.call-start = ((), (), s32[]{:S(2)}) async-start(), calls=%async_computation.24 | async-start | bytes 2621440 | tf_op jit(solution)/shard_map/all_gather | solution.py:29
  303.6 118.3 %all-gather.33.cloned.1.call-start = ((), (), s32[]{:S(2)}) async-start(), calls=%async_computation.34 | async-start | bytes 1572864 | tf_op jit(solution)/shard_map/all_gather | solution.py:271
  357.7 87.0 %all-gather.31.cloned.1.call-start = ((), (), s32[]{:S(2)}) async-start(), calls=%async_computation.33 | async-start | bytes 1572864 | tf_op jit(solution)/shard_map/all_gather | solution.py:272
  358.5 109.7 %all-gather.23.cloned.1.call-start = ((), (), s32[]{:S(2)}) async-start(), calls=%async_computation.26 | async-start | bytes 1572864 | tf_op jit(solution)/shard_map/all_gather | solution.py:271
  404.3 86.0 %all-gather.21.cloned.1.call-start = ((), (), s32[]{:S(2)}) async-start(), calls=%async_computation.25 | async-start | bytes 1572864 | tf_op jit(solution)/shard_map/all_gather | solution.py:272
  406.7 162.8 %reduce-scatter.31.cloned.1.call-start = ((), (), s32[]{:S(2)}) async-start(), calls=%async_computation.35 | async-start | bytes 5242880 | tf_op jit(solution)/shard_map/reduce_scatter | solution.py:61
  465.3 183.8 %reduce-scatter.25.cloned.1.call-start = ((), (), s32[]{:S(2)}) async-start(), calls=%async_computation.27 | async-start | bytes 5242880 | tf_op jit(solution)/shard_map/reduce_scatter | solution.py:61
  510.7 138.4 %copy-start.12 = (f32[1024,256]{1,0:T(8,128)S(1)}, f32[1024,256]{1,0:T(8,128)}, u32[]{:S(2)}) copy-start(f32[1024,256]{1,0:T(8,128)} %get-tuple-element.84) | copy-start | bytes 3145732
  510.7 185.3 %all-gather.37.cloned.1.call-start = ((), (), s32[]{:S(2)}) async-start(), calls=%async_computation.38 | async-start | bytes 2621440 | tf_op jit(solution)/shard_map/all_gather | solution.py:65
  511.5 231.1 %all-gather.25.cloned.1.call-start = ((), (), s32[]{:S(2)}) async-start(), calls=%async_computation.28 | async-start | bytes 2621440 | tf_op jit(solution)/shard_map/all_gather | solution.py:29
  665.2 132.0 %reduce-scatter.35.cloned.1.call-start = ((), (), s32[]{:S(2)}) async-start(), calls=%async_computation.39 | async-start | bytes 2621440 | tf_op jit(solution)/shard_map/reduce_scatter | solution.py:54
  755.9 89.3 %all-gather.43.cloned.1.call-start = ((), (), s32[]{:S(2)}) async-start(), calls=%async_computation.46 | async-start | bytes 2621440 | tf_op jit(solution)/shard_map/all_gather | solution.py:65
  756.5 135.3 %all-gather.35.cloned.1.call-start = ((), (), s32[]{:S(2)}) async-start(), calls=%async_computation.36 | async-start | bytes 2621440 | tf_op jit(solution)/shard_map/all_gather | solution.py:29
  800.7 145.7 %reduce-scatter.45.cloned.1.call-start = ((), (), s32[]{:S(2)}) async-start(), calls=%async_computation.47 | async-start | bytes 2621440 | tf_op jit(solution)/shard_map/reduce_scatter | solution.py:54
  905.2 122.5 %reduce-scatter.27.cloned.1.call-start = ((), (), s32[]{:S(2)}) async-start(), calls=%async_computation.29 | async-start | bytes 5242880 | tf_op jit(solution)/shard_map/reduce_scatter | solution.py:61
  913.6 193.5 %reduce-scatter.33.cloned.1.call-start = ((), (), s32[]{:S(2)}) async-start(), calls=%async_computation.37 | async-start | bytes 5242880 | tf_op jit(solution)/shard_map/reduce_scatter | solution.py:61
  920.5 186.6 %copy-start.15 = (f32[1024,256]{1,0:T(8,128)S(1)}, f32[1024,256]{1,0:T(8,128)}, u32[]{:S(2)}) copy-start(f32[1024,256]{1,0:T(8,128)} %get-tuple-element.82) | copy-start | bytes 3145732
  920.5 237.6 %all-gather.45.cloned.1.call-start = ((), (), s32[]{:S(2)}) async-start(), calls=%async_computation.48 | async-start | bytes 2621440 | tf_op jit(solution)/shard_map/all_gather | solution.py:65
  1112.7 91.4 %all-gather.39.cloned.1.call-start = ((), (), s32[]{:S(2)}) async-start(), calls=%async_computation.40 | async-start | bytes 2621440 | tf_op jit(solution)/shard_map/all_gather | solution.py:65
  1113.5 128.2 %reduce-scatter.47.cloned.1.call-start = ((), (), s32[]{:S(2)}) async-start(), calls=%async_computation.49 | async-start | bytes 1572864 | tf_op jit(solution)/shard_map/reduce_scatter | solution.py:315
  1117.3 40.7 %copy-start.59 = (bf16[256,1024]{1,0:T(8,128)(2,1)S(1)}, bf16[256,1024]{1,0:T(8,128)(2,1)}, u32[]{:S(2)}) copy-start(bf16[256,1024]{1,0:T(8,128)(2,1)} %param.23) | copy-start | bytes 1572868
  1179.0 69.9 %reduce-scatter.49.cloned.1.call-start = ((), (), s32[]{:S(2)}) async-start(), calls=%async_computation.50 | async-start | bytes 1572864 | tf_op jit(solution)/shard_map/reduce_scatter | solution.py:323
  1188.3 83.2 %reduce-scatter.37.cloned.1.call-start = ((), (), s32[]{:S(2)}) async-start(), calls=%async_computation.41 | async-start | bytes 1572864 | tf_op jit(solution)/shard_map/reduce_scatter | solution.py:315
  1225.0 69.0 %reduce-scatter.39.cloned.1.call-start = ((), (), s32[]{:S(2)}) async-start(), calls=%async_computation.42 | async-start | bytes 1572864 | tf_op jit(solution)/shard_map/reduce_scatter | solution.py:323
  1234.1 103.6 %reduce-scatter.51.cloned.1.call-start = ((), (), s32[]{:S(2)}) async-start(), calls=%async_computation.51 | async-start | bytes 2621440 | tf_op jit(solution)/shard_map/reduce_scatter | solution.py:54
  1255.6 128.3 %reduce-scatter.41.cloned.1.call-start = ((), (), s32[]{:S(2)}) async-start(), calls=%async_computation.43 | async-start | bytes 2621440 | tf_op jit(solution)/shard_map/reduce_scatter | solution.py:54
  1263.8 36.9 %copy-start.81 = (bf16[1,1024,256]{2,1,0:T(8,128)(2,1)}, bf16[1,1024,256]{2,1,0:T(8,128)(2,1)S(1)}, u32[]{:S(2)}) copy-start(bf16[1,1024,256]{2,1,0:T(8,128)(2,1)S(1)} %reshape.519) | copy-start | bytes 1572868
  1300.7 83.2 %copy-start.13 = (f32[1024,256]{1,0:T(8,128)S(1)}, f32[1024,256]{1,0:T(8,128)}, u32[]{:S(2)}) copy-start(f32[1024,256]{1,0:T(8,128)} %get-tuple-element.108) | copy-start | bytes 3145732
  1300.7 98.5 %copy-start.46 = (f32[1024,256]{1,0:T(8,128)S(1)}, f32[1024,256]{1,0:T(8,128)}, u32[]{:S(2)}) copy-start(f32[1024,256]{1,0:T(8,128)} %get-tuple-element.79) | copy-start | bytes 3145732
  1300.7 153.1 %all-gather.47.cloned.1.call-start = ((), (), s32[]{:S(2)}) async-start(), calls=%async_computation.52 | async-start | bytes 2621440 | tf_op jit(solution)/shard_map/all_gather | solution.py:65
  1404.1 96.2 %all-gather.41.cloned.1.call-start = ((), (), s32[]{:S(2)}) async-start(), calls=%async_computation.44 | async-start | bytes 2621440 | tf_op jit(solution)/shard_map/all_gather | solution.py:65
  1404.7 168.5 %reduce-scatter.53.cloned.1.call-start = ((), (), s32[]{:S(2)}) async-start(), calls=%async_computation.53 | async-start | bytes 2621440 | tf_op jit(solution)/shard_map/reduce_scatter | solution.py:54
  1476.6 113.4 %reduce-scatter.43.cloned.1.call-start = ((), (), s32[]{:S(2)}) async-start(), calls=%async_computation.45 | async-start | bytes 2621440 | tf_op jit(solution)/shard_map/reduce_scatter | solution.py:54
  1522.8 124.3 %reduce-scatter.65.cloned.1.call-start = ((), (), s32[]{:S(2)}) async-start(), calls=%async_computation.59 | async-start | bytes 4718592 | tf_op jit(solution)/shard_map/reduce_scatter | solution.py:86
  1534.4 168.4 %reduce-scatter.63.cloned.1.call-start = ((), (), s32[]{:S(2)}) async-start(), calls=%async_computation.58 | async-start | bytes 4718592 | tf_op jit(solution)/shard_map/reduce_scatter | solution.py:85
  1544.8 197.7 %reduce-scatter.61.cloned.1.call-start = ((), (), s32[]{:S(2)}) async-start(), calls=%async_computation.57 | async-start | bytes 1179648 | tf_op jit(solution)/shard_map/reduce_scatter | solution.py:84
  1550.1 242.6 %reduce-scatter.59.cloned.1.call-start = ((), (), s32[]{:S(2)}) async-start(), calls=%async_computation.56 | async-start | bytes 3538944 | tf_op jit(solution)/shard_map/reduce_scatter | solution.py:83
  1557.7 274.8 %reduce-scatter.57.cloned.1.call-start = ((), (), s32[]{:S(2)}) async-start(), calls=%async_computation.55 | async-start | bytes 1179648 | tf_op jit(solution)/shard_map/reduce_scatter | solution.py:82
  1562.9 320.3 %reduce-scatter.55.cloned.1.call-start = ((), (), s32[]{:S(2)}) async-start(), calls=%async_computation.54 | async-start | bytes 3538944 | tf_op jit(solution)/shard_map/reduce_scatter | solution.py:81
  1629.2 254.0 %copy-start.1 = (bf16[1024,1024]{1,0:T(8,128)(2,1)S(1)}, bf16[1024,1024]{1,0:T(8,128)(2,1)}, u32[]{:S(2)}) copy-start(bf16[1024,1024]{1,0:T(8,128)(2,1)} %param.24) | copy-start | bytes 6291460
  (119 other events, 699.2 us)
Sparse Core Ops, SparseCore 0:
  29.8 49.9 all-gather.26
  82.0 44.4 all-gather.16
  128.8 76.4 reduce-scatter.28
  207.6 77.2 reduce-scatter.22
  303.1 49.6 all-gather.28
  354.8 44.4 all-gather.18
  400.8 20.9 all-gather.32
  423.4 21.2 all-gather.30
  446.3 21.2 all-gather.22
  469.0 21.2 all-gather.20
  492.7 76.8 reduce-scatter.30
  571.8 77.2 reduce-scatter.24
  650.6 45.3 all-gather.36
  698.0 44.4 all-gather.24
  756.0 41.1 reduce-scatter.34
  798.7 46.4 all-gather.42
  847.3 44.4 all-gather.34
  905.3 41.1 reduce-scatter.44
  948.8 78.8 reduce-scatter.26
  1029.9 77.0 reduce-scatter.32
  1112.8 45.2 all-gather.44
  1159.6 44.4 all-gather.38
  1206.4 19.9 reduce-scatter.46
  1228.6 20.3 reduce-scatter.48
  1251.2 20.3 reduce-scatter.36
  1273.7 20.3 reduce-scatter.38
  1296.2 41.4 reduce-scatter.50
  1340.7 43.1 reduce-scatter.40
  1404.2 49.5 all-gather.46
  1455.8 44.4 all-gather.40
  1502.6 41.1 reduce-scatter.52
  1546.7 43.1 reduce-scatter.42
  1593.7 53.3 reduce-scatter.64
  1651.5 51.3 reduce-scatter.62
  1706.6 35.8 reduce-scatter.60
  1746.3 46.3 reduce-scatter.58
  1796.6 35.9 reduce-scatter.56
  1836.9 46.3 reduce-scatter.54
where the time goes:
time: 1900 us; the launch traced here: 1890 us
  waiting for transfers between devices  1360 us (72%)
  matrix products  184 us (10%)
  local copies, waits for them, and re-layouts  169 us (9%)
  blocking collectives  91.6 us (5%)
  other arithmetic  64.5 us (3%)
    reduce_scatter x6, waiting for transfers between devices, branch_out(): return lax.psum_scatter(partial_rows, 'mp', scatter_dimension=1, tiled=True)  414 us
    all_gather x6, waiting for transfers between devices, norm_forward_pass(): normalized_rows = lax.all_gather(shard_rows, 'mp', axis=1, tiled=True)  244 us
    all_gather x6, waiting for transfers between devices, branch_back(): lax.all_gather(grad_resid.astype(jnp.bfloat16), 'mp', axis=1, tiled=True)  192 us
    reduce_scatter x6, waiting for transfers between devices, sum_features(): lax.psum_scatter(grad_full.astype(jnp.bfloat16), 'mp', scatter_dimension=...  166 us
    reduce_scatter x1, waiting for transfers between devices, reduce_grads(): lax.psum_scatter(local_grads[4], ('tm', 'clip'), scatter_dimension=0, til...  55.7 us
    reduce_scatter x1, waiting for transfers between devices, reduce_grads(): lax.psum_scatter(local_grads[0], ('tm', 'clip'), scatter_dimension=0, til...  50.7 us
    reduce_scatter x1, waiting for transfers between devices, reduce_grads(): lax.psum_scatter(local_grads[2], ('tm', 'clip'), scatter_dimension=0, til...  50.1 us
    another operation x16, local copies, waits for them, and re-layouts  49.7 us
  transfers between devices with their start and end apart: 38, of which 35 were waited for; matrix products, arithmetic and copies ran while one was open for 18% of the time, Pallas kernels for 0%

commit v1 on v0

--- a/solution.py
+++ b/solution.py
@@ -3,6 +3,8 @@
 import jax
 import jax.numpy as jnp
 from jax import lax
+from jax.experimental import pallas as pl
+from jax.experimental.pallas import tpu as pltpu
 from jax.sharding import PartitionSpec as P
 
 HEAD_DIM = 64
@@ -401,9 +403,486 @@
     )
 
 
+AXES = ("tm", "clip", "mp")
+F32 = jnp.float32
+BF16 = jnp.bfloat16
+BLK = 256
+
+
+def device_pairs(move):
+    pairs = []
+    for y in range(2):
+        for x in range(2):
+            for c in range(2):
+                for z in range(4):
+                    there = move(y, x, c, z)
+                    pairs.append(tuple((q[0] * 4 + q[1] * 2 + q[2]) * 4 + q[3] for q in ((y, x, c, z), there)))
+    return pairs
+
+
+def hop_y(v):
+    return lax.ppermute(v, AXES, device_pairs(lambda y, x, c, z: (1 - y, x, c, z)))
+
+
+def hop_x(v):
+    return lax.ppermute(v, AXES, device_pairs(lambda y, x, c, z: (y, 1 - x, c, z)))
+
+
+def hop_c(v):
+    return lax.ppermute(v, AXES, device_pairs(lambda y, x, c, z: (y, x, 1 - c, z)))
+
+
+def hop_z(v, shift):
+    return lax.ppermute(v, AXES, device_pairs(lambda y, x, c, z: (y, x, c, (z + shift) % 4)))
+
+
+def spread_pairs(r):
+    def move(y, x, c, z):
+        k = z ^ r
+        return (y, x, k & 1, 2 * c + (k >> 1))
+
+    return device_pairs(move)
+
+
+def dot_nn(a, b):
+    return lax.dot_general(a, b, (((1,), (0,)), ((), ())), preferred_element_type=F32)
+
+
+def dot_nt(a, b):
+    return lax.dot_general(a, b, (((1,), (1,)), ((), ())), preferred_element_type=F32)
+
+
+def dot_tn(a, b):
+    return lax.dot_general(a, b, (((0,), (0,)), ((), ())), preferred_element_type=F32)
+
+
+def attention_probs(q, k, bias, scale):
+    scores = dot_nt(q, k) * scale
+    if bias is not None:
+        scores = scores + bias
+    exponent = jnp.exp(scores - jnp.max(scores, axis=-1, keepdims=True))
+    return exponent / jnp.sum(exponent, axis=-1, keepdims=True)
+
+
+def attend_kernel(heads, scale, qkv_ref, bias_ref, out_ref):
+    width = heads * HEAD_DIM
+    bias = None if bias_ref is None else bias_ref[...]
+    rows = qkv_ref.size // (3 * width)
+
+    def load(part, h):
+        lo = part * width + h * HEAD_DIM
+        if len(qkv_ref.shape) == 2:
+            return qkv_ref[:, lo : lo + HEAD_DIM]
+        return qkv_ref[:, :, lo : lo + HEAD_DIM].astype(F32).reshape(rows, HEAD_DIM).astype(BF16)
+
+    done = []
+    for h in range(heads):
+        p = attention_probs(load(0, h), load(1, h), bias, scale)
+        done.append(dot_nn(p.astype(BF16), load(2, h)))
+    out = jnp.concatenate(done, axis=1)
+    if len(out_ref.shape) == 2:
+        out_ref[...] = out.astype(BF16)
+    else:
+        out_ref[...] = out.reshape(out_ref.shape).astype(BF16)
+
+
+def attend_back_kernel(heads, scale, qkv_ref, grad_ref, bias_ref, out_ref):
+    width = heads * HEAD_DIM
+    bias = None if bias_ref is None else bias_ref[...]
+    rows = qkv_ref.size // (3 * width)
+
+    def load(ref, lo):
+        if len(ref.shape) == 2:
+            return ref[:, lo : lo + HEAD_DIM]
+        return ref[:, :, lo : lo + HEAD_DIM].astype(F32).reshape(rows, HEAD_DIM).astype(BF16)
+
+    parts = ([], [], [])
+    for h in range(heads):
+        q = load(qkv_ref, h * HEAD_DIM)
+        k = load(qkv_ref, width + h * HEAD_DIM)
+        v = load(qkv_ref, 2 * width + h * HEAD_DIM)
+        g = load(grad_ref, h * HEAD_DIM)
+        p = attention_probs(q, k, bias, scale)
+        dp = dot_nt(g, v)
+        ds = (p * (dp - jnp.sum(p * dp, axis=-1, keepdims=True))).astype(BF16)
+        parts[0].append(dot_nn(ds, k) * scale)
+        parts[1].append(dot_tn(ds, q) * scale)
+        parts[2].append(dot_tn(p.astype(BF16), g))
+    out = jnp.concatenate(parts[0] + parts[1] + parts[2], axis=1)
+    if len(out_ref.shape) == 2:
+        out_ref[...] = out.astype(BF16)
+    else:
+        out_ref[...] = out.reshape(out_ref.shape).astype(BF16)
+
+
+def attention_cost(groups, rows, heads, products):
+    return pl.CostEstimate(
+        flops=2 * products * groups * heads * rows * rows * HEAD_DIM,
+        transcendentals=groups * heads * rows * rows,
+        bytes_accessed=2 * groups * rows * heads * HEAD_DIM * 2 * products,
+    )
+
+
+def space_attend(qkv, frames, patches, heads, scale):
+    width = heads * HEAD_DIM
+    return pl.pallas_call(
+        lambda q, o: attend_kernel(heads, scale, q, None, o),
+        grid=(frames,),
+        in_specs=[pl.BlockSpec((patches, 3 * width), lambda i: (i, 0))],
+        out_specs=pl.BlockSpec((patches, width), lambda i: (i, 0)),
+        out_shape=jax.ShapeDtypeStruct((frames * patches, width), BF16),
+        cost_estimate=attention_cost(frames, patches, heads, 2),
+        name="space_attend",
+    )(qkv)
+
+
+def space_attend_back(qkv, grad, frames, patches, heads, scale):
+    width = heads * HEAD_DIM
+    return pl.pallas_call(
+        lambda q, g, o: attend_back_kernel(heads, scale, q, g, None, o),
+        grid=(frames,),
+        in_specs=[
+            pl.BlockSpec((patches, 3 * width), lambda i: (i, 0)),
+            pl.BlockSpec((patches, width), lambda i: (i, 0)),
+        ],
+        out_specs=pl.BlockSpec((patches, 3 * width), lambda i: (i, 0)),
+        out_shape=jax.ShapeDtypeStruct((frames * patches, 3 * width), BF16),
+        cost_estimate=attention_cost(frames, patches, heads, 5),
+        name="space_attend_back",
+    )(qkv, grad)
+
+
+GROUP = 8
+
+
+def time_attend(qkv, bias, frames, patches, heads, scale):
+    width = heads * HEAD_DIM
+    rows = frames * GROUP
+    return pl.pallas_call(
+        lambda q, b, o: attend_kernel(heads, scale, q, b, o),
+        grid=(patches // GROUP,),
+        in_specs=[
+            pl.BlockSpec((frames, GROUP, 3 * width), lambda i: (0, i, 0)),
+            pl.BlockSpec((rows, rows), lambda i: (0, 0)),
+        ],
+        out_specs=pl.BlockSpec((frames, GROUP, width), lambda i: (0, i, 0)),
+        out_shape=jax.ShapeDtypeStruct((frames, patches, width), BF16),
+        cost_estimate=attention_cost(patches // GROUP, rows, heads, 2),
+        name="time_attend",
+    )(qkv.reshape(frames, patches, 3 * width), bias).reshape(frames * patches, width)
+
+
+def time_attend_back(qkv, grad, bias, frames, patches, heads, scale):
+    width = heads * HEAD_DIM
+    rows = frames * GROUP
+    return pl.pallas_call(
+        lambda q, g, b, o: attend_back_kernel(heads, scale, q, g, b, o),
+        grid=(patches // GROUP,),
+        in_specs=[
+            pl.BlockSpec((frames, GROUP, 3 * width), lambda i: (0, i, 0)),
+            pl.BlockSpec((frames, GROUP, width), lambda i: (0, i, 0)),
+            pl.BlockSpec((rows, rows), lambda i: (0, 0)),
+        ],
+        out_specs=pl.BlockSpec((frames, GROUP, 3 * width), lambda i: (0, i, 0)),
+        out_shape=jax.ShapeDtypeStruct((frames, patches, 3 * width), BF16),
+        cost_estimate=attention_cost(patches // GROUP, rows, heads, 5),
+        name="time_attend_back",
+    )(
+        qkv.reshape(frames, patches, 3 * width), grad.reshape(frames, patches, width), bias
+    ).reshape(frames * patches, 3 * width)
+
+
+def norm_rows(resid):
+    mean = jnp.mean(resid, axis=-1, keepdims=True)
+    centered = resid - mean
+    inverse = lax.rsqrt(jnp.mean(centered * centered, axis=-1, keepdims=True) + eps_norm)
+    return (centered * inverse, inverse)
+
+
+def norm_rows_back(grad, standardized, inverse, gain):
+    gain_grad = jnp.sum(grad * standardized, axis=0)
+    inner = grad * gain
+    mean = jnp.mean(inner, axis=-1, keepdims=True)
+    along = jnp.mean(inner * standardized, axis=-1, keepdims=True)
+    return ((inner - mean - standardized * along) * inverse, gain_grad)
+
+
+def swap_y(v):
+    return jnp.concatenate(
+        [v[:, BLK : 2 * BLK], v[:, :BLK], v[:, 3 * BLK :], v[:, 2 * BLK : 3 * BLK]], axis=1
+    )
+
+
+def cols(parts):
+    return jnp.concatenate(parts, axis=1)
+
+
+def rows_of(parts):
+    return jnp.concatenate(parts, axis=0)
+
+
+def token_parallel(
+    tokens,
+    cotangent,
+    ratio,
+    priority,
+    frame_order,
+    mask_embed,
+    gains,
+    qkv_space,
+    out_space,
+    qkv_time,
+    out_time,
+    w_in,
+    w_out,
+):
+    scale = 1.0 / math.sqrt(HEAD_DIM)
+    y = lax.axis_index("tm")
+    x = lax.axis_index("clip") // 2
+    c = lax.axis_index("clip") % 2
+    z = lax.axis_index("mp")
+    patches = tokens.shape[2]
+    width = qkv_space.shape[0]
+    frames_own = tokens.shape[0] * tokens.shape[1] // 4
+    frames_all = frame_order.shape[1]
+    own = frames_own * patches
+    hidden_own = w_in.shape[1] // 2
+    block_at = [2 * (y ^ (i & 1)) + (x ^ (i >> 1)) for i in range(4)]
+
+    def rel_rows(w):
+        return rows_of([lax.dynamic_slice_in_dim(w, b * BLK, BLK, 0) for b in block_at])
+
+    def to_absolute(v):
+        v = jnp.swapaxes(v.reshape(-1, 2, 2, BLK), 1, 2)
+        v = jnp.where(y == 1, v[:, ::-1], v)
+        return jnp.where(x == 1, v[:, :, ::-1], v).reshape(-1, width)
+
+    k_own = 2 * (z % 2) + c
+
+    def gather_rows(v, extra):
+        pieces = v.reshape(4, own, BLK)
+        landed = []
+        for r in range(4):
+            piece = lax.dynamic_index_in_dim(pieces, z ^ r, 0, keepdims=False)
+            if extra is not None:
+                piece = rows_of([piece, extra])
+            landed.append(lax.ppermute(piece, AXES, spread_pairs(r)))
+        landed = jnp.stack(landed)
+        return cols(
+            [lax.dynamic_index_in_dim(landed, k_own ^ b, 0, keepdims=False) for b in block_at]
+        )
+
+    def return_rows(v):
+        pieces = jnp.stack([v[:, i * BLK : (i + 1) * BLK] for i in range(4)])
+        landed = []
+        for r in range(4):
+            block = k_own ^ r
+            place = 2 * ((block % 2) ^ x) + ((block // 2) ^ y)
+            piece = lax.dynamic_index_in_dim(pieces, place, 0, keepdims=False)
+            landed.append(lax.ppermute(piece, AXES, [(b, a) for a, b in spread_pairs(r)]))
+        landed = jnp.stack(landed)
+        return jnp.stack(
+            [lax.dynamic_index_in_dim(landed, k ^ z, 0, keepdims=False) for k in range(4)]
+        ).reshape(tokens.shape)
+
+    vectors = rows_of([mask_embed[None], gains, jnp.zeros((4, BLK), BF16)])
+    arrived = gather_rows(tokens, vectors)
+    source = arrived[:own].astype(F32)
+    embed_row = arrived[own : own + 1].astype(F32)
+    gain = [arrived[own + 1 + i : own + 2 + i].astype(F32) for i in range(3)]
+    upstream = gather_rows(cotangent, None)
+
+    masked_here = (priority < ratio[:, None, None]).astype(jnp.int32).reshape(2, -1)
+    info = cols([masked_here, frame_order])
+    info = jnp.where(z // 2 == c, info, hop_c(info))
+    info = lax.dynamic_index_in_dim(info, z % 2, 0, keepdims=False)
+    masked = lax.dynamic_slice_in_dim(info, c * own, own, 0)[:, None] != 0
+    order = info[2 * own :].reshape(2, 2, frames_own)
+    order = jnp.where(y == 1, order[::-1], order)
+    order = jnp.where(c == 1, order[:, ::-1], order).swapaxes(0, 1).reshape(frames_all)
+    order = jnp.repeat(order, GROUP)
+    patch = jnp.arange(frames_all * GROUP) % GROUP
+    visible = (order[None, :] <= order[:, None]) & (patch[None, :] == patch[:, None])
+    bias = jnp.where(visible, 0.0, -1e30).astype(F32)
+
+    def fetch(mine):
+        landed = cols([hop_z(mine, -r) for r in (1, 2, 3)])
+        return landed
+
+    half = qkv_space.shape[2] // 2
+    sp_qkv = rel_rows(lax.dynamic_slice_in_dim(qkv_space, c * half, half, 2))
+    sp_out = rel_rows(lax.dynamic_slice_in_dim(out_space, c * half, half, 0).T)
+    sp_own = cols([sp_qkv.reshape(width, -1), sp_out])
+    sp_far = fetch(sp_own[:BLK])
+    sp_far = rows_of([sp_far, hop_y(sp_far)])
+    sp_far = rows_of([sp_far, hop_x(sp_far)])
+    sp_all = [sp_own] + [sp_far[:, r * 4 * half : (r + 1) * 4 * half] for r in range(3)]
+    ws_qkv = cols([w[:, j * half : (j + 1) * half] for j in range(3) for w in sp_all])
+    ws_out = cols([w[:, 3 * half :] for w in sp_all])
+
+    head = (2 * y + c) * HEAD_DIM
+    ti_qkv = rel_rows(lax.dynamic_slice_in_dim(qkv_time, head, HEAD_DIM, 2))
+    ti_out = rel_rows(lax.dynamic_slice_in_dim(out_time, head, HEAD_DIM, 0).T)
+    ti_own = cols([ti_qkv.reshape(width, -1), ti_out])
+    ti_far = fetch(ti_own[: 2 * BLK])
+    ti_far = rows_of([ti_far, hop_x(ti_far)])
+    ti_all = [ti_own] + [ti_far[:, r * 4 * HEAD_DIM : (r + 1) * 4 * HEAD_DIM] for r in range(3)]
+    wt_qkv = cols([w[:, j * HEAD_DIM : (j + 1) * HEAD_DIM] for j in range(3) for w in ti_all])
+    wt_out = cols([w[:, 3 * HEAD_DIM :] for w in ti_all])
+
+    ff_in = rel_rows(lax.dynamic_slice_in_dim(w_in, c * hidden_own, hidden_own, 1))
+    ff_out = rel_rows(lax.dynamic_slice_in_dim(w_out, c * hidden_own, hidden_own, 0).T)
+    far = []
+    for w in (ff_in, ff_out):
+        w_far = fetch(w[:BLK])
+        w_far = rows_of([w_far, hop_y(w_far)])
+        w_far = rows_of([w_far, hop_x(w_far)])
+        far.append(cols([w, w_far]))
+    wf_in, wf_out = far
+
+    def pair_gather(v):
+        return rows_of([v, hop_c(v)])
+
+    def pair_scatter(v):
+        return v[:own] + hop_c(v[own:].astype(BF16)).astype(F32)
+
+    def quad_gather(v):
+        both = rows_of([v, hop_y(swap_y(v))])
+        return rows_of([both, hop_c(both)])
+
+    def quad_scatter(v):
+        both = v[: 2 * own] + hop_c(v[2 * own :].astype(BF16)).astype(F32)
+        return both[:own] + hop_y(swap_y(both[own:].astype(BF16))).astype(F32)
+
+    heads_s = 4 * half // HEAD_DIM
+    heads_t = 4
+    frames_pair = 2 * frames_own
+    resid0 = jnp.where(masked, embed_row, source)
+    std0, inv0 = norm_rows(resid0)
+    normed0 = pair_gather((std0 * gain[0]).astype(BF16))
+    joined0 = dot_nn(normed0, ws_qkv).astype(BF16)
+    mixed0 = space_attend(joined0, frames_pair, patches, heads_s, scale)
+    resid1 = resid0 + pair_scatter(dot_nt(mixed0, ws_out))
+    std1, inv1 = norm_rows(resid1)
+    normed1 = quad_gather((std1 * gain[1]).astype(BF16))
+    joined1 = dot_nn(normed1, wt_qkv).astype(BF16)
+    mixed1 = time_attend(joined1, bias, frames_all, patches, heads_t, scale)
+    resid2 = resid1 + quad_scatter(dot_nt(mixed1, wt_out))
+    std2, inv2 = norm_rows(resid2)
+    normed2 = pair_gather((std2 * gain[2]).astype(BF16))
+    inner = dot_nn(normed2, wf_in)
+    activated, gelu_pull = jax.vjp(gelu_tanh, inner)
+    hidden = activated.astype(BF16)
+    block_out = return_rows((resid2 + pair_scatter(dot_nt(hidden, wf_out))).astype(BF16))
+
+    def reduce_plane(lhs, rhs):
+        sent = hop_x(dot_tn(lhs[:, 2 * BLK :], rhs).astype(BF16))
+        kept = dot_tn(lhs[:, : 2 * BLK], rhs) + sent.astype(F32)
+        return kept
+
+    def reduce_y(kept):
+        return kept[:BLK] + hop_y(kept[BLK:].astype(BF16)).astype(F32)
+
+    def reduce_z(pieces):
+        total = pieces[0]
+        for r in (1, 2, 3):
+            total = total + hop_z(pieces[r].astype(BF16), r).astype(F32)
+        return total
+
+    def swap_c(total):
+        rows = BLK // 2
+        kept = lax.dynamic_slice_in_dim(total, c * rows, rows, 0)
+        sent = hop_c(lax.dynamic_slice_in_dim(total, (1 - c) * rows, rows, 0).astype(BF16))
+        return (kept, sent.astype(F32))
+
+    def by_core(kept, landed):
+        return jnp.where(c == 0, jnp.concatenate([kept, landed], -1), jnp.concatenate([landed, kept], -1))
+
+    grad3 = jnp.where(masked, upstream, jnp.zeros((), BF16))
+    gb3 = pair_gather(grad3)
+    grad_inner = gelu_pull(dot_nn(gb3, wf_out))[0].astype(BF16)
+    g_w_out = reduce_y(reduce_plane(gb3, hidden))
+    g_w_out = reduce_z([g_w_out[:, r * hidden_own : (r + 1) * hidden_own] for r in range(4)])
+    g_w_in = reduce_y(reduce_plane(normed2, grad_inner))
+    g_w_in = reduce_z([g_w_in[:, r * hidden_own : (r + 1) * hidden_own] for r in range(4)])
+    back2, gain_grad2 = norm_rows_back(pair_scatter(dot_nt(grad_inner, wf_in)), std2, inv2, gain[2])
+    grad2 = grad3.astype(F32) + back2
+
+    gb2 = quad_gather(grad2.astype(BF16))
+    dmixed1 = dot_nn(gb2, wt_out).astype(BF16)
+    djoined1 = time_attend_back(joined1, dmixed1, bias, frames_all, patches, heads_t, scale)
+    g_t_out = reduce_plane(gb2, mixed1)
+    g_t_qkv = reduce_plane(normed1, djoined1)
+    span = heads_t * HEAD_DIM
+    g_time = reduce_z(
+        [
+            cols(
+                [g_t_qkv[:, j * span + r * HEAD_DIM : j * span + (r + 1) * HEAD_DIM] for j in range(3)]
+                + [g_t_out[:, r * HEAD_DIM : (r + 1) * HEAD_DIM]]
+            )
+            for r in range(4)
+        ]
+    )
+    back1, gain_grad1 = norm_rows_back(quad_scatter(dot_nt(djoined1, wt_qkv)), std1, inv1, gain[1])
+    grad1 = grad2 + back1
+
+    gb1 = pair_gather(grad1.astype(BF16))
+    dmixed0 = dot_nn(gb1, ws_out).astype(BF16)
+    djoined0 = space_attend_back(joined0, dmixed0, frames_pair, patches, heads_s, scale)
+    g_s_out = reduce_y(reduce_plane(gb1, mixed0))
+    g_s_qkv = reduce_y(reduce_plane(normed0, djoined0))
+    span = 4 * half
+    g_space = reduce_z(
+        [
+            cols(
+                [g_s_qkv[:, j * span + r * half : j * span + (r + 1) * half] for j in range(3)]
+                + [g_s_out[:, r * half : (r + 1) * half]]
+            )
+            for r in range(4)
+        ]
+    )
+    back0, gain_grad0 = norm_rows_back(pair_scatter(dot_nt(djoined0, ws_qkv)), std0, inv0, gain[0])
+    grad0 = grad1 + back0
+    grad_tokens = return_rows(jnp.where(masked, 0.0, grad0).astype(BF16)).astype(F32)
+    grad_embed = jnp.sum(jnp.where(masked, grad0, 0.0), axis=0)
+    small = lax.psum(to_absolute(jnp.stack([gain_grad0, gain_grad1, gain_grad2, grad_embed])), AXES)
+    small = lax.dynamic_slice_in_dim(small, z * BLK, BLK, 1)
+
+    rows = BLK // 2
+    kept, landed = swap_c(g_space)
+    grad_qkv_space = by_core(
+        kept[:, : 3 * half].reshape(rows, 3, half), landed[:, : 3 * half].reshape(rows, 3, half)
+    )
+    grad_out_space = by_core(kept[:, 3 * half :], landed[:, 3 * half :]).T
+    kept, landed = swap_c(cols([g_w_in, g_w_out]))
+    grad_w_in = by_core(kept[:, :hidden_own], landed[:, :hidden_own])
+    grad_w_out = by_core(kept[:, hidden_own:], landed[:, hidden_own:]).T
+    both = cols([g_time[:BLK], hop_y(g_time[BLK:].astype(BF16)).astype(F32)])
+    kept, landed = swap_c(both)
+    quad = jnp.stack([kept, landed], 1).reshape(rows, 2, 2, 4, HEAD_DIM)
+    quad = jnp.where(c == 1, quad[:, ::-1], quad)
+    quad = jnp.where(y == 1, quad[:, :, ::-1], quad)
+    quad = jnp.transpose(quad, (0, 3, 2, 1, 4)).reshape(rows, 4, 4 * HEAD_DIM)
+    grad_qkv_time = quad[:, :3]
+    grad_out_time = quad[:, 3].T
+    return (
+        block_out,
+        grad_tokens,
+        small[3],
+        small[:3],
+        grad_qkv_space,
+        grad_out_space,
+        grad_qkv_time,
+        grad_out_time,
+        grad_w_in,
+        grad_w_out,
+    )
+
+
 def solution(mesh):
+    sizes = (mesh.shape["tm"], mesh.shape["clip"], mesh.shape["mp"])
     return jax.shard_map(
-        shards,
+        token_parallel if sizes == (2, 4, 4) else shards,
         mesh=mesh,
         in_specs=(
             P("clip", "tm", None, "mp"),

time: 1900 us -> 872 us (0.46)
  waiting for transfers between devices: 1360 us -> 323 us
  Pallas kernels: 0 us -> 120 us
  starting transfers between devices: 4.7 us -> 120 us
  local copies, waits for them, and re-layouts: 169 us -> 62.6 us
  matrix products: 184 us -> 118 us
  blocking collectives: 91.6 us -> 51.2 us
    reduce_scatter x22 -> x0, waiting for transfers between devices: 867 us -> none  [the longest x6 414 us: branch_out(): return lax.psum_scatter(partial_rows, 'mp', scatter_dimension=1, tiled=True)]
    all_gather x16 -> x0, waiting for transfers between devices: 488 us -> none  [the longest x6 244 us: norm_forward_pass(): normalized_rows = lax.all_gather(shard_rows, 'mp', axis=1, tiled=True)]
    ppermute x0 -> x78, waiting for transfers between devices: none -> 323 us  [the longest x10 151 us: hop_x(): lax.ppermute(v, AXES, device_pairs(lambda y, x, c, z: (y, 1 - x, c, z)))]
    ppermute x0 -> x78, starting transfers between devices: none -> 120 us  [the longest x24 36.6 us: hop_z(): lax.ppermute(v, AXES, device_pairs(lambda y, x, c, z: (y, x, c, (z + shif...]
    pallas_call x0 -> x4, Pallas kernels: none -> 120 us  [the longest x1 35 us: time_attend_back(): pl.pallas_call(lambda q, g, b, o: attend_back_kernel(heads, scale, q, g,...]
    another operation x46 -> x7, local copies, waits for them, and re-layouts: 89.5 us -> 3.41 us  [the longest x4 3.18 us: token_parallel(): jnp.stack([gain_grad0, gain_grad1, gain_grad2, grad_embed])]
    dot_general x60 -> x24, matrix products: 184 us -> 118 us  [the longest x6 50.9 us: dot_nn(): lax.dot_general(a, b, (((1,), (0,)), ((), ())), preferred_element_type=F32)]
    psum x7 -> x1, blocking collectives: 91.6 us -> 51.2 us  [token_parallel(): lax.psum(to_absolute(jnp.stack([gain_grad0, gain_grad1, gain_grad2, grad_...]
  transfers between devices with their start and end apart: 38 -> 78, of which waited for: 35 -> 33; matrix products, arithmetic and copies ran while one was open for 18% -> 17% of each run, Pallas kernels for 0% -> 0%
where the time goes in v1:
time: 872 us; the launch traced here: 867 us
  waiting for transfers between devices  323 us (37%)
  starting transfers between devices  120 us (14%)
  Pallas kernels  120 us (14%)
  matrix products  118 us (14%)
  other arithmetic  68.3 us (8%)
  local copies, waits for them, and re-layouts  62.6 us (7%)
  blocking collectives  51.2 us (6%)
    ppermute x10, waiting for transfers between devices, hop_x(): lax.ppermute(v, AXES, device_pairs(lambda y, x, c, z: (y, 1 - x, c, z)))  151 us
    ppermute x24, waiting for transfers between devices, hop_z(): lax.ppermute(v, AXES, device_pairs(lambda y, x, c, z: (y, x, c, (z + shif...  132 us
    psum x1, blocking collectives, token_parallel(): lax.psum(to_absolute(jnp.stack([gain_grad0, gain_grad1, gain_grad2, grad_...  51.2 us
    dot_general x6, matrix products, dot_nn(): lax.dot_general(a, b, (((1,), (0,)), ((), ())), preferred_element_type=F32)  50.9 us
    ppermute x24, starting transfers between devices, hop_z(): lax.ppermute(v, AXES, device_pairs(lambda y, x, c, z: (y, x, c, (z + shif...  36.6 us
    pallas_call x1, Pallas kernels, time_attend_back(): pl.pallas_call(lambda q, g, b, o: attend_back_kernel(heads, scale, q, g,...  35 us
    dot_general x6, matrix products, dot_nt(): lax.dot_general(a, b, (((1,), (1,)), ((), ())), preferred_element_type=F32)  34.7 us
    pallas_call x1, Pallas kernels, space_attend_back(): pl.pallas_call(lambda q, g, o: attend_back_kernel(heads, scale, q, g, Non...  33.4 us
  transfers between devices with their start and end apart: 78, of which 33 were waited for; matrix products, arithmetic and copies ran while one was open for 17% of the time, Pallas kernels for 0%

profile of v1, /device:TPU:9, one launch (start us, length us, event | category | flops | bytes accessed | tf_op | source)
XLA Modules:
  0.0 866.8 jit_solution(4542834897295582362)
XLA Ops:
  12.7 16.0 %collective-permute-done.6 = bf16[256,512]{0,1:T(8,128)(2,1)} collective-permute-done((bf16[256,512]{0,1:T(8,128)(2,1)S(1)}, bf16[256,512]{0,1:T(8,128)(2,1)}, u32[]{:S(2)}, u32[]{:S(2)}) %collective-permute-start.6) | collective-permute-done | bytes 262176 | tf_op jit(solution)/shard_map/ppermute | solution.py:436
  32.5 4.1 collective-permute-start.1
  38.7 5.1 collective-permute-start.4
  48.7 7.4 collective-permute-done.2
  63.7 17.6 %collective-permute-done.10 = bf16[512,1536]{0,1:T(8,128)(2,1)S(1)} collective-permute-done((bf16[512,1536]{0,1:T(8,128)(2,1)S(1)}, bf16[512,1536]{0,1:T(8,128)(2,1)S(1)}, u32[]{:S(2)}, u32[]{:S(2)}) %collective-permute-start.10) | collective-permute-done | bytes 1572896 | tf_op jit(solution)/shard_map/ppermute | solution.py:428
  84.2 4.9 convolution_convert_fusion.q
  89.1 24.9 %space_attend.1 = bf16[1024,512]{1,0:T(8,128)(2,1)} custom-call(bf16[1024,1536]{1,0:T(8,128)(2,1)} %convolution_convert_fusion.q), custom_call_target="tpu_custom_call" | custom-call | flops 268435456 | bytes 4194304 | tf_op jit(solution)/shard_map/space_attend/pallas_call | solution.py:528
  132.0 4.4 collective-permute-start.14
  138.1 20.0 %collective-permute-done.14 = bf16[512,256]{0,1:T(8,128)(2,1)S(1)} collective-permute-done((bf16[512,256]{0,1:T(8,128)(2,1)S(1)}, bf16[512,256]{0,1:T(8,128)(2,1)S(1)}, u32[]{:S(2)}, u32[]{:S(2)}) %collective-permute-start.14) | collective-permute-done | bytes 262176 | tf_op jit(solution)/shard_map/ppermute | solution.py:436
  164.0 12.8 %collective-permute-done.17 = bf16[512,768]{0,1:T(8,128)(2,1)S(1)} collective-permute-done((bf16[512,768]{0,1:T(8,128)(2,1)S(1)}, bf16[512,768]{0,1:T(8,128)(2,1)S(1)}, u32[]{:S(2)}, u32[]{:S(2)}) %collective-permute-start.17) | collective-permute-done | bytes 786464 | tf_op jit(solution)/shard_map/ppermute | solution.py:428
  185.7 7.0 convolution_convert_fusion.1
  192.7 26.5 %time_attend.1 = bf16[16,128,256]{2,1,0:T(8,128)(2,1)} custom-call(bf16[16,128,768]{2,1,0:T(8,128)(2,1)} %bitcast.169, f32[128,128]{1,0:T(8,128)} %and_select_fusion.b), custom_call_target="tpu_custom_call" | custom-call | flops 268435456 | bytes 4194304 | tf_op jit(solution)/shard_map/time_attend/pallas_call | solution.py:561
  230.9 17.5 %collective-permute-done.21 = bf16[256,512]{1,0:T(8,128)(2,1)S(1)} collective-permute-done((bf16[256,512]{1,0:T(8,128)(2,1)S(1)}, bf16[256,512]{1,0:T(8,128)(2,1)S(1)}, u32[]{:S(2)}, u32[]{:S(2)}) %collective-permute-start.21) | collective-permute-done | bytes 262176 | tf_op jit(solution)/shard_map/ppermute | solution.py:436
  249.1 3.7 fusion.122
  256.0 6.8 collective-permute-start.26
  270.4 10.4 %collective-permute-done.27 = bf16[256,512]{0,1:T(8,128)(2,1)S(1)} collective-permute-done((bf16[256,512]{0,1:T(8,128)(2,1)S(1)}, bf16[256,512]{0,1:T(8,128)(2,1)S(1)}, u32[]{:S(2)}, u32[]{:S(2)}) %collective-permute-start.27) | collective-permute-done | bytes 262176 | tf_op jit(solution)/shard_map/ppermute | solution.py:436
  280.8 6.2 collective-permute-start.39
  300.7 4.7 collective-permute-done.38
  305.4 3.7 collective-permute-done.37
  310.5 6.4 collective-permute-done.29
  319.6 12.4 %collective-permute-done.25 = bf16[512,1536]{1,0:T(8,128)(2,1)} collective-permute-done((bf16[512,1536]{1,0:T(8,128)(2,1)}, bf16[512,1536]{1,0:T(8,128)(2,1)}, u32[]{:S(2)}, u32[]{:S(2)}) %collective-permute-start.25) | collective-permute-done | bytes 1572896 | tf_op jit(solution)/shard_map/ppermute | solution.py:428
  332.1 13.7 %multiply_convert_fusion = (bf16[1024,2048]{1,0:T(8,128)(2,1)S(1)}, f32[1024,2048]{1,0:T(8,128)}) fusion(bf16[512,1536]{1,0:T(8,128)(2,1)} %collective-permute-done.25, bf16[256,1536]{1,0:T(8,128)(2,1)S(1)} %copy-done.43, bf16[256,1536]{1,0:T(8,128)(2,1)S(1)} %copy-done.33, bf16[256,512]{1,0:T(8,128)(2,1)S(1)} %copy-done.66, ...), kind=kOutput, calls=%fused_computation.9 | convolution fusion | flops 4347396096 | bytes 18874368 | tf_op jit(solution)/shard_map/dot_general | solution.py:448
  345.8 19.1 %collective-permute-done.30 = bf16[512,1536]{0,1:T(8,128)(2,1)S(1)} collective-permute-done((bf16[512,1536]{0,1:T(8,128)(2,1)S(1)}, bf16[512,1536]{0,1:T(8,128)(2,1)S(1)}, u32[]{:S(2)}, u32[]{:S(2)}) %collective-permute-start.30) | collective-permute-done | bytes 1572896 | tf_op jit(solution)/shard_map/ppermute | solution.py:428
  364.9 6.4 fusion.111
  373.7 16.8 %fusion.6 = bf16[1024,2048]{1,0:T(8,128)(2,1)S(1)} fusion(f32[1024,2048]{1,0:T(8,128)} %get-tuple-element.208, bf16[512,1024]{1,0:T(8,128)(2,1)S(1)} %collective-permute-done.40, bf16[512,1024]{1,0:T(8,128)(2,1)S(1)} %maximum_select_fusion, bf16[512,1536]{0,1:T(8,128)(2,1)} %copy-done.105, bf16[256,1536]{0,1:T(8,128)(2,1)} %collective-permute-done.29, ...), kind=kOutput, calls=%fused_computation.8 | convolution fusion | flops 4370464768 | bytes 18874368 | tf_op jit(solution)/shard_map/dot_general | solution.py:448
  390.6 13.8 %fusion.112 = f32[1024,1024]{1,0:T(8,128)S(1)} fusion(bf16[1024,2048]{1,0:T(8,128)(2,1)S(1)} %fusion.6, bf16[512,1536]{1,0:T(8,128)(2,1)} %collective-permute-done.25, bf16[256,1536]{1,0:T(8,128)(2,1)S(1)} %copy-done.43, bf16[256,1536]{1,0:T(8,128)(2,1)S(1)} %copy-done.33, bf16[256,512]{1,0:T(8,128)(2,1)S(1)} %copy-done.66, ...), kind=kOutput, calls=%fused_computation.388 | convolution fusion | flops 4324327424 | bytes 12582912 | tf_op jit(solution)/shard_map/dot_general | solution.py:452
  408.6 5.0 convolution_convert_fusion.3
  419.5 4.4 collective-permute-start.32
  426.4 28.3 %collective-permute-done.72 = bf16[512,2048]{1,0:T(8,128)(2,1)S(1)} collective-permute-done((bf16[512,2048]{1,0:T(8,128)(2,1)S(1)}, bf16[512,2048]{1,0:T(8,128)(2,1)S(1)}, u32[]{:S(2)}, u32[]{:S(2)}) %collective-permute-start.72) | collective-permute-done | bytes 2097184 | tf_op jit(solution)/shard_map/ppermute | solution.py:428
  465.6 6.8 collective-permute-start.35
  472.5 27.2 %collective-permute-done.67 = bf16[512,2048]{1,0:T(8,128)(2,1)} collective-permute-done((bf16[512,2048]{1,0:T(8,128)(2,1)}, bf16[512,2048]{1,0:T(8,128)(2,1)}, u32[]{:S(2)}, u32[]{:S(2)}) %collective-permute-start.67) | collective-permute-done | bytes 2097184 | tf_op jit(solution)/shard_map/ppermute | solution.py:428
  500.9 5.7 convert_add_fusion.1
  519.2 10.0 %collective-permute-done.68 = bf16[256,2048]{1,0:T(8,128)(2,1)S(1)} collective-permute-done((bf16[256,2048]{1,0:T(8,128)(2,1)S(1)}, bf16[256,2048]{1,0:T(8,128)(2,1)S(1)}, u32[]{:S(2)}, u32[]{:S(2)}) %collective-permute-start.68) | collective-permute-done | bytes 1048608 | tf_op jit(solution)/shard_map/ppermute | solution.py:424
  529.7 4.4 collective-permute-start.69
  540.2 16.7 %collective-permute-done.69 = bf16[256,512]{1,0:T(8,128)(2,1)S(1)} collective-permute-done((bf16[256,512]{1,0:T(8,128)(2,1)S(1)}, bf16[256,512]{1,0:T(8,128)(2,1)S(1)}, u32[]{:S(2)}, u32[]{:S(2)}) %collective-permute-start.69) | collective-permute-done | bytes 262176 | tf_op jit(solution)/shard_map/ppermute | solution.py:436
  562.4 4.9 convolution_convert_fusion.5
  567.4 35.0 %time_attend_back.1 = bf16[16,128,768]{2,1,0:T(8,128)(2,1)} custom-call(bf16[16,128,768]{2,1,0:T(8,128)(2,1)} %bitcast.170, bf16[16,128,256]{2,1,0:T(8,128)(2,1)} %bitcast.188, f32[128,128]{1,0:T(8,128)} %and_select_fusion.b), custom_call_target="tpu_custom_call" | custom-call | flops 671088640 | bytes 10485760 | tf_op jit(solution)/shard_map/time_attend_back/pallas_call | solution.py:578
  602.4 6.1 fusion.144
  615.6 21.3 %collective-permute-done.61 = bf16[512,256]{1,0:T(8,128)(2,1)S(1)} collective-permute-done((bf16[512,256]{1,0:T(8,128)(2,1)S(1)}, bf16[512,256]{1,0:T(8,128)(2,1)S(1)}, u32[]{:S(2)}, u32[]{:S(2)}) %collective-permute-start.61) | collective-permute-done | bytes 262176 | tf_op jit(solution)/shard_map/ppermute | solution.py:428
  649.3 12.3 %collective-permute-done.63 = bf16[512,256]{1,0:T(8,128)(2,1)S(1)} collective-permute-done((bf16[512,256]{1,0:T(8,128)(2,1)S(1)}, bf16[512,256]{1,0:T(8,128)(2,1)S(1)}, u32[]{:S(2)}, u32[]{:S(2)}) %collective-permute-start.63) | collective-permute-done | bytes 262176 | tf_op jit(solution)/shard_map/ppermute | solution.py:436
  661.6 6.7 collective-permute-done.64
  682.0 33.4 %space_attend_back.1 = bf16[1024,1536]{1,0:T(8,128)(2,1)} custom-call(bf16[1024,1536]{1,0:T(8,128)(2,1)} %convolution_convert_fusion.q, bf16[1024,512]{1,0:T(8,128)(2,1)} %fusion.25.g), custom_call_target="tpu_custom_call" | custom-call | flops 671088640 | bytes 10485760 | tf_op jit(solution)/shard_map/space_attend_back/pallas_call | solution.py:541
  747.3 4.1 select_reduce_fusion
  759.1 4.7 collective-permute-start.51
  765.2 9.1 %collective-permute-done.52 = bf16[512,1536]{1,0:T(8,128)(2,1)} collective-permute-done((bf16[512,1536]{1,0:T(8,128)(2,1)}, bf16[512,1536]{1,0:T(8,128)(2,1)}, u32[]{:S(2)}, u32[]{:S(2)}) %collective-permute-start.52) | collective-permute-done | bytes 1572896 | tf_op jit(solution)/shard_map/ppermute | solution.py:428
  780.0 51.2 %psum.7 = f32[4,1024]{1,0:T(4,128)} all-reduce(f32[4,1024]{1,0:T(4,128)S(1)} %reshape.197), channel_id=1, replica_groups=mesh['tm'=2,'clip'=4,'mp'=4] {'tm','clip','mp'}, use_global_device_ids=true, to_apply=%region_16.17 | all-reduce | flops 4096 | bytes 32768 | tf_op jit(solution)/shard_map/psum | solution.py:848
  839.0 14.4 %collective-permute-done.57 = bf16[256,512]{1,0:T(8,128)(2,1)S(1)} collective-permute-done((bf16[256,512]{1,0:T(8,128)(2,1)S(1)}, bf16[256,512]{1,0:T(8,128)(2,1)S(1)}, u32[]{:S(2)}, u32[]{:S(2)}) %collective-permute-start.57) | collective-permute-done | bytes 262176 | tf_op jit(solution)/shard_map/ppermute | solution.py:436
  853.4 6.7 collective-permute-done.58
  (562 shorter events, 252.8 us)
Async XLA Ops:
  4.4 25.2 %collective-permute-start.7 = (bf16[256,512]{0,1:T(8,128)(2,1)S(1)}, bf16[256,512]{0,1:T(8,128)(2,1)S(1)}, u32[]{:S(2)}, u32[]{:S(2)}) collective-permute-start(bf16[256,512]{0,1:T(8,128)(2,1)S(1)} %pad_maximum_fusion.49), channel_id=1, source_target_pairs={{0,2},{1,3},{2,0},{3,1},{4,6},{5,7},{6,4},{7,5},{8,10},{9,11},{10,... | collective-permute-start | bytes 786440 | tf_op jit(solution)/shard_map/ppermute | solution.py:436
  6.8 21.8 %collective-permute-start.6 = (bf16[256,512]{0,1:T(8,128)(2,1)S(1)}, bf16[256,512]{0,1:T(8,128)(2,1)}, u32[]{:S(2)}, u32[]{:S(2)}) collective-permute-start(bf16[256,512]{0,1:T(8,128)(2,1)S(1)} %pad_maximum_fusion.49), channel_id=1, source_target_pairs={{0,3},{1,0},{2,1},{3,2},{4,7},{5,4},{6,5},{7,6},{8,11},{9,8},{10,9... | collective-permute-start | bytes 786440 | tf_op jit(solution)/shard_map/ppermute | solution.py:436
  7.0 22.7 %collective-permute-start.8 = (bf16[256,512]{0,1:T(8,128)(2,1)S(1)}, bf16[256,512]{0,1:T(8,128)(2,1)S(1)}, u32[]{:S(2)}, u32[]{:S(2)}) collective-permute-start(bf16[256,512]{0,1:T(8,128)(2,1)S(1)} %pad_maximum_fusion.49), channel_id=1, source_target_pairs={{0,1},{1,2},{2,3},{3,0},{4,5},{5,6},{6,7},{7,4},{8,9},{9,10},{10,1... | collective-permute-start | bytes 786440 | tf_op jit(solution)/shard_map/ppermute | solution.py:436
  10.8 27.8 %collective-permute-start = (s32[2,1040]{1,0:T(2,128)}, s32[2,1040]{1,0:T(2,128)}, u32[]{:S(2)}, u32[]{:S(2)}) collective-permute-start(s32[2,1040]{1,0:T(2,128)} %constant_dynamic-update-slice_fusion), channel_id=1, source_target_pairs={{0,4},{1,5},{2,6},{3,7},{4,0},{5,1},{6,2},{7,3},{8,12},{9,13},{10,... | collective-permute-start | bytes 24968 | tf_op jit(solution)/shard_map/ppermute | solution.py:432
  38.7 21.5 %collective-permute-start.4 = (bf16[520,256]{1,0:T(8,128)(2,1)S(1)}, bf16[520,256]{1,0:T(8,128)(2,1)S(1)}, u32[]{:S(2)}, u32[]{:S(2)}) collective-permute-start(bf16[520,256]{1,0:T(8,128)(2,1)S(1)} %get-tuple-element.206), channel_id=1, source_target_pairs={{0,5},{1,1},{2,4},{3,0},{4,7},{5,3},{6,6},{7,2},{8,13},{9,9},{10,1... | collective-permute-start | bytes 798728 | tf_op jit(solution)/shard_map/ppermute | solution.py:669
  47.6 33.7 %collective-permute-start.10 = (bf16[512,1536]{0,1:T(8,128)(2,1)S(1)}, bf16[512,1536]{0,1:T(8,128)(2,1)S(1)}, u32[]{:S(2)}, u32[]{:S(2)}) collective-permute-start(bf16[512,1536]{0,1:T(8,128)(2,1)S(1)} %pad_maximum_fusion.15), channel_id=1, source_target_pairs={{0,8},{1,9},{2,10},{3,11},{4,12},{5,13},{6,14},{7,15},{8,0},{9,1},... | collective-permute-start | bytes 4718600 | tf_op jit(solution)/shard_map/ppermute | solution.py:428
  129.4 30.1 %collective-permute-start.12 = (bf16[512,1024]{1,0:T(8,128)(2,1)}, bf16[512,1024]{1,0:T(8,128)(2,1)}, u32[]{:S(2)}, u32[]{:S(2)}) collective-permute-start(bf16[512,1024]{1,0:T(8,128)(2,1)} %pad_maximum_fusion.23), channel_id=1, source_target_pairs={{0,16},{1,17},{2,18},{3,19},{4,20},{5,21},{6,22},{7,23},{8,24},{9,... | collective-permute-start | bytes 3145736 | tf_op jit(solution)/shard_map/ppermute | solution.py:424
  132.0 26.1 %collective-permute-start.15 = (bf16[512,256]{0,1:T(8,128)(2,1)S(1)}, bf16[512,256]{0,1:T(8,128)(2,1)S(1)}, u32[]{:S(2)}, u32[]{:S(2)}) collective-permute-start(bf16[512,256]{0,1:T(8,128)(2,1)S(1)} %pad_maximum_fusion.45), channel_id=1, source_target_pairs={{0,2},{1,3},{2,0},{3,1},{4,6},{5,7},{6,4},{7,5},{8,10},{9,11},{10,... | collective-permute-start | bytes 786440 | tf_op jit(solution)/shard_map/ppermute | solution.py:436
  132.0 26.0 %collective-permute-start.14 = (bf16[512,256]{0,1:T(8,128)(2,1)S(1)}, bf16[512,256]{0,1:T(8,128)(2,1)S(1)}, u32[]{:S(2)}, u32[]{:S(2)}) collective-permute-start(bf16[512,256]{0,1:T(8,128)(2,1)S(1)} %pad_maximum_fusion.45), channel_id=1, source_target_pairs={{0,3},{1,0},{2,1},{3,2},{4,7},{5,4},{6,5},{7,6},{8,11},{9,8},{10,9... | collective-permute-start | bytes 786440 | tf_op jit(solution)/shard_map/ppermute | solution.py:436
  136.4 21.7 %collective-permute-start.16 = (bf16[512,256]{0,1:T(8,128)(2,1)S(1)}, bf16[512,256]{0,1:T(8,128)(2,1)S(1)}, u32[]{:S(2)}, u32[]{:S(2)}) collective-permute-start(bf16[512,256]{0,1:T(8,128)(2,1)S(1)} %pad_maximum_fusion.45), channel_id=1, source_target_pairs={{0,1},{1,2},{2,3},{3,0},{4,5},{5,6},{6,7},{7,4},{8,9},{9,10},{10,1... | collective-permute-start | bytes 786440 | tf_op jit(solution)/shard_map/ppermute | solution.py:436
  162.2 21.9 %collective-permute-start.13 = (bf16[1024,1024]{1,0:T(8,128)(2,1)}, bf16[1024,1024]{1,0:T(8,128)(2,1)}, u32[]{:S(2)}, u32[]{:S(2)}) collective-permute-start(bf16[1024,1024]{1,0:T(8,128)(2,1)} %pad_maximum_fusion.13), channel_id=1, source_target_pairs={{0,4},{1,5},{2,6},{3,7},{4,0},{5,1},{6,2},{7,3},{8,12},{9,13},{10,... | collective-permute-start | bytes 6291464 | tf_op jit(solution)/shard_map/ppermute | solution.py:432
  225.4 23.6 %collective-permute-start.18 = (bf16[1024,1024]{1,0:T(8,128)(2,1)S(1)}, bf16[1024,1024]{1,0:T(8,128)(2,1)}, u32[]{:S(2)}, u32[]{:S(2)}) collective-permute-start(bf16[1024,1024]{1,0:T(8,128)(2,1)S(1)} %slice.1120), channel_id=1, source_target_pairs={{0,4},{1,5},{2,6},{3,7},{4,0},{5,1},{6,2},{7,3},{8,12},{9,13},{10,... | collective-permute-start | bytes 6291464 | tf_op jit(solution)/shard_map/ppermute | solution.py:432
  248.6 44.0 %collective-permute-start.24 = (bf16[256,1536]{1,0:T(8,128)(2,1)S(1)}, bf16[256,1536]{1,0:T(8,128)(2,1)S(1)}, u32[]{:S(2)}, u32[]{:S(2)}) collective-permute-start(bf16[256,1536]{1,0:T(8,128)(2,1)S(1)} %constant_dynamic-update-slice_fusion.8), channel_id=1, source_target_pairs={{0,16},{1,17},{2,18},{3,19},{4,20},{5,21},{6,22},{7,23},{8,24},{9,... | collective-permute-start | bytes 2359304 | tf_op jit(solution)/shard_map/ppermute | solution.py:424
  253.0 42.5 %collective-permute-start.19 = (bf16[512,1024]{1,0:T(8,128)(2,1)S(1)}, bf16[512,1024]{1,0:T(8,128)(2,1)S(1)}, u32[]{:S(2)}, u32[]{:S(2)}) collective-permute-start(bf16[512,1024]{1,0:T(8,128)(2,1)S(1)} %pad_maximum_fusion.24), channel_id=1, source_target_pairs={{0,16},{1,17},{2,18},{3,19},{4,20},{5,21},{6,22},{7,23},{8,24},{9,... | collective-permute-start | bytes 3145736 | tf_op jit(solution)/shard_map/ppermute | solution.py:424
  262.8 25.5 %collective-permute-start.28 = (bf16[256,512]{0,1:T(8,128)(2,1)S(1)}, bf16[256,512]{0,1:T(8,128)(2,1)S(1)}, u32[]{:S(2)}, u32[]{:S(2)}) collective-permute-start(bf16[256,512]{0,1:T(8,128)(2,1)S(1)} %get-tuple-element.81), channel_id=1, source_target_pairs={{0,1},{1,2},{2,3},{3,0},{4,5},{5,6},{6,7},{7,4},{8,9},{9,10},{10,1... | collective-permute-start | bytes 786440 | tf_op jit(solution)/shard_map/ppermute | solution.py:436
  267.8 29.6 %collective-permute-start.36 = (bf16[512,256]{1,0:T(8,128)(2,1)S(1)}, bf16[512,256]{1,0:T(8,128)(2,1)S(1)}, u32[]{:S(2)}, u32[]{:S(2)}) collective-permute-start(bf16[512,256]{1,0:T(8,128)(2,1)S(1)} %get-tuple-element.143), channel_id=1, source_target_pairs={{0,0},{1,4},{2,1},{3,5},{4,2},{5,6},{6,3},{7,7},{8,8},{9,12},{10,9... | collective-permute-start | bytes 786440 | tf_op jit(solution)/shard_map/ppermute | solution.py:669
  295.5 36.6 %collective-permute-start.25 = (bf16[512,1536]{1,0:T(8,128)(2,1)}, bf16[512,1536]{1,0:T(8,128)(2,1)}, u32[]{:S(2)}, u32[]{:S(2)}) collective-permute-start(bf16[512,1536]{1,0:T(8,128)(2,1)} %pad_maximum_fusion.16), channel_id=1, source_target_pairs={{0,8},{1,9},{2,10},{3,11},{4,12},{5,13},{6,14},{7,15},{8,0},{9,1},... | collective-permute-start | bytes 4718600 | tf_op jit(solution)/shard_map/ppermute | solution.py:428
  300.7 31.3 %collective-permute-start.20 = (bf16[512,1024]{1,0:T(8,128)(2,1)}, bf16[512,1024]{1,0:T(8,128)(2,1)}, u32[]{:S(2)}, u32[]{:S(2)}) collective-permute-start(bf16[512,1024]{1,0:T(8,128)(2,1)} %multiply_convert_fusion.1), channel_id=1, source_target_pairs={{0,4},{1,5},{2,6},{3,7},{4,0},{5,1},{6,2},{7,3},{8,12},{9,13},{10,... | collective-permute-start | bytes 3145736 | tf_op jit(solution)/shard_map/ppermute | solution.py:432
  318.5 46.5 %collective-permute-start.30 = (bf16[512,1536]{0,1:T(8,128)(2,1)S(1)}, bf16[512,1536]{0,1:T(8,128)(2,1)S(1)}, u32[]{:S(2)}, u32[]{:S(2)}) collective-permute-start(bf16[512,1536]{0,1:T(8,128)(2,1)S(1)} %pad_maximum_fusion.17), channel_id=1, source_target_pairs={{0,8},{1,9},{2,10},{3,11},{4,12},{5,13},{6,14},{7,15},{8,0},{9,1},... | collective-permute-start | bytes 4718600 | tf_op jit(solution)/shard_map/ppermute | solution.py:428
  319.2 53.5 %collective-permute-start.40 = (bf16[512,1024]{1,0:T(8,128)(2,1)S(1)}, bf16[512,1024]{1,0:T(8,128)(2,1)S(1)}, u32[]{:S(2)}, u32[]{:S(2)}) collective-permute-start(bf16[512,1024]{1,0:T(8,128)(2,1)S(1)} %maximum_select_fusion), channel_id=1, source_target_pairs={{0,4},{1,5},{2,6},{3,7},{4,0},{5,1},{6,2},{7,3},{8,12},{9,13},{10,... | collective-permute-start | bytes 3145736 | tf_op jit(solution)/shard_map/ppermute | solution.py:432
  407.5 47.2 %collective-permute-start.72 = (bf16[512,2048]{1,0:T(8,128)(2,1)S(1)}, bf16[512,2048]{1,0:T(8,128)(2,1)S(1)}, u32[]{:S(2)}, u32[]{:S(2)}) collective-permute-start(bf16[512,2048]{1,0:T(8,128)(2,1)S(1)} %convolution_convert_fusion.2), channel_id=1, source_target_pairs={{0,8},{1,9},{2,10},{3,11},{4,12},{5,13},{6,14},{7,15},{8,0},{9,1},... | collective-permute-start | bytes 6291464 | tf_op jit(solution)/shard_map/ppermute | solution.py:428
  413.6 86.1 %collective-permute-start.67 = (bf16[512,2048]{1,0:T(8,128)(2,1)}, bf16[512,2048]{1,0:T(8,128)(2,1)}, u32[]{:S(2)}, u32[]{:S(2)}) collective-permute-start(bf16[512,2048]{1,0:T(8,128)(2,1)} %convolution_convert_fusion.3), channel_id=1, source_target_pairs={{0,8},{1,9},{2,10},{3,11},{4,12},{5,13},{6,14},{7,15},{8,0},{9,1},... | collective-permute-start | bytes 6291464 | tf_op jit(solution)/shard_map/ppermute | solution.py:428
  419.5 53.0 %collective-permute-start.32 = (bf16[512,256]{1,0:T(8,128)(2,1)}, bf16[512,256]{1,0:T(8,128)(2,1)}, u32[]{:S(2)}, u32[]{:S(2)}) collective-permute-start(bf16[512,256]{1,0:T(8,128)(2,1)} %get-tuple-element.151), channel_id=1, source_target_pairs={{0,0},{4,1},{1,2},{5,3},{2,4},{6,5},{3,6},{7,7},{8,8},{12,9},{9,10... | collective-permute-start | bytes 786440 | tf_op jit(solution)/shard_map/ppermute | solution.py:682
  425.1 84.8 %collective-permute-start.42 = (bf16[512,1024]{1,0:T(8,128)(2,1)}, bf16[512,1024]{1,0:T(8,128)(2,1)S(1)}, u32[]{:S(2)}, u32[]{:S(2)}) collective-permute-start(bf16[512,1024]{1,0:T(8,128)(2,1)} %pad_maximum_fusion.29), channel_id=1, source_target_pairs={{0,16},{1,17},{2,18},{3,19},{4,20},{5,21},{6,22},{7,23},{8,24},{9,... | collective-permute-start | bytes 3145736 | tf_op jit(solution)/shard_map/ppermute | solution.py:424
  460.3 52.6 %collective-permute-start.73 = (bf16[256,2048]{1,0:T(8,128)(2,1)}, bf16[256,2048]{1,0:T(8,128)(2,1)}, u32[]{:S(2)}, u32[]{:S(2)}) collective-permute-start(bf16[256,2048]{1,0:T(8,128)(2,1)} %slice.1121), channel_id=1, source_target_pairs={{0,16},{1,17},{2,18},{3,19},{4,20},{5,21},{6,22},{7,23},{8,24},{9,... | collective-permute-start | bytes 3145736 | tf_op jit(solution)/shard_map/ppermute | solution.py:424
  465.6 41.2 %collective-permute-start.35 = (bf16[512,256]{1,0:T(8,128)(2,1)S(1)}, bf16[512,256]{1,0:T(8,128)(2,1)S(1)}, u32[]{:S(2)}, u32[]{:S(2)}) collective-permute-start(bf16[512,256]{1,0:T(8,128)(2,1)S(1)} %copy-done.46), channel_id=1, source_target_pairs={{5,0},{1,1},{4,2},{0,3},{7,4},{3,5},{6,6},{2,7},{13,8},{9,9},{12,1... | collective-permute-start | bytes 786440 | tf_op jit(solution)/shard_map/ppermute | solution.py:682
  472.5 35.4 %collective-permute-start.34 = (bf16[512,256]{1,0:T(8,128)(2,1)S(1)}, bf16[512,256]{1,0:T(8,128)(2,1)S(1)}, u32[]{:S(2)}, u32[]{:S(2)}) collective-permute-start(bf16[512,256]{1,0:T(8,128)(2,1)S(1)} %copy-done.45), channel_id=1, source_target_pairs={{1,0},{5,1},{0,2},{4,3},{3,4},{7,5},{2,6},{6,7},{9,8},{13,9},{8,10... | collective-permute-start | bytes 786440 | tf_op jit(solution)/shard_map/ppermute | solution.py:682
  506.8 22.4 %collective-permute-start.68 = (bf16[256,2048]{1,0:T(8,128)(2,1)S(1)}, bf16[256,2048]{1,0:T(8,128)(2,1)S(1)}, u32[]{:S(2)}, u32[]{:S(2)}) collective-permute-start(bf16[256,2048]{1,0:T(8,128)(2,1)S(1)} %slice.1122), channel_id=1, source_target_pairs={{0,16},{1,17},{2,18},{3,19},{4,20},{5,21},{6,22},{7,23},{8,24},{9,... | collective-permute-start | bytes 3145736 | tf_op jit(solution)/shard_map/ppermute | solution.py:424
  510.1 52.3 %collective-permute-start.43 = (bf16[1024,1024]{1,0:T(8,128)(2,1)S(1)}, bf16[1024,1024]{1,0:T(8,128)(2,1)S(1)}, u32[]{:S(2)}, u32[]{:S(2)}) collective-permute-start(bf16[1024,1024]{1,0:T(8,128)(2,1)S(1)} %pad_maximum_fusion.14), channel_id=1, source_target_pairs={{0,4},{1,5},{2,6},{3,7},{4,0},{5,1},{6,2},{7,3},{8,12},{9,13},{10,... | collective-permute-start | bytes 6291464 | tf_op jit(solution)/shard_map/ppermute | solution.py:432
  517.2 22.9 %collective-permute-start.75 = (bf16[256,512]{1,0:T(8,128)(2,1)S(1)}, bf16[256,512]{1,0:T(8,128)(2,1)S(1)}, u32[]{:S(2)}, u32[]{:S(2)}) collective-permute-start(bf16[256,512]{1,0:T(8,128)(2,1)S(1)} %get-tuple-element.119), channel_id=1, source_target_pairs={{0,2},{1,3},{2,0},{3,1},{4,6},{5,7},{6,4},{7,5},{8,10},{9,11},{10,... | collective-permute-start | bytes 786440 | tf_op jit(solution)/shard_map/ppermute | solution.py:436
  529.7 27.2 %collective-permute-start.69 = (bf16[256,512]{1,0:T(8,128)(2,1)S(1)}, bf16[256,512]{1,0:T(8,128)(2,1)S(1)}, u32[]{:S(2)}, u32[]{:S(2)}) collective-permute-start(bf16[256,512]{1,0:T(8,128)(2,1)S(1)} %get-tuple-element.120), channel_id=1, source_target_pairs={{0,1},{1,2},{2,3},{3,0},{4,5},{5,6},{6,7},{7,4},{8,9},{9,10},{10,1... | collective-permute-start | bytes 786440 | tf_op jit(solution)/shard_map/ppermute | solution.py:436
  534.2 24.8 %collective-permute-start.71 = (bf16[256,512]{1,0:T(8,128)(2,1)S(1)}, bf16[256,512]{1,0:T(8,128)(2,1)S(1)}, u32[]{:S(2)}, u32[]{:S(2)}) collective-permute-start(bf16[256,512]{1,0:T(8,128)(2,1)S(1)} %get-tuple-element.121), channel_id=1, source_target_pairs={{0,3},{1,0},{2,1},{3,2},{4,7},{5,4},{6,5},{7,6},{8,11},{9,8},{10,9... | collective-permute-start | bytes 786440 | tf_op jit(solution)/shard_map/ppermute | solution.py:436
  535.4 26.8 %collective-permute-start.70 = (bf16[256,512]{1,0:T(8,128)(2,1)S(1)}, bf16[256,512]{1,0:T(8,128)(2,1)S(1)}, u32[]{:S(2)}, u32[]{:S(2)}) collective-permute-start(bf16[256,512]{1,0:T(8,128)(2,1)S(1)} %get-tuple-element.122), channel_id=1, source_target_pairs={{0,2},{1,3},{2,0},{3,1},{4,6},{5,7},{6,4},{7,5},{8,10},{9,11},{10,... | collective-permute-start | bytes 786440 | tf_op jit(solution)/shard_map/ppermute | solution.py:436
  608.9 30.7 %collective-permute-start.44 = (bf16[1024,1024]{1,0:T(8,128)(2,1)S(1)}, bf16[1024,1024]{1,0:T(8,128)(2,1)S(1)}, u32[]{:S(2)}, u32[]{:S(2)}) collective-permute-start(bf16[1024,1024]{1,0:T(8,128)(2,1)S(1)} %slice.1119), channel_id=1, source_target_pairs={{0,4},{1,5},{2,6},{3,7},{4,0},{5,1},{6,2},{7,3},{8,12},{9,13},{10,... | collective-permute-start | bytes 6291464 | tf_op jit(solution)/shard_map/ppermute | solution.py:432
  612.3 25.4 %collective-permute-start.60 = (bf16[512,768]{1,0:T(8,128)(2,1)S(1)}, bf16[512,768]{1,0:T(8,128)(2,1)S(1)}, u32[]{:S(2)}, u32[]{:S(2)}) collective-permute-start(bf16[512,768]{1,0:T(8,128)(2,1)S(1)} %fusion.28), channel_id=1, source_target_pairs={{0,8},{1,9},{2,10},{3,11},{4,12},{5,13},{6,14},{7,15},{8,0},{9,1},... | collective-permute-start | bytes 2359304 | tf_op jit(solution)/shard_map/ppermute | solution.py:428
  615.0 21.9 %collective-permute-start.61 = (bf16[512,256]{1,0:T(8,128)(2,1)S(1)}, bf16[512,256]{1,0:T(8,128)(2,1)S(1)}, u32[]{:S(2)}, u32[]{:S(2)}) collective-permute-start(bf16[512,256]{1,0:T(8,128)(2,1)S(1)} %fusion.34), channel_id=1, source_target_pairs={{0,8},{1,9},{2,10},{3,11},{4,12},{5,13},{6,14},{7,15},{8,0},{9,1},... | collective-permute-start | bytes 786440 | tf_op jit(solution)/shard_map/ppermute | solution.py:428
  640.9 28.9 %collective-permute-start.45 = (bf16[512,1024]{1,0:T(8,128)(2,1)S(1)}, bf16[512,1024]{1,0:T(8,128)(2,1)S(1)}, u32[]{:S(2)}, u32[]{:S(2)}) collective-permute-start(bf16[512,1024]{1,0:T(8,128)(2,1)S(1)} %pad_maximum_fusion.30), channel_id=1, source_target_pairs={{0,16},{1,17},{2,18},{3,19},{4,20},{5,21},{6,22},{7,23},{8,24},{9,... | collective-permute-start | bytes 3145736 | tf_op jit(solution)/shard_map/ppermute | solution.py:424
  644.8 23.5 %collective-permute-start.64 = (bf16[512,256]{1,0:T(8,128)(2,1)S(1)}, bf16[512,256]{1,0:T(8,128)(2,1)S(1)}, u32[]{:S(2)}, u32[]{:S(2)}) collective-permute-start(bf16[512,256]{1,0:T(8,128)(2,1)S(1)} %pad_maximum_fusion.58), channel_id=1, source_target_pairs={{0,3},{1,0},{2,1},{3,2},{4,7},{5,4},{6,5},{7,6},{8,11},{9,8},{10,9... | collective-permute-start | bytes 786440 | tf_op jit(solution)/shard_map/ppermute | solution.py:436
  645.7 22.6 %collective-permute-start.62 = (bf16[512,256]{1,0:T(8,128)(2,1)S(1)}, bf16[512,256]{1,0:T(8,128)(2,1)S(1)}, u32[]{:S(2)}, u32[]{:S(2)}) collective-permute-start(bf16[512,256]{1,0:T(8,128)(2,1)S(1)} %pad_maximum_fusion.56), channel_id=1, source_target_pairs={{0,1},{1,2},{2,3},{3,0},{4,5},{5,6},{6,7},{7,4},{8,9},{9,10},{10,1... | collective-permute-start | bytes 786440 | tf_op jit(solution)/shard_map/ppermute | solution.py:436
  647.0 27.4 %collective-permute-start.77 = (bf16[128,1024]{1,0:T(8,128)(2,1)S(1)}, bf16[128,1024]{1,0:T(8,128)(2,1)S(1)}, u32[]{:S(2)}, u32[]{:S(2)}) collective-permute-start(bf16[128,1024]{1,0:T(8,128)(2,1)S(1)} %fusion.59), channel_id=1, source_target_pairs={{0,4},{1,5},{2,6},{3,7},{4,0},{5,1},{6,2},{7,3},{8,12},{9,13},{10,... | collective-permute-start | bytes 786440 | tf_op jit(solution)/shard_map/ppermute | solution.py:432
  739.2 35.1 %collective-permute-start.52 = (bf16[512,1536]{1,0:T(8,128)(2,1)}, bf16[512,1536]{1,0:T(8,128)(2,1)}, u32[]{:S(2)}, u32[]{:S(2)}) collective-permute-start(bf16[512,1536]{1,0:T(8,128)(2,1)} %convolution_convert_fusion.4), channel_id=1, source_target_pairs={{0,8},{1,9},{2,10},{3,11},{4,12},{5,13},{6,14},{7,15},{8,0},{9,1},... | collective-permute-start | bytes 4718600 | tf_op jit(solution)/shard_map/ppermute | solution.py:428
  755.7 78.2 %collective-permute-start.48 = (bf16[512,256]{1,0:T(8,128)(2,1)}, bf16[512,256]{1,0:T(8,128)(2,1)}, u32[]{:S(2)}, u32[]{:S(2)}) collective-permute-start(bf16[512,256]{1,0:T(8,128)(2,1)} %get-tuple-element.127), channel_id=1, source_target_pairs={{0,0},{4,1},{1,2},{5,3},{2,4},{6,5},{3,6},{7,7},{8,8},{12,9},{9,10... | collective-permute-start | bytes 786440 | tf_op jit(solution)/shard_map/ppermute | solution.py:682
  759.1 74.8 %collective-permute-start.51 = (bf16[512,256]{1,0:T(8,128)(2,1)}, bf16[512,256]{1,0:T(8,128)(2,1)}, u32[]{:S(2)}, u32[]{:S(2)}) collective-permute-start(bf16[512,256]{1,0:T(8,128)(2,1)} %get-tuple-element.128), channel_id=1, source_target_pairs={{5,0},{1,1},{4,2},{0,3},{7,4},{3,5},{6,6},{2,7},{13,8},{9,9},{12,1... | collective-permute-start | bytes 786440 | tf_op jit(solution)/shard_map/ppermute | solution.py:682
  763.8 70.1 %collective-permute-start.50 = (bf16[512,256]{1,0:T(8,128)(2,1)}, bf16[512,256]{1,0:T(8,128)(2,1)}, u32[]{:S(2)}, u32[]{:S(2)}) collective-permute-start(bf16[512,256]{1,0:T(8,128)(2,1)} %get-tuple-element.129), channel_id=1, source_target_pairs={{1,0},{5,1},{0,2},{4,3},{3,4},{7,5},{2,6},{6,7},{9,8},{13,9},{8,10... | collective-permute-start | bytes 786440 | tf_op jit(solution)/shard_map/ppermute | solution.py:682
  765.1 68.8 %collective-permute-start.49 = (bf16[512,256]{1,0:T(8,128)(2,1)}, bf16[512,256]{1,0:T(8,128)(2,1)}, u32[]{:S(2)}, u32[]{:S(2)}) collective-permute-start(bf16[512,256]{1,0:T(8,128)(2,1)} %get-tuple-element.130), channel_id=1, source_target_pairs={{4,0},{0,1},{5,2},{1,3},{6,4},{2,5},{7,6},{3,7},{12,8},{8,9},{13,1... | collective-permute-start | bytes 786440 | tf_op jit(solution)/shard_map/ppermute | solution.py:682
  778.6 56.9 %collective-permute-start.53 = (bf16[256,1536]{1,0:T(8,128)(2,1)}, bf16[256,1536]{1,0:T(8,128)(2,1)}, u32[]{:S(2)}, u32[]{:S(2)}) collective-permute-start(bf16[256,1536]{1,0:T(8,128)(2,1)} %slice.1127), channel_id=1, source_target_pairs={{0,16},{1,17},{2,18},{3,19},{4,20},{5,21},{6,22},{7,23},{8,24},{9,... | collective-permute-start | bytes 2359304 | tf_op jit(solution)/shard_map/ppermute | solution.py:424
  837.2 23.0 %collective-permute-start.58 = (bf16[256,512]{1,0:T(8,128)(2,1)S(1)}, bf16[256,512]{1,0:T(8,128)(2,1)S(1)}, u32[]{:S(2)}, u32[]{:S(2)}) collective-permute-start(bf16[256,512]{1,0:T(8,128)(2,1)S(1)} %pad_maximum_fusion.55), channel_id=1, source_target_pairs={{0,3},{1,0},{2,1},{3,2},{4,7},{5,4},{6,5},{7,6},{8,11},{9,8},{10,9... | collective-permute-start | bytes 786440 | tf_op jit(solution)/shard_map/ppermute | solution.py:436
  838.8 21.3 %collective-permute-start.56 = (bf16[256,512]{1,0:T(8,128)(2,1)S(1)}, bf16[256,512]{1,0:T(8,128)(2,1)S(1)}, u32[]{:S(2)}, u32[]{:S(2)}) collective-permute-start(bf16[256,512]{1,0:T(8,128)(2,1)S(1)} %pad_maximum_fusion.53), channel_id=1, source_target_pairs={{0,1},{1,2},{2,3},{3,0},{4,5},{5,6},{6,7},{7,4},{8,9},{9,10},{10,1... | collective-permute-start | bytes 786440 | tf_op jit(solution)/shard_map/ppermute | solution.py:436
  (137 other events, 1895.6 us)

commit v2 on v1

--- a/solution.py
+++ b/solution.py
@@ -403,10 +403,11 @@
     )
 
 
-AXES = ("tm", "clip", "mp")
+AXES = ("tm", "x", "c", "mp")
 F32 = jnp.float32
 BF16 = jnp.bfloat16
 BLK = 256
+MESH = pl.DeviceIdType.MESH
 
 
 def device_pairs(move):
@@ -416,7 +417,7 @@
             for c in range(2):
                 for z in range(4):
                     there = move(y, x, c, z)
-                    pairs.append(tuple((q[0] * 4 + q[1] * 2 + q[2]) * 4 + q[3] for q in ((y, x, c, z), there)))
+                    pairs.append(tuple(((q[0] * 2 + q[1]) * 2 + q[2]) * 4 + q[3] for q in ((y, x, c, z), there)))
     return pairs
 
 
@@ -444,6 +445,209 @@
     return device_pairs(move)
 
 
+def arrive_kernel(
+    tok, vec, mine, rows_out, vec_out, wq, wo,
+    z_send, z_recv, y_send, y_recv, x_send, x_recv, p_send, p_recv, q_send, q_recv,
+    t_send, t_recv, v_send, v_recv, local,
+):
+    y, x, c, z = (lax.axis_index(name) for name in AXES)
+    half = wo.shape[1] // 4
+    wide = 3 * half
+
+    barrier = pltpu.get_barrier_semaphore()
+    for dc in range(2):
+        for dz in range(4):
+            if dc or dz:
+                peer = (y, x, (c + dc) % 2, (z + dz) % 4)
+                pl.semaphore_signal(barrier, inc=1, device_id=peer, device_id_type=MESH)
+    near_y, near_x = (1 - y, x, c, z), (y, 1 - x, c, z)
+    for peer in (near_y, near_x):
+        pl.semaphore_signal(barrier, inc=1, device_id=peer, device_id_type=MESH)
+    pl.semaphore_wait(barrier, 9)
+
+    def rows(dy, dx):
+        return pl.ds(pl.multiple_of(BLK * (2 * ((y + dy) % 2) + (x + dx) % 2), BLK), BLK)
+
+    def piece(dy, dx, r, split=False):
+        s = (z + r) % 4
+        at = pl.multiple_of(s * wide, half)
+        out = wo.at[rows(dy, dx), pl.ds(pl.multiple_of(s * half, half), half)]
+        if split:
+            late = pl.multiple_of(s * wide + 2 * half, half)
+            return (wq.at[rows(dy, dx), pl.ds(at, 2 * half)], wq.at[rows(dy, dx), pl.ds(late, half)], out)
+        return (wq.at[rows(dy, dx), pl.ds(at, wide)], out)
+
+    def copies(sources, targets, send, recv, peer):
+        return [
+            pltpu.make_async_remote_copy(
+                src_ref=src, dst_ref=dst, send_sem=send.at[i], recv_sem=recv.at[i], device_id=peer, device_id_type=MESH
+            )
+            for i, (src, dst) in enumerate(zip(sources, targets))
+        ]
+
+    own_rows = rows(0, 0)
+    own_slice = (mine.at[own_rows, pl.ds(0, wide)], mine.at[own_rows, pl.ds(wide, half)])
+
+    def z_copies(right, step):
+        if right:
+            r = 0 if step == 0 else 4 - step
+            peer, lands = (y, x, c, (z + 1) % 4), 3 - step
+        else:
+            r = step
+            peer, lands = (y, x, c, (z + 3) % 4), step + 1
+        target = piece(0, 0, r)
+        source = own_slice if step == 0 else target
+        return copies(source, target, z_send.at[int(right), step], z_recv.at[lands], peer)
+
+    def y_copies(r):
+        return copies(piece(0, 0, r), piece(0, 0, r), y_send.at[r], y_recv.at[r], near_y)
+
+    def x_copies(r):
+        return copies(piece(0, 0, r), piece(0, 0, r), x_send.at[r], x_recv.at[r], near_x)
+
+    def corner_x(r):
+        part = piece(1, 0, r, split=True)[:1]
+        return copies(part, part, p_send.at[r], p_recv.at[r], near_x)
+
+    def corner_y(r):
+        part = piece(0, 1, r, split=True)[1:]
+        return copies(part, part, q_send.at[r], q_recv.at[r], near_y)
+
+    def start(all_copies):
+        for copy in all_copies:
+            copy.start()
+
+    def landed(all_copies):
+        for copy in all_copies:
+            copy.wait_recv()
+
+    def sent(all_copies):
+        for copy in all_copies:
+            copy.wait_send()
+
+    def token_copies(k):
+        peer = (y, x, k % 2, 2 * c + k // 2)
+        at = pl.ds(pl.multiple_of(z * BLK, BLK), BLK)
+        return [
+            pltpu.make_async_remote_copy(
+                src_ref=src, dst_ref=dst, send_sem=send.at[k], recv_sem=recv.at[z], device_id=peer, device_id_type=MESH
+            )
+            for src, dst, send, recv in (
+                (tok.at[k], rows_out.at[:, at], t_send, t_recv),
+                (vec, vec_out.at[:, at], v_send, v_recv),
+            )
+        ]
+
+    def token_local(k):
+        at = pl.ds(pl.multiple_of(z * BLK, BLK), BLK)
+        return [
+            pltpu.make_async_copy(tok.at[k], rows_out.at[:, at], local.at[2]),
+            pltpu.make_async_copy(vec, vec_out.at[:, at], local.at[3]),
+        ]
+
+    def stays(k):
+        return jnp.logical_and(2 * c + k // 2 == z, c == k % 2)
+
+    def from_right(j):
+        return z <= 2 - j
+
+    def from_left(j):
+        return z >= j + 1
+
+    pl.when(z < 3)(lambda: start(z_copies(True, 0)))
+    pl.when(z > 0)(lambda: start(z_copies(False, 0)))
+    keep = [
+        pltpu.make_async_copy(mine.at[:, pl.ds(0, wide)], wq.at[:, pl.ds(pl.multiple_of(z * wide, half), wide)], local.at[0]),
+        pltpu.make_async_copy(mine.at[:, pl.ds(wide, half)], wo.at[:, pl.ds(pl.multiple_of(z * half, half), half)], local.at[1]),
+    ]
+    start(keep)
+
+    def forward(j, left):
+        r = 3 - j if left else j + 1
+        landed(copies(piece(0, 0, r), piece(0, 0, r), z_send.at[0, 0], z_recv.at[r], near_y))
+        if j < 2:
+            pl.when(z < 3 if left else z > 0)(lambda: start(z_copies(left, j + 1)))
+        start(y_copies(r))
+        start(x_copies(r))
+
+    def corners(j, left):
+        r = 3 - j if left else j + 1
+        landed(copies(piece(1, 0, r), piece(1, 0, r), y_send.at[r], y_recv.at[r], near_y))
+        start(corner_x(r))
+        landed(copies(piece(0, 1, r), piece(0, 1, r), x_send.at[r], x_recv.at[r], near_x))
+        start(corner_y(r))
+
+    for j in range(3):
+        for left in (True, False):
+            pl.when(from_left(j) if left else from_right(j))(lambda j=j, left=left: forward(j, left))
+        if j == 0:
+            for k in range(4):
+                pl.when(stays(k))(lambda k=k: start(token_local(k)))
+                pl.when(jnp.logical_not(stays(k)))(lambda k=k: start(token_copies(k)))
+        else:
+            for left in (True, False):
+                pl.when(from_left(j - 1) if left else from_right(j - 1))(lambda j=j, left=left: corners(j - 1, left))
+    for left in (True, False):
+        pl.when(from_left(2) if left else from_right(2))(lambda left=left: corners(2, left))
+
+    for copy in keep:
+        copy.wait()
+    for r in (1, 2, 3):
+        part = piece(1, 1, r, split=True)
+        landed(copies(part[:1], part[:1], p_send.at[r], p_recv.at[r], near_x))
+        landed(copies(part[1:], part[1:], q_send.at[r], q_recv.at[r], near_y))
+        for group in (y_copies(r), x_copies(r), corner_x(r), corner_y(r)):
+            sent(group)
+    for step in range(3):
+        pl.when(jnp.logical_and(z >= step, z < 3))(lambda step=step: sent(z_copies(True, step)))
+        pl.when(jnp.logical_and(z + step <= 3, z > 0))(lambda step=step: sent(z_copies(False, step)))
+    for k in range(4):
+        def finish_local(k=k):
+            for copy in token_local(k):
+                copy.wait()
+
+        pl.when(stays(k))(finish_local)
+        pl.when(jnp.logical_not(stays(k)))(lambda k=k: sent(token_copies(k)))
+    for s in range(4):
+        at = pl.ds(s * BLK, BLK)
+        away = jnp.logical_not(jnp.logical_and(z == s, z // 2 == c))
+
+        def arrived(s=s, at=at):
+            for src, dst, send, recv in (
+                (tok.at[0], rows_out.at[:, at], t_send, t_recv),
+                (vec, vec_out.at[:, at], v_send, v_recv),
+            ):
+                pltpu.make_async_remote_copy(
+                    src_ref=src, dst_ref=dst, send_sem=send.at[0], recv_sem=recv.at[s], device_id=near_y, device_id_type=MESH
+                ).wait_recv()
+
+        pl.when(away)(arrived)
+
+
+def arrive(tok, vec, mine):
+    own, width, half = tok.shape[1], 4 * tok.shape[2], mine.shape[1] // 4
+    dma = pltpu.SemaphoreType.DMA
+    anywhere = pl.BlockSpec(memory_space=pl.ANY)
+    return pl.pallas_call(
+        arrive_kernel,
+        in_specs=[anywhere] * 3,
+        out_specs=[anywhere] * 4,
+        out_shape=[
+            jax.ShapeDtypeStruct((own, width), BF16),
+            jax.ShapeDtypeStruct((vec.shape[0], width), BF16),
+            jax.ShapeDtypeStruct((width, 12 * half), BF16),
+            jax.ShapeDtypeStruct((width, 4 * half), BF16),
+        ],
+        scratch_shapes=[
+            dma((2, 3, 2)), dma((4, 2)), dma((4, 2)), dma((4, 2)), dma((4, 2)), dma((4, 2)),
+            dma((4, 1)), dma((4, 1)), dma((4, 2)), dma((4, 2)),
+            dma((4,)), dma((4,)), dma((4,)), dma((4,)), dma((4,)),
+        ],
+        compiler_params=pltpu.CompilerParams(collective_id=0, has_side_effects=True),
+        name="arrive",
+    )(tok, vec, mine)
+
+
 def dot_nn(a, b):
     return lax.dot_general(a, b, (((1,), (0,)), ((), ())), preferred_element_type=F32)
 
@@ -456,68 +660,79 @@
     return lax.dot_general(a, b, (((0,), (0,)), ((), ())), preferred_element_type=F32)
 
 
-def attention_probs(q, k, bias, scale):
-    scores = dot_nt(q, k) * scale
-    if bias is not None:
-        scores = scores + bias
-    exponent = jnp.exp(scores - jnp.max(scores, axis=-1, keepdims=True))
-    return exponent / jnp.sum(exponent, axis=-1, keepdims=True)
-
-
-def attend_kernel(heads, scale, qkv_ref, bias_ref, out_ref):
+def row_reader(ref):
+    if len(ref.shape) == 2:
+        return lambda lo, width: ref[:, lo : lo + width]
+    rows = ref.shape[0] * ref.shape[1]
+    return lambda lo, width: ref[:, :, lo : lo + width].astype(F32).reshape(rows, width).astype(BF16)
+
+
+def row_writer(ref):
+    def write(lo, v):
+        if len(ref.shape) == 2:
+            ref[:, lo : lo + v.shape[1]] = v.astype(BF16)
+        else:
+            ref[:, :, lo : lo + v.shape[1]] = v.reshape(ref.shape[:2] + v.shape[1:]).astype(BF16)
+
+    return write
+
+
+def by_pair(lo):
+    return (3 * lo, 3 * lo + 2 * HEAD_DIM, 3 * lo + 4 * HEAD_DIM)
+
+
+def by_part(width):
+    return lambda lo: (lo, width + lo, 2 * width + lo)
+
+
+def attend_kernel(heads, scale, places, qkv_ref, bias_ref, out_ref, total_ref):
     width = heads * HEAD_DIM
-    bias = None if bias_ref is None else bias_ref[...]
-    rows = qkv_ref.size // (3 * width)
-
-    def load(part, h):
-        lo = part * width + h * HEAD_DIM
-        if len(qkv_ref.shape) == 2:
-            return qkv_ref[:, lo : lo + HEAD_DIM]
-        return qkv_ref[:, :, lo : lo + HEAD_DIM].astype(F32).reshape(rows, HEAD_DIM).astype(BF16)
-
-    done = []
-    for h in range(heads):
-        p = attention_probs(load(0, h), load(1, h), bias, scale)
-        done.append(dot_nn(p.astype(BF16), load(2, h)))
-    out = jnp.concatenate(done, axis=1)
-    if len(out_ref.shape) == 2:
-        out_ref[...] = out.astype(BF16)
-    else:
-        out_ref[...] = out.reshape(out_ref.shape).astype(BF16)
-
-
-def attend_back_kernel(heads, scale, qkv_ref, grad_ref, bias_ref, out_ref):
+    read, write = row_reader(qkv_ref), row_writer(out_ref)
+    for lo in range(0, width, 2 * HEAD_DIM):
+        q, k, v = (read(at, 2 * HEAD_DIM) for at in places(lo))
+        mixed = []
+        for i in range(2):
+            mine = slice(i * HEAD_DIM, (i + 1) * HEAD_DIM)
+            h = lo // HEAD_DIM + i
+            scores = dot_nt(k[:, mine], q[:, mine]) * scale
+            if bias_ref is not None:
+                scores = scores + bias_ref[...]
+            highest = jnp.max(scores, axis=0, keepdims=True)
+            exponent = jnp.exp(scores - highest)
+            total = jnp.sum(exponent, axis=0, keepdims=True)
+            total_ref[0, h : h + 1, :] = highest + jnp.log(total)
+            mixed.append(dot_tn(v[:, mine], exponent.astype(BF16)) * (1.0 / total))
+        write(lo, jnp.concatenate(mixed, axis=0).T)
+
+
+def attend_back_kernel(heads, scale, places, qkv_ref, grad_ref, total_ref, bias_ref, out_ref):
     width = heads * HEAD_DIM
-    bias = None if bias_ref is None else bias_ref[...]
-    rows = qkv_ref.size // (3 * width)
-
-    def load(ref, lo):
-        if len(ref.shape) == 2:
-            return ref[:, lo : lo + HEAD_DIM]
-        return ref[:, :, lo : lo + HEAD_DIM].astype(F32).reshape(rows, HEAD_DIM).astype(BF16)
-
-    parts = ([], [], [])
-    for h in range(heads):
-        q = load(qkv_ref, h * HEAD_DIM)
-        k = load(qkv_ref, width + h * HEAD_DIM)
-        v = load(qkv_ref, 2 * width + h * HEAD_DIM)
-        g = load(grad_ref, h * HEAD_DIM)
-        p = attention_probs(q, k, bias, scale)
-        dp = dot_nt(g, v)
-        ds = (p * (dp - jnp.sum(p * dp, axis=-1, keepdims=True))).astype(BF16)
-        parts[0].append(dot_nn(ds, k) * scale)
-        parts[1].append(dot_tn(ds, q) * scale)
-        parts[2].append(dot_tn(p.astype(BF16), g))
-    out = jnp.concatenate(parts[0] + parts[1] + parts[2], axis=1)
-    if len(out_ref.shape) == 2:
-        out_ref[...] = out.astype(BF16)
-    else:
-        out_ref[...] = out.reshape(out_ref.shape).astype(BF16)
+    read, read_grad, write = row_reader(qkv_ref), row_reader(grad_ref), row_writer(out_ref)
+    for lo in range(0, width, 2 * HEAD_DIM):
+        q, k, v = (read(at, 2 * HEAD_DIM) for at in places(lo))
+        g = read_grad(lo, 2 * HEAD_DIM)
+        grads = ([], [], [])
+        for i in range(2):
+            mine = slice(i * HEAD_DIM, (i + 1) * HEAD_DIM)
+            h = lo // HEAD_DIM + i
+            scores = dot_nt(k[:, mine], q[:, mine]) * scale
+            if bias_ref is not None:
+                scores = scores + bias_ref[...]
+            p = jnp.exp(scores - total_ref[0, h : h + 1, :])
+            dp = dot_nt(v[:, mine], g[:, mine])
+            ds = (p * (dp - jnp.sum(p * dp, axis=0, keepdims=True))).astype(BF16)
+            grads[0].append(dot_tn(k[:, mine], ds) * scale)
+            grads[1].append(dot_nn(ds, q[:, mine]) * scale)
+            grads[2].append(dot_nn(p.astype(BF16), g[:, mine]))
+        at_q, at_k, at_v = places(lo)
+        write(at_q, jnp.concatenate(grads[0], axis=0).T)
+        write(at_k, jnp.concatenate(grads[1], axis=1))
+        write(at_v, jnp.concatenate(grads[2], axis=1))
 
 
 def attention_cost(groups, rows, heads, products):
     return pl.CostEstimate(
-        flops=2 * products * groups * heads * rows * rows * HEAD_DIM,
+        flops=8 * products * groups * heads * rows * rows * HEAD_DIM,
         transcendentals=groups * heads * rows * rows,
         bytes_accessed=2 * groups * rows * heads * HEAD_DIM * 2 * products,
     )
@@ -526,30 +741,37 @@
 def space_attend(qkv, frames, patches, heads, scale):
     width = heads * HEAD_DIM
     return pl.pallas_call(
-        lambda q, o: attend_kernel(heads, scale, q, None, o),
+        lambda q, o, t: attend_kernel(heads, scale, by_pair, q, None, o, t),
         grid=(frames,),
         in_specs=[pl.BlockSpec((patches, 3 * width), lambda i: (i, 0))],
-        out_specs=pl.BlockSpec((patches, width), lambda i: (i, 0)),
-        out_shape=jax.ShapeDtypeStruct((frames * patches, width), BF16),
+        out_specs=[
+            pl.BlockSpec((patches, width), lambda i: (i, 0)),
+            pl.BlockSpec((1, heads, patches), lambda i: (i, 0, 0)),
+        ],
+        out_shape=[
+            jax.ShapeDtypeStruct((frames * patches, width), BF16),
+            jax.ShapeDtypeStruct((frames, heads, patches), F32),
+        ],
         cost_estimate=attention_cost(frames, patches, heads, 2),
         name="space_attend",
     )(qkv)
 
 
-def space_attend_back(qkv, grad, frames, patches, heads, scale):
+def space_attend_back(qkv, grad, total, frames, patches, heads, scale):
     width = heads * HEAD_DIM
     return pl.pallas_call(
-        lambda q, g, o: attend_back_kernel(heads, scale, q, g, None, o),
+        lambda q, g, t, o: attend_back_kernel(heads, scale, by_pair, q, g, t, None, o),
         grid=(frames,),
         in_specs=[
             pl.BlockSpec((patches, 3 * width), lambda i: (i, 0)),
             pl.BlockSpec((patches, width), lambda i: (i, 0)),
+            pl.BlockSpec((1, heads, patches), lambda i: (i, 0, 0)),
         ],
         out_specs=pl.BlockSpec((patches, 3 * width), lambda i: (i, 0)),
         out_shape=jax.ShapeDtypeStruct((frames * patches, 3 * width), BF16),
         cost_estimate=attention_cost(frames, patches, heads, 5),
         name="space_attend_back",
-    )(qkv, grad)
+    )(qkv, grad, total)
 
 
 GROUP = 8
@@ -558,38 +780,55 @@
 def time_attend(qkv, bias, frames, patches, heads, scale):
     width = heads * HEAD_DIM
     rows = frames * GROUP
-    return pl.pallas_call(
-        lambda q, b, o: attend_kernel(heads, scale, q, b, o),
-        grid=(patches // GROUP,),
+    groups = patches // GROUP
+    mixed, total = pl.pallas_call(
+        lambda q, b, o, t: attend_kernel(heads, scale, by_part(width), q, b, o, t),
+        grid=(groups,),
         in_specs=[
             pl.BlockSpec((frames, GROUP, 3 * width), lambda i: (0, i, 0)),
             pl.BlockSpec((rows, rows), lambda i: (0, 0)),
         ],
-        out_specs=pl.BlockSpec((frames, GROUP, width), lambda i: (0, i, 0)),
-        out_shape=jax.ShapeDtypeStruct((frames, patches, width), BF16),
-        cost_estimate=attention_cost(patches // GROUP, rows, heads, 2),
+        out_specs=[
+            pl.BlockSpec((frames, GROUP, width), lambda i: (0, i, 0)),
+            pl.BlockSpec((1, heads, rows), lambda i: (i, 0, 0)),
+        ],
+        out_shape=[
+            jax.ShapeDtypeStruct((frames, patches, width), BF16),
+            jax.ShapeDtypeStruct((groups, heads, rows), F32),
+        ],
+        cost_estimate=attention_cost(groups, rows, heads, 2),
         name="time_attend",
-    )(qkv.reshape(frames, patches, 3 * width), bias).reshape(frames * patches, width)
-
-
-def time_attend_back(qkv, grad, bias, frames, patches, heads, scale):
+    )(qkv.reshape(frames, patches, 3 * width), bias)
+    return (mixed.reshape(frames * patches, width), total)
+
+
+def time_attend_back(qkv, grad, total, bias, frames, patches, heads, scale):
     width = heads * HEAD_DIM
     rows = frames * GROUP
+    groups = patches // GROUP
     return pl.pallas_call(
-        lambda q, g, b, o: attend_back_kernel(heads, scale, q, g, b, o),
-        grid=(patches // GROUP,),
+        lambda q, g, t, b, o: attend_back_kernel(heads, scale, by_part(width), q, g, t, b, o),
+        grid=(groups,),
         in_specs=[
             pl.BlockSpec((frames, GROUP, 3 * width), lambda i: (0, i, 0)),
             pl.BlockSpec((frames, GROUP, width), lambda i: (0, i, 0)),
+            pl.BlockSpec((1, heads, rows), lambda i: (i, 0, 0)),
             pl.BlockSpec((rows, rows), lambda i: (0, 0)),
         ],
         out_specs=pl.BlockSpec((frames, GROUP, 3 * width), lambda i: (0, i, 0)),
         out_shape=jax.ShapeDtypeStruct((frames, patches, 3 * width), BF16),
-        cost_estimate=attention_cost(patches // GROUP, rows, heads, 5),
+        cost_estimate=attention_cost(groups, rows, heads, 5),
         name="time_attend_back",
     )(
-        qkv.reshape(frames, patches, 3 * width), grad.reshape(frames, patches, width), bias
+        qkv.reshape(frames, patches, 3 * width),
+        grad.reshape(frames, patches, width),
+        total,
+        bias,
     ).reshape(frames * patches, 3 * width)
+
+
+def tie(*values):
+    return lax.optimization_barrier(values)
 
 
 def norm_rows(resid):
@@ -605,12 +844,6 @@
     mean = jnp.mean(inner, axis=-1, keepdims=True)
     along = jnp.mean(inner * standardized, axis=-1, keepdims=True)
     return ((inner - mean - standardized * along) * inverse, gain_grad)
-
-
-def swap_y(v):
-    return jnp.concatenate(
-        [v[:, BLK : 2 * BLK], v[:, :BLK], v[:, 3 * BLK :], v[:, 2 * BLK : 3 * BLK]], axis=1
-    )
 
 
 def cols(parts):
@@ -637,60 +870,42 @@
     w_out,
 ):
     scale = 1.0 / math.sqrt(HEAD_DIM)
-    y = lax.axis_index("tm")
-    x = lax.axis_index("clip") // 2
-    c = lax.axis_index("clip") % 2
-    z = lax.axis_index("mp")
+    y, x, c, z = (lax.axis_index(name) for name in AXES)
     patches = tokens.shape[2]
     width = qkv_space.shape[0]
     frames_own = tokens.shape[0] * tokens.shape[1] // 4
     frames_all = frame_order.shape[1]
     own = frames_own * patches
     hidden_own = w_in.shape[1] // 2
-    block_at = [2 * (y ^ (i & 1)) + (x ^ (i >> 1)) for i in range(4)]
-
-    def rel_rows(w):
-        return rows_of([lax.dynamic_slice_in_dim(w, b * BLK, BLK, 0) for b in block_at])
-
-    def to_absolute(v):
-        v = jnp.swapaxes(v.reshape(-1, 2, 2, BLK), 1, 2)
-        v = jnp.where(y == 1, v[:, ::-1], v)
-        return jnp.where(x == 1, v[:, :, ::-1], v).reshape(-1, width)
-
+    plane = 2 * y + x
     k_own = 2 * (z % 2) + c
 
-    def gather_rows(v, extra):
+    def gather_rows(v):
         pieces = v.reshape(4, own, BLK)
-        landed = []
-        for r in range(4):
-            piece = lax.dynamic_index_in_dim(pieces, z ^ r, 0, keepdims=False)
-            if extra is not None:
-                piece = rows_of([piece, extra])
-            landed.append(lax.ppermute(piece, AXES, spread_pairs(r)))
-        landed = jnp.stack(landed)
-        return cols(
-            [lax.dynamic_index_in_dim(landed, k_own ^ b, 0, keepdims=False) for b in block_at]
-        )
+        landed = jnp.stack(
+            [
+                lax.ppermute(
+                    lax.dynamic_index_in_dim(pieces, z ^ r, 0, keepdims=False), AXES, spread_pairs(r)
+                )
+                for r in range(4)
+            ]
+        )
+        return cols([lax.dynamic_index_in_dim(landed, k_own ^ b, 0, keepdims=False) for b in range(4)])
 
     def return_rows(v):
-        pieces = jnp.stack([v[:, i * BLK : (i + 1) * BLK] for i in range(4)])
-        landed = []
-        for r in range(4):
-            block = k_own ^ r
-            place = 2 * ((block % 2) ^ x) + ((block // 2) ^ y)
-            piece = lax.dynamic_index_in_dim(pieces, place, 0, keepdims=False)
-            landed.append(lax.ppermute(piece, AXES, [(b, a) for a, b in spread_pairs(r)]))
-        landed = jnp.stack(landed)
+        landed = jnp.stack(
+            [
+                lax.ppermute(
+                    lax.dynamic_slice_in_dim(v, (k_own ^ r) * BLK, BLK, 1),
+                    AXES,
+                    [(b, a) for a, b in spread_pairs(r)],
+                )
+                for r in range(4)
+            ]
+        )
         return jnp.stack(
             [lax.dynamic_index_in_dim(landed, k ^ z, 0, keepdims=False) for k in range(4)]
         ).reshape(tokens.shape)
-
-    vectors = rows_of([mask_embed[None], gains, jnp.zeros((4, BLK), BF16)])
-    arrived = gather_rows(tokens, vectors)
-    source = arrived[:own].astype(F32)
-    embed_row = arrived[own : own + 1].astype(F32)
-    gain = [arrived[own + 1 + i : own + 2 + i].astype(F32) for i in range(3)]
-    upstream = gather_rows(cotangent, None)
 
     masked_here = (priority < ratio[:, None, None]).astype(jnp.int32).reshape(2, -1)
     info = cols([masked_here, frame_order])
@@ -702,43 +917,36 @@
     order = jnp.where(c == 1, order[:, ::-1], order).swapaxes(0, 1).reshape(frames_all)
     order = jnp.repeat(order, GROUP)
     patch = jnp.arange(frames_all * GROUP) % GROUP
-    visible = (order[None, :] <= order[:, None]) & (patch[None, :] == patch[:, None])
+    visible = (order[:, None] <= order[None, :]) & (patch[:, None] == patch[None, :])
     bias = jnp.where(visible, 0.0, -1e30).astype(F32)
 
-    def fetch(mine):
-        landed = cols([hop_z(mine, -r) for r in (1, 2, 3)])
-        return landed
-
     half = qkv_space.shape[2] // 2
-    sp_qkv = rel_rows(lax.dynamic_slice_in_dim(qkv_space, c * half, half, 2))
-    sp_out = rel_rows(lax.dynamic_slice_in_dim(out_space, c * half, half, 0).T)
-    sp_own = cols([sp_qkv.reshape(width, -1), sp_out])
-    sp_far = fetch(sp_own[:BLK])
-    sp_far = rows_of([sp_far, hop_y(sp_far)])
-    sp_far = rows_of([sp_far, hop_x(sp_far)])
-    sp_all = [sp_own] + [sp_far[:, r * 4 * half : (r + 1) * 4 * half] for r in range(3)]
-    ws_qkv = cols([w[:, j * half : (j + 1) * half] for j in range(3) for w in sp_all])
-    ws_out = cols([w[:, 3 * half :] for w in sp_all])
+    sp_own = cols(
+        [
+            lax.dynamic_slice_in_dim(qkv_space, c * half, half, 2).reshape(width, -1),
+            lax.dynamic_slice_in_dim(out_space, c * half, half, 0).T,
+        ]
+    )
+    vectors = rows_of([mask_embed[None], gains, jnp.zeros((4, BLK), BF16)])
+    arrived, vectors, ws_qkv, ws_out = arrive(tokens.reshape(4, own, BLK), vectors, sp_own)
+    source = arrived.astype(F32)
+    embed_row = vectors[:1].astype(F32)
+    gain = [vectors[1 + i : 2 + i].astype(F32) for i in range(3)]
 
     head = (2 * y + c) * HEAD_DIM
-    ti_qkv = rel_rows(lax.dynamic_slice_in_dim(qkv_time, head, HEAD_DIM, 2))
-    ti_out = rel_rows(lax.dynamic_slice_in_dim(out_time, head, HEAD_DIM, 0).T)
-    ti_own = cols([ti_qkv.reshape(width, -1), ti_out])
-    ti_far = fetch(ti_own[: 2 * BLK])
-    ti_far = rows_of([ti_far, hop_x(ti_far)])
-    ti_all = [ti_own] + [ti_far[:, r * 4 * HEAD_DIM : (r + 1) * 4 * HEAD_DIM] for r in range(3)]
-    wt_qkv = cols([w[:, j * HEAD_DIM : (j + 1) * HEAD_DIM] for j in range(3) for w in ti_all])
-    wt_out = cols([w[:, 3 * HEAD_DIM :] for w in ti_all])
-
-    ff_in = rel_rows(lax.dynamic_slice_in_dim(w_in, c * hidden_own, hidden_own, 1))
-    ff_out = rel_rows(lax.dynamic_slice_in_dim(w_out, c * hidden_own, hidden_own, 0).T)
-    far = []
-    for w in (ff_in, ff_out):
-        w_far = fetch(w[:BLK])
-        w_far = rows_of([w_far, hop_y(w_far)])
-        w_far = rows_of([w_far, hop_x(w_far)])
-        far.append(cols([w, w_far]))
-    wf_in, wf_out = far
+    ff_in = lax.dynamic_slice(w_in, (plane * BLK, c * hidden_own), (BLK, hidden_own))
+    ff_out = lax.dynamic_slice(w_out, (c * hidden_own, plane * BLK), (hidden_own, BLK)).T
+    ti_own = cols(
+        [
+            lax.dynamic_slice_in_dim(qkv_time, head, HEAD_DIM, 2).reshape(width, -1),
+            lax.dynamic_slice_in_dim(out_time, head, HEAD_DIM, 0).T,
+        ]
+    )
+    arrived, ff_in, ff_out, ti_own = tie(arrived, ff_in, ff_out, ti_own)
+
+    def gather_ff(w):
+        w = lax.all_gather(w, ("tm", "x", "mp")).reshape(4, 4, BLK, hidden_own)
+        return jnp.swapaxes(w, 1, 2).reshape(width, 4 * hidden_own)
 
     def pair_gather(v):
         return rows_of([v, hop_c(v)])
@@ -747,12 +955,12 @@
         return v[:own] + hop_c(v[own:].astype(BF16)).astype(F32)
 
     def quad_gather(v):
-        both = rows_of([v, hop_y(swap_y(v))])
+        both = rows_of([v, hop_y(v)])
         return rows_of([both, hop_c(both)])
 
     def quad_scatter(v):
         both = v[: 2 * own] + hop_c(v[2 * own :].astype(BF16)).astype(F32)
-        return both[:own] + hop_y(swap_y(both[own:].astype(BF16))).astype(F32)
+        return both[:own] + hop_y(both[own:].astype(BF16)).astype(F32)
 
     heads_s = 4 * half // HEAD_DIM
     heads_t = 4
@@ -760,28 +968,55 @@
     resid0 = jnp.where(masked, embed_row, source)
     std0, inv0 = norm_rows(resid0)
     normed0 = pair_gather((std0 * gain[0]).astype(BF16))
+    ti_half = lax.dynamic_slice_in_dim(ti_own, x * 2 * BLK, 2 * BLK, 0)
+    ti_z = [hop_z(ti_half, -r) for r in (1, 2, 3)]
+    wf_in, wf_out = gather_ff(ff_in), gather_ff(ff_out)
     joined0 = dot_nn(normed0, ws_qkv).astype(BF16)
-    mixed0 = space_attend(joined0, frames_pair, patches, heads_s, scale)
+    mixed0, total0 = space_attend(joined0, frames_pair, patches, heads_s, scale)
+    mixed0, ti_z = tie(mixed0, ti_z)
+    ti_z = cols(ti_z)
+    ti_x = hop_x(ti_z)
+    ti_far = jnp.where(x == 0, rows_of([ti_z, ti_x]), rows_of([ti_x, ti_z]))
     resid1 = resid0 + pair_scatter(dot_nt(mixed0, ws_out))
     std1, inv1 = norm_rows(resid1)
     normed1 = quad_gather((std1 * gain[1]).astype(BF16))
+    normed1, ti_far, cotangent = tie(normed1, ti_far, cotangent)
+    ti_all = [ti_own] + [ti_far[:, r * 4 * HEAD_DIM : (r + 1) * 4 * HEAD_DIM] for r in range(3)]
+    wt_qkv = cols([w[:, j * HEAD_DIM : (j + 1) * HEAD_DIM] for j in range(3) for w in ti_all])
+    wt_out = cols([w[:, 3 * HEAD_DIM :] for w in ti_all])
+    upstream = gather_rows(cotangent)
     joined1 = dot_nn(normed1, wt_qkv).astype(BF16)
-    mixed1 = time_attend(joined1, bias, frames_all, patches, heads_t, scale)
+    mixed1, total1 = time_attend(joined1, bias, frames_all, patches, heads_t, scale)
+    mixed1, upstream = tie(mixed1, upstream)
+    grad3 = jnp.where(masked, upstream, jnp.zeros((), BF16))
+    gb3 = pair_gather(grad3)
     resid2 = resid1 + quad_scatter(dot_nt(mixed1, wt_out))
     std2, inv2 = norm_rows(resid2)
     normed2 = pair_gather((std2 * gain[2]).astype(BF16))
     inner = dot_nn(normed2, wf_in)
     activated, gelu_pull = jax.vjp(gelu_tanh, inner)
     hidden = activated.astype(BF16)
-    block_out = return_rows((resid2 + pair_scatter(dot_nt(hidden, wf_out))).astype(BF16))
-
-    def reduce_plane(lhs, rhs):
-        sent = hop_x(dot_tn(lhs[:, 2 * BLK :], rhs).astype(BF16))
-        kept = dot_tn(lhs[:, : 2 * BLK], rhs) + sent.astype(F32)
-        return kept
-
-    def reduce_y(kept):
-        return kept[:BLK] + hop_y(kept[BLK:].astype(BF16)).astype(F32)
+
+    def plane_scatter(lhs, rhs):
+        return lax.psum_scatter(dot_tn(lhs, rhs).astype(BF16), ("tm", "x"), scatter_dimension=0, tiled=True)
+
+    def line_scatter(v):
+        v = jnp.swapaxes(v.reshape(BLK, 4, -1), 0, 1)
+        return lax.psum_scatter(v, "mp", scatter_dimension=0).astype(F32)
+
+    def send_x(lhs, rhs):
+        there = jnp.where(x == 0, cols([lhs[:, BLK : 2 * BLK], lhs[:, 3 * BLK :]]), cols([lhs[:, :BLK], lhs[:, 2 * BLK : 3 * BLK]]))
+        return hop_x(dot_tn(there, rhs).astype(BF16))
+
+    def keep_x(lhs, rhs, landed):
+        here = jnp.where(x == 1, cols([lhs[:, BLK : 2 * BLK], lhs[:, 3 * BLK :]]), cols([lhs[:, :BLK], lhs[:, 2 * BLK : 3 * BLK]]))
+        return dot_tn(here, rhs) + landed.astype(F32)
+
+    def mine_y(v):
+        return jnp.where(y == 0, v[:BLK], v[BLK:])
+
+    def other_y(v):
+        return jnp.where(y == 1, v[:BLK], v[BLK:])
 
     def reduce_z(pieces):
         total = pieces[0]
@@ -798,55 +1033,73 @@
     def by_core(kept, landed):
         return jnp.where(c == 0, jnp.concatenate([kept, landed], -1), jnp.concatenate([landed, kept], -1))
 
-    grad3 = jnp.where(masked, upstream, jnp.zeros((), BF16))
-    gb3 = pair_gather(grad3)
+    w_out_part = plane_scatter(gb3, hidden)
     grad_inner = gelu_pull(dot_nn(gb3, wf_out))[0].astype(BF16)
-    g_w_out = reduce_y(reduce_plane(gb3, hidden))
-    g_w_out = reduce_z([g_w_out[:, r * hidden_own : (r + 1) * hidden_own] for r in range(4)])
-    g_w_in = reduce_y(reduce_plane(normed2, grad_inner))
-    g_w_in = reduce_z([g_w_in[:, r * hidden_own : (r + 1) * hidden_own] for r in range(4)])
-    back2, gain_grad2 = norm_rows_back(pair_scatter(dot_nt(grad_inner, wf_in)), std2, inv2, gain[2])
+    part2 = pair_scatter(dot_nt(grad_inner, wf_in))
+    w_in_part = plane_scatter(normed2, grad_inner)
+    back2, gain_grad2 = norm_rows_back(part2, std2, inv2, gain[2])
     grad2 = grad3.astype(F32) + back2
-
     gb2 = quad_gather(grad2.astype(BF16))
+    block_part = dot_nt(hidden, wf_out)
+    block_out = return_rows((resid2 + pair_scatter(block_part)).astype(BF16))
+
     dmixed1 = dot_nn(gb2, wt_out).astype(BF16)
-    djoined1 = time_attend_back(joined1, dmixed1, bias, frames_all, patches, heads_t, scale)
-    g_t_out = reduce_plane(gb2, mixed1)
-    g_t_qkv = reduce_plane(normed1, djoined1)
+    djoined1 = time_attend_back(joined1, dmixed1, total1, bias, frames_all, patches, heads_t, scale)
+    djoined1, block_out = tie(djoined1, block_out)
+    part1 = quad_scatter(dot_nt(djoined1, wt_qkv))
+    back1, gain_grad1 = norm_rows_back(part1, std1, inv1, gain[1])
+    grad1 = grad2 + back1
+    gb1 = pair_gather(grad1.astype(BF16))
+    t_out_x = send_x(gb2, mixed1)
+    t_qkv_x = send_x(normed1, djoined1)
+    dmixed0 = dot_nn(gb1, ws_out).astype(BF16)
+    s_out_x = send_x(gb1, mixed0)
+    djoined0 = space_attend_back(joined0, dmixed0, total0, frames_pair, patches, heads_s, scale)
+    djoined0, t_out_x, t_qkv_x, w_out_part, s_out_x = tie(djoined0, t_out_x, t_qkv_x, w_out_part, s_out_x)
+    g_w_out = line_scatter(w_out_part)
+    s_qkv_x = send_x(normed0, djoined0)
+    part0 = pair_scatter(dot_nt(djoined0, ws_qkv))
+    s_out_kept = keep_x(gb1, mixed0, s_out_x)
+    s_out_y = hop_y(other_y(s_out_kept).astype(BF16))
+    g_w_in = line_scatter(w_in_part)
+    g_t_out = keep_x(gb2, mixed1, t_out_x)
+    g_t_qkv = keep_x(normed1, djoined1, t_qkv_x)
+    z_at = [(z + r) % 4 for r in range(4)]
     span = heads_t * HEAD_DIM
     g_time = reduce_z(
         [
             cols(
-                [g_t_qkv[:, j * span + r * HEAD_DIM : j * span + (r + 1) * HEAD_DIM] for j in range(3)]
-                + [g_t_out[:, r * HEAD_DIM : (r + 1) * HEAD_DIM]]
+                [lax.dynamic_slice_in_dim(g_t_qkv, j * span + r * HEAD_DIM, HEAD_DIM, 1) for j in range(3)]
+                + [lax.dynamic_slice_in_dim(g_t_out, r * HEAD_DIM, HEAD_DIM, 1)]
             )
             for r in range(4)
         ]
     )
-    back1, gain_grad1 = norm_rows_back(quad_scatter(dot_nt(djoined1, wt_qkv)), std1, inv1, gain[1])
-    grad1 = grad2 + back1
-
-    gb1 = pair_gather(grad1.astype(BF16))
-    dmixed0 = dot_nn(gb1, ws_out).astype(BF16)
-    djoined0 = space_attend_back(joined0, dmixed0, frames_pair, patches, heads_s, scale)
-    g_s_out = reduce_y(reduce_plane(gb1, mixed0))
-    g_s_qkv = reduce_y(reduce_plane(normed0, djoined0))
-    span = 4 * half
+    s_qkv_kept = keep_x(normed0, djoined0, s_qkv_x)
+    s_qkv = mine_y(s_qkv_kept) + hop_y(other_y(s_qkv_kept).astype(BF16)).astype(F32)
+    s_out = mine_y(s_out_kept) + s_out_y.astype(F32)
     g_space = reduce_z(
         [
             cols(
-                [g_s_qkv[:, j * span + r * half : j * span + (r + 1) * half] for j in range(3)]
-                + [g_s_out[:, r * half : (r + 1) * half]]
+                [
+                    lax.dynamic_slice_in_dim(s_qkv, s * 3 * half, 3 * half, 1),
+                    lax.dynamic_slice_in_dim(s_out, s * half, half, 1),
+                ]
             )
-            for r in range(4)
+            for s in z_at
         ]
     )
-    back0, gain_grad0 = norm_rows_back(pair_scatter(dot_nt(djoined0, ws_qkv)), std0, inv0, gain[0])
+    back0, gain_grad0 = norm_rows_back(part0, std0, inv0, gain[0])
     grad0 = grad1 + back0
     grad_tokens = return_rows(jnp.where(masked, 0.0, grad0).astype(BF16)).astype(F32)
     grad_embed = jnp.sum(jnp.where(masked, grad0, 0.0), axis=0)
-    small = lax.psum(to_absolute(jnp.stack([gain_grad0, gain_grad1, gain_grad2, grad_embed])), AXES)
-    small = lax.dynamic_slice_in_dim(small, z * BLK, BLK, 1)
+    small = jnp.stack([gain_grad0, gain_grad1, gain_grad2, grad_embed])
+    for hop in (hop_c, hop_y, hop_x):
+        small = small + hop(small)
+    small_at = [lax.dynamic_slice_in_dim(small, s * BLK, BLK, 1) for s in z_at]
+    small = small_at[0]
+    for r in (1, 2, 3):
+        small = small + hop_z(small_at[r], r)
 
     rows = BLK // 2
     kept, landed = swap_c(g_space)
@@ -857,7 +1110,7 @@
     kept, landed = swap_c(cols([g_w_in, g_w_out]))
     grad_w_in = by_core(kept[:, :hidden_own], landed[:, :hidden_own])
     grad_w_out = by_core(kept[:, hidden_own:], landed[:, hidden_own:]).T
-    both = cols([g_time[:BLK], hop_y(g_time[BLK:].astype(BF16)).astype(F32)])
+    both = cols([mine_y(g_time), hop_y(other_y(g_time).astype(BF16)).astype(F32)])
     kept, landed = swap_c(both)
     quad = jnp.stack([kept, landed], 1).reshape(rows, 2, 2, 4, HEAD_DIM)
     quad = jnp.where(c == 1, quad[:, ::-1], quad)
@@ -881,15 +1134,20 @@
 
 def solution(mesh):
     sizes = (mesh.shape["tm"], mesh.shape["clip"], mesh.shape["mp"])
+    if sizes == (2, 4, 4):
+        mesh = jax.sharding.Mesh(mesh.devices.reshape(2, 2, 2, 4), AXES)
+        step, clip = token_parallel, ("x", "c")
+    else:
+        step, clip = shards, ("clip",)
     return jax.shard_map(
-        token_parallel if sizes == (2, 4, 4) else shards,
+        step,
         mesh=mesh,
         in_specs=(
-            P("clip", "tm", None, "mp"),
-            P("clip", "tm", None, "mp"),
-            P("clip"),
-            P("clip", "tm", None),
-            P("clip", None),
+            P(clip, "tm", None, "mp"),
+            P(clip, "tm", None, "mp"),
+            P(clip),
+            P(clip, "tm", None),
+            P(clip, None),
             P("mp"),
             P(None, "mp"),
             P(None, None, "mp"),
@@ -900,16 +1158,16 @@
             P("mp", None),
         ),
         out_specs=(
-            P("clip", "tm", None, "mp"),
-            P("clip", "tm", None, "mp"),
+            P(clip, "tm", None, "mp"),
+            P(clip, "tm", None, "mp"),
             P("mp"),
             P(None, "mp"),
-            P(("tm", "clip"), None, "mp"),
-            P("mp", ("tm", "clip")),
-            P(("tm", "clip"), None, "mp"),
-            P("mp", ("tm", "clip")),
-            P(("tm", "clip"), "mp"),
-            P("mp", ("tm", "clip")),
+            P(("tm",) + clip, None, "mp"),
+            P("mp", ("tm",) + clip),
+            P(("tm",) + clip, None, "mp"),
+            P("mp", ("tm",) + clip),
+            P(("tm",) + clip, "mp"),
+            P("mp", ("tm",) + clip),
         ),
         check_vma=False,
     )

time: 872 us -> 658 us (0.75)
  waiting for transfers between devices: 323 us -> 185 us
  blocking collectives: 51.2 us -> 0 us
  starting transfers between devices: 120 us -> 84.8 us
  local copies, waits for them, and re-layouts: 62.6 us -> 81.9 us
  matrix products: 118 us -> 102 us
  between operations: 3.32 us -> 16.4 us
    ppermute x10 -> x6, waiting for transfers between devices: 151 us -> 18.6 us  [hop_x(): lax.ppermute(v, AXES, device_pairs(lambda y, x, c, z: (y, 1 - x, c, z)))]
    ppermute x24 -> x12, waiting for transfers between devices: 132 us -> 29.9 us  [hop_z(): lax.ppermute(v, AXES, device_pairs(lambda y, x, c, z: (y, x, c, (z + shif...]
    ppermute x12 -> x8, waiting for transfers between devices: 20.2 us -> 111 us  [hop_y(): lax.ppermute(v, AXES, device_pairs(lambda y, x, c, z: (1 - y, x, c, z)))]
    psum x1 -> x0, blocking collectives: 51.2 us -> none  [token_parallel(): lax.psum(to_absolute(jnp.stack([gain_grad0, gain_grad1, gain_grad2, grad_...]
    reshape x1 -> x6, local copies, waits for them, and re-layouts: 0.74 us -> 31.2 us  [the longest x3 25.4 us: gather_ff(): w = lax.all_gather(w, ('tm', 'x', 'mp')).reshape(4, 4, BLK, hidden_own)]
    ppermute x16 -> x12, starting transfers between devices: 45.8 us -> 31.5 us  [the longest x8 19.9 us: return_rows(): lax.ppermute(lax.dynamic_slice_in_dim(v, (k_own ^ r) * BLK, BLK, 1), AXES...]
    dot_general x6, matrix products: 50.9 us -> 37.5 us  [dot_nn(): lax.dot_general(a, b, (((1,), (0,)), ((), ())), preferred_element_type=F32)]
    ppermute x24 -> x12, starting transfers between devices: 36.6 us -> 25.3 us  [hop_z(): lax.ppermute(v, AXES, device_pairs(lambda y, x, c, z: (y, x, c, (z + shif...]
  transfers between devices with their start and end apart: 78 -> 61, of which waited for: 33 -> 23; matrix products, arithmetic and copies ran while one was open for 17% -> 33% of each run, Pallas kernels for 0% -> 18%
where the time goes in v2:
time: 658 us; the launch traced here: 648 us
  waiting for transfers between devices  185 us (28%)
  Pallas kernels  113 us (17%)
  matrix products  102 us (16%)
  starting transfers between devices  84.8 us (13%)
  local copies, waits for them, and re-layouts  81.9 us (12%)
  other arithmetic  63.8 us (10%)
  between operations  16.4 us (2%)
    ppermute x8, waiting for transfers between devices, hop_y(): lax.ppermute(v, AXES, device_pairs(lambda y, x, c, z: (1 - y, x, c, z)))  111 us
    pallas_call x1, Pallas kernels, arrive(): pl.pallas_call(arrive_kernel, in_specs=[anywhere] * 3, out_specs=[anywher...  41.2 us
    dot_general x6, matrix products, dot_nn(): lax.dot_general(a, b, (((1,), (0,)), ((), ())), preferred_element_type=F32)  37.5 us
    dot_general x10, matrix products, dot_tn(): lax.dot_general(a, b, (((0,), (0,)), ((), ())), preferred_element_type=F32)  37.4 us
    unnamed x204, local copies, waits for them, and re-layouts  29.9 us
    ppermute x12, waiting for transfers between devices, hop_z(): lax.ppermute(v, AXES, device_pairs(lambda y, x, c, z: (y, x, c, (z + shif...  29.9 us
    dot_general x6, matrix products, dot_nt(): lax.dot_general(a, b, (((1,), (1,)), ((), ())), preferred_element_type=F32)  27.2 us
    reshape x3, local copies, waits for them, and re-layouts, gather_ff(): w = lax.all_gather(w, ('tm', 'x', 'mp')).reshape(4, 4, BLK, hidden_own)  25.4 us
  transfers between devices with their start and end apart: 61, of which 23 were waited for; matrix products, arithmetic and copies ran while one was open for 33% of the time, Pallas kernels for 18%

profile of v2, /device:TPU:9, one launch (start us, length us, event | category | flops | bytes accessed | tf_op | source)
XLA Modules:
  0.0 647.9 jit_solution(605779234499377659)
XLA Ops:
  23.2 41.2 %arrive.1 = (bf16[512,1024]{1,0:T(8,128)(2,1)}, bf16[8,1024]{1,0:T(8,128)(2,1)}, bf16[1024,1536]{1,0:T(8,128)(2,1)}, bf16[1024,512]{1,0:T(8,128)(2,1)}) custom-call(bf16[4,512,256]{2,1,0:T(8,128)(2,1)} %bitcast.137, bf16[8,256]{1,0:T(8,128)(2,1)} %maximum_maximum_fusion.vec, bf16[1024,512]{1,0:T(8,128)(2,1)} %pad_maximum_fusion.30.mine), custom_call_target="tpu_custom_call" | custom-call | tf_op jit(solution)/shard_map/arrive/pallas_call | solution.py:631
  71.6 9.3 %collective-permute-start.2 = (bf16[512,256]{0,1:T(8,128)(2,1)S(1)}, bf16[512,256]{0,1:T(8,128)(2,1)S(1)}, u32[]{:S(2)}, u32[]{:S(2)}) collective-permute-start(bf16[512,256]{0,1:T(8,128)(2,1)S(1)} %constant_dynamic-slice_fusion.24), channel_id=1, source_target_pairs={{0,3},{1,0},{2,1},{3,2},{4,7},{5,4},{6,5},{7,6},{8,11},{9,8},{10,9... | collective-permute-start | bytes 786440 | tf_op jit(solution)/shard_map/ppermute | solution.py:437
  85.1 7.4 %convolution_convert_fusion.q = bf16[1024,1536]{1,0:T(8,128)(2,1)} fusion(bf16[1024,1536]{1,0:T(8,128)(2,1)} %get-tuple-element.39, bf16[512,1024]{1,0:T(8,128)(2,1)} %collective-permute-done.1, bf16[512,1024]{1,0:T(8,128)(2,1)S(1)} %multiply_convert_fusion.3), kind=kOutput, calls=%fused_computation.16 | convolution fusion | flops 3226992640 | bytes 8388608 | tf_op jit(solution)/shard_map/dot_general | solution.py:652
  92.5 16.2 %space_attend.1 = (bf16[1024,512]{1,0:T(8,128)(2,1)}, f32[8,8,128]{2,1,0:T(8,128)}) custom-call(bf16[1024,1536]{1,0:T(8,128)(2,1)} %convolution_convert_fusion.q), custom_call_target="tpu_custom_call" | custom-call | flops 1073741824 | bytes 4194304 | tf_op jit(solution)/shard_map/space_attend/pallas_call | solution.py:743
  119.6 29.2 %collective-permute-done.6 = bf16[512,1024]{1,0:T(8,128)(2,1)S(1)} collective-permute-done((bf16[512,1024]{1,0:T(8,128)(2,1)S(1)}, bf16[512,1024]{1,0:T(8,128)(2,1)S(1)}, u32[]{:S(2)}, u32[]{:S(2)}) %collective-permute-start.6) | collective-permute-done | bytes 1048608 | tf_op jit(solution)/shard_map/ppermute | solution.py:425
  160.8 17.6 %collective-permute-done.8 = bf16[512,768]{0,1:T(8,128)(2,1)} collective-permute-done((bf16[512,768]{0,1:T(8,128)(2,1)}, bf16[512,768]{0,1:T(8,128)(2,1)}, u32[]{:S(2)}, u32[]{:S(2)}) %collective-permute-start.8) | collective-permute-done | bytes 786464 | tf_op jit(solution)/shard_map/ppermute | solution.py:429
  183.0 5.3 collective-permute-start.9
  189.4 5.4 collective-permute-start.12
  195.7 4.8 convolution_convert_fusion.3
  200.5 18.0 %time_attend.1 = (bf16[16,128,256]{2,1,0:T(8,128)(2,1)}, f32[16,4,128]{2,1,0:T(4,128)}) custom-call(bf16[16,128,768]{2,1,0:T(8,128)(2,1)} %bitcast.179, f32[128,128]{1,0:T(8,128)} %and_select_fusion.b), custom_call_target="tpu_custom_call" | custom-call | flops 1073741824 | bytes 4194304 | tf_op jit(solution)/shard_map/time_attend/pallas_call | solution.py:784
  225.4 4.1 collective-permute-done.14
  232.3 31.2 %collective-permute-done.15 = bf16[512,1024]{1,0:T(8,128)(2,1)S(1)} collective-permute-done((bf16[512,1024]{1,0:T(8,128)(2,1)S(1)}, bf16[512,1024]{1,0:T(8,128)(2,1)S(1)}, u32[]{:S(2)}, u32[]{:S(2)}) %collective-permute-start.15) | collective-permute-done | bytes 1048608 | tf_op jit(solution)/shard_map/ppermute | solution.py:425
  267.4 5.4 copy.64
  272.8 3.4 copy.87
  276.2 7.8 %reshape.204 = bf16[4,4,256,512]{2,1,0,3:T(4,128)(2,1)} reshape(bf16[4096,512]{0,1:T(8,128)(2,1)} %all-gather.5.cloned.1.call-done) | data formatting | bytes 8388608 | tf_op jit(solution)/shard_map/reshape | solution.py:948
  284.0 12.2 %copy.63 = bf16[4,4,256,512]{3,1,2,0:T(4,128)(2,1)} copy(bf16[4,4,256,512]{2,1,0,3:T(4,128)(2,1)} %reshape.204) | data formatting | bytes 8388608 | tf_op jit(solution)/shard_map/reshape | solution.py:948
  296.2 3.7 copy.86
  300.0 7.6 %fusion.31 = f32[1024,2048]{1,0:T(8,128)S(1)} fusion(bf16[1024,2048]{1,0:T(8,128)(2,1)S(1)} %bitcast.123, bf16[512,1024]{1,0:T(8,128)(2,1)} %collective-permute-done.16, bf16[512,1024]{1,0:T(8,128)(2,1)} %multiply_convert_fusion.1), kind=kOutput, calls=%fused_computation.111 | convolution fusion | flops 4299161600 | bytes 14680064 | tf_op jit(solution)/shard_map/dot_general | solution.py:652
  307.6 11.4 %fusion.6 = bf16[1024,2048]{1,0:T(8,128)(2,1)S(1)} fusion(f32[1024,2048]{1,0:T(8,128)S(1)} %fusion.31, bf16[1024,2048]{1,0:T(8,128)(2,1)S(1)} %bitcast.125, bf16[512,1024]{1,0:T(8,128)(2,1)} %collective-permute-done.13, bf16[512,1024]{1,0:T(8,128)(2,1)} %broadcast_select_fusion), kind=kOutput, calls=%fused_computation.8 | convolution fusion | flops 4341104640 | bytes 18874368 | tf_op jit(solution)/shard_map/dot_general | solution.py:652
  321.0 7.8 %convolution_convert_fusion.1 = bf16[1024,2048]{1,0:T(8,128)(2,1)} fusion(bf16[1024,2048]{1,0:T(8,128)(2,1)S(1)} %fusion.6, bf16[512,1024]{1,0:T(8,128)(2,1)} %collective-permute-done.16, bf16[512,1024]{1,0:T(8,128)(2,1)} %multiply_convert_fusion.1), kind=kOutput, calls=%fused_computation.17 | convolution fusion | flops 4301258752 | bytes 10485760 | tf_op jit(solution)/shard_map/dot_general | solution.py:660
  328.9 9.1 %fusion.86 = f32[1024,1024]{1,0:T(8,128)S(1)} fusion(bf16[1024,2048]{1,0:T(8,128)(2,1)} %bitcast.126, f32[1024,2048]{1,0:T(8,128)} %copy-done.88), kind=kOutput, calls=%fused_computation.291 | convolution fusion | flops 4313841664 | bytes 16777216 | tf_op jit(solution)/shard_map/dot_general | solution.py:656
  338.7 4.7 fusion.105
  353.2 4.3 collective-permute-start.21
  358.2 4.5 collective-permute-start.24
  362.7 26.6 %collective-permute-done.18 = bf16[512,1024]{1,0:T(8,128)(2,1)S(1)} collective-permute-done((bf16[512,1024]{1,0:T(8,128)(2,1)}, bf16[512,1024]{1,0:T(8,128)(2,1)S(1)}, u32[]{:S(2)}, u32[]{:S(2)}) %collective-permute-start.18) | collective-permute-done | bytes 1048608 | tf_op jit(solution)/shard_map/ppermute | solution.py:425
  389.3 3.1 pad_maximum_fusion.9
  393.4 10.9 %convolution_convert_fusion.2 = bf16[1024,2048]{1,0:T(8,128)(2,1)} fusion(bf16[512,1024]{1,0:T(8,128)(2,1)} %collective-permute-done.13, bf16[512,1024]{1,0:T(8,128)(2,1)} %broadcast_select_fusion, f32[1024,2048]{1,0:T(8,128)} %copy-done.88), kind=kOutput, calls=%fused_computation.18 | convolution fusion | flops 4320133120 | bytes 14680064 | tf_op jit(solution)/shard_map/dot_general | solution.py:660
  407.1 4.1 convolution_convert_fusion.5
  411.3 20.2 %time_attend_back.1 = bf16[16,128,768]{2,1,0:T(8,128)(2,1)} custom-call(bf16[16,128,768]{2,1,0:T(8,128)(2,1)} %bitcast.180, bf16[16,128,256]{2,1,0:T(8,128)(2,1)} %bitcast.184, f32[16,4,128]{2,1,0:T(4,128)} %get-tuple-element.55.t, f32[128,128]{1,0:T(8,128)} %and_select_fusion.b), custom_call_target="tpu_custom_call" | custom-call | flops 2684354560 | bytes 10485760 | tf_op jit(solution)/shard_map/time_attend_back/pallas_call | solution.py:809
  431.5 5.8 fusion.106
  437.3 3.3 copy-done.13
  460.2 17.3 %collective-permute-done.26 = bf16[512,1024]{1,0:T(8,128)(2,1)S(1)} collective-permute-done((bf16[512,1024]{1,0:T(8,128)(2,1)S(1)}, bf16[512,1024]{1,0:T(8,128)(2,1)S(1)}, u32[]{:S(2)}, u32[]{:S(2)}) %collective-permute-start.26) | collective-permute-done | bytes 1048608 | tf_op jit(solution)/shard_map/ppermute | solution.py:425
  484.1 3.1 fusion.14
  495.3 17.9 %space_attend_back.1 = bf16[1024,1536]{1,0:T(8,128)(2,1)} custom-call(bf16[1024,1536]{1,0:T(8,128)(2,1)} %convolution_convert_fusion.q, bf16[1024,512]{1,0:T(8,128)(2,1)} %fusion.27.g, f32[8,8,128]{2,1,0:T(8,128)} %get-tuple-element.58.t), custom_call_target="tpu_custom_call" | custom-call | flops 2684354560 | bytes 10485760 | tf_op jit(solution)/shard_map/space_attend_back/pallas_call | solution.py:762
  515.5 3.1 fusion.87
  527.7 3.0 convolution_convert_fusion.4
  533.7 3.4 fusion.107
  542.4 3.2 collective-permute-done.50
  545.5 3.2 collective-permute-done.51
  551.5 3.0 collective-permute-done.52
  569.8 3.1 collective-permute-start.40
  574.4 5.0 collective-permute-start.32
  580.1 4.7 collective-permute-start.35
  585.5 4.2 convolution_add_fusion
  590.0 11.8 %collective-permute-done.33 = bf16[512,256]{1,0:T(8,128)(2,1)S(1)} collective-permute-done((bf16[512,256]{1,0:T(8,128)(2,1)S(1)}, bf16[512,256]{1,0:T(8,128)(2,1)S(1)}, u32[]{:S(2)}, u32[]{:S(2)}) %collective-permute-start.33) | collective-permute-done | bytes 262176 | tf_op jit(solution)/shard_map/ppermute | solution.py:898
  610.6 3.4 collective-permute-start.46
  616.7 15.8 %collective-permute-done.46 = bf16[256,512]{1,0:T(8,128)(2,1)S(1)} collective-permute-done((bf16[256,512]{1,0:T(8,128)(2,1)S(1)}, bf16[256,512]{1,0:T(8,128)(2,1)S(1)}, u32[]{:S(2)}, u32[]{:S(2)}) %collective-permute-start.46) | collective-permute-done | bytes 262176 | tf_op jit(solution)/shard_map/ppermute | solution.py:437
  632.4 3.9 collective-permute-done.47
  (465 shorter events, 176.5 us)
Async XLA Ops:
  7.2 260.2 %all-gather.7.cloned.1.call-start = ((), (), s32[]{:S(2)}) async-start(), calls=%async_computation.9 | async-start | bytes 4456448 | tf_op jit(solution)/shard_map/all_gather | solution.py:948
  8.8 56.6 %collective-permute-start = (s32[2,1040]{1,0:T(2,128)S(1)}, s32[2,1040]{1,0:T(2,128)}, u32[]{:S(2)}, u32[]{:S(2)}) collective-permute-start(s32[2,1040]{1,0:T(2,128)S(1)} %constant_dynamic-update-slice_fusion), channel_id=1, source_target_pairs={{0,4},{1,5},{2,6},{3,7},{4,0},{5,1},{6,2},{7,3},{8,12},{9,13},{10,... | collective-permute-start | bytes 24968 | tf_op jit(solution)/shard_map/ppermute | solution.py:433
  64.5 211.7 %all-gather.5.cloned.1.call-start = ((), (), s32[]{:S(2)}) async-start(), calls=%async_computation.8 | async-start | bytes 4456448 | tf_op jit(solution)/shard_map/all_gather | solution.py:948
  68.9 16.2 %collective-permute-start.1 = (bf16[512,1024]{1,0:T(8,128)(2,1)S(1)}, bf16[512,1024]{1,0:T(8,128)(2,1)}, u32[]{:S(2)}, u32[]{:S(2)}) collective-permute-start(bf16[512,1024]{1,0:T(8,128)(2,1)S(1)} %multiply_convert_fusion.3), channel_id=1, source_target_pairs={{0,4},{1,5},{2,6},{3,7},{4,0},{5,1},{6,2},{7,3},{8,12},{9,13},{10,... | collective-permute-start | bytes 3145736 | tf_op jit(solution)/shard_map/ppermute | solution.py:433
  71.6 37.1 %collective-permute-start.2 = (bf16[512,256]{0,1:T(8,128)(2,1)S(1)}, bf16[512,256]{0,1:T(8,128)(2,1)S(1)}, u32[]{:S(2)}, u32[]{:S(2)}) collective-permute-start(bf16[512,256]{0,1:T(8,128)(2,1)S(1)} %constant_dynamic-slice_fusion.24), channel_id=1, source_target_pairs={{0,3},{1,0},{2,1},{3,2},{4,7},{5,4},{6,5},{7,6},{8,11},{9,8},{10,9... | collective-permute-start | bytes 786440 | tf_op jit(solution)/shard_map/ppermute | solution.py:437
  80.9 27.8 %collective-permute-start.3 = (bf16[512,256]{0,1:T(8,128)(2,1)S(1)}, bf16[512,256]{0,1:T(8,128)(2,1)S(1)}, u32[]{:S(2)}, u32[]{:S(2)}) collective-permute-start(bf16[512,256]{0,1:T(8,128)(2,1)S(1)} %constant_dynamic-slice_fusion.24), channel_id=1, source_target_pairs={{0,2},{1,3},{2,0},{3,1},{4,6},{5,7},{6,4},{7,5},{8,10},{9,11},{10,... | collective-permute-start | bytes 786440 | tf_op jit(solution)/shard_map/ppermute | solution.py:437
  82.8 28.1 %collective-permute-start.4 = (bf16[512,256]{0,1:T(8,128)(2,1)S(1)}, bf16[512,256]{0,1:T(8,128)(2,1)S(1)}, u32[]{:S(2)}, u32[]{:S(2)}) collective-permute-start(bf16[512,256]{0,1:T(8,128)(2,1)S(1)} %constant_dynamic-slice_fusion.24), channel_id=1, source_target_pairs={{0,1},{1,2},{2,3},{3,0},{4,5},{5,6},{6,7},{7,4},{8,9},{9,10},{10,1... | collective-permute-start | bytes 786440 | tf_op jit(solution)/shard_map/ppermute | solution.py:437
  118.6 30.2 %collective-permute-start.6 = (bf16[512,1024]{1,0:T(8,128)(2,1)S(1)}, bf16[512,1024]{1,0:T(8,128)(2,1)S(1)}, u32[]{:S(2)}, u32[]{:S(2)}) collective-permute-start(bf16[512,1024]{1,0:T(8,128)(2,1)S(1)} %multiply_convert_fusion.2), channel_id=1, source_target_pairs={{0,16},{1,17},{2,18},{3,19},{4,20},{5,21},{6,22},{7,23},{8,24},{9,... | collective-permute-start | bytes 3145736 | tf_op jit(solution)/shard_map/ppermute | solution.py:425
  150.4 30.5 %collective-permute-start.7 = (bf16[1024,1024]{1,0:T(8,128)(2,1)}, bf16[1024,1024]{1,0:T(8,128)(2,1)}, u32[]{:S(2)}, u32[]{:S(2)}) collective-permute-start(bf16[1024,1024]{1,0:T(8,128)(2,1)} %pad_maximum_fusion.6), channel_id=1, source_target_pairs={{0,4},{1,5},{2,6},{3,7},{4,0},{5,1},{6,2},{7,3},{8,12},{9,13},{10,... | collective-permute-start | bytes 6291464 | tf_op jit(solution)/shard_map/ppermute | solution.py:433
  153.1 337.5 %reduce-scatter.7.cloned.1.call-start = ((), (), s32[]{:S(2)}) async-start(), calls=%async_computation.5 | async-start | bytes 5242880 | tf_op jit(solution)/shard_map/reduce_scatter | solution.py:1001
  158.9 19.5 %collective-permute-start.8 = (bf16[512,768]{0,1:T(8,128)(2,1)}, bf16[512,768]{0,1:T(8,128)(2,1)}, u32[]{:S(2)}, u32[]{:S(2)}) collective-permute-start(bf16[512,768]{0,1:T(8,128)(2,1)} %constant_dynamic-update-slice_fusion.2), channel_id=1, source_target_pairs={{0,8},{1,9},{2,10},{3,11},{4,12},{5,13},{6,14},{7,15},{8,0},{9,1},... | collective-permute-start | bytes 2359304 | tf_op jit(solution)/shard_map/ppermute | solution.py:429
  183.0 35.4 %collective-permute-start.9 = (bf16[512,256]{1,0:T(8,128)(2,1)S(1)}, bf16[512,256]{1,0:T(8,128)(2,1)}, u32[]{:S(2)}, u32[]{:S(2)}) collective-permute-start(bf16[512,256]{1,0:T(8,128)(2,1)S(1)} %get-tuple-element.164), channel_id=1, source_target_pairs={{0,0},{1,4},{2,1},{3,5},{4,2},{5,6},{6,3},{7,7},{8,8},{9,12},{10,9... | collective-permute-start | bytes 786440 | tf_op jit(solution)/shard_map/ppermute | solution.py:887
  188.3 30.1 %collective-permute-start.10 = (bf16[512,256]{1,0:T(8,128)(2,1)S(1)}, bf16[512,256]{1,0:T(8,128)(2,1)}, u32[]{:S(2)}, u32[]{:S(2)}) collective-permute-start(bf16[512,256]{1,0:T(8,128)(2,1)S(1)} %get-tuple-element.167), channel_id=1, source_target_pairs={{0,4},{1,0},{2,5},{3,1},{4,6},{5,2},{6,7},{7,3},{8,12},{9,8},{10,1... | collective-permute-start | bytes 786440 | tf_op jit(solution)/shard_map/ppermute | solution.py:887
  189.2 29.3 %collective-permute-start.11 = (bf16[512,256]{1,0:T(8,128)(2,1)S(1)}, bf16[512,256]{1,0:T(8,128)(2,1)}, u32[]{:S(2)}, u32[]{:S(2)}) collective-permute-start(bf16[512,256]{1,0:T(8,128)(2,1)S(1)} %get-tuple-element.166), channel_id=1, source_target_pairs={{0,1},{1,5},{2,0},{3,4},{4,3},{5,7},{6,2},{7,6},{8,9},{9,13},{10,8... | collective-permute-start | bytes 786440 | tf_op jit(solution)/shard_map/ppermute | solution.py:887
  189.4 31.8 %collective-permute-start.12 = (bf16[512,256]{1,0:T(8,128)(2,1)S(1)}, bf16[512,256]{1,0:T(8,128)(2,1)}, u32[]{:S(2)}, u32[]{:S(2)}) collective-permute-start(bf16[512,256]{1,0:T(8,128)(2,1)S(1)} %get-tuple-element.165), channel_id=1, source_target_pairs={{0,5},{1,1},{2,4},{3,0},{4,7},{5,3},{6,6},{7,2},{8,13},{9,9},{10,1... | collective-permute-start | bytes 786440 | tf_op jit(solution)/shard_map/ppermute | solution.py:887
  230.8 32.8 %collective-permute-start.15 = (bf16[512,1024]{1,0:T(8,128)(2,1)S(1)}, bf16[512,1024]{1,0:T(8,128)(2,1)S(1)}, u32[]{:S(2)}, u32[]{:S(2)}) collective-permute-start(bf16[512,1024]{1,0:T(8,128)(2,1)S(1)} %slice.511), channel_id=1, source_target_pairs={{0,16},{1,17},{2,18},{3,19},{4,20},{5,21},{6,22},{7,23},{8,24},{9,... | collective-permute-start | bytes 3145736 | tf_op jit(solution)/shard_map/ppermute | solution.py:425
  265.7 34.2 %collective-permute-start.16 = (bf16[512,1024]{1,0:T(8,128)(2,1)}, bf16[512,1024]{1,0:T(8,128)(2,1)}, u32[]{:S(2)}, u32[]{:S(2)}) collective-permute-start(bf16[512,1024]{1,0:T(8,128)(2,1)} %multiply_convert_fusion.1), channel_id=1, source_target_pairs={{0,4},{1,5},{2,6},{3,7},{4,0},{5,1},{6,2},{7,3},{8,12},{9,13},{10,... | collective-permute-start | bytes 3145736 | tf_op jit(solution)/shard_map/ppermute | solution.py:433
  267.3 40.2 %collective-permute-start.13 = (bf16[512,1024]{1,0:T(8,128)(2,1)}, bf16[512,1024]{1,0:T(8,128)(2,1)}, u32[]{:S(2)}, u32[]{:S(2)}) collective-permute-start(bf16[512,1024]{1,0:T(8,128)(2,1)} %broadcast_select_fusion), channel_id=1, source_target_pairs={{0,4},{1,5},{2,6},{3,7},{4,0},{5,1},{6,2},{7,3},{8,12},{9,13},{10,... | collective-permute-start | bytes 3145736 | tf_op jit(solution)/shard_map/ppermute | solution.py:433
  328.8 184.4 %reduce-scatter.5.cloned.1.call-start = ((), (), s32[]{:S(2)}) async-start(), calls=%async_computation.4 | async-start | bytes 5242880 | tf_op jit(solution)/shard_map/reduce_scatter | solution.py:1001
  350.7 38.6 %collective-permute-start.18 = (bf16[512,1024]{1,0:T(8,128)(2,1)}, bf16[512,1024]{1,0:T(8,128)(2,1)S(1)}, u32[]{:S(2)}, u32[]{:S(2)}) collective-permute-start(bf16[512,1024]{1,0:T(8,128)(2,1)} %get-tuple-element.109), channel_id=1, source_target_pairs={{0,16},{1,17},{2,18},{3,19},{4,20},{5,21},{6,22},{7,23},{8,24},{9,... | collective-permute-start | bytes 3145736 | tf_op jit(solution)/shard_map/ppermute | solution.py:425
  353.2 51.3 %collective-permute-start.21 = (bf16[512,256]{1,0:T(8,128)(2,1)}, bf16[512,256]{1,0:T(8,128)(2,1)}, u32[]{:S(2)}, u32[]{:S(2)}) collective-permute-start(bf16[512,256]{1,0:T(8,128)(2,1)} %get-tuple-element.156), channel_id=1, source_target_pairs={{0,0},{4,1},{1,2},{5,3},{2,4},{6,5},{3,6},{7,7},{8,8},{12,9},{9,10... | collective-permute-start | bytes 786440 | tf_op jit(solution)/shard_map/ppermute | solution.py:898
  357.5 47.0 %collective-permute-start.22 = (bf16[512,256]{1,0:T(8,128)(2,1)}, bf16[512,256]{1,0:T(8,128)(2,1)}, u32[]{:S(2)}, u32[]{:S(2)}) collective-permute-start(bf16[512,256]{1,0:T(8,128)(2,1)} %get-tuple-element.159), channel_id=1, source_target_pairs={{4,0},{0,1},{5,2},{1,3},{6,4},{2,5},{7,6},{3,7},{12,8},{8,9},{13,1... | collective-permute-start | bytes 786440 | tf_op jit(solution)/shard_map/ppermute | solution.py:898
  357.6 46.9 %collective-permute-start.23 = (bf16[512,256]{1,0:T(8,128)(2,1)}, bf16[512,256]{1,0:T(8,128)(2,1)}, u32[]{:S(2)}, u32[]{:S(2)}) collective-permute-start(bf16[512,256]{1,0:T(8,128)(2,1)} %get-tuple-element.158), channel_id=1, source_target_pairs={{1,0},{5,1},{0,2},{4,3},{3,4},{7,5},{2,6},{6,7},{9,8},{13,9},{8,10... | collective-permute-start | bytes 786440 | tf_op jit(solution)/shard_map/ppermute | solution.py:898
  358.2 46.3 %collective-permute-start.24 = (bf16[512,256]{1,0:T(8,128)(2,1)}, bf16[512,256]{1,0:T(8,128)(2,1)}, u32[]{:S(2)}, u32[]{:S(2)}) collective-permute-start(bf16[512,256]{1,0:T(8,128)(2,1)} %get-tuple-element.157), channel_id=1, source_target_pairs={{5,0},{1,1},{4,2},{0,3},{7,4},{3,5},{6,6},{2,7},{13,8},{9,9},{12,1... | collective-permute-start | bytes 786440 | tf_op jit(solution)/shard_map/ppermute | solution.py:898
  392.5 14.6 %collective-permute-start.19 = (bf16[1024,1024]{1,0:T(8,128)(2,1)}, bf16[1024,1024]{1,0:T(8,128)(2,1)}, u32[]{:S(2)}, u32[]{:S(2)}) collective-permute-start(bf16[1024,1024]{1,0:T(8,128)(2,1)} %pad_maximum_fusion.9), channel_id=1, source_target_pairs={{0,4},{1,5},{2,6},{3,7},{4,0},{5,1},{6,2},{7,3},{8,12},{9,13},{10,... | collective-permute-start | bytes 6291464 | tf_op jit(solution)/shard_map/ppermute | solution.py:433
  404.3 199.5 %reduce-scatter.9.cloned.1.call-start = ((), (), s32[]{:S(2)}) async-start(), calls=%async_computation.6 | async-start | bytes 1310720 | tf_op jit(solution)/shard_map/reduce_scatter | solution.py:1005
  452.1 25.4 %collective-permute-start.26 = (bf16[512,1024]{1,0:T(8,128)(2,1)S(1)}, bf16[512,1024]{1,0:T(8,128)(2,1)S(1)}, u32[]{:S(2)}, u32[]{:S(2)}) collective-permute-start(bf16[512,1024]{1,0:T(8,128)(2,1)S(1)} %slice.508), channel_id=1, source_target_pairs={{0,16},{1,17},{2,18},{3,19},{4,20},{5,21},{6,22},{7,23},{8,24},{9,... | collective-permute-start | bytes 3145736 | tf_op jit(solution)/shard_map/ppermute | solution.py:425
  456.0 57.2 %collective-permute-start.29 = (bf16[512,768]{1,0:T(8,128)(2,1)}, bf16[512,768]{1,0:T(8,128)(2,1)}, u32[]{:S(2)}, u32[]{:S(2)}) collective-permute-start(bf16[512,768]{1,0:T(8,128)(2,1)} %fusion.28), channel_id=1, source_target_pairs={{0,8},{1,9},{2,10},{3,11},{4,12},{5,13},{6,14},{7,15},{8,0},{9,1},... | collective-permute-start | bytes 2359304 | tf_op jit(solution)/shard_map/ppermute | solution.py:429
  482.9 30.3 %collective-permute-start.28 = (bf16[512,256]{1,0:T(8,128)(2,1)}, bf16[512,256]{1,0:T(8,128)(2,1)S(1)}, u32[]{:S(2)}, u32[]{:S(2)}) collective-permute-start(bf16[512,256]{1,0:T(8,128)(2,1)} %fusion.36), channel_id=1, source_target_pairs={{0,8},{1,9},{2,10},{3,11},{4,12},{5,13},{6,14},{7,15},{8,0},{9,1},... | collective-permute-start | bytes 786440 | tf_op jit(solution)/shard_map/ppermute | solution.py:429
  490.3 22.9 %collective-permute-start.30 = (bf16[512,512]{1,0:T(8,128)(2,1)}, bf16[512,512]{1,0:T(8,128)(2,1)}, u32[]{:S(2)}, u32[]{:S(2)}) collective-permute-start(bf16[512,512]{1,0:T(8,128)(2,1)} %convolution_convert_fusion.6), channel_id=1, source_target_pairs={{0,8},{1,9},{2,10},{3,11},{4,12},{5,13},{6,14},{7,15},{8,0},{9,1},... | collective-permute-start | bytes 1572872 | tf_op jit(solution)/shard_map/ppermute | solution.py:429
  493.1 110.7 %reduce-scatter.11.cloned.1.call-start = ((), (), s32[]{:S(2)}) async-start(), calls=%async_computation.7 | async-start | bytes 1310720 | tf_op jit(solution)/shard_map/reduce_scatter | solution.py:1005
  522.0 18.5 %collective-permute-start.49 = (bf16[512,256]{1,0:T(8,128)(2,1)}, bf16[512,256]{1,0:T(8,128)(2,1)}, u32[]{:S(2)}, u32[]{:S(2)}) collective-permute-start(bf16[512,256]{1,0:T(8,128)(2,1)} %pad_maximum_fusion.55), channel_id=1, source_target_pairs={{0,1},{1,2},{2,3},{3,0},{4,5},{5,6},{6,7},{7,4},{8,9},{9,10},{10,1... | collective-permute-start | bytes 786440 | tf_op jit(solution)/shard_map/ppermute | solution.py:437
  524.2 21.4 %collective-permute-start.50 = (bf16[512,256]{1,0:T(8,128)(2,1)}, bf16[512,256]{1,0:T(8,128)(2,1)}, u32[]{:S(2)}, u32[]{:S(2)}) collective-permute-start(bf16[512,256]{1,0:T(8,128)(2,1)} %pad_maximum_fusion.56), channel_id=1, source_target_pairs={{0,2},{1,3},{2,0},{3,1},{4,6},{5,7},{6,4},{7,5},{8,10},{9,11},{10,... | collective-permute-start | bytes 786440 | tf_op jit(solution)/shard_map/ppermute | solution.py:437
  526.2 22.6 %collective-permute-start.51 = (bf16[512,256]{1,0:T(8,128)(2,1)}, bf16[512,256]{1,0:T(8,128)(2,1)}, u32[]{:S(2)}, u32[]{:S(2)}) collective-permute-start(bf16[512,256]{1,0:T(8,128)(2,1)} %pad_maximum_fusion.57), channel_id=1, source_target_pairs={{0,3},{1,0},{2,1},{3,2},{4,7},{5,4},{6,5},{7,6},{8,11},{9,8},{10,9... | collective-permute-start | bytes 786440 | tf_op jit(solution)/shard_map/ppermute | solution.py:437
  530.7 54.7 %collective-permute-start.42 = (bf16[512,1536]{1,0:T(8,128)(2,1)}, bf16[512,1536]{1,0:T(8,128)(2,1)}, u32[]{:S(2)}, u32[]{:S(2)}) collective-permute-start(bf16[512,1536]{1,0:T(8,128)(2,1)} %convolution_convert_fusion.4), channel_id=1, source_target_pairs={{0,8},{1,9},{2,10},{3,11},{4,12},{5,13},{6,14},{7,15},{8,0},{9,1},... | collective-permute-start | bytes 4718600 | tf_op jit(solution)/shard_map/ppermute | solution.py:429
  538.0 12.3 %collective-permute-start.44 = (bf16[256,512]{1,0:T(8,128)(2,1)}, bf16[256,512]{1,0:T(8,128)(2,1)}, u32[]{:S(2)}, u32[]{:S(2)}) collective-permute-start(bf16[256,512]{1,0:T(8,128)(2,1)} %select_convert_fusion.2), channel_id=1, source_target_pairs={{0,16},{1,17},{2,18},{3,19},{4,20},{5,21},{6,22},{7,23},{8,24},{9,... | collective-permute-start | bytes 786440 | tf_op jit(solution)/shard_map/ppermute | solution.py:425
  540.5 17.5 %collective-permute-start.31 = (bf16[512,1024]{1,0:T(8,128)(2,1)}, bf16[512,1024]{1,0:T(8,128)(2,1)S(1)}, u32[]{:S(2)}, u32[]{:S(2)}) collective-permute-start(bf16[512,1024]{1,0:T(8,128)(2,1)} %slice.507), channel_id=1, source_target_pairs={{0,4},{1,5},{2,6},{3,7},{4,0},{5,1},{6,2},{7,3},{8,12},{9,13},{10,... | collective-permute-start | bytes 3145736 | tf_op jit(solution)/shard_map/ppermute | solution.py:433
  569.8 9.7 %collective-permute-start.39 = (f32[4,256]{1,0:T(4,128)S(1)}, f32[4,256]{1,0:T(4,128)S(1)}, u32[]{:S(2)}, u32[]{:S(2)}) collective-permute-start(f32[4,256]{1,0:T(4,128)S(1)} %get-tuple-element.187), channel_id=1, source_target_pairs={{0,1},{1,2},{2,3},{3,0},{4,5},{5,6},{6,7},{7,4},{8,9},{9,10},{10,1... | collective-permute-start | bytes 12296 | tf_op jit(solution)/shard_map/ppermute | solution.py:437
  569.8 9.8 %collective-permute-start.40 = (f32[4,256]{1,0:T(4,128)S(1)}, f32[4,256]{1,0:T(4,128)S(1)}, u32[]{:S(2)}, u32[]{:S(2)}) collective-permute-start(f32[4,256]{1,0:T(4,128)S(1)} %get-tuple-element.189), channel_id=1, source_target_pairs={{0,2},{1,3},{2,0},{3,1},{4,6},{5,7},{6,4},{7,5},{8,10},{9,11},{10,... | collective-permute-start | bytes 12296 | tf_op jit(solution)/shard_map/ppermute | solution.py:437
  572.9 7.2 %collective-permute-start.41 = (f32[4,256]{1,0:T(4,128)S(1)}, f32[4,256]{1,0:T(4,128)S(1)}, u32[]{:S(2)}, u32[]{:S(2)}) collective-permute-start(f32[4,256]{1,0:T(4,128)S(1)} %get-tuple-element.188), channel_id=1, source_target_pairs={{0,3},{1,0},{2,1},{3,2},{4,7},{5,4},{6,5},{7,6},{8,11},{9,8},{10,9... | collective-permute-start | bytes 12296 | tf_op jit(solution)/shard_map/ppermute | solution.py:437
  574.4 15.5 %collective-permute-start.32 = (bf16[512,256]{1,0:T(8,128)(2,1)S(1)}, bf16[512,256]{1,0:T(8,128)(2,1)S(1)}, u32[]{:S(2)}, u32[]{:S(2)}) collective-permute-start(bf16[512,256]{1,0:T(8,128)(2,1)S(1)} %get-tuple-element.148), channel_id=1, source_target_pairs={{0,0},{4,1},{1,2},{5,3},{2,4},{6,5},{3,6},{7,7},{8,8},{12,9},{9,10... | collective-permute-start | bytes 786440 | tf_op jit(solution)/shard_map/ppermute | solution.py:898
  579.5 22.3 %collective-permute-start.33 = (bf16[512,256]{1,0:T(8,128)(2,1)S(1)}, bf16[512,256]{1,0:T(8,128)(2,1)S(1)}, u32[]{:S(2)}, u32[]{:S(2)}) collective-permute-start(bf16[512,256]{1,0:T(8,128)(2,1)S(1)} %get-tuple-element.151), channel_id=1, source_target_pairs={{4,0},{0,1},{5,2},{1,3},{6,4},{2,5},{7,6},{3,7},{12,8},{8,9},{13,1... | collective-permute-start | bytes 786440 | tf_op jit(solution)/shard_map/ppermute | solution.py:898
  579.6 22.2 %collective-permute-start.34 = (bf16[512,256]{1,0:T(8,128)(2,1)S(1)}, bf16[512,256]{1,0:T(8,128)(2,1)S(1)}, u32[]{:S(2)}, u32[]{:S(2)}) collective-permute-start(bf16[512,256]{1,0:T(8,128)(2,1)S(1)} %get-tuple-element.150), channel_id=1, source_target_pairs={{1,0},{5,1},{0,2},{4,3},{3,4},{7,5},{2,6},{6,7},{9,8},{13,9},{8,10... | collective-permute-start | bytes 786440 | tf_op jit(solution)/shard_map/ppermute | solution.py:898
  580.1 21.7 %collective-permute-start.35 = (bf16[512,256]{1,0:T(8,128)(2,1)S(1)}, bf16[512,256]{1,0:T(8,128)(2,1)S(1)}, u32[]{:S(2)}, u32[]{:S(2)}) collective-permute-start(bf16[512,256]{1,0:T(8,128)(2,1)S(1)} %get-tuple-element.149), channel_id=1, source_target_pairs={{5,0},{1,1},{4,2},{0,3},{7,4},{3,5},{6,6},{2,7},{13,8},{9,9},{12,1... | collective-permute-start | bytes 786440 | tf_op jit(solution)/shard_map/ppermute | solution.py:898
  589.9 18.0 %collective-permute-start.43 = (bf16[256,1536]{1,0:T(8,128)(2,1)S(1)}, bf16[256,1536]{1,0:T(8,128)(2,1)}, u32[]{:S(2)}, u32[]{:S(2)}) collective-permute-start(bf16[256,1536]{1,0:T(8,128)(2,1)S(1)} %select_convert_fusion.1), channel_id=1, source_target_pairs={{0,16},{1,17},{2,18},{3,19},{4,20},{5,21},{6,22},{7,23},{8,24},{9,... | collective-permute-start | bytes 2359304 | tf_op jit(solution)/shard_map/ppermute | solution.py:425
  604.9 9.2 %collective-permute-start.54 = (bf16[128,1024]{0,1:T(8,128)(2,1)S(1)}, bf16[128,1024]{0,1:T(8,128)(2,1)S(1)}, u32[]{:S(2)}, u32[]{:S(2)}) collective-permute-start(bf16[128,1024]{0,1:T(8,128)(2,1)S(1)} %dynamic-slice_convert_fusion), channel_id=1, source_target_pairs={{0,4},{1,5},{2,6},{3,7},{4,0},{5,1},{6,2},{7,3},{8,12},{9,13},{10,... | collective-permute-start | bytes 786440 | tf_op jit(solution)/shard_map/ppermute | solution.py:433
  610.6 21.8 %collective-permute-start.46 = (bf16[256,512]{1,0:T(8,128)(2,1)S(1)}, bf16[256,512]{1,0:T(8,128)(2,1)S(1)}, u32[]{:S(2)}, u32[]{:S(2)}) collective-permute-start(bf16[256,512]{1,0:T(8,128)(2,1)S(1)} %pad_maximum_fusion.53), channel_id=1, source_target_pairs={{0,2},{1,3},{2,0},{3,1},{4,6},{5,7},{6,4},{7,5},{8,10},{9,11},{10,... | collective-permute-start | bytes 786440 | tf_op jit(solution)/shard_map/ppermute | solution.py:437
  614.0 22.2 %collective-permute-start.47 = (bf16[256,512]{1,0:T(8,128)(2,1)S(1)}, bf16[256,512]{1,0:T(8,128)(2,1)S(1)}, u32[]{:S(2)}, u32[]{:S(2)}) collective-permute-start(bf16[256,512]{1,0:T(8,128)(2,1)S(1)} %pad_maximum_fusion.54), channel_id=1, source_target_pairs={{0,3},{1,0},{2,1},{3,2},{4,7},{5,4},{6,5},{7,6},{8,11},{9,8},{10,9... | collective-permute-start | bytes 786440 | tf_op jit(solution)/shard_map/ppermute | solution.py:437
  (104 other events, 882.4 us)
Sparse Core Ops, SparseCore 0:
  64.6 103.1 all-gather.6
  170.5 93.6 all-gather.4
  328.9 66.1 reduce-scatter.6
  404.4 52.2 reduce-scatter.4
  493.2 25.4 reduce-scatter.8
  540.6 25.4 reduce-scatter.10

commit v3 on v2

--- a/solution.py
+++ b/solution.py
@@ -1,3 +1,4 @@
+import functools
 import math
 
 import jax
@@ -446,9 +447,9 @@
 
 
 def arrive_kernel(
-    tok, vec, mine, rows_out, vec_out, wq, wo,
+    tok, vec, mine, later, rows_out, vec_out, wq, wo, wt,
     z_send, z_recv, y_send, y_recv, x_send, x_recv, p_send, p_recv, q_send, q_recv,
-    t_send, t_recv, v_send, v_recv, local,
+    t_send, t_recv, v_send, v_recv, u_send, u_recv, w_send, w_recv, local,
 ):
     y, x, c, z = (lax.axis_index(name) for name in AXES)
     half = wo.shape[1] // 4
@@ -512,6 +513,45 @@
     def corner_y(r):
         part = piece(0, 1, r, split=True)[1:]
         return copies(part, part, q_send.at[r], q_recv.at[r], near_y)
+
+    span = wt.shape[1] // 4
+
+    def time_piece(dx, r):
+        at = pl.ds(pl.multiple_of(((z + r) % 4) * span, span), span)
+        return wt.at[pl.ds(pl.multiple_of(2 * BLK * ((x + dx) % 2), BLK), 2 * BLK), at]
+
+    def time_z(right, step):
+        if right:
+            r = 0 if step == 0 else 4 - step
+            peer, lands = (y, x, c, (z + 1) % 4), 3 - step
+        else:
+            r = step
+            peer, lands = (y, x, c, (z + 3) % 4), step + 1
+        source = later.at[pl.ds(pl.multiple_of(2 * BLK * x, BLK), 2 * BLK)] if step == 0 else time_piece(0, r)
+        return [
+            pltpu.make_async_remote_copy(
+                src_ref=source, dst_ref=time_piece(0, r), send_sem=u_send.at[int(right), step], recv_sem=u_recv.at[lands],
+                device_id=peer, device_id_type=MESH,
+            )
+        ]
+
+    def time_x(dx, r):
+        return [
+            pltpu.make_async_remote_copy(
+                src_ref=time_piece(dx, r), dst_ref=time_piece(dx, r), send_sem=w_send.at[r], recv_sem=w_recv.at[r],
+                device_id=near_x, device_id_type=MESH,
+            )
+        ]
+
+    def time_forward(j, left):
+        r = 3 - j if left else j + 1
+        pltpu.make_async_remote_copy(
+            src_ref=time_piece(0, r), dst_ref=time_piece(0, r), send_sem=u_send.at[0, 0], recv_sem=u_recv.at[r],
+            device_id=near_x, device_id_type=MESH,
+        ).wait_recv()
+        if j < 2:
+            pl.when(z < 3 if left else z > 0)(lambda: start(time_z(left, j + 1)))
+        start(time_x(0, r))
 
     def start(all_copies):
         for copy in all_copies:
@@ -559,6 +599,7 @@
     keep = [
         pltpu.make_async_copy(mine.at[:, pl.ds(0, wide)], wq.at[:, pl.ds(pl.multiple_of(z * wide, half), wide)], local.at[0]),
         pltpu.make_async_copy(mine.at[:, pl.ds(wide, half)], wo.at[:, pl.ds(pl.multiple_of(z * half, half), half)], local.at[1]),
+        pltpu.make_async_copy(later, wt.at[:, pl.ds(pl.multiple_of(z * span, span), span)], local.at[4]),
     ]
     start(keep)
 
@@ -584,11 +625,16 @@
             for k in range(4):
                 pl.when(stays(k))(lambda k=k: start(token_local(k)))
                 pl.when(jnp.logical_not(stays(k)))(lambda k=k: start(token_copies(k)))
+            pl.when(z < 3)(lambda: start(time_z(True, 0)))
+            pl.when(z > 0)(lambda: start(time_z(False, 0)))
         else:
             for left in (True, False):
                 pl.when(from_left(j - 1) if left else from_right(j - 1))(lambda j=j, left=left: corners(j - 1, left))
     for left in (True, False):
         pl.when(from_left(2) if left else from_right(2))(lambda left=left: corners(2, left))
+    for j in range(3):
+        for left in (True, False):
+            pl.when(from_left(j) if left else from_right(j))(lambda j=j, left=left: time_forward(j, left))
 
     for copy in keep:
         copy.wait()
@@ -596,11 +642,12 @@
         part = piece(1, 1, r, split=True)
         landed(copies(part[:1], part[:1], p_send.at[r], p_recv.at[r], near_x))
         landed(copies(part[1:], part[1:], q_send.at[r], q_recv.at[r], near_y))
-        for group in (y_copies(r), x_copies(r), corner_x(r), corner_y(r)):
+        for group in (y_copies(r), x_copies(r), corner_x(r), corner_y(r), time_x(0, r)):
             sent(group)
+        landed(time_x(1, r))
     for step in range(3):
-        pl.when(jnp.logical_and(z >= step, z < 3))(lambda step=step: sent(z_copies(True, step)))
-        pl.when(jnp.logical_and(z + step <= 3, z > 0))(lambda step=step: sent(z_copies(False, step)))
+        pl.when(jnp.logical_and(z >= step, z < 3))(lambda step=step: sent(z_copies(True, step) + time_z(True, step)))
+        pl.when(jnp.logical_and(z + step <= 3, z > 0))(lambda step=step: sent(z_copies(False, step) + time_z(False, step)))
     for k in range(4):
         def finish_local(k=k):
             for copy in token_local(k):
@@ -624,28 +671,30 @@
         pl.when(away)(arrived)
 
 
-def arrive(tok, vec, mine):
+def arrive(tok, vec, mine, later):
     own, width, half = tok.shape[1], 4 * tok.shape[2], mine.shape[1] // 4
     dma = pltpu.SemaphoreType.DMA
     anywhere = pl.BlockSpec(memory_space=pl.ANY)
     return pl.pallas_call(
         arrive_kernel,
-        in_specs=[anywhere] * 3,
-        out_specs=[anywhere] * 4,
+        in_specs=[anywhere] * 4,
+        out_specs=[anywhere] * 5,
         out_shape=[
             jax.ShapeDtypeStruct((own, width), BF16),
             jax.ShapeDtypeStruct((vec.shape[0], width), BF16),
             jax.ShapeDtypeStruct((width, 12 * half), BF16),
             jax.ShapeDtypeStruct((width, 4 * half), BF16),
+            jax.ShapeDtypeStruct((width, 4 * later.shape[1]), BF16),
         ],
         scratch_shapes=[
             dma((2, 3, 2)), dma((4, 2)), dma((4, 2)), dma((4, 2)), dma((4, 2)), dma((4, 2)),
             dma((4, 1)), dma((4, 1)), dma((4, 2)), dma((4, 2)),
-            dma((4,)), dma((4,)), dma((4,)), dma((4,)), dma((4,)),
+            dma((4,)), dma((4,)), dma((4,)), dma((4,)),
+            dma((2, 3)), dma((4,)), dma((4,)), dma((4,)), dma((5,)),
         ],
         compiler_params=pltpu.CompilerParams(collective_id=0, has_side_effects=True),
         name="arrive",
-    )(tok, vec, mine)
+    )(tok, vec, mine, later)
 
 
 def dot_nn(a, b):
@@ -660,74 +709,60 @@
     return lax.dot_general(a, b, (((0,), (0,)), ((), ())), preferred_element_type=F32)
 
 
-def row_reader(ref):
-    if len(ref.shape) == 2:
-        return lambda lo, width: ref[:, lo : lo + width]
-    rows = ref.shape[0] * ref.shape[1]
-    return lambda lo, width: ref[:, :, lo : lo + width].astype(F32).reshape(rows, width).astype(BF16)
-
-
-def row_writer(ref):
-    def write(lo, v):
-        if len(ref.shape) == 2:
-            ref[:, lo : lo + v.shape[1]] = v.astype(BF16)
-        else:
-            ref[:, :, lo : lo + v.shape[1]] = v.reshape(ref.shape[:2] + v.shape[1:]).astype(BF16)
-
-    return write
-
-
-def by_pair(lo):
-    return (3 * lo, 3 * lo + 2 * HEAD_DIM, 3 * lo + 4 * HEAD_DIM)
-
-
-def by_part(width):
-    return lambda lo: (lo, width + lo, 2 * width + lo)
-
-
-def attend_kernel(heads, scale, places, qkv_ref, bias_ref, out_ref, total_ref):
-    width = heads * HEAD_DIM
-    read, write = row_reader(qkv_ref), row_writer(out_ref)
-    for lo in range(0, width, 2 * HEAD_DIM):
-        q, k, v = (read(at, 2 * HEAD_DIM) for at in places(lo))
-        mixed = []
-        for i in range(2):
-            mine = slice(i * HEAD_DIM, (i + 1) * HEAD_DIM)
-            h = lo // HEAD_DIM + i
-            scores = dot_nt(k[:, mine], q[:, mine]) * scale
-            if bias_ref is not None:
-                scores = scores + bias_ref[...]
-            highest = jnp.max(scores, axis=0, keepdims=True)
-            exponent = jnp.exp(scores - highest)
-            total = jnp.sum(exponent, axis=0, keepdims=True)
-            total_ref[0, h : h + 1, :] = highest + jnp.log(total)
-            mixed.append(dot_tn(v[:, mine], exponent.astype(BF16)) * (1.0 / total))
-        write(lo, jnp.concatenate(mixed, axis=0).T)
-
-
-def attend_back_kernel(heads, scale, places, qkv_ref, grad_ref, total_ref, bias_ref, out_ref):
-    width = heads * HEAD_DIM
-    read, read_grad, write = row_reader(qkv_ref), row_reader(grad_ref), row_writer(out_ref)
-    for lo in range(0, width, 2 * HEAD_DIM):
-        q, k, v = (read(at, 2 * HEAD_DIM) for at in places(lo))
-        g = read_grad(lo, 2 * HEAD_DIM)
-        grads = ([], [], [])
-        for i in range(2):
-            mine = slice(i * HEAD_DIM, (i + 1) * HEAD_DIM)
-            h = lo // HEAD_DIM + i
-            scores = dot_nt(k[:, mine], q[:, mine]) * scale
-            if bias_ref is not None:
-                scores = scores + bias_ref[...]
-            p = jnp.exp(scores - total_ref[0, h : h + 1, :])
-            dp = dot_nt(v[:, mine], g[:, mine])
-            ds = (p * (dp - jnp.sum(p * dp, axis=0, keepdims=True))).astype(BF16)
-            grads[0].append(dot_tn(k[:, mine], ds) * scale)
-            grads[1].append(dot_nn(ds, q[:, mine]) * scale)
-            grads[2].append(dot_nn(p.astype(BF16), g[:, mine]))
-        at_q, at_k, at_v = places(lo)
-        write(at_q, jnp.concatenate(grads[0], axis=0).T)
-        write(at_k, jnp.concatenate(grads[1], axis=1))
-        write(at_v, jnp.concatenate(grads[2], axis=1))
+def attend_pair(q, k, v, bias, scale):
+    mixed, totals = [], []
+    for i in range(2):
+        mine = slice(i * HEAD_DIM, (i + 1) * HEAD_DIM)
+        scores = dot_nt(k[:, mine], q[:, mine]) * scale
+        if bias is not None:
+            scores = scores + bias
+        highest = jnp.max(scores, axis=0, keepdims=True)
+        exponent = jnp.exp(scores - highest)
+        total = jnp.sum(exponent, axis=0, keepdims=True)
+        totals.append(highest + jnp.log(total))
+        mixed.append(dot_tn(v[:, mine], exponent.astype(BF16)) * (1.0 / total))
+    return (jnp.concatenate(mixed, axis=0).T, totals)
+
+
+def attend_pair_back(q, k, v, g, totals, bias, scale):
+    grads = ([], [], [])
+    for i in range(2):
+        mine = slice(i * HEAD_DIM, (i + 1) * HEAD_DIM)
+        scores = dot_nt(k[:, mine], q[:, mine]) * scale
+        if bias is not None:
+            scores = scores + bias
+        p = jnp.exp(scores - totals[i])
+        dp = dot_nt(v[:, mine], g[:, mine])
+        ds = (p * (dp - jnp.sum(p * dp, axis=0, keepdims=True))).astype(BF16)
+        grads[0].append(dot_tn(k[:, mine], ds) * scale)
+        grads[1].append(dot_nn(ds, q[:, mine]) * scale)
+        grads[2].append(dot_nn(p.astype(BF16), g[:, mine]))
+    return (
+        jnp.concatenate(grads[0], axis=0).T,
+        jnp.concatenate(grads[1], axis=1),
+        jnp.concatenate(grads[2], axis=1),
+    )
+
+
+PAIR = 2 * HEAD_DIM
+
+
+def space_attend_kernel(scale, qkv_ref, out_ref, total_ref):
+    for i in range(out_ref.shape[1] // PAIR):
+        q, k, v = (qkv_ref[:, (3 * i + part) * PAIR : (3 * i + part + 1) * PAIR] for part in range(3))
+        mixed, totals = attend_pair(q, k, v, None, scale)
+        out_ref[:, i * PAIR : (i + 1) * PAIR] = mixed.astype(BF16)
+        for h in range(2):
+            total_ref[0, 2 * i + h : 2 * i + h + 1, :] = totals[h]
+
+
+def space_attend_back_kernel(scale, qkv_ref, grad_ref, total_ref, out_ref):
+    for i in range(grad_ref.shape[1] // PAIR):
+        q, k, v = (qkv_ref[:, (3 * i + part) * PAIR : (3 * i + part + 1) * PAIR] for part in range(3))
+        totals = [total_ref[0, 2 * i + h : 2 * i + h + 1, :] for h in range(2)]
+        grads = attend_pair_back(q, k, v, grad_ref[:, i * PAIR : (i + 1) * PAIR], totals, None, scale)
+        for part in range(3):
+            out_ref[:, (3 * i + part) * PAIR : (3 * i + part + 1) * PAIR] = grads[part].astype(BF16)
 
 
 def attention_cost(groups, rows, heads, products):
@@ -741,7 +776,7 @@
 def space_attend(qkv, frames, patches, heads, scale):
     width = heads * HEAD_DIM
     return pl.pallas_call(
-        lambda q, o, t: attend_kernel(heads, scale, by_pair, q, None, o, t),
+        functools.partial(space_attend_kernel, scale),
         grid=(frames,),
         in_specs=[pl.BlockSpec((patches, 3 * width), lambda i: (i, 0))],
         out_specs=[
@@ -760,7 +795,7 @@
 def space_attend_back(qkv, grad, total, frames, patches, heads, scale):
     width = heads * HEAD_DIM
     return pl.pallas_call(
-        lambda q, g, t, o: attend_back_kernel(heads, scale, by_pair, q, g, t, None, o),
+        functools.partial(space_attend_back_kernel, scale),
         grid=(frames,),
         in_specs=[
             pl.BlockSpec((patches, 3 * width), lambda i: (i, 0)),
@@ -775,56 +810,237 @@
 
 
 GROUP = 8
-
-
-def time_attend(qkv, bias, frames, patches, heads, scale):
+CHUNK = 32
+
+
+def time_kernel(back, scale, heads, *refs):
+    if back:
+        (own_ref, rider_ref, joined_ref, total_ref, wq_ref, wo_ref, bias_ref, all_ref, out_ref, delta_ref, rider_out) = refs[:11]
+        refs = refs[11:]
+    else:
+        (own_ref, rider_ref, wq_ref, wo_ref, bias_ref, all_ref, out_ref, mixed_ref, total_ref, delta_ref, rider_out) = refs[:11]
+        refs = refs[11:]
+    (
+        held, wide, narrow, kept, core_out, core_in, near_out, near_in,
+        gy_send, gy_recv, gc_send, gc_recv, gd_send, gd_recv, sc_send, sc_recv, sy_send, sy_recv,
+        r_send, r_recv, r_local, out_sem,
+    ) = refs
+    y, x, c, z = (lax.axis_index(name) for name in AXES)
+    near, pair = (1 - y, x, c, z), (y, x, 1 - c, z)
+    frames = held.shape[0] // 4
+    chunks = held.shape[1] // CHUNK
     width = heads * HEAD_DIM
-    rows = frames * GROUP
-    groups = patches // GROUP
-    mixed, total = pl.pallas_call(
-        lambda q, b, o, t: attend_kernel(heads, scale, by_part(width), q, b, o, t),
-        grid=(groups,),
-        in_specs=[
-            pl.BlockSpec((frames, GROUP, 3 * width), lambda i: (0, i, 0)),
-            pl.BlockSpec((rows, rows), lambda i: (0, 0)),
-        ],
-        out_specs=[
-            pl.BlockSpec((frames, GROUP, width), lambda i: (0, i, 0)),
-            pl.BlockSpec((1, heads, rows), lambda i: (i, 0, 0)),
-        ],
-        out_shape=[
-            jax.ShapeDtypeStruct((frames, patches, width), BF16),
-            jax.ShapeDtypeStruct((groups, heads, rows), F32),
-        ],
-        cost_estimate=attention_cost(groups, rows, heads, 2),
-        name="time_attend",
-    )(qkv.reshape(frames, patches, 3 * width), bias)
-    return (mixed.reshape(frames * patches, width), total)
-
-
-def time_attend_back(qkv, grad, total, bias, frames, patches, heads, scale):
-    width = heads * HEAD_DIM
-    rows = frames * GROUP
-    groups = patches // GROUP
+    groups = CHUNK // GROUP
+
+    barrier = pltpu.get_barrier_semaphore()
+    for dc in range(2):
+        for dz in range(4):
+            if dc or dz:
+                pl.semaphore_signal(barrier, inc=1, device_id=(y, x, (c + dc) % 2, (z + dz) % 4), device_id_type=MESH)
+    pl.semaphore_signal(barrier, inc=1, device_id=near, device_id_type=MESH)
+    pl.semaphore_wait(barrier, 8)
+
+    def remote(src, dst, send, recv, peer):
+        return pltpu.make_async_remote_copy(
+            src_ref=src, dst_ref=dst, send_sem=send, recv_sem=recv, device_id=peer, device_id_type=MESH
+        )
+
+    def patches(k):
+        return pl.ds(pl.multiple_of(k * CHUNK, CHUNK), CHUNK)
+
+    def block(b, k):
+        return held.at[pl.ds(b * frames, frames), patches(k)]
+
+    def gather_y(k):
+        return remote(own_ref.at[:, patches(k)], block(1, k), gy_send.at[k], gy_recv.at[k], near)
+
+    def gather_c(k):
+        return remote(own_ref.at[:, patches(k)], block(2, k), gc_send.at[k], gc_recv.at[k], pair)
+
+    def gather_d(k):
+        return remote(block(1, k), block(3, k), gd_send.at[k], gd_recv.at[k], pair)
+
+    def scatter_c(k):
+        return remote(core_out.at[k], core_in.at[k], sc_send.at[k], sc_recv.at[k], pair)
+
+    def scatter_y(k):
+        return remote(near_out.at[k], near_in.at[k], sy_send.at[k], sy_recv.at[k], near)
+
+    def save(k):
+        return pltpu.make_async_copy(held.at[:, patches(k)], all_ref.at[:, patches(k)], out_sem.at[k])
+
+    def columns(s):
+        return pl.ds(pl.multiple_of(s * BLK, BLK), BLK)
+
+    def stays(k):
+        if back:
+            return jnp.logical_and(z == k, z // 2 == c)
+        return jnp.logical_and(2 * c + k // 2 == z, c == k % 2)
+
+    def ride(k):
+        if back:
+            src, dst = rider_ref.at[:, columns(k)], rider_out.at[2 * (z % 2) + c]
+            peer, slot = (y, x, z // 2, k), 2 * (z % 2) + c
+        else:
+            src, dst = rider_ref.at[k], rider_out.at[:, columns(z)]
+            peer, slot = (y, x, k % 2, 2 * c + k // 2), z
+        return src, dst, peer, slot
+
+    def ride_remote(k):
+        src, dst, peer, slot = ride(k)
+        return remote(src, dst, r_send.at[k], r_recv.at[slot], peer)
+
+    def ride_local(k):
+        src, dst, _, _ = ride(k)
+        return pltpu.make_async_copy(src, dst, r_local.at[0])
+
+    def ride_landed(k):
+        if back:
+            src, dst = rider_ref.at[:, columns(k)], rider_out.at[k]
+        else:
+            src, dst = rider_ref.at[k], rider_out.at[:, columns(k)]
+        return remote(src, dst, r_send.at[k], r_recv.at[k], near)
+
+    def from_self(k):
+        if back:
+            return jnp.logical_and(2 * c + k // 2 == z, c == k % 2)
+        return jnp.logical_and(z == k, z // 2 == c)
+
+    for k in range(chunks):
+        gather_y(k).start()
+        gather_c(k).start()
+    for k in range(4):
+        pl.when(stays(k))(lambda k=k: ride_local(k).start())
+        pl.when(jnp.logical_not(stays(k)))(lambda k=k: ride_remote(k).start())
+    held[:frames] = own_ref[...]
+
+    def finish(k):
+        scatter_c(k).wait_recv()
+        both = kept[:, patches(k)] + core_in[k].astype(F32)
+        near_out[k] = both[frames:].astype(BF16)
+        delta_ref[:, patches(k)] = both[:frames]
+        scatter_y(k).start()
+
+    def pass_on(k):
+        gather_y(k).wait_recv()
+        gather_d(k).start()
+
+    def one_group(i, rows):
+        at = pl.ds(pl.multiple_of(i * GROUP, GROUP), GROUP)
+        count = 4 * frames * GROUP
+        bias = bias_ref[...]
+        for lo in range(0, width, PAIR):
+            q, k, v = (
+                wide[:, at, part * width + lo : part * width + lo + PAIR].reshape(count, PAIR).astype(BF16)
+                for part in range(3)
+            )
+            h = lo // HEAD_DIM
+            if back:
+                g = narrow[:, at, lo : lo + PAIR].reshape(count, PAIR).astype(BF16)
+                totals = [total_ref[rows * groups + i, h + j : h + j + 1, :] for j in range(2)]
+                grads = attend_pair_back(q, k, v, g, totals, bias, scale)
+                for part in range(3):
+                    wide[:, at, part * width + lo : part * width + lo + PAIR] = grads[part].reshape(
+                        4 * frames, GROUP, PAIR
+                    )
+            else:
+                mixed, totals = attend_pair(q, k, v, bias, scale)
+                narrow[:, at, lo : lo + PAIR] = mixed.reshape(4 * frames, GROUP, PAIR)
+                for j in range(2):
+                    total_ref[rows * groups + i, h + j : h + j + 1, :] = totals[j]
+
+    def one_chunk(k, carry):
+        pl.when(k + 1 < chunks)(lambda: pass_on(k + 1))
+        gather_c(k).wait_recv()
+        gather_d(k).wait_recv()
+        count = 4 * frames * CHUNK
+        lhs = held[:, patches(k)].reshape(count, held.shape[2])
+        if back:
+            wide[...] = joined_ref[:, patches(k)].astype(F32)
+            narrow[...] = dot_nn(lhs, wo_ref[...]).astype(BF16).astype(F32).reshape(narrow.shape)
+        else:
+            joined = dot_nn(lhs, wq_ref[...]).astype(BF16)
+            out_ref[:, patches(k)] = joined.reshape(wide.shape)
+            wide[...] = joined.astype(F32).reshape(wide.shape)
+        save(k).start()
+        lax.fori_loop(0, groups, lambda i, carry: (one_group(i, k), carry)[1], 0)
+        if back:
+            grads = wide[...].astype(BF16)
+            out_ref[:, patches(k)] = grads
+            partial = dot_nt(grads.reshape(count, 3 * width), wq_ref[...])
+        else:
+            mixed = narrow[...].astype(BF16)
+            mixed_ref[:, patches(k)] = mixed
+            partial = dot_nt(mixed.reshape(count, width), wo_ref[...])
+        partial = partial.reshape(4 * frames, CHUNK, held.shape[2])
+        kept[:, patches(k)] = partial[: 2 * frames]
+        core_out[k] = partial[2 * frames :].astype(BF16)
+        scatter_c(k).start()
+        pl.when(k > 0)(lambda: finish(k - 1))
+        return carry
+
+    pass_on(0)
+    lax.fori_loop(0, chunks, one_chunk, 0)
+    finish(chunks - 1)
+    for k in range(chunks):
+        scatter_y(k).wait_recv()
+        delta_ref[:, patches(k)] = delta_ref[:, patches(k)] + near_in[k].astype(F32)
+    for k in range(chunks):
+        for copy in (gather_y(k), gather_c(k), gather_d(k), scatter_c(k), scatter_y(k)):
+            copy.wait_send()
+        save(k).wait()
+    for k in range(4):
+        pl.when(stays(k))(lambda k=k: ride_local(k).wait())
+        pl.when(jnp.logical_not(stays(k)))(lambda k=k: ride_remote(k).wait_send())
+        pl.when(jnp.logical_not(from_self(k)))(lambda k=k: ride_landed(k).wait_recv())
+
+
+def time_call(back, own, rider, saved, wq, wo, bias, scale):
+    frames, patches, features = own.shape
+    width = wo.shape[1]
+    heads = width // HEAD_DIM
+    chunks = patches // CHUNK
+    rows = 4 * frames * GROUP
+    dma = pltpu.SemaphoreType.DMA
+    anywhere = pl.BlockSpec(memory_space=pl.ANY)
+    whole = pl.BlockSpec(memory_space=pltpu.VMEM)
+    out_shape = [
+        jax.ShapeDtypeStruct((4 * frames, patches, features), BF16),
+        jax.ShapeDtypeStruct((4 * frames, patches, 3 * width), BF16),
+    ]
+    if not back:
+        out_shape += [
+            jax.ShapeDtypeStruct((4 * frames, patches, width), BF16),
+            jax.ShapeDtypeStruct((patches // GROUP, heads, rows), F32),
+        ]
+    rider_shape = (4, frames * patches, BLK) if back else (frames * patches, features)
+    out_shape += [
+        jax.ShapeDtypeStruct((frames, patches, features), F32),
+        jax.ShapeDtypeStruct(rider_shape, BF16),
+    ]
     return pl.pallas_call(
-        lambda q, g, t, b, o: attend_back_kernel(heads, scale, by_part(width), q, g, t, b, o),
-        grid=(groups,),
-        in_specs=[
-            pl.BlockSpec((frames, GROUP, 3 * width), lambda i: (0, i, 0)),
-            pl.BlockSpec((frames, GROUP, width), lambda i: (0, i, 0)),
-            pl.BlockSpec((1, heads, rows), lambda i: (i, 0, 0)),
-            pl.BlockSpec((rows, rows), lambda i: (0, 0)),
-        ],
-        out_specs=pl.BlockSpec((frames, GROUP, 3 * width), lambda i: (0, i, 0)),
-        out_shape=jax.ShapeDtypeStruct((frames, patches, 3 * width), BF16),
-        cost_estimate=attention_cost(groups, rows, heads, 5),
-        name="time_attend_back",
-    )(
-        qkv.reshape(frames, patches, 3 * width),
-        grad.reshape(frames, patches, width),
-        total,
-        bias,
-    ).reshape(frames * patches, 3 * width)
+        functools.partial(time_kernel, back, scale, heads),
+        in_specs=[whole, anywhere] + [whole] * (len(saved) + 3),
+        out_specs=[anywhere] + [whole] * (len(out_shape) - 2) + [anywhere],
+        out_shape=out_shape,
+        scratch_shapes=[
+            pltpu.VMEM((4 * frames, patches, features), BF16),
+            pltpu.VMEM((4 * frames, CHUNK, 3 * width), F32),
+            pltpu.VMEM((4 * frames, CHUNK, width), F32),
+            pltpu.VMEM((2 * frames, patches, features), F32),
+            pltpu.VMEM((chunks, 2 * frames, CHUNK, features), BF16),
+            pltpu.VMEM((chunks, 2 * frames, CHUNK, features), BF16),
+            pltpu.VMEM((chunks, frames, CHUNK, features), BF16),
+            pltpu.VMEM((chunks, frames, CHUNK, features), BF16),
+        ]
+        + [dma((chunks,))] * 10
+        + [dma((4,)), dma((4,)), dma((1,)), dma((chunks,))],
+        compiler_params=pltpu.CompilerParams(
+            collective_id=2 if back else 1, has_side_effects=True, vmem_limit_bytes=48 * 1024 * 1024
+        ),
+        cost_estimate=pl.CostEstimate(flops=10**10, transcendentals=10**6, bytes_accessed=10**8),
+        name="time_back" if back else "time_forward",
+    )(own, rider, *saved, wq, wo, bias)
 
 
 def tie(*values):
@@ -880,18 +1096,6 @@
     plane = 2 * y + x
     k_own = 2 * (z % 2) + c
 
-    def gather_rows(v):
-        pieces = v.reshape(4, own, BLK)
-        landed = jnp.stack(
-            [
-                lax.ppermute(
-                    lax.dynamic_index_in_dim(pieces, z ^ r, 0, keepdims=False), AXES, spread_pairs(r)
-                )
-                for r in range(4)
-            ]
-        )
-        return cols([lax.dynamic_index_in_dim(landed, k_own ^ b, 0, keepdims=False) for b in range(4)])
-
     def return_rows(v):
         landed = jnp.stack(
             [
@@ -928,25 +1132,28 @@
         ]
     )
     vectors = rows_of([mask_embed[None], gains, jnp.zeros((4, BLK), BF16)])
-    arrived, vectors, ws_qkv, ws_out = arrive(tokens.reshape(4, own, BLK), vectors, sp_own)
-    source = arrived.astype(F32)
-    embed_row = vectors[:1].astype(F32)
-    gain = [vectors[1 + i : 2 + i].astype(F32) for i in range(3)]
-
     head = (2 * y + c) * HEAD_DIM
-    ff_in = lax.dynamic_slice(w_in, (plane * BLK, c * hidden_own), (BLK, hidden_own))
-    ff_out = lax.dynamic_slice(w_out, (c * hidden_own, plane * BLK), (hidden_own, BLK)).T
     ti_own = cols(
         [
             lax.dynamic_slice_in_dim(qkv_time, head, HEAD_DIM, 2).reshape(width, -1),
             lax.dynamic_slice_in_dim(out_time, head, HEAD_DIM, 0).T,
         ]
     )
-    arrived, ff_in, ff_out, ti_own = tie(arrived, ff_in, ff_out, ti_own)
+    arrived, vectors, ws_qkv, ws_out, wt_all = arrive(tokens.reshape(4, own, BLK), vectors, sp_own, ti_own)
+    wt_all = wt_all.reshape(width, 4, 4, HEAD_DIM)
+    wt_qkv = jnp.swapaxes(wt_all[:, :, :3], 1, 2).reshape(width, 12 * HEAD_DIM)
+    wt_out = wt_all[:, :, 3].reshape(width, 4 * HEAD_DIM)
+    source = arrived.astype(F32)
+    embed_row = vectors[:1].astype(F32)
+    gain = [vectors[1 + i : 2 + i].astype(F32) for i in range(3)]
+
+    ff_in = lax.dynamic_slice(w_in, (plane * BLK, c * hidden_own), (BLK, hidden_own))
+    ff_out = lax.dynamic_slice(w_out, (c * hidden_own, plane * BLK), (hidden_own, BLK)).T
+    arrived, ff_in, ff_out = tie(arrived, ff_in, ff_out)
 
     def gather_ff(w):
-        w = lax.all_gather(w, ("tm", "x", "mp")).reshape(4, 4, BLK, hidden_own)
-        return jnp.swapaxes(w, 1, 2).reshape(width, 4 * hidden_own)
+        w = lax.all_gather(w, ("mp", "tm", "x")).reshape(4, width, hidden_own)
+        return [w[s] for s in range(4)]
 
     def pair_gather(v):
         return rows_of([v, hop_c(v)])
@@ -954,54 +1161,46 @@
     def pair_scatter(v):
         return v[:own] + hop_c(v[own:].astype(BF16)).astype(F32)
 
-    def quad_gather(v):
-        both = rows_of([v, hop_y(v)])
-        return rows_of([both, hop_c(both)])
-
-    def quad_scatter(v):
-        both = v[: 2 * own] + hop_c(v[2 * own :].astype(BF16)).astype(F32)
-        return both[:own] + hop_y(both[own:].astype(BF16)).astype(F32)
-
     heads_s = 4 * half // HEAD_DIM
-    heads_t = 4
     frames_pair = 2 * frames_own
     resid0 = jnp.where(masked, embed_row, source)
     std0, inv0 = norm_rows(resid0)
     normed0 = pair_gather((std0 * gain[0]).astype(BF16))
-    ti_half = lax.dynamic_slice_in_dim(ti_own, x * 2 * BLK, 2 * BLK, 0)
-    ti_z = [hop_z(ti_half, -r) for r in (1, 2, 3)]
     wf_in, wf_out = gather_ff(ff_in), gather_ff(ff_out)
     joined0 = dot_nn(normed0, ws_qkv).astype(BF16)
     mixed0, total0 = space_attend(joined0, frames_pair, patches, heads_s, scale)
-    mixed0, ti_z = tie(mixed0, ti_z)
-    ti_z = cols(ti_z)
-    ti_x = hop_x(ti_z)
-    ti_far = jnp.where(x == 0, rows_of([ti_z, ti_x]), rows_of([ti_x, ti_z]))
     resid1 = resid0 + pair_scatter(dot_nt(mixed0, ws_out))
     std1, inv1 = norm_rows(resid1)
-    normed1 = quad_gather((std1 * gain[1]).astype(BF16))
-    normed1, ti_far, cotangent = tie(normed1, ti_far, cotangent)
-    ti_all = [ti_own] + [ti_far[:, r * 4 * HEAD_DIM : (r + 1) * 4 * HEAD_DIM] for r in range(3)]
-    wt_qkv = cols([w[:, j * HEAD_DIM : (j + 1) * HEAD_DIM] for j in range(3) for w in ti_all])
-    wt_out = cols([w[:, 3 * HEAD_DIM :] for w in ti_all])
-    upstream = gather_rows(cotangent)
-    joined1 = dot_nn(normed1, wt_qkv).astype(BF16)
-    mixed1, total1 = time_attend(joined1, bias, frames_all, patches, heads_t, scale)
-    mixed1, upstream = tie(mixed1, upstream)
+    normed1, joined1, mixed1, total1, delta, upstream = time_call(
+        False,
+        (std1 * gain[1]).astype(BF16).reshape(frames_own, patches, width),
+        cotangent.reshape(4, own, BLK),
+        [],
+        wt_qkv,
+        wt_out,
+        bias,
+        scale,
+    )
+    normed1 = normed1.reshape(4 * own, width)
+    mixed1 = mixed1.reshape(4 * own, -1)
     grad3 = jnp.where(masked, upstream, jnp.zeros((), BF16))
     gb3 = pair_gather(grad3)
-    resid2 = resid1 + quad_scatter(dot_nt(mixed1, wt_out))
+    resid2 = resid1 + delta.reshape(own, width)
     std2, inv2 = norm_rows(resid2)
     normed2 = pair_gather((std2 * gain[2]).astype(BF16))
-    inner = dot_nn(normed2, wf_in)
-    activated, gelu_pull = jax.vjp(gelu_tanh, inner)
-    hidden = activated.astype(BF16)
-
-    def plane_scatter(lhs, rhs):
-        return lax.psum_scatter(dot_tn(lhs, rhs).astype(BF16), ("tm", "x"), scatter_dimension=0, tiled=True)
+    hidden, pulls = [], []
+    for w in wf_in:
+        activated, pull = jax.vjp(gelu_tanh, dot_nn(normed2, w))
+        hidden.append(activated.astype(BF16))
+        pulls.append(pull)
+    block_part = sum(dot_nt(h, w) for h, w in zip(hidden, wf_out))
+    block_rows = (resid2 + pair_scatter(block_part)).astype(BF16)
+
+    def plane_scatter(lhs, parts):
+        parts = jnp.stack([dot_tn(lhs, rhs).astype(BF16) for rhs in parts])
+        return lax.psum_scatter(parts, ("tm", "x"), scatter_dimension=1, tiled=True)
 
     def line_scatter(v):
-        v = jnp.swapaxes(v.reshape(BLK, 4, -1), 0, 1)
         return lax.psum_scatter(v, "mp", scatter_dimension=0).astype(F32)
 
     def send_x(lhs, rhs):
@@ -1034,19 +1233,25 @@
         return jnp.where(c == 0, jnp.concatenate([kept, landed], -1), jnp.concatenate([landed, kept], -1))
 
     w_out_part = plane_scatter(gb3, hidden)
-    grad_inner = gelu_pull(dot_nn(gb3, wf_out))[0].astype(BF16)
-    part2 = pair_scatter(dot_nt(grad_inner, wf_in))
+    grad_inner = [pull(dot_nn(gb3, w))[0].astype(BF16) for pull, w in zip(pulls, wf_out)]
+    part2 = pair_scatter(sum(dot_nt(g, w) for g, w in zip(grad_inner, wf_in)))
     w_in_part = plane_scatter(normed2, grad_inner)
     back2, gain_grad2 = norm_rows_back(part2, std2, inv2, gain[2])
     grad2 = grad3.astype(F32) + back2
-    gb2 = quad_gather(grad2.astype(BF16))
-    block_part = dot_nt(hidden, wf_out)
-    block_out = return_rows((resid2 + pair_scatter(block_part)).astype(BF16))
-
-    dmixed1 = dot_nn(gb2, wt_out).astype(BF16)
-    djoined1 = time_attend_back(joined1, dmixed1, total1, bias, frames_all, patches, heads_t, scale)
-    djoined1, block_out = tie(djoined1, block_out)
-    part1 = quad_scatter(dot_nt(djoined1, wt_qkv))
+    gb2, djoined1, part1, block_out = time_call(
+        True,
+        grad2.astype(BF16).reshape(frames_own, patches, width),
+        block_rows,
+        [joined1, total1],
+        wt_qkv,
+        wt_out,
+        bias,
+        scale,
+    )
+    block_out = block_out.reshape(tokens.shape)
+    gb2 = gb2.reshape(4 * own, width)
+    djoined1 = djoined1.reshape(4 * own, -1)
+    part1 = part1.reshape(own, width)
     back1, gain_grad1 = norm_rows_back(part1, std1, inv1, gain[1])
     grad1 = grad2 + back1
     gb1 = pair_gather(grad1.astype(BF16))
@@ -1065,14 +1270,14 @@
     g_t_out = keep_x(gb2, mixed1, t_out_x)
     g_t_qkv = keep_x(normed1, djoined1, t_qkv_x)
     z_at = [(z + r) % 4 for r in range(4)]
-    span = heads_t * HEAD_DIM
+    span = 4 * HEAD_DIM
     g_time = reduce_z(
         [
             cols(
-                [lax.dynamic_slice_in_dim(g_t_qkv, j * span + r * HEAD_DIM, HEAD_DIM, 1) for j in range(3)]
-                + [lax.dynamic_slice_in_dim(g_t_out, r * HEAD_DIM, HEAD_DIM, 1)]
+                [lax.dynamic_slice_in_dim(g_t_qkv, j * span + s * HEAD_DIM, HEAD_DIM, 1) for j in range(3)]
+                + [lax.dynamic_slice_in_dim(g_t_out, s * HEAD_DIM, HEAD_DIM, 1)]
             )
-            for r in range(4)
+            for s in z_at
         ]
     )
     s_qkv_kept = keep_x(normed0, djoined0, s_qkv_x)

time: 658 us -> 633 us (0.962)
  Pallas kernels: 113 us -> 252 us
  waiting for transfers between devices: 185 us -> 98.6 us
  starting transfers between devices: 84.8 us -> 41.5 us
  local copies, waits for them, and re-layouts: 81.9 us -> 54.6 us
  other arithmetic: 63.8 us -> 51.9 us
  matrix products: 102 us -> 112 us
    pallas_call x5, Pallas kernels: 113 us -> 252 us  [the longest x2 156 us: time_call(): pl.pallas_call(functools.partial(time_kernel, back, scale, heads), in_spe...]
    ppermute x8 -> x4, waiting for transfers between devices: 111 us -> 2.65 us  [hop_y(): lax.ppermute(v, AXES, device_pairs(lambda y, x, c, z: (1 - y, x, c, z)))]
    all_gather x2, waiting for transfers between devices: 0.01 us -> 34.2 us  [gather_ff(): w = lax.all_gather(w, ('mp', 'tm', 'x')).reshape(4, width, hidden_own)]
    reshape x5 -> x2, local copies, waits for them, and re-layouts: 30 us -> 1.76 us  [the longest x1 1.55 us: token_parallel(): wt_qkv = jnp.swapaxes(wt_all[:, :, :3], 1, 2).reshape(width, 12 * HEAD_DIM)]
    ppermute x6 -> x5, waiting for transfers between devices: 18.6 us -> 4.03 us  [hop_x(): lax.ppermute(v, AXES, device_pairs(lambda y, x, c, z: (y, 1 - x, c, z)))]
    ppermute x12 -> x9, starting transfers between devices: 25.3 us -> 11 us  [hop_z(): lax.ppermute(v, AXES, device_pairs(lambda y, x, c, z: (y, x, c, (z + shif...]
    unnamed x204 -> x184, local copies, waits for them, and re-layouts: 29.9 us -> 16.9 us
    ppermute x4 -> x0, starting transfers between devices: 11.7 us -> none  [gather_rows(): lax.ppermute(lax.dynamic_index_in_dim(pieces, z ^ r, 0, keepdims=False),...]
  transfers between devices with their start and end apart: 61 -> 41, of which waited for: 23 -> 15; matrix products, arithmetic and copies ran while one was open for 33% -> 30% of each run, Pallas kernels for 18% -> 30%
where the time goes in v3:
time: 633 us; the launch traced here: 627 us
  Pallas kernels  252 us (40%)
  matrix products  112 us (18%)
  waiting for transfers between devices  98.6 us (16%)
  local copies, waits for them, and re-layouts  54.6 us (9%)
  other arithmetic  51.9 us (8%)
  starting transfers between devices  41.5 us (7%)
  between operations  16 us (3%)
    pallas_call x2, Pallas kernels, time_call(): pl.pallas_call(functools.partial(time_kernel, back, scale, heads), in_spe...  156 us
    pallas_call x1, Pallas kernels, arrive(): pl.pallas_call(arrive_kernel, in_specs=[anywhere] * 4, out_specs=[anywher...  61.2 us
    dot_general x16, matrix products, dot_tn(): lax.dot_general(a, b, (((0,), (0,)), ((), ())), preferred_element_type=F32)  49 us
    ppermute x9, waiting for transfers between devices, hop_z(): lax.ppermute(v, AXES, device_pairs(lambda y, x, c, z: (y, x, c, (z + shif...  40.7 us
    dot_general x10, matrix products, dot_nn(): lax.dot_general(a, b, (((1,), (0,)), ((), ())), preferred_element_type=F32)  38.8 us
    all_gather x2, waiting for transfers between devices, gather_ff(): w = lax.all_gather(w, ('mp', 'tm', 'x')).reshape(4, width, hidden_own)  34.2 us
    dot_general x10, matrix products, dot_nt(): lax.dot_general(a, b, (((1,), (1,)), ((), ())), preferred_element_type=F32)  24.3 us
    pallas_call x1, Pallas kernels, space_attend_back(): pl.pallas_call(functools.partial(space_attend_back_kernel, scale), grid=(...  18 us
  transfers between devices with their start and end apart: 41, of which 15 were waited for; matrix products, arithmetic and copies ran while one was open for 30% of the time, Pallas kernels for 30%

profile of v3, /device:TPU:9, one launch (start us, length us, event | category | flops | bytes accessed | tf_op | source)
XLA Modules:
  0.0 626.7 jit_solution(8864396229877631292)
XLA Ops:
  19.2 61.2 %arrive.1 = (bf16[512,1024]{1,0:T(8,128)(2,1)}, bf16[8,1024]{1,0:T(8,128)(2,1)}, bf16[1024,1536]{1,0:T(8,128)(2,1)}, bf16[1024,512]{1,0:T(8,128)(2,1)}, bf16[1024,1024]{1,0:T(8,128)(2,1)}) custom-call(bf16[4,512,256]{2,1,0:T(8,128)(2,1)} %bitcast.129, bf16[8,256]{1,0:T(8,128)(2,1)} %maximum_maximum_fusion.vec, bf16[1024,512]{1,0:T(8,128)(2,1)} %pad_maximum_fusion.22.mine, ...), custom_call_target="tpu_custom_call" | custom-call | tf_op jit(solution)/shard_map/arrive/pallas_call | solution.py:678
  87.2 2.9 copy.69
  91.0 7.6 %convolution_convert_fusion.qkv_ref = bf16[1024,1536]{1,0:T(8,128)(2,1)} fusion(bf16[1024,1536]{1,0:T(8,128)(2,1)} %get-tuple-element.36, bf16[512,1024]{1,0:T(8,128)(2,1)} %collective-permute-done.1, bf16[512,1024]{1,0:T(8,128)(2,1)} %multiply_convert_fusion.6), kind=kOutput, calls=%fused_computation.4 | convolution fusion | flops 3226992640 | bytes 8388608 | tf_op jit(solution)/shard_map/dot_general | solution.py:701
  98.5 16.2 %space_attend.1 = (bf16[1024,512]{1,0:T(8,128)(2,1)}, f32[8,8,128]{2,1,0:T(8,128)}) custom-call(bf16[1024,1536]{1,0:T(8,128)(2,1)} %convolution_convert_fusion.qkv_ref), custom_call_target="tpu_custom_call" | custom-call | flops 1073741824 | bytes 4194304 | tf_op jit(solution)/shard_map/space_attend/pallas_call | solution.py:778
  114.8 4.8 fusion.155
  119.6 2.7 slice.466
  129.8 74.2 %time_forward.1 = (bf16[16,128,1024]{2,1,0:T(8,128)(2,1)}, bf16[16,128,768]{2,1,0:T(8,128)(2,1)}, bf16[16,128,256]{2,1,0:T(8,128)(2,1)S(1)}, f32[16,4,128]{2,1,0...) custom-call(bf16[4,128,1024]{2,1,0:T(8,128)(2,1)S(1)} %bitcast.113, ...), custom_call_target="tpu_custom_call" | custom-call | flops 10000000000 | bytes 100000000 | tf_op jit(solution)/shard_map/time_forward/pallas_call | solution.py:1021
  212.1 2.9 fusion.94
  215.1 3.2 fusion.84
  218.3 3.2 fusion.76
  221.5 3.2 fusion.104
  224.8 3.7 fusion.55
  228.5 3.0 fusion.56
  231.6 3.0 fusion.57
  234.6 3.0 fusion.54
  240.4 34.2 %all-gather.5.cloned.1.call-done = bf16[4096,512]{0,1:T(8,128)(2,1)} async-done(((bf16[256,512]{0,1:T(8,128)(2,1)}), bf16[4096,512]{0,1:T(8,128)(2,1)}) %all-gather.5.cloned.1.call-update) | async-done | bytes 4194320 | tf_op jit(solution)/shard_map/all_gather | solution.py:1155
  274.6 3.4 fusion.110
  285.4 4.3 fusion.13
  289.7 2.9 fusion.59
  292.6 4.0 fusion.20
  296.7 2.9 fusion.60
  299.6 4.1 fusion.27
  303.8 2.9 fusion.61
  306.8 4.0 fusion.6
  310.7 2.9 fusion.58
  317.2 2.7 fusion.106
  328.1 3.0 fusion.119
  331.1 4.6 fusion.151
  341.2 82.3 %time_back.1 = (bf16[16,128,1024]{2,1,0:T(8,128)(2,1)}, bf16[16,128,768]{2,1,0:T(8,128)(2,1)}, f32[4,128,1024]{2,1,0:T(8,128)}, bf16[4,512,256]{2,1,0:T(8,128)(2,1)S(1)}) custom-call(bf16[4,128,1024]{2,1,0:T(8,128)(2,1)S(1)} %bitcast.112, bf16[512,1024]{1,0:T(8,128)(2,1)S(1)} %get-tuple-element.122.refs_1_, bf16[16,128,768]{2,1,0:T(8,128)(2,1)} %get-tuple-element.44.refs_2_, ...), custom_call_target="tpu_custom_call" | custom-call | flops 10000000000 | bytes 100000000 | tf_op jit(solution)/shard_map/time_back/pallas_call | solution.py:1021
  433.9 2.8 fusion.51
  445.2 18.0 %space_attend_back.1 = bf16[1024,1536]{1,0:T(8,128)(2,1)} custom-call(bf16[1024,1536]{1,0:T(8,128)(2,1)} %convolution_convert_fusion.qkv_ref, bf16[1024,512]{1,0:T(8,128)(2,1)} %fusion.48.grad_ref, f32[8,8,128]{2,1,0:T(8,128)} %get-tuple-element.48.total_ref), custom_call_target="tpu_custom_call" | custom-call | flops 2684354560 | bytes 10485760 | tf_op jit(solution)/shard_map/space_attend_back/pallas_call | solution.py:797
  463.2 2.9 collective-permute-done.10
  471.0 5.3 convert_add_fusion
  483.0 5.0 fusion.156
  488.1 2.8 slice.463
  490.8 3.6 collective-permute-start.11
  494.4 5.6 convolution_convert_fusion.1
  500.4 8.7 %collective-permute-done.30 = bf16[512,256]{1,0:T(8,128)(2,1)S(1)} collective-permute-done((bf16[512,256]{1,0:T(8,128)(2,1)}, bf16[512,256]{1,0:T(8,128)(2,1)S(1)}, u32[]{:S(2)}, u32[]{:S(2)}) %collective-permute-start.30) | collective-permute-done | bytes 262176 | tf_op jit(solution)/shard_map/ppermute | solution.py:438
  510.4 10.0 %collective-permute-done.31 = bf16[512,256]{1,0:T(8,128)(2,1)} collective-permute-done((bf16[512,256]{1,0:T(8,128)(2,1)}, bf16[512,256]{1,0:T(8,128)(2,1)}, u32[]{:S(2)}, u32[]{:S(2)}) %collective-permute-start.31) | collective-permute-done | bytes 262176 | tf_op jit(solution)/shard_map/ppermute | solution.py:438
  533.2 2.9 multiply_reduce_fusion.1
  536.1 3.3 select_reduce_fusion
  548.2 6.9 %collective-permute-start.12 = (bf16[512,256]{1,0:T(8,128)(2,1)S(1)}, bf16[512,256]{1,0:T(8,128)(2,1)S(1)}, u32[]{:S(2)}, u32[]{:S(2)}) collective-permute-start(bf16[512,256]{1,0:T(8,128)(2,1)S(1)} %get-tuple-element.144), channel_id=1, source_target_pairs={{0,0},{4,1},{1,2},{5,3},{2,4},{6,5},{3,6},{7,7},{8,8},{12,9},{9,10... | collective-permute-start | bytes 786440 | tf_op jit(solution)/shard_map/ppermute | solution.py:1102
  558.1 4.2 convolution_add_fusion
  563.4 8.7 %collective-permute-done.12 = bf16[512,256]{1,0:T(8,128)(2,1)S(1)} collective-permute-done((bf16[512,256]{1,0:T(8,128)(2,1)S(1)}, bf16[512,256]{1,0:T(8,128)(2,1)S(1)}, u32[]{:S(2)}, u32[]{:S(2)}) %collective-permute-start.12) | collective-permute-done | bytes 262176 | tf_op jit(solution)/shard_map/ppermute | solution.py:1102
  572.0 5.6 collective-permute-done.13
  583.6 4.1 collective-permute-start.26
  589.5 15.0 %collective-permute-done.26 = bf16[256,512]{1,0:T(8,128)(2,1)S(1)} collective-permute-done((bf16[256,512]{1,0:T(8,128)(2,1)S(1)}, bf16[256,512]{1,0:T(8,128)(2,1)S(1)}, u32[]{:S(2)}, u32[]{:S(2)}) %collective-permute-start.26) | collective-permute-done | bytes 262176 | tf_op jit(solution)/shard_map/ppermute | solution.py:438
  604.5 6.9 %collective-permute-done.27 = bf16[256,512]{1,0:T(8,128)(2,1)S(1)} collective-permute-done((bf16[256,512]{1,0:T(8,128)(2,1)S(1)}, bf16[256,512]{1,0:T(8,128)(2,1)S(1)}, u32[]{:S(2)}, u32[]{:S(2)}) %collective-permute-start.27) | collective-permute-done | bytes 262176 | tf_op jit(solution)/shard_map/ppermute | solution.py:438
  (401 shorter events, 135.2 us)
Async XLA Ops:
  7.2 204.9 %all-gather.7.cloned.1.call-start = ((), (), s32[]{:S(2)}) async-start(), calls=%async_computation.9 | async-start | bytes 4456448 | tf_op jit(solution)/shard_map/all_gather | solution.py:1155
  17.5 63.0 %copy-start.65 = (s32[2,8,128]{2,1,0:T(8,128)S(1)}, s32[2,8,128]{2,1,0:T(8,128)}, u32[]{:S(2)}) copy-start(s32[2,8,128]{2,1,0:T(8,128)} %param.16) | copy-start | bytes 24580
  17.5 63.0 %copy-start.69 = (s32[2]{0:T(128)S(1)}, s32[2]{0:T(128)}, u32[]{:S(2)}) copy-start(s32[2]{0:T(128)} %param.15) | copy-start | bytes 28
  17.5 63.1 %copy-start.68 = (s32[2,16]{1,0:T(2,128)S(1)}, s32[2,16]{1,0:T(2,128)}, u32[]{:S(2)}) copy-start(s32[2,16]{1,0:T(2,128)} %param.17) | copy-start | bytes 388
  80.5 194.1 %all-gather.5.cloned.1.call-start = ((), (), s32[]{:S(2)}) async-start(), calls=%async_computation.8 | async-start | bytes 4456448 | tf_op jit(solution)/shard_map/all_gather | solution.py:1155
  80.7 1.2 collective-permute-start
  81.6 43.7 %copy-start.54 = (f32[1,1024]{1,0:T(1,128)}, f32[1,1024]{1,0:T(1,128)S(1)}, u32[]{:S(2)}) copy-start(f32[1,1024]{1,0:T(1,128)S(1)} %get-tuple-element.162) | copy-start | bytes 12292
  82.0 257.4 %copy-start.60 = (pred[512]{0:T(512)(128)(4,1)}, pred[512]{0:T(512)(128)(4,1)S(1)}, u32[]{:S(2)}) copy-start(pred[512]{0:T(512)(128)(4,1)S(1)} %compare_reduce_fusion) | copy-start | bytes 1540
  86.3 4.6 collective-permute-start.1
  86.7 379.5 %reduce-scatter.5.cloned.1.call-start = ((), (), s32[]{:S(2)}) async-start(), calls=%async_computation.4 | async-start | bytes 5242880 | tf_op jit(solution)/shard_map/reduce_scatter | solution.py:1201
  122.3 3.0 collective-permute-start.2
  127.8 76.2 %copy-start.6 = (f32[512,1024]{1,0:T(8,128)}, f32[512,1024]{1,0:T(8,128)S(1)}, u32[]{:S(2)}) copy-start(f32[512,1024]{1,0:T(8,128)S(1)} %get-tuple-element.105) | copy-start | bytes 6291460
  207.6 4.5 collective-permute-start.4
  210.8 14.0 %collective-permute-start.3 = (bf16[512,1024]{1,0:T(8,128)(2,1)}, bf16[512,1024]{1,0:T(8,128)(2,1)}, u32[]{:S(2)}, u32[]{:S(2)}) collective-permute-start(bf16[512,1024]{1,0:T(8,128)(2,1)} %broadcast_select_fusion), channel_id=1, source_target_pairs={{0,4},{1,5},{2,6},{3,7},{4,0},{5,1},{6,2},{7,3},{8,12},{9,13},{10,... | collective-permute-start | bytes 3145736 | tf_op jit(solution)/shard_map/ppermute | solution.py:434
  239.9 230.5 %reduce-scatter.7.cloned.1.call-start = ((), (), s32[]{:S(2)}) async-start(), calls=%async_computation.5 | async-start | bytes 5242880 | tf_op jit(solution)/shard_map/reduce_scatter | solution.py:1201
  284.5 51.1 %collective-permute-start.6 = (bf16[512,1024]{1,0:T(8,128)(2,1)}, bf16[512,1024]{1,0:T(8,128)(2,1)}, u32[]{:S(2)}, u32[]{:S(2)}) collective-permute-start(bf16[512,1024]{1,0:T(8,128)(2,1)} %slice.464), channel_id=1, source_target_pairs={{0,4},{1,5},{2,6},{3,7},{4,0},{5,1},{6,2},{7,3},{8,12},{9,13},{10,... | collective-permute-start | bytes 3145736 | tf_op jit(solution)/shard_map/ppermute | solution.py:434
  316.0 263.6 %reduce-scatter.9.cloned.1.call-start = ((), (), s32[]{:S(2)}) async-start(), calls=%async_computation.6 | async-start | bytes 1310720 | tf_op jit(solution)/shard_map/reduce_scatter | solution.py:1204
  327.2 8.5 %collective-permute-start.5 = (bf16[512,1024]{1,0:T(8,128)(2,1)}, bf16[512,1024]{1,0:T(8,128)(2,1)S(1)}, u32[]{:S(2)}, u32[]{:S(2)}) collective-permute-start(bf16[512,1024]{1,0:T(8,128)(2,1)} %slice.465), channel_id=1, source_target_pairs={{0,4},{1,5},{2,6},{3,7},{4,0},{5,1},{6,2},{7,3},{8,12},{9,13},{10,... | collective-permute-start | bytes 3145736 | tf_op jit(solution)/shard_map/ppermute | solution.py:434
  427.6 35.7 %collective-permute-start.8 = (bf16[512,256]{1,0:T(8,128)(2,1)}, bf16[512,256]{1,0:T(8,128)(2,1)S(1)}, u32[]{:S(2)}, u32[]{:S(2)}) collective-permute-start(bf16[512,256]{1,0:T(8,128)(2,1)} %fusion.62), channel_id=1, source_target_pairs={{0,8},{1,9},{2,10},{3,11},{4,12},{5,13},{6,14},{7,15},{8,0},{9,1},... | collective-permute-start | bytes 786440 | tf_op jit(solution)/shard_map/ppermute | solution.py:430
  432.1 7.4 %collective-permute-start.7 = (bf16[512,1024]{1,0:T(8,128)(2,1)S(1)}, bf16[512,1024]{1,0:T(8,128)(2,1)S(1)}, u32[]{:S(2)}, u32[]{:S(2)}) collective-permute-start(bf16[512,1024]{1,0:T(8,128)(2,1)S(1)} %get-tuple-element.98), channel_id=1, source_target_pairs={{0,4},{1,5},{2,6},{3,7},{4,0},{5,1},{6,2},{7,3},{8,12},{9,13},{10,... | collective-permute-start | bytes 3145736 | tf_op jit(solution)/shard_map/ppermute | solution.py:434
  436.7 26.5 %collective-permute-start.9 = (bf16[512,768]{1,0:T(8,128)(2,1)}, bf16[512,768]{1,0:T(8,128)(2,1)}, u32[]{:S(2)}, u32[]{:S(2)}) collective-permute-start(bf16[512,768]{1,0:T(8,128)(2,1)} %fusion.51), channel_id=1, source_target_pairs={{0,8},{1,9},{2,10},{3,11},{4,12},{5,13},{6,14},{7,15},{8,0},{9,1},... | collective-permute-start | bytes 2359304 | tf_op jit(solution)/shard_map/ppermute | solution.py:430
  442.6 23.5 %collective-permute-start.10 = (bf16[512,512]{1,0:T(8,128)(2,1)}, bf16[512,512]{1,0:T(8,128)(2,1)}, u32[]{:S(2)}, u32[]{:S(2)}) collective-permute-start(bf16[512,512]{1,0:T(8,128)(2,1)} %convolution_convert_fusion.10), channel_id=1, source_target_pairs={{0,8},{1,9},{2,10},{3,11},{4,12},{5,13},{6,14},{7,15},{8,0},{9,1},... | collective-permute-start | bytes 1572872 | tf_op jit(solution)/shard_map/ppermute | solution.py:430
  470.0 52.5 %collective-permute-start.24 = (bf16[256,512]{1,0:T(8,128)(2,1)}, bf16[256,512]{1,0:T(8,128)(2,1)}, u32[]{:S(2)}, u32[]{:S(2)}) collective-permute-start(bf16[256,512]{1,0:T(8,128)(2,1)} %select_convert_fusion.2), channel_id=1, source_target_pairs={{0,16},{1,17},{2,18},{3,19},{4,20},{5,21},{6,22},{7,23},{8,24},{9,... | collective-permute-start | bytes 786440 | tf_op jit(solution)/shard_map/ppermute | solution.py:426
  470.5 109.1 %reduce-scatter.11.cloned.1.call-start = ((), (), s32[]{:S(2)}) async-start(), calls=%async_computation.7 | async-start | bytes 1310720 | tf_op jit(solution)/shard_map/reduce_scatter | solution.py:1204
  477.6 31.6 %collective-permute-start.30 = (bf16[512,256]{1,0:T(8,128)(2,1)}, bf16[512,256]{1,0:T(8,128)(2,1)S(1)}, u32[]{:S(2)}, u32[]{:S(2)}) collective-permute-start(bf16[512,256]{1,0:T(8,128)(2,1)} %pad_maximum_fusion.43), channel_id=1, source_target_pairs={{0,2},{1,3},{2,0},{3,1},{4,6},{5,7},{6,4},{7,5},{8,10},{9,11},{10,... | collective-permute-start | bytes 786440 | tf_op jit(solution)/shard_map/ppermute | solution.py:438
  480.7 39.7 %collective-permute-start.31 = (bf16[512,256]{1,0:T(8,128)(2,1)}, bf16[512,256]{1,0:T(8,128)(2,1)}, u32[]{:S(2)}, u32[]{:S(2)}) collective-permute-start(bf16[512,256]{1,0:T(8,128)(2,1)} %pad_maximum_fusion.44), channel_id=1, source_target_pairs={{0,3},{1,0},{2,1},{3,2},{4,7},{5,4},{6,5},{7,6},{8,11},{9,8},{10,9... | collective-permute-start | bytes 786440 | tf_op jit(solution)/shard_map/ppermute | solution.py:438
  481.8 38.6 %collective-permute-start.29 = (bf16[512,256]{1,0:T(8,128)(2,1)}, bf16[512,256]{1,0:T(8,128)(2,1)}, u32[]{:S(2)}, u32[]{:S(2)}) collective-permute-start(bf16[512,256]{1,0:T(8,128)(2,1)} %pad_maximum_fusion.42), channel_id=1, source_target_pairs={{0,1},{1,2},{2,3},{3,0},{4,5},{5,6},{6,7},{7,4},{8,9},{9,10},{10,1... | collective-permute-start | bytes 786440 | tf_op jit(solution)/shard_map/ppermute | solution.py:438
  490.8 42.3 %collective-permute-start.11 = (bf16[512,1024]{1,0:T(8,128)(2,1)}, bf16[512,1024]{1,0:T(8,128)(2,1)S(1)}, u32[]{:S(2)}, u32[]{:S(2)}) collective-permute-start(bf16[512,1024]{1,0:T(8,128)(2,1)} %slice.463), channel_id=1, source_target_pairs={{0,4},{1,5},{2,6},{3,7},{4,0},{5,1},{6,2},{7,3},{8,12},{9,13},{10,... | collective-permute-start | bytes 3145736 | tf_op jit(solution)/shard_map/ppermute | solution.py:434
  500.1 22.4 %copy-start.24 = (f32[512,512]{1,0:T(8,128)S(1)}, f32[512,512]{1,0:T(8,128)}, u32[]{:S(2)}) copy-start(f32[512,512]{1,0:T(8,128)} %copy-done.23) | copy-start | bytes 3145732
  509.2 48.9 %collective-permute-start.22 = (bf16[512,1536]{1,0:T(8,128)(2,1)}, bf16[512,1536]{1,0:T(8,128)(2,1)}, u32[]{:S(2)}, u32[]{:S(2)}) collective-permute-start(bf16[512,1536]{1,0:T(8,128)(2,1)} %convolution_convert_fusion.1), channel_id=1, source_target_pairs={{0,8},{1,9},{2,10},{3,11},{4,12},{5,13},{6,14},{7,15},{8,0},{9,1},... | collective-permute-start | bytes 4718600 | tf_op jit(solution)/shard_map/ppermute | solution.py:430
  521.8 4.5 collective-permute-start.32
  527.0 3.3 collective-permute-start.33
  539.4 1.2 collective-permute-start.16
  540.6 3.1 collective-permute-start.17
  543.7 2.7 collective-permute-start.18
  546.4 8.7 %collective-permute-start.19 = (f32[4,256]{1,0:T(4,128)S(1)}, f32[4,256]{1,0:T(4,128)S(1)}, u32[]{:S(2)}, u32[]{:S(2)}) collective-permute-start(f32[4,256]{1,0:T(4,128)S(1)} %get-tuple-element.156), channel_id=1, source_target_pairs={{0,1},{1,2},{2,3},{3,0},{4,5},{5,6},{6,7},{7,4},{8,9},{9,10},{10,1... | collective-permute-start | bytes 12296 | tf_op jit(solution)/shard_map/ppermute | solution.py:438
  546.8 10.3 %collective-permute-start.21 = (f32[4,256]{1,0:T(4,128)S(1)}, f32[4,256]{1,0:T(4,128)S(1)}, u32[]{:S(2)}, u32[]{:S(2)}) collective-permute-start(f32[4,256]{1,0:T(4,128)S(1)} %get-tuple-element.157), channel_id=1, source_target_pairs={{0,3},{1,0},{2,1},{3,2},{4,7},{5,4},{6,5},{7,6},{8,11},{9,8},{10,9... | collective-permute-start | bytes 12296 | tf_op jit(solution)/shard_map/ppermute | solution.py:438
  547.9 9.2 %collective-permute-start.20 = (f32[4,256]{1,0:T(4,128)S(1)}, f32[4,256]{1,0:T(4,128)S(1)}, u32[]{:S(2)}, u32[]{:S(2)}) collective-permute-start(f32[4,256]{1,0:T(4,128)S(1)} %get-tuple-element.158), channel_id=1, source_target_pairs={{0,2},{1,3},{2,0},{3,1},{4,6},{5,7},{6,4},{7,5},{8,10},{9,11},{10,... | collective-permute-start | bytes 12296 | tf_op jit(solution)/shard_map/ppermute | solution.py:438
  548.2 23.8 %collective-permute-start.12 = (bf16[512,256]{1,0:T(8,128)(2,1)S(1)}, bf16[512,256]{1,0:T(8,128)(2,1)S(1)}, u32[]{:S(2)}, u32[]{:S(2)}) collective-permute-start(bf16[512,256]{1,0:T(8,128)(2,1)S(1)} %get-tuple-element.144), channel_id=1, source_target_pairs={{0,0},{4,1},{1,2},{5,3},{2,4},{6,5},{3,6},{7,7},{8,8},{12,9},{9,10... | collective-permute-start | bytes 786440 | tf_op jit(solution)/shard_map/ppermute | solution.py:1102
  555.1 16.9 %collective-permute-start.15 = (bf16[512,256]{1,0:T(8,128)(2,1)S(1)}, bf16[512,256]{1,0:T(8,128)(2,1)S(1)}, u32[]{:S(2)}, u32[]{:S(2)}) collective-permute-start(bf16[512,256]{1,0:T(8,128)(2,1)S(1)} %get-tuple-element.145), channel_id=1, source_target_pairs={{5,0},{1,1},{4,2},{0,3},{7,4},{3,5},{6,6},{2,7},{13,8},{9,9},{12,1... | collective-permute-start | bytes 786440 | tf_op jit(solution)/shard_map/ppermute | solution.py:1102
  557.1 15.0 %collective-permute-start.14 = (bf16[512,256]{1,0:T(8,128)(2,1)S(1)}, bf16[512,256]{1,0:T(8,128)(2,1)S(1)}, u32[]{:S(2)}, u32[]{:S(2)}) collective-permute-start(bf16[512,256]{1,0:T(8,128)(2,1)S(1)} %get-tuple-element.146), channel_id=1, source_target_pairs={{1,0},{5,1},{0,2},{4,3},{3,4},{7,5},{2,6},{6,7},{9,8},{13,9},{8,10... | collective-permute-start | bytes 786440 | tf_op jit(solution)/shard_map/ppermute | solution.py:1102
  557.2 20.5 %collective-permute-start.13 = (bf16[512,256]{1,0:T(8,128)(2,1)S(1)}, bf16[512,256]{1,0:T(8,128)(2,1)S(1)}, u32[]{:S(2)}, u32[]{:S(2)}) collective-permute-start(bf16[512,256]{1,0:T(8,128)(2,1)S(1)} %get-tuple-element.147), channel_id=1, source_target_pairs={{4,0},{0,1},{5,2},{1,3},{6,4},{2,5},{7,6},{3,7},{12,8},{8,9},{13,1... | collective-permute-start | bytes 786440 | tf_op jit(solution)/shard_map/ppermute | solution.py:1102
  562.5 19.4 %collective-permute-start.23 = (bf16[256,1536]{1,0:T(8,128)(2,1)S(1)}, bf16[256,1536]{1,0:T(8,128)(2,1)}, u32[]{:S(2)}, u32[]{:S(2)}) collective-permute-start(bf16[256,1536]{1,0:T(8,128)(2,1)S(1)} %select_convert_fusion.1), channel_id=1, source_target_pairs={{0,16},{1,17},{2,18},{3,19},{4,20},{5,21},{6,22},{7,23},{8,24},{9,... | collective-permute-start | bytes 2359304 | tf_op jit(solution)/shard_map/ppermute | solution.py:426
  580.9 8.4 %collective-permute-start.34 = (bf16[128,1024]{1,0:T(8,128)(2,1)S(1)}, bf16[128,1024]{1,0:T(8,128)(2,1)S(1)}, u32[]{:S(2)}, u32[]{:S(2)}) collective-permute-start(bf16[128,1024]{1,0:T(8,128)(2,1)S(1)} %dynamic-slice_convert_fusion), channel_id=1, source_target_pairs={{0,4},{1,5},{2,6},{3,7},{4,0},{5,1},{6,2},{7,3},{8,12},{9,13},{10,... | collective-permute-start | bytes 786440 | tf_op jit(solution)/shard_map/ppermute | solution.py:434
  583.6 20.9 %collective-permute-start.26 = (bf16[256,512]{1,0:T(8,128)(2,1)S(1)}, bf16[256,512]{1,0:T(8,128)(2,1)S(1)}, u32[]{:S(2)}, u32[]{:S(2)}) collective-permute-start(bf16[256,512]{1,0:T(8,128)(2,1)S(1)} %pad_maximum_fusion.40), channel_id=1, source_target_pairs={{0,2},{1,3},{2,0},{3,1},{4,6},{5,7},{6,4},{7,5},{8,10},{9,11},{10,... | collective-permute-start | bytes 786440 | tf_op jit(solution)/shard_map/ppermute | solution.py:438
  587.8 23.6 %collective-permute-start.27 = (bf16[256,512]{1,0:T(8,128)(2,1)S(1)}, bf16[256,512]{1,0:T(8,128)(2,1)S(1)}, u32[]{:S(2)}, u32[]{:S(2)}) collective-permute-start(bf16[256,512]{1,0:T(8,128)(2,1)S(1)} %pad_maximum_fusion.41), channel_id=1, source_target_pairs={{0,3},{1,0},{2,1},{3,2},{4,7},{5,4},{6,5},{7,6},{8,11},{9,8},{10,9... | collective-permute-start | bytes 786440 | tf_op jit(solution)/shard_map/ppermute | solution.py:438
  587.9 23.5 %collective-permute-start.25 = (bf16[256,512]{1,0:T(8,128)(2,1)S(1)}, bf16[256,512]{1,0:T(8,128)(2,1)S(1)}, u32[]{:S(2)}, u32[]{:S(2)}) collective-permute-start(bf16[256,512]{1,0:T(8,128)(2,1)S(1)} %pad_maximum_fusion.39), channel_id=1, source_target_pairs={{0,1},{1,2},{2,3},{3,0},{4,5},{5,6},{6,7},{7,4},{8,9},{9,10},{10,1... | collective-permute-start | bytes 786440 | tf_op jit(solution)/shard_map/ppermute | solution.py:438
  611.6 3.3 collective-permute-start.28
  (80 other events, 428.3 us)
Sparse Core Ops, SparseCore 0:
  80.6 98.6 all-gather.6
  182.6 91.8 all-gather.4
  277.5 52.3 reduce-scatter.4
  333.1 81.6 reduce-scatter.6
  470.6 47.6 reduce-scatter.8
  520.5 24.8 reduce-scatter.10

commit v4 on v3

--- a/solution.py
+++ b/solution.py
@@ -1043,6 +1043,268 @@
     )(own, rider, *saved, wq, wo, bias)
 
 
+def settle_kernel(
+    dj, go, lhs, weight_hbm, std_hbm, base_hbm, inverse, masked, gain, small_in,
+    kept_out, landed_out, rows_out, small_out,
+    weight, std, base, grads, a1_out, a1_in, b1_out, b1_in, a2_out, a2_in, b2_out, b2_in, z_out, z_in,
+    half_out, half_in, ready, core_out, core_in, sums, sum_out, sum_in, share_in,
+    a1_send, a1_recv, b1_send, b1_recv, a2_send, a2_recv, b2_send, b2_recv, z_send, z_recv,
+    h_send, h_recv, r_send, r_recv, c_send, c_recv, s_send, s_recv, p_send, p_recv, local,
+):
+    y, x, c, z = (lax.axis_index(name) for name in AXES)
+    near_y, near_x, pair = (1 - y, x, c, z), (y, 1 - x, c, z), (y, x, 1 - c, z)
+    own = std.shape[0]
+    third = go.shape[1] // 4
+    wide = 3 * third
+    two = 2 * third
+
+    fetches = [
+        pltpu.make_async_copy(weight_hbm, weight, local.at[0]),
+        pltpu.make_async_copy(std_hbm, std, local.at[1]),
+        pltpu.make_async_copy(base_hbm, base, local.at[2]),
+    ]
+    for copy in fetches:
+        copy.start()
+
+    barrier = pltpu.get_barrier_semaphore()
+    for dc in range(2):
+        for dz in range(4):
+            if dc or dz:
+                pl.semaphore_signal(barrier, inc=1, device_id=(y, x, (c + dc) % 2, (z + dz) % 4), device_id_type=MESH)
+    for peer in (near_y, near_x):
+        pl.semaphore_signal(barrier, inc=1, device_id=peer, device_id_type=MESH)
+    pl.semaphore_wait(barrier, 9)
+
+    def remote(src, dst, send, recv, peer):
+        return pltpu.make_async_remote_copy(
+            src_ref=src, dst_ref=dst, send_sem=send, recv_sem=recv, device_id=peer, device_id_type=MESH
+        )
+
+    def block(yb, xb):
+        return pl.ds(pl.multiple_of(BLK * (2 * yb + xb), BLK), BLK)
+
+    def a1(i):
+        return remote(a1_out.at[i], a1_in.at[i], a1_send.at[i], a1_recv.at[i], near_x)
+
+    def b1(i):
+        return remote(b1_out.at[i], b1_in.at[i], b1_send.at[i], b1_recv.at[i], near_y)
+
+    def a2(i):
+        return remote(a2_out.at[i], a2_in.at[i], a2_send.at[i], a2_recv.at[i], near_y)
+
+    def b2(i):
+        return remote(b2_out.at[i], b2_in.at[i], b2_send.at[i], b2_recv.at[i], near_x)
+
+    def to_z(r):
+        return remote(z_out.at[r], z_in.at[r], z_send.at[r], z_recv.at[r], (y, x, c, (z + r) % 4))
+
+    def piece(i, carry):
+        s = (z + i + 1) % 4
+        made = dot_nn(lhs[...], dj[:, pl.ds(pl.multiple_of(s * wide, third), wide)])
+        grads[i, :, :wide] = made
+        grads[i, :, wide:] = go[:, pl.ds(pl.multiple_of(s * third, third), third)].astype(F32)
+        for b in range(2):
+            a1_out[i, b] = grads[i, block(b, 1 - x), :two].astype(BF16)
+            b1_out[i, b] = grads[i, block(1 - y, b), two:].astype(BF16)
+        a1(i).start()
+        b1(i).start()
+        return carry
+
+    lax.fori_loop(0, 4, piece, 0)
+
+    def second(i):
+        a1(i).wait_recv()
+        a2_out[i] = (grads[i, block(1 - y, x), :two] + a1_in[i, 1 - y].astype(F32)).astype(BF16)
+        a2(i).start()
+        b1(i).wait_recv()
+        b2_out[i] = (grads[i, block(y, 1 - x), two:] + b1_in[i, 1 - x].astype(F32)).astype(BF16)
+        b2(i).start()
+        grads[i, block(y, x), :two] = grads[i, block(y, x), :two] + a1_in[i, y].astype(F32)
+        grads[i, block(y, x), two:] = grads[i, block(y, x), two:] + b1_in[i, x].astype(F32)
+
+    def third_step(i):
+        a2(i).wait_recv()
+        b2(i).wait_recv()
+        grads[i, block(y, x), :two] = grads[i, block(y, x), :two] + a2_in[i].astype(F32)
+        grads[i, block(y, x), two:] = grads[i, block(y, x), two:] + b2_in[i].astype(F32)
+        if i < 3:
+            z_out[i + 1] = grads[i, block(y, x), :].astype(BF16)
+            to_z(i + 1).start()
+
+    step = own // 2
+    fetches[0].wait()
+
+    def away(i, carry):
+        rows = pl.ds(pl.multiple_of(own + i * step, step), step)
+        half_out[pl.ds(pl.multiple_of(i * step, step), step)] = dot_nt(dj[rows], weight[...]).astype(BF16)
+        return carry
+
+    lax.fori_loop(0, 2, away, 0)
+    swap = remote(half_out, half_in, h_send.at[0], h_recv.at[0], pair)
+    swap.start()
+    second(0)
+    for copy in fetches[1:]:
+        copy.wait()
+    sums[...] = small_in[...]
+    swap.wait_recv()
+
+    def home(i, totals):
+        rows = pl.ds(pl.multiple_of(i * step, step), step)
+        grad = dot_nt(dj[rows], weight[...]) + half_in[rows].astype(F32)
+        standard = std[rows]
+        inner = grad * gain[...]
+        mean = jnp.mean(inner, axis=-1, keepdims=True)
+        along = jnp.mean(inner * standard, axis=-1, keepdims=True)
+        full = base[rows] + (inner - mean - standard * along) * inverse[rows]
+        hide = masked[rows] > 0.0
+        ready[rows] = jnp.where(hide, 0.0, full).astype(BF16)
+        return (
+            totals[0] + jnp.sum(grad * standard, axis=0, keepdims=True),
+            totals[1] + jnp.sum(jnp.where(hide, full, 0.0), axis=0, keepdims=True),
+        )
+
+    zero = jnp.zeros((1, std.shape[1]), F32)
+    gain_grad, embed_grad = lax.fori_loop(0, 2, home, (zero, zero))
+    sums[0:1] = gain_grad
+    sums[3:4] = embed_grad
+
+    def columns(s):
+        return pl.ds(pl.multiple_of(s * BLK, BLK), BLK)
+
+    def stays(k):
+        return jnp.logical_and(z == k, z // 2 == c)
+
+    def ride(k):
+        slot = 2 * (z % 2) + c
+        return remote(ready.at[:, columns(k)], rows_out.at[slot], r_send.at[k], r_recv.at[slot], (y, x, z // 2, k))
+
+    def ride_local(k):
+        return pltpu.make_async_copy(ready.at[:, columns(k)], rows_out.at[2 * (z % 2) + c], local.at[3])
+
+    for k in range(4):
+        pl.when(stays(k))(lambda k=k: ride_local(k).start())
+        pl.when(jnp.logical_not(stays(k)))(lambda k=k: ride(k).start())
+
+    def share(h):
+        peer = (pair, near_y, near_x)[h]
+        return remote(sum_out.at[h], sum_in.at[h], s_send.at[h], s_recv.at[h], peer)
+
+    def begin_share(h):
+        sum_out[h] = sums[...]
+        share(h).start()
+
+    def end_share(h):
+        share(h).wait_recv()
+        sums[...] = sums[...] + sum_in[h]
+
+    begin_share(0)
+    second(1)
+    third_step(0)
+    end_share(0)
+    begin_share(1)
+    second(2)
+    third_step(1)
+    end_share(1)
+    begin_share(2)
+    second(3)
+    third_step(2)
+    end_share(2)
+    sum_out[3] = sums[...]
+
+    def deal(r):
+        s = (z + r) % 4
+        return remote(sum_out.at[3, :, columns(s)], share_in.at[r], p_send.at[r], p_recv.at[r], (y, x, c, s))
+
+    for r in (1, 2, 3):
+        deal(r).start()
+    third_step(3)
+    for r in (1, 2, 3):
+        to_z(r).wait_recv()
+    total = grads[3, block(y, x), :]
+    for r in (1, 2, 3):
+        total = total + z_in[r].astype(F32)
+    grads[3, block(y, x), :] = total
+    rows = BLK // 2
+
+    def core_rows(core):
+        return pl.ds(pl.multiple_of(BLK * (2 * y + x) + rows * core, rows), rows)
+
+    core_out[...] = grads[3, core_rows(1 - c), :].astype(BF16)
+    last = remote(core_out, core_in, c_send.at[0], c_recv.at[0], pair)
+    last.start()
+    kept_out[...] = grads[3, core_rows(c), :]
+    result = sums[:, columns(z)]
+    for r in (1, 2, 3):
+        deal(r).wait_recv()
+        result = result + share_in[r]
+    small_out[...] = result
+    last.wait_recv()
+    landed_out[...] = core_in[...].astype(F32)
+
+    last.wait_send()
+    swap.wait_send()
+    for i in range(4):
+        for copy in (a1(i), b1(i), a2(i), b2(i)):
+            copy.wait_send()
+    for r in (1, 2, 3):
+        to_z(r).wait_send()
+        deal(r).wait_send()
+    for h in range(3):
+        share(h).wait_send()
+    for k in range(4):
+        pl.when(stays(k))(lambda k=k: ride_local(k).wait())
+        pl.when(jnp.logical_not(stays(k)))(lambda k=k: ride(k).wait_send())
+        from_self = jnp.logical_and(2 * c + k // 2 == z, c == k % 2)
+
+        def landed(k=k):
+            remote(ready.at[:, columns(k)], rows_out.at[k], r_send.at[k], r_recv.at[k], near_y).wait_recv()
+
+        pl.when(jnp.logical_not(from_self))(landed)
+
+
+def settle(dj, go, lhs, weight, std, base, inverse, masked, gain, small):
+    own, features = std.shape
+    cols4 = go.shape[1]
+    quarter = cols4 // 4
+    dma = pltpu.SemaphoreType.DMA
+    anywhere = pl.BlockSpec(memory_space=pl.ANY)
+    whole = pl.BlockSpec(memory_space=pltpu.VMEM)
+
+    def low(*shape):
+        return pltpu.VMEM(shape, BF16)
+
+    def high(*shape):
+        return pltpu.VMEM(shape, F32)
+
+    return pl.pallas_call(
+        settle_kernel,
+        in_specs=[whole] * 3 + [anywhere] * 3 + [whole] * 4,
+        out_specs=[whole, whole, anywhere, whole],
+        out_shape=[
+            jax.ShapeDtypeStruct((BLK // 2, cols4), F32),
+            jax.ShapeDtypeStruct((BLK // 2, cols4), F32),
+            jax.ShapeDtypeStruct((4, own, BLK), BF16),
+            jax.ShapeDtypeStruct((8, BLK), F32),
+        ],
+        scratch_shapes=[
+            low(*weight.shape), high(own, features), high(own, features), high(4, features, cols4),
+            low(4, 2, BLK, 2 * quarter), low(4, 2, BLK, 2 * quarter), low(4, 2, BLK, 2 * quarter), low(4, 2, BLK, 2 * quarter),
+            low(4, BLK, 2 * quarter), low(4, BLK, 2 * quarter), low(4, BLK, 2 * quarter), low(4, BLK, 2 * quarter),
+            low(4, BLK, cols4), low(4, BLK, cols4),
+            low(own, features), low(own, features), low(own, features),
+            low(BLK // 2, cols4), low(BLK // 2, cols4),
+            high(8, features), high(4, 8, features), high(3, 8, features), high(4, 8, BLK),
+        ]
+        + [dma((4,))] * 10
+        + [dma((1,)), dma((1,)), dma((4,)), dma((4,)), dma((1,)), dma((1,)), dma((3,)), dma((3,)), dma((4,)), dma((4,)), dma((4,))],
+        compiler_params=pltpu.CompilerParams(
+            collective_id=3, has_side_effects=True, vmem_limit_bytes=56 * 1024 * 1024
+        ),
+        cost_estimate=pl.CostEstimate(flops=10**10, transcendentals=10**6, bytes_accessed=10**8),
+        name="settle",
+    )(dj, go, lhs, weight, std, base, inverse, masked, gain, small)
+
+
 def tie(*values):
     return lax.optimization_barrier(values)
 
@@ -1096,21 +1358,6 @@
     plane = 2 * y + x
     k_own = 2 * (z % 2) + c
 
-    def return_rows(v):
-        landed = jnp.stack(
-            [
-                lax.ppermute(
-                    lax.dynamic_slice_in_dim(v, (k_own ^ r) * BLK, BLK, 1),
-                    AXES,
-                    [(b, a) for a, b in spread_pairs(r)],
-                )
-                for r in range(4)
-            ]
-        )
-        return jnp.stack(
-            [lax.dynamic_index_in_dim(landed, k ^ z, 0, keepdims=False) for k in range(4)]
-        ).reshape(tokens.shape)
-
     masked_here = (priority < ratio[:, None, None]).astype(jnp.int32).reshape(2, -1)
     info = cols([masked_here, frame_order])
     info = jnp.where(z // 2 == c, info, hop_c(info))
@@ -1196,12 +1443,12 @@
     block_part = sum(dot_nt(h, w) for h, w in zip(hidden, wf_out))
     block_rows = (resid2 + pair_scatter(block_part)).astype(BF16)
 
-    def plane_scatter(lhs, parts):
+    def line_scatter(lhs, parts):
         parts = jnp.stack([dot_tn(lhs, rhs).astype(BF16) for rhs in parts])
-        return lax.psum_scatter(parts, ("tm", "x"), scatter_dimension=1, tiled=True)
-
-    def line_scatter(v):
-        return lax.psum_scatter(v, "mp", scatter_dimension=0).astype(F32)
+        return lax.psum_scatter(parts, "mp", scatter_dimension=0)
+
+    def plane_scatter(v):
+        return lax.psum_scatter(v, ("tm", "x"), scatter_dimension=0, tiled=True).astype(F32)
 
     def send_x(lhs, rhs):
         there = jnp.where(x == 0, cols([lhs[:, BLK : 2 * BLK], lhs[:, 3 * BLK :]]), cols([lhs[:, :BLK], lhs[:, 2 * BLK : 3 * BLK]]))
@@ -1232,10 +1479,10 @@
     def by_core(kept, landed):
         return jnp.where(c == 0, jnp.concatenate([kept, landed], -1), jnp.concatenate([landed, kept], -1))
 
-    w_out_part = plane_scatter(gb3, hidden)
+    w_out_part = line_scatter(gb3, hidden)
     grad_inner = [pull(dot_nn(gb3, w))[0].astype(BF16) for pull, w in zip(pulls, wf_out)]
     part2 = pair_scatter(sum(dot_nt(g, w) for g, w in zip(grad_inner, wf_in)))
-    w_in_part = plane_scatter(normed2, grad_inner)
+    w_in_part = line_scatter(normed2, grad_inner)
     back2, gain_grad2 = norm_rows_back(part2, std2, inv2, gain[2])
     grad2 = grad3.astype(F32) + back2
     gb2, djoined1, part1, block_out = time_call(
@@ -1255,18 +1502,15 @@
     back1, gain_grad1 = norm_rows_back(part1, std1, inv1, gain[1])
     grad1 = grad2 + back1
     gb1 = pair_gather(grad1.astype(BF16))
+    gb1, w_out_part = tie(gb1, w_out_part)
+    g_w_out = plane_scatter(w_out_part)
     t_out_x = send_x(gb2, mixed1)
     t_qkv_x = send_x(normed1, djoined1)
     dmixed0 = dot_nn(gb1, ws_out).astype(BF16)
-    s_out_x = send_x(gb1, mixed0)
+    go = dot_tn(gb1, mixed0).astype(BF16)
     djoined0 = space_attend_back(joined0, dmixed0, total0, frames_pair, patches, heads_s, scale)
-    djoined0, t_out_x, t_qkv_x, w_out_part, s_out_x = tie(djoined0, t_out_x, t_qkv_x, w_out_part, s_out_x)
-    g_w_out = line_scatter(w_out_part)
-    s_qkv_x = send_x(normed0, djoined0)
-    part0 = pair_scatter(dot_nt(djoined0, ws_qkv))
-    s_out_kept = keep_x(gb1, mixed0, s_out_x)
-    s_out_y = hop_y(other_y(s_out_kept).astype(BF16))
-    g_w_in = line_scatter(w_in_part)
+    djoined0, t_out_x, t_qkv_x, w_in_part, go = tie(djoined0, t_out_x, t_qkv_x, w_in_part, go)
+    g_w_in = plane_scatter(w_in_part)
     g_t_out = keep_x(gb2, mixed1, t_out_x)
     g_t_qkv = keep_x(normed1, djoined1, t_qkv_x)
     z_at = [(z + r) % 4 for r in range(4)]
@@ -1280,34 +1524,13 @@
             for s in z_at
         ]
     )
-    s_qkv_kept = keep_x(normed0, djoined0, s_qkv_x)
-    s_qkv = mine_y(s_qkv_kept) + hop_y(other_y(s_qkv_kept).astype(BF16)).astype(F32)
-    s_out = mine_y(s_out_kept) + s_out_y.astype(F32)
-    g_space = reduce_z(
-        [
-            cols(
-                [
-                    lax.dynamic_slice_in_dim(s_qkv, s * 3 * half, 3 * half, 1),
-                    lax.dynamic_slice_in_dim(s_out, s * half, half, 1),
-                ]
-            )
-            for s in z_at
-        ]
-    )
-    back0, gain_grad0 = norm_rows_back(part0, std0, inv0, gain[0])
-    grad0 = grad1 + back0
-    grad_tokens = return_rows(jnp.where(masked, 0.0, grad0).astype(BF16)).astype(F32)
-    grad_embed = jnp.sum(jnp.where(masked, grad0, 0.0), axis=0)
-    small = jnp.stack([gain_grad0, gain_grad1, gain_grad2, grad_embed])
-    for hop in (hop_c, hop_y, hop_x):
-        small = small + hop(small)
-    small_at = [lax.dynamic_slice_in_dim(small, s * BLK, BLK, 1) for s in z_at]
-    small = small_at[0]
-    for r in (1, 2, 3):
-        small = small + hop_z(small_at[r], r)
+    small = rows_of([jnp.zeros((1, width), F32), gain_grad1[None], gain_grad2[None], jnp.zeros((5, width), F32)])
+    kept, landed, grad_tokens, small = settle(
+        djoined0, go, normed0.T, ws_qkv, std0, grad1, inv0, masked.astype(F32), gain[0], small
+    )
+    grad_tokens = grad_tokens.reshape(tokens.shape).astype(F32)
 
     rows = BLK // 2
-    kept, landed = swap_c(g_space)
     grad_qkv_space = by_core(
         kept[:, : 3 * half].reshape(rows, 3, half), landed[:, : 3 * half].reshape(rows, 3, half)
     )

time: 633 us -> 568 us (0.90)
  waiting for transfers between devices: 98.6 us -> 36 us
  Pallas kernels: 252 us -> 294 us
  starting transfers between devices: 41.5 us -> 14 us
  matrix products: 112 us -> 96.8 us
  other arithmetic: 51.9 us -> 44.6 us
    pallas_call x0 -> x1, Pallas kernels: none -> 69.8 us  [settle(): pl.pallas_call(settle_kernel, in_specs=[whole] * 3 + [anywhere] * 3 + [wh...]
    ppermute x9 -> x3, waiting for transfers between devices: 40.7 us -> 0.01 us  [hop_z(): lax.ppermute(v, AXES, device_pairs(lambda y, x, c, z: (y, x, c, (z + shif...]
    pallas_call x2, Pallas kernels: 156 us -> 129 us  [time_call(): pl.pallas_call(functools.partial(time_kernel, back, scale, heads), in_spe...]
    ppermute x4 -> x0, waiting for transfers between devices: 14.3 us -> none  [return_rows(): lax.ppermute(lax.dynamic_slice_in_dim(v, (k_own ^ r) * BLK, BLK, 1), AXES...]
    ppermute x4 -> x0, starting transfers between devices: 9.18 us -> none  [return_rows(): lax.ppermute(lax.dynamic_slice_in_dim(v, (k_own ^ r) * BLK, BLK, 1), AXES...]
    dot_general x16 -> x13, matrix products: 49 us -> 39.8 us  [dot_tn(): lax.dot_general(a, b, (((0,), (0,)), ((), ())), preferred_element_type=F32)]
    ppermute x9 -> x3, starting transfers between devices: 11 us -> 3.97 us  [hop_z(): lax.ppermute(v, AXES, device_pairs(lambda y, x, c, z: (y, x, c, (z + shif...]
    dot_general x10 -> x9, matrix products: 24.3 us -> 17.5 us  [dot_nt(): lax.dot_general(a, b, (((1,), (1,)), ((), ())), preferred_element_type=F32)]
  transfers between devices with their start and end apart: 41 -> 22, of which waited for: 15 -> 5; matrix products, arithmetic and copies ran while one was open for 30% -> 31% of each run, Pallas kernels for 30% -> 41%
where the time goes in v4:
time: 568 us; the launch traced here: 561 us
  Pallas kernels  294 us (52%)
  matrix products  96.8 us (17%)
  local copies, waits for them, and re-layouts  60.2 us (11%)
  other arithmetic  44.6 us (8%)
  waiting for transfers between devices  36 us (6%)
  between operations  15.9 us (3%)
  starting transfers between devices  14 us (2%)
    pallas_call x2, Pallas kernels, time_call(): pl.pallas_call(functools.partial(time_kernel, back, scale, heads), in_spe...  129 us
    pallas_call x1, Pallas kernels, settle(): pl.pallas_call(settle_kernel, in_specs=[whole] * 3 + [anywhere] * 3 + [wh...  69.8 us
    pallas_call x1, Pallas kernels, arrive(): pl.pallas_call(arrive_kernel, in_specs=[anywhere] * 4, out_specs=[anywher...  61.2 us
    dot_general x13, matrix products, dot_tn(): lax.dot_general(a, b, (((0,), (0,)), ((), ())), preferred_element_type=F32)  39.8 us
    dot_general x10, matrix products, dot_nn(): lax.dot_general(a, b, (((1,), (0,)), ((), ())), preferred_element_type=F32)  39.5 us
    all_gather x2, waiting for transfers between devices, gather_ff(): w = lax.all_gather(w, ('mp', 'tm', 'x')).reshape(4, width, hidden_own)  29.2 us
    pallas_call x1, Pallas kernels, space_attend_back(): pl.pallas_call(functools.partial(space_attend_back_kernel, scale), grid=(...  17.9 us
    dot_general x9, matrix products, dot_nt(): lax.dot_general(a, b, (((1,), (1,)), ((), ())), preferred_element_type=F32)  17.5 us
  transfers between devices with their start and end apart: 22, of which 5 were waited for; matrix products, arithmetic and copies ran while one was open for 31% of the time, Pallas kernels for 41%

profile of v4, /device:TPU:9, one launch (start us, length us, event | category | flops | bytes accessed | tf_op | source)
XLA Modules:
  0.0 561.1 jit_solution(6505645473014984409)
XLA Ops:
  19.2 61.2 %arrive.1 = (bf16[512,1024]{1,0:T(8,128)(2,1)}, bf16[8,1024]{1,0:T(8,128)(2,1)}, bf16[1024,1536]{1,0:T(8,128)(2,1)}, bf16[1024,512]{1,0:T(8,128)(2,1)}, bf16[1024,1024]{1,0:T(8,128)(2,1)}) custom-call(bf16[4,512,256]{2,1,0:T(8,128)(2,1)} %bitcast.124, bf16[8,256]{1,0:T(8,128)(2,1)} %maximum_maximum_fusion.1.vec, bf16[1024,512]{1,0:T(8,128)(2,1)} %pad_maximum_fusion.19.mine, ...), custom_call_target="tpu_custom_call" | custom-call | tf_op jit(solution)/shard_map/arrive/pallas_call | solution.py:678
  84.1 2.4 fusion.42
  87.0 3.9 copy.71
  92.9 7.4 %convolution_convert_fusion.qkv_ref = bf16[1024,1536]{1,0:T(8,128)(2,1)} fusion(bf16[1024,1536]{1,0:T(8,128)(2,1)} %get-tuple-element.42.weight_hbm, bf16[512,1024]{1,0:T(8,128)(2,1)} %collective-permute-done.1, bf16[512,1024]{1,0:T(8,128)(2,1)S(1)} %get-tuple-element.135), kind=kOutput, calls=%fused_computation.4 | convolution fusion | flops 3226992640 | bytes 8388608 | tf_op jit(solution)/shard_map/dot_general | solution.py:701
  100.3 16.3 %space_attend.1 = (bf16[1024,512]{1,0:T(8,128)(2,1)}, f32[8,8,128]{2,1,0:T(8,128)}) custom-call(bf16[1024,1536]{1,0:T(8,128)(2,1)} %convolution_convert_fusion.qkv_ref), custom_call_target="tpu_custom_call" | custom-call | flops 1073741824 | bytes 4194304 | tf_op jit(solution)/shard_map/space_attend/pallas_call | solution.py:778
  116.5 2.7 fusion.125
  123.8 2.6 copy.74.refs_2_.refs_4_
  127.3 2.5 fusion.119
  131.7 73.2 %time_forward.1 = (bf16[16,128,1024]{2,1,0:T(8,128)(2,1)}, bf16[16,128,768]{2,1,0:T(8,128)(2,1)}, bf16[16,128,256]{2,1,0:T(8,128)(2,1)S(1)}, f32[16,4,128]{2,1,0...) custom-call(bf16[4,128,1024]{2,1,0:T(8,128)(2,1)S(1)} %bitcast.109, ...), custom_call_target="tpu_custom_call" | custom-call | flops 10000000000 | bytes 100000000 | tf_op jit(solution)/shard_map/time_forward/pallas_call | solution.py:1021
  204.9 2.3 fusion.118
  212.2 2.9 fusion.82
  215.1 3.2 fusion.72
  218.4 3.2 fusion.64
  221.6 3.2 fusion.92
  224.9 3.7 fusion.53
  228.6 3.0 fusion.54
  231.6 3.0 fusion.55
  234.6 3.1 fusion.52
  237.8 2.3 pad_maximum_fusion
  240.5 29.2 %all-gather.5.cloned.1.call-done = bf16[4096,512]{0,1:T(8,128)(2,1)} async-done(((bf16[256,512]{0,1:T(8,128)(2,1)}), bf16[4096,512]{0,1:T(8,128)(2,1)}) %all-gather.5.cloned.1.call-update) | async-done | bytes 4194320 | tf_op jit(solution)/shard_map/all_gather | solution.py:1402
  269.7 3.4 fusion.98
  280.6 3.9 fusion.13
  284.5 2.9 fusion.57
  287.5 4.0 fusion.20
  291.4 2.9 fusion.58
  294.4 4.1 fusion.27
  298.5 2.9 fusion.59
  301.5 4.0 fusion.6
  305.5 2.9 fusion.56
  308.4 2.4 pad_maximum_fusion.1
  311.1 3.0 fusion.94
  323.5 3.0 fusion.60
  326.5 3.9 copy.78.lhs
  330.5 2.7 fusion.121
  333.5 2.5 copy-done.11
  335.9 3.3 multiply_reduce_fusion
  340.6 55.3 %time_back.1 = (bf16[16,128,1024]{2,1,0:T(8,128)(2,1)}, bf16[16,128,768]{2,1,0:T(8,128)(2,1)}, f32[4,128,1024]{2,1,0:T(8,128)}, bf16[4,512,256]{2,1,0:T(8,128)(2,1)S(1)}) custom-call(bf16[4,128,1024]{2,1,0:T(8,128)(2,1)S(1)} %bitcast.108, bf16[512,1024]{1,0:T(8,128)(2,1)S(1)} %get-tuple-element.121.refs_1_, bf16[16,128,768]{2,1,0:T(8,128)(2,1)} %get-tuple-element.50.refs_2_, ...), custom_call_target="tpu_custom_call" | custom-call | flops 10000000000 | bytes 100000000 | tf_op jit(solution)/shard_map/time_back/pallas_call | solution.py:1021
  396.0 2.6 fusion.122
  402.4 2.1 fusion.116
  406.2 2.8 fusion.49
  413.9 4.3 convolution_convert_fusion.1.go
  418.6 3.4 convolution_convert_fusion.6.grad_ref
  422.0 17.9 %space_attend_back.1.dj = bf16[1024,1536]{1,0:T(8,128)(2,1)} custom-call(bf16[1024,1536]{1,0:T(8,128)(2,1)} %convolution_convert_fusion.qkv_ref, bf16[1024,512]{1,0:T(8,128)(2,1)} %convolution_convert_fusion.6.grad_ref, f32[8,8,128]{2,1,0:T(8,128)} %get-tuple-element.55.total_ref), custom_call_target="tpu_custom_call" | custom-call | flops 2684354560 | bytes 10485760 | tf_op jit(solution)/shard_map/space_attend_back/pallas_call | solution.py:797
  440.2 5.2 convert_add_fusion
  446.6 2.2 collective-permute-start.11
  452.4 69.8 %settle.1 = (f32[128,512]{1,0:T(8,128)}, f32[128,512]{1,0:T(8,128)}, bf16[4,512,256]{2,1,0:T(8,128)(2,1)}, f32[8,256]{1,0:T(8,128)}) custom-call(bf16[1024,1536]{1,0:T(8,128)(2,1)} %space_attend_back.1.dj, bf16[1024,512]{1,0:T(8,128)(2,1)} %convolution_convert_fusion.1.go, bf16[1024,1024]{1,0:T(8,128)(2,1)} %copy.78.lhs, ...), custom_call_target="tpu_custom_call" | custom-call | flops 10000000000 | bytes 100000000 | tf_op jit(solution)/shard_map/settle/pallas_call | solution.py:1279
  532.6 4.3 collective-permute-done.13
  548.8 2.0 copy.90
  (273 shorter events, 90.1 us)
Async XLA Ops:
  7.2 4.8 copy-start
  7.2 205.0 %all-gather.7.cloned.1.call-start = ((), (), s32[]{:S(2)}) async-start(), calls=%async_computation.9 | async-start | bytes 4456448 | tf_op jit(solution)/shard_map/all_gather | solution.py:1402
  17.5 63.0 %copy-start.36 = (s32[2,8,128]{2,1,0:T(8,128)S(1)}, s32[2,8,128]{2,1,0:T(8,128)}, u32[]{:S(2)}) copy-start(s32[2,8,128]{2,1,0:T(8,128)} %param.16) | copy-start | bytes 24580
  17.5 63.0 %copy-start.40 = (s32[2]{0:T(128)S(1)}, s32[2]{0:T(128)}, u32[]{:S(2)}) copy-start(s32[2]{0:T(128)} %param.15) | copy-start | bytes 28
  17.5 63.1 %copy-start.39 = (s32[2,16]{1,0:T(2,128)S(1)}, s32[2,16]{1,0:T(2,128)}, u32[]{:S(2)}) copy-start(s32[2,16]{1,0:T(2,128)} %param.17) | copy-start | bytes 388
  80.5 189.3 %all-gather.5.cloned.1.call-start = ((), (), s32[]{:S(2)}) async-start(), calls=%async_computation.8 | async-start | bytes 4456448 | tf_op jit(solution)/shard_map/all_gather | solution.py:1402
  80.7 1.2 collective-permute-start
  81.6 4.9 copy-start.35
  86.5 6.4 %copy-start.16 = (bf16[512,1024]{1,0:T(8,128)(2,1)}, bf16[512,1024]{1,0:T(8,128)(2,1)S(1)}, u32[]{:S(2)}) copy-start(bf16[512,1024]{1,0:T(8,128)(2,1)S(1)} %get-tuple-element.135) | copy-start | bytes 3145732
  86.5 6.3 %collective-permute-start.1 = (bf16[512,1024]{1,0:T(8,128)(2,1)S(1)}, bf16[512,1024]{1,0:T(8,128)(2,1)}, u32[]{:S(2)}, u32[]{:S(2)}) collective-permute-start(bf16[512,1024]{1,0:T(8,128)(2,1)S(1)} %get-tuple-element.135), channel_id=1, source_target_pairs={{0,4},{1,5},{2,6},{3,7},{4,0},{5,1},{6,2},{7,3},{8,12},{9,13},{10,... | collective-permute-start | bytes 3145736 | tf_op jit(solution)/shard_map/ppermute | solution.py:434
  86.8 327.1 %reduce-scatter.5.cloned.1.call-start = ((), (), s32[]{:S(2)}) async-start(), calls=%async_computation.4 | async-start | bytes 5242880 | tf_op jit(solution)/shard_map/reduce_scatter | solution.py:1448
  100.3 16.3 %copy-start.41 = (bf16[1024,512]{1,0:T(8,128)(2,1)S(1)}, bf16[1024,512]{1,0:T(8,128)(2,1)}, u32[]{:S(2)}) copy-start(bf16[1024,512]{1,0:T(8,128)(2,1)} %get-tuple-element.44) | copy-start | bytes 3145732
  121.7 5.5 collective-permute-start.2
  129.7 75.2 %copy-start.6 = (f32[512,1024]{1,0:T(8,128)}, f32[512,1024]{1,0:T(8,128)S(1)}, u32[]{:S(2)}) copy-start(f32[512,1024]{1,0:T(8,128)S(1)} %get-tuple-element.112) | copy-start | bytes 6291460
  208.5 3.6 collective-permute-start.4
  210.9 14.0 %collective-permute-start.3 = (bf16[512,1024]{1,0:T(8,128)(2,1)}, bf16[512,1024]{1,0:T(8,128)(2,1)}, u32[]{:S(2)}, u32[]{:S(2)}) collective-permute-start(bf16[512,1024]{1,0:T(8,128)(2,1)} %broadcast_select_fusion), channel_id=1, source_target_pairs={{0,4},{1,5},{2,6},{3,7},{4,0},{5,1},{6,2},{7,3},{8,12},{9,13},{10,... | collective-permute-start | bytes 3145736 | tf_op jit(solution)/shard_map/ppermute | solution.py:434
  215.1 9.8 %copy-start.52 = (f32[1024,512]{1,0:T(8,128)}, f32[1024,512]{1,0:T(8,128)S(1)}, u32[]{:S(2)}) copy-start(f32[1024,512]{1,0:T(8,128)S(1)} %fusion.82) | copy-start | bytes 6291460
  218.4 10.3 %copy-start.50 = (f32[1024,512]{1,0:T(8,128)}, f32[1024,512]{1,0:T(8,128)S(1)}, u32[]{:S(2)}) copy-start(f32[1024,512]{1,0:T(8,128)S(1)} %fusion.72) | copy-start | bytes 6291460
  221.6 10.0 %copy-start.18 = (f32[1024,512]{1,0:T(8,128)}, f32[1024,512]{1,0:T(8,128)S(1)}, u32[]{:S(2)}) copy-start(f32[1024,512]{1,0:T(8,128)S(1)} %fusion.64) | copy-start | bytes 6291460
  224.9 9.8 %copy-start.48 = (f32[1024,512]{1,0:T(8,128)}, f32[1024,512]{1,0:T(8,128)S(1)}, u32[]{:S(2)}) copy-start(f32[1024,512]{1,0:T(8,128)S(1)} %fusion.92) | copy-start | bytes 6291460
  240.1 199.8 %reduce-scatter.7.cloned.1.call-start = ((), (), s32[]{:S(2)}) async-start(), calls=%async_computation.5 | async-start | bytes 5242880 | tf_op jit(solution)/shard_map/reduce_scatter | solution.py:1448
  269.7 3.8 copy-start.51
  278.4 6.1 %copy-start.14 = (f32[1024,1024]{1,0:T(8,128)}, f32[1024,1024]{1,0:T(8,128)S(1)}, u32[]{:S(2)}) copy-start(f32[1024,1024]{1,0:T(8,128)S(1)} %add_add_fusion) | copy-start | bytes 12582916
  279.7 53.5 %collective-permute-start.6 = (bf16[512,1024]{1,0:T(8,128)(2,1)}, bf16[512,1024]{1,0:T(8,128)(2,1)}, u32[]{:S(2)}, u32[]{:S(2)}) collective-permute-start(bf16[512,1024]{1,0:T(8,128)(2,1)} %slice.302), channel_id=1, source_target_pairs={{0,4},{1,5},{2,6},{3,7},{4,0},{5,1},{6,2},{7,3},{8,12},{9,13},{10,... | collective-permute-start | bytes 3145736 | tf_op jit(solution)/shard_map/ppermute | solution.py:434
  310.8 233.5 %reduce-scatter.11.cloned.1.call-start = ((), (), s32[]{:S(2)}) async-start(), calls=%async_computation.7 | async-start | bytes 1310720 | tf_op jit(solution)/shard_map/reduce_scatter | solution.py:1451
  321.3 12.0 %collective-permute-start.5 = (bf16[512,1024]{1,0:T(8,128)(2,1)}, bf16[512,1024]{1,0:T(8,128)(2,1)S(1)}, u32[]{:S(2)}, u32[]{:S(2)}) collective-permute-start(bf16[512,1024]{1,0:T(8,128)(2,1)} %slice.303), channel_id=1, source_target_pairs={{0,4},{1,5},{2,6},{3,7},{4,0},{5,1},{6,2},{7,3},{8,12},{9,13},{10,... | collective-permute-start | bytes 3145736 | tf_op jit(solution)/shard_map/ppermute | solution.py:434
  330.5 5.5 copy-start.11
  333.2 73.0 %copy-start.25 = (bf16[2048,256]{1,0:T(8,128)(2,1)}, bf16[2048,256]{1,0:T(8,128)(2,1)S(1)}, u32[]{:S(2)}) copy-start(bf16[2048,256]{1,0:T(8,128)(2,1)S(1)} %get-tuple-element.113) | copy-start | bytes 3145732
  333.2 73.0 %copy-start.26 = (bf16[2048,256]{1,0:T(8,128)(2,1)}, bf16[2048,256]{1,0:T(8,128)(2,1)S(1)}, u32[]{:S(2)}) copy-start(bf16[2048,256]{1,0:T(8,128)(2,1)S(1)} %get-tuple-element.114) | copy-start | bytes 3145732
  333.2 73.0 %copy-start.27 = (bf16[2048,256]{1,0:T(8,128)(2,1)}, bf16[2048,256]{1,0:T(8,128)(2,1)S(1)}, u32[]{:S(2)}) copy-start(bf16[2048,256]{1,0:T(8,128)(2,1)S(1)} %get-tuple-element.115) | copy-start | bytes 3145732
  333.2 73.0 %copy-start.28 = (bf16[2048,256]{1,0:T(8,128)(2,1)}, bf16[2048,256]{1,0:T(8,128)(2,1)S(1)}, u32[]{:S(2)}) copy-start(bf16[2048,256]{1,0:T(8,128)(2,1)S(1)} %get-tuple-element.116) | copy-start | bytes 3145732
  400.1 39.8 %collective-permute-start.8 = (bf16[512,256]{1,0:T(8,128)(2,1)}, bf16[512,256]{1,0:T(8,128)(2,1)S(1)}, u32[]{:S(2)}, u32[]{:S(2)}) collective-permute-start(bf16[512,256]{1,0:T(8,128)(2,1)} %fusion.61), channel_id=1, source_target_pairs={{0,8},{1,9},{2,10},{3,11},{4,12},{5,13},{6,14},{7,15},{8,0},{9,1},... | collective-permute-start | bytes 786440 | tf_op jit(solution)/shard_map/ppermute | solution.py:430
  404.5 7.9 %collective-permute-start.7 = (bf16[512,1024]{1,0:T(8,128)(2,1)S(1)}, bf16[512,1024]{1,0:T(8,128)(2,1)S(1)}, u32[]{:S(2)}, u32[]{:S(2)}) collective-permute-start(bf16[512,1024]{1,0:T(8,128)(2,1)S(1)} %get-tuple-element.105), channel_id=1, source_target_pairs={{0,4},{1,5},{2,6},{3,7},{4,0},{5,1},{6,2},{7,3},{8,12},{9,13},{10,... | collective-permute-start | bytes 3145736 | tf_op jit(solution)/shard_map/ppermute | solution.py:434
  409.0 30.9 %collective-permute-start.9 = (bf16[512,768]{1,0:T(8,128)(2,1)}, bf16[512,768]{1,0:T(8,128)(2,1)}, u32[]{:S(2)}, u32[]{:S(2)}) collective-permute-start(bf16[512,768]{1,0:T(8,128)(2,1)} %fusion.49), channel_id=1, source_target_pairs={{0,8},{1,9},{2,10},{3,11},{4,12},{5,13},{6,14},{7,15},{8,0},{9,1},... | collective-permute-start | bytes 2359304 | tf_op jit(solution)/shard_map/ppermute | solution.py:430
  413.9 4.6 copy-start.20
  418.2 126.1 %reduce-scatter.9.cloned.1.call-start = ((), (), s32[]{:S(2)}) async-start(), calls=%async_computation.6 | async-start | bytes 1310720 | tf_op jit(solution)/shard_map/reduce_scatter | solution.py:1451
  422.0 17.9 %copy-start.29 = (f32[512,256]{1,0:T(8,128)S(1)}, f32[512,256]{1,0:T(8,128)}, u32[]{:S(2)}) copy-start(f32[512,256]{1,0:T(8,128)} %fusion.32) | copy-start | bytes 1572868
  446.6 83.5 %collective-permute-start.11 = (bf16[512,256]{1,0:T(8,128)(2,1)}, bf16[512,256]{1,0:T(8,128)(2,1)}, u32[]{:S(2)}, u32[]{:S(2)}) collective-permute-start(bf16[512,256]{1,0:T(8,128)(2,1)} %pad_maximum_fusion.23), channel_id=1, source_target_pairs={{0,2},{1,3},{2,0},{3,1},{4,6},{5,7},{6,4},{7,5},{8,10},{9,11},{10,... | collective-permute-start | bytes 786440 | tf_op jit(solution)/shard_map/ppermute | solution.py:438
  449.7 80.5 %collective-permute-start.12 = (bf16[512,256]{1,0:T(8,128)(2,1)}, bf16[512,256]{1,0:T(8,128)(2,1)}, u32[]{:S(2)}, u32[]{:S(2)}) collective-permute-start(bf16[512,256]{1,0:T(8,128)(2,1)} %pad_maximum_fusion.24), channel_id=1, source_target_pairs={{0,3},{1,0},{2,1},{3,2},{4,7},{5,4},{6,5},{7,6},{8,11},{9,8},{10,9... | collective-permute-start | bytes 786440 | tf_op jit(solution)/shard_map/ppermute | solution.py:438
  450.8 79.4 %collective-permute-start.10 = (bf16[512,256]{1,0:T(8,128)(2,1)}, bf16[512,256]{1,0:T(8,128)(2,1)}, u32[]{:S(2)}, u32[]{:S(2)}) collective-permute-start(bf16[512,256]{1,0:T(8,128)(2,1)} %pad_maximum_fusion.22), channel_id=1, source_target_pairs={{0,1},{1,2},{2,3},{3,0},{4,5},{5,6},{6,7},{7,4},{8,9},{9,10},{10,1... | collective-permute-start | bytes 786440 | tf_op jit(solution)/shard_map/ppermute | solution.py:438
  530.2 8.3 %copy-start.33 = (f32[128,128]{1,0:T(8,128)S(1)}, f32[128,128]{1,0:T(8,128)}, u32[]{:S(2)}) copy-start(f32[128,128]{1,0:T(8,128)} %slice.184) | copy-start | bytes 196612
  530.2 8.3 %copy-start.34 = (f32[128,128]{1,0:T(8,128)S(1)}, f32[128,128]{1,0:T(8,128)}, u32[]{:S(2)}) copy-start(f32[128,128]{1,0:T(8,128)} %slice.185) | copy-start | bytes 196612
  530.2 8.3 %copy-start.37 = (f32[8,256]{1,0:T(8,128)S(1)}, f32[8,256]{1,0:T(8,128)}, u32[]{:S(2)}) copy-start(f32[8,256]{1,0:T(8,128)} %get-tuple-element.63) | copy-start | bytes 24580
  531.8 9.6 %copy-start.22 = (bf16[4,512,256]{2,1,0:T(8,128)(2,1)S(1)}, bf16[4,512,256]{2,1,0:T(8,128)(2,1)}, u32[]{:S(2)}) copy-start(bf16[4,512,256]{2,1,0:T(8,128)(2,1)} %get-tuple-element.62) | copy-start | bytes 3145732
  531.8 5.0 collective-permute-start.13
  537.6 5.5 collective-permute-start.14
  545.5 1.6 collective-permute-start.15
  547.9 5.7 %copy-start.1 = (bf16[1024,1024]{1,0:T(8,128)(2,1)S(1)}, bf16[1024,1024]{1,0:T(8,128)(2,1)}, u32[]{:S(2)}) copy-start(bf16[1024,1024]{1,0:T(8,128)(2,1)} %param.25) | copy-start | bytes 6291460
  (28 other events, 69.2 us)
Sparse Core Ops, SparseCore 0:
  80.6 97.5 all-gather.6
  181.5 88.2 all-gather.4
  272.0 76.5 reduce-scatter.4
  350.9 87.6 reduce-scatter.6
  441.4 30.9 reduce-scatter.10
  475.4 33.7 reduce-scatter.8

commit v5 on v4

--- a/solution.py
+++ b/solution.py
@@ -815,18 +815,21 @@
 
 def time_kernel(back, scale, heads, *refs):
     if back:
-        (own_ref, rider_ref, joined_ref, total_ref, wq_ref, wo_ref, bias_ref, all_ref, out_ref, delta_ref, rider_out) = refs[:11]
-        refs = refs[11:]
+        (own_ref, rider_ref, joined_ref, total_ref, wide_ref, wq_ref, wo_ref, bias_ref) = refs[:8]
+        (all_ref, out_ref, delta_ref, halved_ref, rider_out) = refs[8:13]
+        (halved_in, halved_own, half_send, half_recv, half_local) = refs[-5:]
+        refs = refs[13:-5]
     else:
-        (own_ref, rider_ref, wq_ref, wo_ref, bias_ref, all_ref, out_ref, mixed_ref, total_ref, delta_ref, rider_out) = refs[:11]
-        refs = refs[11:]
+        (own_ref, rider_ref, far_ref, near_ref, wq_ref, wo_ref, bias_ref) = refs[:7]
+        (all_ref, out_ref, mixed_ref, total_ref, delta_ref, rider_out, spread_out) = refs[7:14]
+        refs = refs[14:]
     (
         held, wide, narrow, kept, core_out, core_in, near_out, near_in,
         gy_send, gy_recv, gc_send, gc_recv, gd_send, gd_recv, sc_send, sc_recv, sy_send, sy_recv,
-        r_send, r_recv, r_local, out_sem,
+        r_send, r_recv, r_local, out_sem, wy_send, wy_recv, wx_send, wx_recv, wd_send, wd_recv, w_local,
     ) = refs
     y, x, c, z = (lax.axis_index(name) for name in AXES)
-    near, pair = (1 - y, x, c, z), (y, x, 1 - c, z)
+    near, pair, near_x = (1 - y, x, c, z), (y, x, 1 - c, z), (y, 1 - x, c, z)
     frames = held.shape[0] // 4
     chunks = held.shape[1] // CHUNK
     width = heads * HEAD_DIM
@@ -838,7 +841,8 @@
             if dc or dz:
                 pl.semaphore_signal(barrier, inc=1, device_id=(y, x, (c + dc) % 2, (z + dz) % 4), device_id_type=MESH)
     pl.semaphore_signal(barrier, inc=1, device_id=near, device_id_type=MESH)
-    pl.semaphore_wait(barrier, 8)
+    pl.semaphore_signal(barrier, inc=1, device_id=near_x, device_id_type=MESH)
+    pl.semaphore_wait(barrier, 9)
 
     def remote(src, dst, send, recv, peer):
         return pltpu.make_async_remote_copy(
@@ -906,9 +910,59 @@
             return jnp.logical_and(2 * c + k // 2 == z, c == k % 2)
         return jnp.logical_and(z == k, z // 2 == c)
 
+    def place(dy, dx, r):
+        size = far_ref.shape[1]
+        at = pl.multiple_of(size * (2 * ((y + dy) % 2) + (x + dx) % 2), size)
+        return spread_out.at[(z + r) % 4, pl.ds(at, size)]
+
+    def spread_y(r, dy=0):
+        src = far_ref.at[r - 1] if dy == 0 else place(1, 0, r)
+        return remote(src, place(dy, 0, r), wy_send.at[r], wy_recv.at[r], near)
+
+    def spread_x(r, dx=0):
+        src = far_ref.at[r - 1] if dx == 0 else place(0, 1, r)
+        return remote(src, place(0, dx, r), wx_send.at[r], wx_recv.at[r], near_x)
+
+    def spread_d(r, dx=0):
+        return remote(place(1, dx, r), place(1, dx, r), wd_send.at[r], wd_recv.at[r], near_x)
+
+    def spread_keep(r):
+        if r == 0:
+            size = 4 * far_ref.shape[1]
+            here = near_ref.at[pl.ds(pl.multiple_of(c * size, size), size)]
+            return pltpu.make_async_copy(here, spread_out.at[z], w_local.at[0])
+        return pltpu.make_async_copy(far_ref.at[r - 1], place(0, 0, r), w_local.at[r])
+
+    def spread_on(r):
+        spread_y(r, 1).wait_recv()
+        spread_d(r).start()
+
+    gather_y(0).start()
     for k in range(chunks):
-        gather_y(k).start()
+        if k > 0:
+            gather_y(k).start()
         gather_c(k).start()
+    def half_rows(yb, xb):
+        return pl.ds(pl.multiple_of(BLK * (2 * yb + xb), BLK), BLK)
+
+    def half_away(i):
+        src = wide_ref.at[i % 4, half_rows(i // 4, 1 - x)]
+        return remote(src, halved_in.at[i // 4, i % 4], half_send.at[i], half_recv.at[i], near_x)
+
+    def half_here(i):
+        src = wide_ref.at[i % 4, half_rows(i // 4, x)]
+        return pltpu.make_async_copy(src, halved_own.at[i // 4, i % 4], half_local.at[i])
+
+    if back:
+        for i in range(8):
+            half_away(i).start()
+            half_here(i).start()
+    else:
+        for r in (1, 2, 3):
+            spread_x(r).start()
+            spread_y(r).start()
+        for r in range(4):
+            spread_keep(r).start()
     for k in range(4):
         pl.when(stays(k))(lambda k=k: ride_local(k).start())
         pl.when(jnp.logical_not(stays(k)))(lambda k=k: ride_remote(k).start())
@@ -977,11 +1031,21 @@
         core_out[k] = partial[2 * frames :].astype(BF16)
         scatter_c(k).start()
         pl.when(k > 0)(lambda: finish(k - 1))
+        if not back:
+            for r in (1, 2, 3):
+                pl.when(k == r)(lambda r=r: spread_on(r))
         return carry
 
     pass_on(0)
     lax.fori_loop(0, chunks, one_chunk, 0)
     finish(chunks - 1)
+    if back:
+        for i in range(8):
+            half_away(i).wait_recv()
+            half_here(i).wait()
+            at = (i // 4, i % 4)
+            halved_ref[at] = (halved_own[at].astype(F32) + halved_in[at].astype(F32)).astype(BF16)
+            half_away(i).wait_send()
     for k in range(chunks):
         scatter_y(k).wait_recv()
         delta_ref[:, patches(k)] = delta_ref[:, patches(k)] + near_in[k].astype(F32)
@@ -989,6 +1053,14 @@
         for copy in (gather_y(k), gather_c(k), gather_d(k), scatter_c(k), scatter_y(k)):
             copy.wait_send()
         save(k).wait()
+    if not back:
+        for r in (1, 2, 3):
+            spread_x(r, 1).wait_recv()
+            spread_d(r, 1).wait_recv()
+            for copy in (spread_x(r), spread_y(r), spread_d(r)):
+                copy.wait_send()
+        for r in range(4):
+            spread_keep(r).wait()
     for k in range(4):
         pl.when(stays(k))(lambda k=k: ride_local(k).wait())
         pl.when(jnp.logical_not(stays(k)))(lambda k=k: ride_remote(k).wait_send())
@@ -1018,10 +1090,17 @@
         jax.ShapeDtypeStruct((frames, patches, features), F32),
         jax.ShapeDtypeStruct(rider_shape, BF16),
     ]
+    held = 2
+    halves = (2, 4, BLK, saved[2].shape[2]) if back else None
+    if back:
+        out_shape.insert(-1, jax.ShapeDtypeStruct(halves, BF16))
+    else:
+        out_shape.append(jax.ShapeDtypeStruct((4, 4 * saved[0].shape[1], features), BF16))
+        held = 3
     return pl.pallas_call(
         functools.partial(time_kernel, back, scale, heads),
-        in_specs=[whole, anywhere] + [whole] * (len(saved) + 3),
-        out_specs=[anywhere] + [whole] * (len(out_shape) - 2) + [anywhere],
+        in_specs=[whole, anywhere] + ([whole, whole, anywhere] if back else [anywhere] * 2) + [whole] * 3,
+        out_specs=[anywhere] + [whole] * (len(out_shape) - held) + [anywhere] * (held - 1),
         out_shape=out_shape,
         scratch_shapes=[
             pltpu.VMEM((4 * frames, patches, features), BF16),
@@ -1034,13 +1113,191 @@
             pltpu.VMEM((chunks, frames, CHUNK, features), BF16),
         ]
         + [dma((chunks,))] * 10
-        + [dma((4,)), dma((4,)), dma((1,)), dma((chunks,))],
+        + [dma((4,)), dma((4,)), dma((1,)), dma((chunks,))]
+        + [dma((4,))] * 7
+        + ([pltpu.VMEM(halves, BF16), pltpu.VMEM(halves, BF16), dma((8,)), dma((8,)), dma((8,))] if back else []),
         compiler_params=pltpu.CompilerParams(
             collective_id=2 if back else 1, has_side_effects=True, vmem_limit_bytes=48 * 1024 * 1024
         ),
         cost_estimate=pl.CostEstimate(flops=10**10, transcendentals=10**6, bytes_accessed=10**8),
         name="time_back" if back else "time_forward",
     )(own, rider, *saved, wq, wo, bias)
+
+
+def feed_kernel(
+    resid, delta, upstream, masked, gain, w_in_hbm, w_out_hbm,
+    g_in_hbm, g_out_hbm, grad_out, low_out, rows_out, gain_out,
+    w_in, w_out, standard, inverse, normed, grads, normed_t, grads_t, hidden, pulled, g_in, g_out, back, ahead,
+    back_out, back_in, ahead_out, ahead_in,
+    w_sem, g_sem, n_send, n_recv, b_send, b_recv,
+):
+    y, x, c, z = (lax.axis_index(name) for name in AXES)
+    pair = (y, x, 1 - c, z)
+    own = resid.shape[0]
+    step = own // 2
+    slab = 128
+
+    def fetch(s):
+        return (
+            pltpu.make_async_copy(w_in_hbm.at[s], w_in.at[s], w_sem.at[0, s]),
+            pltpu.make_async_copy(w_out_hbm.at[s], w_out.at[s], w_sem.at[1, s]),
+        )
+
+    for s in range(4):
+        for copy in fetch(s):
+            copy.start()
+    barrier = pltpu.get_barrier_semaphore()
+    pl.semaphore_signal(barrier, inc=1, device_id=pair, device_id_type=MESH)
+
+    def remote(src, dst, send, recv):
+        return pltpu.make_async_remote_copy(
+            src_ref=src, dst_ref=dst, send_sem=send, recv_sem=recv, device_id=pair, device_id_type=MESH
+        )
+
+    def at(i, size):
+        return pl.ds(pl.multiple_of(i * size, size), size)
+
+    def prepare(i, carry):
+        rows = at(i, step)
+        grads[rows] = jnp.where(masked[rows] > 0.0, upstream[rows].astype(F32), 0.0).astype(BF16)
+        std, inv = norm_rows(resid[rows] + delta[rows])
+        standard[rows] = std
+        inverse[rows] = inv
+        normed[rows] = (std * gain[...]).astype(BF16)
+        return carry
+
+    lax.fori_loop(0, 2, prepare, 0)
+    pl.semaphore_wait(barrier, 1)
+    mine, theirs = pl.ds(0, own), pl.ds(own, own)
+    give_grads = remote(grads.at[mine], grads.at[theirs], n_send.at[0], n_recv.at[0])
+    give_normed = remote(normed.at[mine], normed.at[theirs], n_send.at[1], n_recv.at[1])
+    give_normed.start()
+    give_grads.start()
+
+    def turn(i, carry):
+        rows = at(i, slab)
+        normed_t[:, rows] = normed[rows].T
+        grads_t[:, rows] = grads[rows].T
+        return carry
+
+    lax.fori_loop(0, own // slab, turn, 0)
+    back[...] = jnp.zeros_like(back)
+    ahead[...] = jnp.zeros_like(ahead)
+    rate = math.sqrt(2.0 / math.pi)
+
+    def rows_step(s, rows):
+        inner = dot_nn(normed[rows], w_in[s])
+        square = inner * inner
+        bend = jnp.tanh(rate * inner * (1.0 + 0.044715 * square))
+        hidden[rows] = (0.5 * inner * (1.0 + bend)).astype(BF16)
+        slope = 0.5 * (1.0 + bend) + 0.5 * inner * (1.0 - bend * bend) * (rate * (1.0 + 3.0 * 0.044715 * square))
+        pulled[rows] = (dot_nt(grads[rows], w_out[s]) * slope).astype(BF16)
+        ahead[rows] = ahead[rows] + dot_nn(hidden[rows], w_out[s])
+        back[rows] = back[rows] + dot_nt(pulled[rows], w_in[s])
+
+    def keep(s):
+        return (
+            pltpu.make_async_copy(g_in.at[s], g_in_hbm.at[s], g_sem.at[0, s]),
+            pltpu.make_async_copy(g_out.at[s], g_out_hbm.at[s], g_sem.at[1, s]),
+        )
+
+    def meet():
+        give_normed.wait_recv()
+        give_grads.wait_recv()
+        lax.fori_loop(own // slab, 2 * own // slab, turn, 0)
+
+    def one_piece(s, carry):
+        for copy in fetch(s):
+            copy.wait()
+
+        def one_half(t, carry):
+            pl.when(jnp.logical_and(s == 0, t == 1))(meet)
+            rows_step(s, at(t, own))
+            return carry
+
+        lax.fori_loop(0, 2, one_half, 0)
+        g_out[s] = dot_nn(grads_t[...], hidden[...]).astype(BF16)
+        g_in[s] = dot_nn(normed_t[...], pulled[...]).astype(BF16)
+        for copy in keep(s):
+            copy.start()
+        return carry
+
+    lax.fori_loop(0, 4, one_piece, 0)
+    back_out[...] = back[theirs].astype(BF16)
+    give_back = remote(back_out, back_in, b_send.at[0], b_recv.at[0])
+    give_back.start()
+    ahead_out[...] = ahead[theirs].astype(BF16)
+    give_ahead = remote(ahead_out, ahead_in, b_send.at[1], b_recv.at[1])
+    give_ahead.start()
+    give_back.wait_recv()
+
+    def finish(i, total):
+        rows = at(i, step)
+        grad = back[rows] + back_in[rows].astype(F32)
+        std = standard[rows]
+        inner = grad * gain[...]
+        mean = jnp.mean(inner, axis=-1, keepdims=True)
+        along = jnp.mean(inner * std, axis=-1, keepdims=True)
+        full = grads[rows].astype(F32) + (inner - mean - std * along) * inverse[rows]
+        grad_out[rows] = full
+        low_out[rows] = full.astype(BF16)
+        return total + jnp.sum(grad * std, axis=0, keepdims=True)
+
+    gain_out[...] = lax.fori_loop(0, 2, finish, jnp.zeros((1, resid.shape[1]), F32))
+    give_ahead.wait_recv()
+
+    def emit(i, carry):
+        rows = at(i, step)
+        rows_out[rows] = (resid[rows] + delta[rows] + ahead[rows] + ahead_in[rows].astype(F32)).astype(BF16)
+        return carry
+
+    lax.fori_loop(0, 2, emit, 0)
+    for copy in (give_normed, give_grads, give_back, give_ahead):
+        copy.wait_send()
+    for s in range(4):
+        for copy in keep(s):
+            copy.wait()
+
+
+def feed(resid, delta, upstream, masked, gain, w_in, w_out):
+    own, features = resid.shape
+    units = w_in.shape[2]
+    dma = pltpu.SemaphoreType.DMA
+    anywhere = pl.BlockSpec(memory_space=pl.ANY)
+    whole = pl.BlockSpec(memory_space=pltpu.VMEM)
+
+    def low(*shape):
+        return pltpu.VMEM(shape, BF16)
+
+    def high(*shape):
+        return pltpu.VMEM(shape, F32)
+
+    return pl.pallas_call(
+        feed_kernel,
+        in_specs=[whole] * 5 + [anywhere] * 2,
+        out_specs=[anywhere] * 2 + [whole] * 4,
+        out_shape=[
+            jax.ShapeDtypeStruct((4, features, units), BF16),
+            jax.ShapeDtypeStruct((4, features, units), BF16),
+            jax.ShapeDtypeStruct((own, features), F32),
+            jax.ShapeDtypeStruct((own, features), BF16),
+            jax.ShapeDtypeStruct((own, features), BF16),
+            jax.ShapeDtypeStruct((1, features), F32),
+        ],
+        scratch_shapes=[
+            low(4, features, units), low(4, units, features), high(own, features), high(own, 1),
+            low(2 * own, features), low(2 * own, features), low(features, 2 * own), low(features, 2 * own),
+            low(2 * own, units), low(2 * own, units), low(4, features, units), low(4, features, units),
+            high(2 * own, features), high(2 * own, features),
+            low(own, features), low(own, features), low(own, features), low(own, features),
+            dma((2, 4)), dma((2, 4)), dma((2,)), dma((2,)), dma((2,)), dma((2,)),
+        ],
+        compiler_params=pltpu.CompilerParams(
+            collective_id=4, has_side_effects=True, vmem_limit_bytes=60 * 1024 * 1024
+        ),
+        cost_estimate=pl.CostEstimate(flops=26 * 10**9, transcendentals=2 * 10**6, bytes_accessed=10**8),
+        name="feed",
+    )(resid, delta, upstream, masked, gain, w_in, w_out)
 
 
 def settle_kernel(
@@ -1395,12 +1652,11 @@
     gain = [vectors[1 + i : 2 + i].astype(F32) for i in range(3)]
 
     ff_in = lax.dynamic_slice(w_in, (plane * BLK, c * hidden_own), (BLK, hidden_own))
-    ff_out = lax.dynamic_slice(w_out, (c * hidden_own, plane * BLK), (hidden_own, BLK)).T
-    arrived, ff_in, ff_out = tie(arrived, ff_in, ff_out)
-
-    def gather_ff(w):
-        w = lax.all_gather(w, ("mp", "tm", "x")).reshape(4, width, hidden_own)
-        return [w[s] for s in range(4)]
+    arrived, ff_in, w_out = tie(arrived, ff_in, w_out)
+    out_size = hidden_own // 4
+    out_slice = lax.dynamic_slice_in_dim(w_out, c * hidden_own + plane * out_size, out_size, 0)
+    out_far = [hop_z(out_slice, -r) for r in (1, 2, 3)]
+    wf_in = lax.all_gather(ff_in, ("mp", "tm", "x")).reshape(4, width, hidden_own)
 
     def pair_gather(v):
         return rows_of([v, hop_c(v)])
@@ -1413,16 +1669,16 @@
     resid0 = jnp.where(masked, embed_row, source)
     std0, inv0 = norm_rows(resid0)
     normed0 = pair_gather((std0 * gain[0]).astype(BF16))
-    wf_in, wf_out = gather_ff(ff_in), gather_ff(ff_out)
     joined0 = dot_nn(normed0, ws_qkv).astype(BF16)
     mixed0, total0 = space_attend(joined0, frames_pair, patches, heads_s, scale)
+    mixed0, out_far = tie(mixed0, out_far)
     resid1 = resid0 + pair_scatter(dot_nt(mixed0, ws_out))
     std1, inv1 = norm_rows(resid1)
-    normed1, joined1, mixed1, total1, delta, upstream = time_call(
+    normed1, joined1, mixed1, total1, delta, upstream, wf_out = time_call(
         False,
         (std1 * gain[1]).astype(BF16).reshape(frames_own, patches, width),
         cotangent.reshape(4, own, BLK),
-        [],
+        [jnp.stack(out_far), w_out],
         wt_qkv,
         wt_out,
         bias,
@@ -1430,21 +1686,11 @@
     )
     normed1 = normed1.reshape(4 * own, width)
     mixed1 = mixed1.reshape(4 * own, -1)
-    grad3 = jnp.where(masked, upstream, jnp.zeros((), BF16))
-    gb3 = pair_gather(grad3)
-    resid2 = resid1 + delta.reshape(own, width)
-    std2, inv2 = norm_rows(resid2)
-    normed2 = pair_gather((std2 * gain[2]).astype(BF16))
-    hidden, pulls = [], []
-    for w in wf_in:
-        activated, pull = jax.vjp(gelu_tanh, dot_nn(normed2, w))
-        hidden.append(activated.astype(BF16))
-        pulls.append(pull)
-    block_part = sum(dot_nt(h, w) for h, w in zip(hidden, wf_out))
-    block_rows = (resid2 + pair_scatter(block_part)).astype(BF16)
-
-    def line_scatter(lhs, parts):
-        parts = jnp.stack([dot_tn(lhs, rhs).astype(BF16) for rhs in parts])
+    g_w_in, g_w_out, grad2, grad2_low, block_rows, gain_grad2 = feed(
+        resid1, delta.reshape(own, width), upstream, masked.astype(F32), gain[2], wf_in, wf_out
+    )
+
+    def line_scatter(parts):
         return lax.psum_scatter(parts, "mp", scatter_dimension=0)
 
     def plane_scatter(v):
@@ -1479,17 +1725,12 @@
     def by_core(kept, landed):
         return jnp.where(c == 0, jnp.concatenate([kept, landed], -1), jnp.concatenate([landed, kept], -1))
 
-    w_out_part = line_scatter(gb3, hidden)
-    grad_inner = [pull(dot_nn(gb3, w))[0].astype(BF16) for pull, w in zip(pulls, wf_out)]
-    part2 = pair_scatter(sum(dot_nt(g, w) for g, w in zip(grad_inner, wf_in)))
-    w_in_part = line_scatter(normed2, grad_inner)
-    back2, gain_grad2 = norm_rows_back(part2, std2, inv2, gain[2])
-    grad2 = grad3.astype(F32) + back2
-    gb2, djoined1, part1, block_out = time_call(
+    w_in_part = line_scatter(g_w_in)
+    gb2, djoined1, part1, w_out_part, block_out = time_call(
         True,
-        grad2.astype(BF16).reshape(frames_own, patches, width),
+        grad2_low.reshape(frames_own, patches, width),
         block_rows,
-        [joined1, total1],
+        [joined1, total1, g_w_out],
         wt_qkv,
         wt_out,
         bias,
@@ -1501,16 +1742,17 @@
     part1 = part1.reshape(own, width)
     back1, gain_grad1 = norm_rows_back(part1, std1, inv1, gain[1])
     grad1 = grad2 + back1
+    w_out_part, w_in_part = tie(w_out_part, w_in_part)
     gb1 = pair_gather(grad1.astype(BF16))
-    gb1, w_out_part = tie(gb1, w_out_part)
-    g_w_out = plane_scatter(w_out_part)
+    w_out_part = lax.psum_scatter(w_out_part, "tm", scatter_dimension=0)
+    g_w_out = lax.psum_scatter(w_out_part, "mp", scatter_dimension=0).astype(F32)
     t_out_x = send_x(gb2, mixed1)
     t_qkv_x = send_x(normed1, djoined1)
     dmixed0 = dot_nn(gb1, ws_out).astype(BF16)
+    g_w_in = plane_scatter(w_in_part)
     go = dot_tn(gb1, mixed0).astype(BF16)
     djoined0 = space_attend_back(joined0, dmixed0, total0, frames_pair, patches, heads_s, scale)
-    djoined0, t_out_x, t_qkv_x, w_in_part, go = tie(djoined0, t_out_x, t_qkv_x, w_in_part, go)
-    g_w_in = plane_scatter(w_in_part)
+    djoined0, t_out_x, t_qkv_x, go = tie(djoined0, t_out_x, t_qkv_x, go)
     g_t_out = keep_x(gb2, mixed1, t_out_x)
     g_t_qkv = keep_x(normed1, djoined1, t_qkv_x)
     z_at = [(z + r) % 4 for r in range(4)]
@@ -1524,7 +1766,7 @@
             for s in z_at
         ]
     )
-    small = rows_of([jnp.zeros((1, width), F32), gain_grad1[None], gain_grad2[None], jnp.zeros((5, width), F32)])
+    small = rows_of([jnp.zeros((1, width), F32), gain_grad1[None], gain_grad2, jnp.zeros((5, width), F32)])
     kept, landed, grad_tokens, small = settle(
         djoined0, go, normed0.T, ws_qkv, std0, grad1, inv0, masked.astype(F32), gain[0], small
     )

time: 568 us -> 556 us (0.979)
  Pallas kernels: 294 us -> 365 us
  matrix products: 96.8 us -> 26.8 us
  other arithmetic: 44.6 us -> 31.1 us
  starting transfers between devices: 14 us -> 23.4 us
  local copies, waits for them, and re-layouts: 60.2 us -> 53.4 us
    pallas_call x0 -> x1, Pallas kernels: none -> 42.6 us  [feed(): pl.pallas_call(feed_kernel, in_specs=[whole] * 5 + [anywhere] * 2, out_sp...]
    reduce_scatter x2 -> x1, waiting for transfers between devices: 0.02 us -> 29.7 us  [line_scatter(): return lax.psum_scatter(parts, 'mp', scatter_dimension=0)]
    all_gather x2 -> x1, waiting for transfers between devices: 29.2 us -> 0.01 us  [token_parallel(): lax.all_gather(ff_in, ('mp', 'tm', 'x')).reshape(4, width, hidden_own)]
    dot_general x10 -> x2, matrix products: 39.5 us -> 10.8 us  [dot_nn(): lax.dot_general(a, b, (((1,), (0,)), ((), ())), preferred_element_type=F32)]
    dot_general x13 -> x5, matrix products: 39.8 us -> 11.4 us  [dot_tn(): lax.dot_general(a, b, (((0,), (0,)), ((), ())), preferred_element_type=F32)]
    pallas_call x1, Pallas kernels: 69.8 us -> 86.2 us  [settle(): pl.pallas_call(settle_kernel, in_specs=[whole] * 3 + [anywhere] * 3 + [wh...]
    ppermute x3 -> x6, starting transfers between devices: 3.97 us -> 17 us  [hop_z(): lax.ppermute(v, AXES, device_pairs(lambda y, x, c, z: (y, x, c, (z + shif...]
    dot_general x9 -> x1, matrix products: 17.5 us -> 4.55 us  [dot_nt(): lax.dot_general(a, b, (((1,), (1,)), ((), ())), preferred_element_type=F32)]
  transfers between devices with their start and end apart: 22 -> 20, of which waited for: 5 -> 3; matrix products, arithmetic and copies ran while one was open for 31% -> 16% of each run, Pallas kernels for 41% -> 48%
where the time goes in v5:
time: 556 us; the launch traced here: 549 us
  Pallas kernels  365 us (66%)
  local copies, waits for them, and re-layouts  53.4 us (10%)
  waiting for transfers between devices  34.4 us (6%)
  other arithmetic  31.1 us (6%)
  matrix products  26.8 us (5%)
  starting transfers between devices  23.4 us (4%)
  between operations  15.1 us (3%)
    pallas_call x2, Pallas kernels, time_call(): pl.pallas_call(functools.partial(time_kernel, back, scale, heads), in_spe...  141 us
    pallas_call x1, Pallas kernels, settle(): pl.pallas_call(settle_kernel, in_specs=[whole] * 3 + [anywhere] * 3 + [wh...  86.2 us
    pallas_call x1, Pallas kernels, arrive(): pl.pallas_call(arrive_kernel, in_specs=[anywhere] * 4, out_specs=[anywher...  61.2 us
    pallas_call x1, Pallas kernels, feed(): pl.pallas_call(feed_kernel, in_specs=[whole] * 5 + [anywhere] * 2, out_sp...  42.6 us
    reduce_scatter x1, waiting for transfers between devices, line_scatter(): return lax.psum_scatter(parts, 'mp', scatter_dimension=0)  29.7 us
    pallas_call x1, Pallas kernels, space_attend_back(): pl.pallas_call(functools.partial(space_attend_back_kernel, scale), grid=(...  17.8 us
    ppermute x6, starting transfers between devices, hop_z(): lax.ppermute(v, AXES, device_pairs(lambda y, x, c, z: (y, x, c, (z + shif...  17 us
    unnamed x72, local copies, waits for them, and re-layouts  16.6 us
  transfers between devices with their start and end apart: 20, of which 3 were waited for; matrix products, arithmetic and copies ran while one was open for 16% of the time, Pallas kernels for 48%

profile of v5, /device:TPU:9, one launch (start us, length us, event | category | flops | bytes accessed | tf_op | source)
XLA Modules:
  0.0 549.4 jit_solution(12699694910748574914)
XLA Ops:
  10.9 1.4 constant_dynamic-slice_fusion.7
  14.7 1.1 pad_maximum_fusion.17.mine
  16.5 1.7 dynamic_slice.90
  18.1 61.2 %arrive.1 = (bf16[512,1024]{1,0:T(8,128)(2,1)}, bf16[8,1024]{1,0:T(8,128)(2,1)}, bf16[1024,1536]{1,0:T(8,128)(2,1)}, bf16[1024,512]{1,0:T(8,128)(2,1)}, bf16[1024,1024]{1,0:T(8,128)(2,1)}) custom-call(bf16[4,512,256]{2,1,0:T(8,128)(2,1)} %bitcast.97, bf16[8,256]{1,0:T(8,128)(2,1)} %maximum_maximum_fusion.1.vec, bf16[1024,512]{1,0:T(8,128)(2,1)} %pad_maximum_fusion.17.mine, ...), custom_call_target="tpu_custom_call" | custom-call | tf_op jit(solution)/shard_map/arrive/pallas_call | solution.py:678
  79.6 1.5 slice_convert_fusion.1
  81.2 1.6 fusion.11
  83.3 2.4 fusion.12
  87.2 1.3 collective-permute-start.4
  88.5 13.7 %collective-permute-start.3 = (bf16[128,1024]{1,0:T(8,128)(2,1)S(1)}, bf16[128,1024]{1,0:T(8,128)(2,1)}, u32[]{:S(2)}, u32[]{:S(2)}) collective-permute-start(bf16[128,1024]{1,0:T(8,128)(2,1)S(1)} %constant_dynamic-slice_fusion.5), channel_id=1, source_target_pairs={{0,2},{1,3},{2,0},{3,1},{4,6},{5,7},{6,4},{7,5},{8,10},{9,11},{10,... | collective-permute-start | bytes 786440 | tf_op jit(solution)/shard_map/ppermute | solution.py:438
  102.7 2.9 copy.72
  105.6 7.4 %convolution_convert_fusion.qkv_ref = bf16[1024,1536]{1,0:T(8,128)(2,1)} fusion(bf16[1024,1536]{1,0:T(8,128)(2,1)} %get-tuple-element.53.weight_hbm, bf16[512,1024]{1,0:T(8,128)(2,1)} %collective-permute-done.1, bf16[512,1024]{1,0:T(8,128)(2,1)S(1)} %get-tuple-element.149), kind=kOutput, calls=%fused_computation | convolution fusion | flops 3226992640 | bytes 8388608 | tf_op jit(solution)/shard_map/dot_general | solution.py:701
  113.1 16.3 %space_attend.1 = (bf16[1024,512]{1,0:T(8,128)(2,1)}, f32[8,8,128]{2,1,0:T(8,128)}) custom-call(bf16[1024,1536]{1,0:T(8,128)(2,1)} %convolution_convert_fusion.qkv_ref), custom_call_target="tpu_custom_call" | custom-call | flops 1073741824 | bytes 4194304 | tf_op jit(solution)/shard_map/space_attend/pallas_call | solution.py:778
  129.4 4.6 fusion.47
  133.9 2.7 slice.168
  137.5 1.4 slice_bitcast_fusion
  138.9 1.6 copy.73
  140.6 1.6 copy.75.refs_4_.refs_5_
  143.8 1.2 pad_maximum_fusion.18.refs_2_
  145.0 2.7 fusion.41
  149.7 82.3 %time_forward.1 = (bf16[16,128,1024]{2,1,0:T(8,128)(2,1)}, bf16[16,128,768]{2,1,0:T(8,128)(2,1)}, bf16[16,128,256]{2,1,0:T(8,128)(2,1)S(1)}, f32[16,4,128]{2,1,0...) custom-call(bf16[4,128,1024]{2,1,0:T(8,128)(2,1)S(1)} %bitcast.81, ...), custom_call_target="tpu_custom_call" | custom-call | flops 10000000000 | bytes 100000000 | tf_op jit(solution)/shard_map/time_forward/pallas_call | solution.py:1100
  234.0 42.6 %feed.1 = (bf16[4,1024,512]{2,1,0:T(8,128)(2,1)}, bf16[4,1024,512]{2,1,0:T(8,128)(2,1)}, f32[512,1024]{1,0:T(8,128)}, bf16[512,1024]{1,0:T(8,128)(2,1)}, bf16[512,1024]{1,0:T(8,128)(2,1)}, /*index=5*/f32[1,1024]{1,0:T(1,128)}) custom-call(f32[512,1024]{1,0:T(8,128)} %copy-done.9, f32[512,1024]{1,0:T(8,128)} %bitcast.123, bf16[512,1024]{1,0:T(8,128)(2,1)} %copy-done.8, ...), custom_call_target="tpu_custom_call" | custom-call | flops 25999998976 | bytes 100000000 | tf_op jit(solution)/shard_map/feed/pallas_call | solution.py:1275
  277.8 2.7 fusion.20
  280.5 4.1 copy.80.lhs
  284.7 1.2 copy-done.6
  285.9 1.2 copy-done.7
  287.1 58.8 %time_back.1 = (bf16[16,128,1024]{2,1,0:T(8,128)(2,1)}, bf16[16,128,768]{2,1,0:T(8,128)(2,1)}, f32[4,128,1024]{2,1,0:T(8,128)}, bf16[2,4,256,512]{3,2,1,0:T(8,128)(2,1)}, bf16[4,512,256]{2,1,0:T(8,128)(2,1)S(1)}) custom-call(bf16[4,128,1024]{2,1,0:T(8,128)(2,1)S(1)} %bitcast.86, bf16[512,1024]{1,0:T(8,128)(2,1)S(1)} %copy-done.7, ...), custom_call_target="tpu_custom_call" | custom-call | flops 10000000000 | bytes 100000000 | tf_op jit(solution)/shard_map/time_back/pallas_call | solution.py:1100
  345.9 29.7 %reduce-scatter.5.cloned.1.call-done = bf16[1,1024,512]{2,1,0:T(8,128)(2,1)} async-done(((bf16[4,1024,512]{2,1,0:T(8,128)(2,1)}), bf16[1,1024,512]{2,1,0:T(8,128)(2,1)}) %reduce-scatter.5.cloned.1.call-update) | async-done | bytes 1048592 | tf_op jit(solution)/shard_map/reduce_scatter | solution.py:1694
  375.7 2.6 fusion.43
  378.8 1.2 copy-done.10
  381.6 2.0 fusion.40
  386.8 1.1 copy-done.30
  387.8 3.1 fusion.4
  391.7 2.9 fusion.17
  395.6 1.2 collective-permute-start.7
  397.1 3.9 convolution_convert_fusion.1.go
  400.9 3.4 convolution_convert_fusion.2.grad_ref
  404.4 17.8 %space_attend_back.1.dj = bf16[1024,1536]{1,0:T(8,128)(2,1)} custom-call(bf16[1024,1536]{1,0:T(8,128)(2,1)} %convolution_convert_fusion.qkv_ref, bf16[1024,512]{1,0:T(8,128)(2,1)} %convolution_convert_fusion.2.grad_ref, f32[8,8,128]{2,1,0:T(8,128)} %get-tuple-element.74.total_ref), custom_call_target="tpu_custom_call" | custom-call | flops 2684354560 | bytes 10485760 | tf_op jit(solution)/shard_map/space_attend_back/pallas_call | solution.py:797
  422.3 1.8 convert_add_fusion
  426.5 1.4 collective-permute-start.11
  428.8 86.2 %settle.1 = (f32[128,512]{1,0:T(8,128)}, f32[128,512]{1,0:T(8,128)}, bf16[4,512,256]{2,1,0:T(8,128)(2,1)}, f32[8,256]{1,0:T(8,128)}) custom-call(bf16[1024,1536]{1,0:T(8,128)(2,1)} %space_attend_back.1.dj, bf16[1024,512]{1,0:T(8,128)(2,1)} %convolution_convert_fusion.1.go, bf16[1024,1024]{1,0:T(8,128)(2,1)} %copy.80.lhs, ...), custom_call_target="tpu_custom_call" | custom-call | flops 10000000000 | bytes 100000000 | tf_op jit(solution)/shard_map/settle/pallas_call | solution.py:1536
  515.0 1.5 slice.126
  517.4 1.5 slice.127
  521.5 1.3 maximum_select_fusion.2
  523.2 1.5 fusion.26
  524.7 1.3 collective-permute-start.12
  526.0 3.7 collective-permute-done.12
  533.6 1.5 convert.60
  536.6 1.1 maximum_convert_fusion
  (184 shorter events, 41.6 us)
Async XLA Ops:
  7.2 5.7 %copy-start = (bf16[1024,3,256]{2,0,1:T(8,128)(2,1)S(1)}, bf16[1024,3,256]{2,0,1:T(8,128)(2,1)}, u32[]{:S(2)}) copy-start(bf16[1024,3,256]{2,0,1:T(8,128)(2,1)} %param.20) | copy-start | bytes 4718596
  7.2 226.8 %all-gather.3.cloned.1.call-start = ((), (), s32[]{:S(2)}) async-start(), calls=%async_computation.8 | async-start | bytes 4456448 | tf_op jit(solution)/shard_map/all_gather | solution.py:1659
  13.0 1.7 copy-start.18
  13.6 2.1 copy-start.25
  15.8 63.6 %copy-start.22 = (s32[2,8,128]{2,1,0:T(8,128)S(1)}, s32[2,8,128]{2,1,0:T(8,128)}, u32[]{:S(2)}) copy-start(s32[2,8,128]{2,1,0:T(8,128)} %param.16) | copy-start | bytes 24580
  15.8 63.6 %copy-start.27 = (s32[2]{0:T(128)S(1)}, s32[2]{0:T(128)}, u32[]{:S(2)}) copy-start(s32[2]{0:T(128)} %param.15) | copy-start | bytes 28
  15.8 63.7 %copy-start.26 = (s32[2,16]{1,0:T(2,128)S(1)}, s32[2,16]{1,0:T(2,128)}, u32[]{:S(2)}) copy-start(s32[2,16]{1,0:T(2,128)} %param.17) | copy-start | bytes 388
  79.3 3.5 copy-start.12
  79.4 296.2 %reduce-scatter.5.cloned.1.call-start = ((), (), s32[]{:S(2)}) async-start(), calls=%async_computation.4 | async-start | bytes 5242880 | tf_op jit(solution)/shard_map/reduce_scatter | solution.py:1694
  79.5 1.6 collective-permute-start
  81.1 4.6 copy-start.21
  85.7 19.9 %copy-start.14 = (bf16[512,1024]{1,0:T(8,128)(2,1)}, bf16[512,1024]{1,0:T(8,128)(2,1)S(1)}, u32[]{:S(2)}) copy-start(bf16[512,1024]{1,0:T(8,128)(2,1)S(1)} %get-tuple-element.149) | copy-start | bytes 3145732
  85.7 19.9 %collective-permute-start.1 = (bf16[512,1024]{1,0:T(8,128)(2,1)S(1)}, bf16[512,1024]{1,0:T(8,128)(2,1)}, u32[]{:S(2)}, u32[]{:S(2)}) collective-permute-start(bf16[512,1024]{1,0:T(8,128)(2,1)S(1)} %get-tuple-element.149), channel_id=1, source_target_pairs={{0,4},{1,5},{2,6},{3,7},{4,0},{5,1},{6,2},{7,3},{8,12},{9,13},{10,... | collective-permute-start | bytes 3145736 | tf_op jit(solution)/shard_map/ppermute | solution.py:434
  87.2 42.2 %collective-permute-start.4 = (bf16[128,1024]{1,0:T(8,128)(2,1)S(1)}, bf16[128,1024]{1,0:T(8,128)(2,1)}, u32[]{:S(2)}, u32[]{:S(2)}) collective-permute-start(bf16[128,1024]{1,0:T(8,128)(2,1)S(1)} %constant_dynamic-slice_fusion.5), channel_id=1, source_target_pairs={{0,1},{1,2},{2,3},{3,0},{4,5},{5,6},{6,7},{7,4},{8,9},{9,10},{10,1... | collective-permute-start | bytes 786440 | tf_op jit(solution)/shard_map/ppermute | solution.py:438
  88.5 40.8 %collective-permute-start.3 = (bf16[128,1024]{1,0:T(8,128)(2,1)S(1)}, bf16[128,1024]{1,0:T(8,128)(2,1)}, u32[]{:S(2)}, u32[]{:S(2)}) collective-permute-start(bf16[128,1024]{1,0:T(8,128)(2,1)S(1)} %constant_dynamic-slice_fusion.5), channel_id=1, source_target_pairs={{0,2},{1,3},{2,0},{3,1},{4,6},{5,7},{6,4},{7,5},{8,10},{9,11},{10,... | collective-permute-start | bytes 786440 | tf_op jit(solution)/shard_map/ppermute | solution.py:438
  102.2 27.1 %collective-permute-start.2 = (bf16[128,1024]{1,0:T(8,128)(2,1)S(1)}, bf16[128,1024]{1,0:T(8,128)(2,1)}, u32[]{:S(2)}, u32[]{:S(2)}) collective-permute-start(bf16[128,1024]{1,0:T(8,128)(2,1)S(1)} %constant_dynamic-slice_fusion.5), channel_id=1, source_target_pairs={{0,3},{1,0},{2,1},{3,2},{4,7},{5,4},{6,5},{7,6},{8,11},{9,8},{10,9... | collective-permute-start | bytes 786440 | tf_op jit(solution)/shard_map/ppermute | solution.py:438
  113.1 16.3 %copy-start.28 = (bf16[1024,512]{1,0:T(8,128)(2,1)S(1)}, bf16[1024,512]{1,0:T(8,128)(2,1)}, u32[]{:S(2)}) copy-start(bf16[1024,512]{1,0:T(8,128)(2,1)} %get-tuple-element.57) | copy-start | bytes 3145732
  136.6 8.4 %collective-permute-start.5 = (bf16[512,1024]{1,0:T(8,128)(2,1)}, bf16[512,1024]{1,0:T(8,128)(2,1)}, u32[]{:S(2)}, u32[]{:S(2)}) collective-permute-start(bf16[512,1024]{1,0:T(8,128)(2,1)} %slice.168), channel_id=1, source_target_pairs={{0,4},{1,5},{2,6},{3,7},{4,0},{5,1},{6,2},{7,3},{8,12},{9,13},{10,... | collective-permute-start | bytes 3145736 | tf_op jit(solution)/shard_map/ppermute | solution.py:434
  147.7 1.3 copy-start.9
  148.1 1.6 copy-start.3
  276.6 1.2 copy-start.15
  276.6 152.2 %reduce-scatter.9.cloned.1.call-start = ((), (), s32[]{:S(2)}) async-start(), calls=%async_computation.6 | async-start | bytes 3145728 | tf_op jit(solution)/shard_map/reduce_scatter | solution.py:1747
  280.5 4.1 copy-start.2
  284.6 1.2 copy-start.6
  285.9 1.2 copy-start.7
  375.6 161.0 %reduce-scatter.7.cloned.1.call-start = ((), (), s32[]{:S(2)}) async-start(), calls=%async_computation.5 | async-start | bytes 1310720 | tf_op jit(solution)/shard_map/reduce_scatter | solution.py:1697
  375.6 2.9 copy-start.11
  378.3 1.7 copy-start.10
  380.0 1.6 copy-start.16
  381.6 3.2 copy-start.13
  383.6 13.5 %collective-permute-start.6 = (bf16[512,1024]{1,0:T(8,128)(2,1)S(1)}, bf16[512,1024]{1,0:T(8,128)(2,1)}, u32[]{:S(2)}, u32[]{:S(2)}) collective-permute-start(bf16[512,1024]{1,0:T(8,128)(2,1)S(1)} %get-tuple-element.124), channel_id=1, source_target_pairs={{0,4},{1,5},{2,6},{3,7},{4,0},{5,1},{6,2},{7,3},{8,12},{9,13},{10,... | collective-permute-start | bytes 3145736 | tf_op jit(solution)/shard_map/ppermute | solution.py:434
  385.9 1.9 copy-start.30
  391.7 3.2 copy-start.23
  394.6 142.0 %reduce-scatter.11.cloned.1.call-start = ((), (), s32[]{:S(2)}) async-start(), calls=%async_computation.7 | async-start | bytes 1310720 | tf_op jit(solution)/shard_map/reduce_scatter | solution.py:1748
  395.6 5.3 copy-start.29
  395.6 26.6 %collective-permute-start.7 = (bf16[512,256]{1,0:T(8,128)(2,1)S(1)}, bf16[512,256]{1,0:T(8,128)(2,1)S(1)}, u32[]{:S(2)}, u32[]{:S(2)}) collective-permute-start(bf16[512,256]{1,0:T(8,128)(2,1)S(1)} %fusion.21), channel_id=1, source_target_pairs={{0,8},{1,9},{2,10},{3,11},{4,12},{5,13},{6,14},{7,15},{8,0},{9,1},... | collective-permute-start | bytes 786440 | tf_op jit(solution)/shard_map/ppermute | solution.py:430
  396.8 25.4 %collective-permute-start.8 = (bf16[512,768]{1,0:T(8,128)(2,1)}, bf16[512,768]{1,0:T(8,128)(2,1)}, u32[]{:S(2)}, u32[]{:S(2)}) collective-permute-start(bf16[512,768]{1,0:T(8,128)(2,1)} %fusion.17), channel_id=1, source_target_pairs={{0,8},{1,9},{2,10},{3,11},{4,12},{5,13},{6,14},{7,15},{8,0},{9,1},... | collective-permute-start | bytes 2359304 | tf_op jit(solution)/shard_map/ppermute | solution.py:430
  425.6 97.5 %collective-permute-start.10 = (bf16[512,256]{1,0:T(8,128)(2,1)}, bf16[512,256]{1,0:T(8,128)(2,1)}, u32[]{:S(2)}, u32[]{:S(2)}) collective-permute-start(bf16[512,256]{1,0:T(8,128)(2,1)} %pad_maximum_fusion.22), channel_id=1, source_target_pairs={{0,2},{1,3},{2,0},{3,1},{4,6},{5,7},{6,4},{7,5},{8,10},{9,11},{10,... | collective-permute-start | bytes 786440 | tf_op jit(solution)/shard_map/ppermute | solution.py:438
  426.5 96.7 %collective-permute-start.11 = (bf16[512,256]{1,0:T(8,128)(2,1)}, bf16[512,256]{1,0:T(8,128)(2,1)}, u32[]{:S(2)}, u32[]{:S(2)}) collective-permute-start(bf16[512,256]{1,0:T(8,128)(2,1)} %pad_maximum_fusion.23), channel_id=1, source_target_pairs={{0,3},{1,0},{2,1},{3,2},{4,7},{5,4},{6,5},{7,6},{8,11},{9,8},{10,9... | collective-permute-start | bytes 786440 | tf_op jit(solution)/shard_map/ppermute | solution.py:438
  428.7 94.4 %collective-permute-start.9 = (bf16[512,256]{1,0:T(8,128)(2,1)}, bf16[512,256]{1,0:T(8,128)(2,1)}, u32[]{:S(2)}, u32[]{:S(2)}) collective-permute-start(bf16[512,256]{1,0:T(8,128)(2,1)} %pad_maximum_fusion.21), channel_id=1, source_target_pairs={{0,1},{1,2},{2,3},{3,0},{4,5},{5,6},{6,7},{7,4},{8,9},{9,10},{10,1... | collective-permute-start | bytes 786440 | tf_op jit(solution)/shard_map/ppermute | solution.py:438
  523.1 7.6 %copy-start.19 = (f32[128,128]{1,0:T(8,128)S(1)}, f32[128,128]{1,0:T(8,128)}, u32[]{:S(2)}) copy-start(f32[128,128]{1,0:T(8,128)} %slice.126) | copy-start | bytes 196612
  523.1 7.6 %copy-start.20 = (f32[128,128]{1,0:T(8,128)S(1)}, f32[128,128]{1,0:T(8,128)}, u32[]{:S(2)}) copy-start(f32[128,128]{1,0:T(8,128)} %slice.127) | copy-start | bytes 196612
  523.2 7.6 %copy-start.24 = (f32[8,256]{1,0:T(8,128)S(1)}, f32[8,256]{1,0:T(8,128)}, u32[]{:S(2)}) copy-start(f32[8,256]{1,0:T(8,128)} %get-tuple-element.83) | copy-start | bytes 24580
  524.6 9.0 %copy-start.17 = (bf16[4,512,256]{2,1,0:T(8,128)(2,1)S(1)}, bf16[4,512,256]{2,1,0:T(8,128)(2,1)}, u32[]{:S(2)}) copy-start(bf16[4,512,256]{2,1,0:T(8,128)(2,1)} %get-tuple-element.82) | copy-start | bytes 3145732
  524.7 5.0 collective-permute-start.12
  529.8 5.6 %collective-permute-start.13 = (bf16[128,512]{1,0:T(8,128)(2,1)S(1)}, bf16[128,512]{1,0:T(8,128)(2,1)S(1)}, u32[]{:S(2)}, u32[]{:S(2)}) collective-permute-start(bf16[128,512]{1,0:T(8,128)(2,1)S(1)} %fusion.29), channel_id=1, source_target_pairs={{0,4},{1,5},{2,6},{3,7},{4,0},{5,1},{6,2},{7,3},{8,12},{9,13},{10,... | collective-permute-start | bytes 393224 | tf_op jit(solution)/shard_map/ppermute | solution.py:434
  537.8 1.6 collective-permute-start.14
  539.5 3.0 copy-start.1
  (3 other events, 3.2 us)
Sparse Core Ops, SparseCore 0:
  79.5 112.1 all-gather.2
  276.7 98.7 reduce-scatter.4
  377.9 30.8 reduce-scatter.8
  411.5 27.7 reduce-scatter.6
  441.5 43.8 reduce-scatter.10

commit v6 on v5

--- a/solution.py
+++ b/solution.py
@@ -446,257 +446,6 @@
     return device_pairs(move)
 
 
-def arrive_kernel(
-    tok, vec, mine, later, rows_out, vec_out, wq, wo, wt,
-    z_send, z_recv, y_send, y_recv, x_send, x_recv, p_send, p_recv, q_send, q_recv,
-    t_send, t_recv, v_send, v_recv, u_send, u_recv, w_send, w_recv, local,
-):
-    y, x, c, z = (lax.axis_index(name) for name in AXES)
-    half = wo.shape[1] // 4
-    wide = 3 * half
-
-    barrier = pltpu.get_barrier_semaphore()
-    for dc in range(2):
-        for dz in range(4):
-            if dc or dz:
-                peer = (y, x, (c + dc) % 2, (z + dz) % 4)
-                pl.semaphore_signal(barrier, inc=1, device_id=peer, device_id_type=MESH)
-    near_y, near_x = (1 - y, x, c, z), (y, 1 - x, c, z)
-    for peer in (near_y, near_x):
-        pl.semaphore_signal(barrier, inc=1, device_id=peer, device_id_type=MESH)
-    pl.semaphore_wait(barrier, 9)
-
-    def rows(dy, dx):
-        return pl.ds(pl.multiple_of(BLK * (2 * ((y + dy) % 2) + (x + dx) % 2), BLK), BLK)
-
-    def piece(dy, dx, r, split=False):
-        s = (z + r) % 4
-        at = pl.multiple_of(s * wide, half)
-        out = wo.at[rows(dy, dx), pl.ds(pl.multiple_of(s * half, half), half)]
-        if split:
-            late = pl.multiple_of(s * wide + 2 * half, half)
-            return (wq.at[rows(dy, dx), pl.ds(at, 2 * half)], wq.at[rows(dy, dx), pl.ds(late, half)], out)
-        return (wq.at[rows(dy, dx), pl.ds(at, wide)], out)
-
-    def copies(sources, targets, send, recv, peer):
-        return [
-            pltpu.make_async_remote_copy(
-                src_ref=src, dst_ref=dst, send_sem=send.at[i], recv_sem=recv.at[i], device_id=peer, device_id_type=MESH
-            )
-            for i, (src, dst) in enumerate(zip(sources, targets))
-        ]
-
-    own_rows = rows(0, 0)
-    own_slice = (mine.at[own_rows, pl.ds(0, wide)], mine.at[own_rows, pl.ds(wide, half)])
-
-    def z_copies(right, step):
-        if right:
-            r = 0 if step == 0 else 4 - step
-            peer, lands = (y, x, c, (z + 1) % 4), 3 - step
-        else:
-            r = step
-            peer, lands = (y, x, c, (z + 3) % 4), step + 1
-        target = piece(0, 0, r)
-        source = own_slice if step == 0 else target
-        return copies(source, target, z_send.at[int(right), step], z_recv.at[lands], peer)
-
-    def y_copies(r):
-        return copies(piece(0, 0, r), piece(0, 0, r), y_send.at[r], y_recv.at[r], near_y)
-
-    def x_copies(r):
-        return copies(piece(0, 0, r), piece(0, 0, r), x_send.at[r], x_recv.at[r], near_x)
-
-    def corner_x(r):
-        part = piece(1, 0, r, split=True)[:1]
-        return copies(part, part, p_send.at[r], p_recv.at[r], near_x)
-
-    def corner_y(r):
-        part = piece(0, 1, r, split=True)[1:]
-        return copies(part, part, q_send.at[r], q_recv.at[r], near_y)
-
-    span = wt.shape[1] // 4
-
-    def time_piece(dx, r):
-        at = pl.ds(pl.multiple_of(((z + r) % 4) * span, span), span)
-        return wt.at[pl.ds(pl.multiple_of(2 * BLK * ((x + dx) % 2), BLK), 2 * BLK), at]
-
-    def time_z(right, step):
-        if right:
-            r = 0 if step == 0 else 4 - step
-            peer, lands = (y, x, c, (z + 1) % 4), 3 - step
-        else:
-            r = step
-            peer, lands = (y, x, c, (z + 3) % 4), step + 1
-        source = later.at[pl.ds(pl.multiple_of(2 * BLK * x, BLK), 2 * BLK)] if step == 0 else time_piece(0, r)
-        return [
-            pltpu.make_async_remote_copy(
-                src_ref=source, dst_ref=time_piece(0, r), send_sem=u_send.at[int(right), step], recv_sem=u_recv.at[lands],
-                device_id=peer, device_id_type=MESH,
-            )
-        ]
-
-    def time_x(dx, r):
-        return [
-            pltpu.make_async_remote_copy(
-                src_ref=time_piece(dx, r), dst_ref=time_piece(dx, r), send_sem=w_send.at[r], recv_sem=w_recv.at[r],
-                device_id=near_x, device_id_type=MESH,
-            )
-        ]
-
-    def time_forward(j, left):
-        r = 3 - j if left else j + 1
-        pltpu.make_async_remote_copy(
-            src_ref=time_piece(0, r), dst_ref=time_piece(0, r), send_sem=u_send.at[0, 0], recv_sem=u_recv.at[r],
-            device_id=near_x, device_id_type=MESH,
-        ).wait_recv()
-        if j < 2:
-            pl.when(z < 3 if left else z > 0)(lambda: start(time_z(left, j + 1)))
-        start(time_x(0, r))
-
-    def start(all_copies):
-        for copy in all_copies:
-            copy.start()
-
-    def landed(all_copies):
-        for copy in all_copies:
-            copy.wait_recv()
-
-    def sent(all_copies):
-        for copy in all_copies:
-            copy.wait_send()
-
-    def token_copies(k):
-        peer = (y, x, k % 2, 2 * c + k // 2)
-        at = pl.ds(pl.multiple_of(z * BLK, BLK), BLK)
-        return [
-            pltpu.make_async_remote_copy(
-                src_ref=src, dst_ref=dst, send_sem=send.at[k], recv_sem=recv.at[z], device_id=peer, device_id_type=MESH
-            )
-            for src, dst, send, recv in (
-                (tok.at[k], rows_out.at[:, at], t_send, t_recv),
-                (vec, vec_out.at[:, at], v_send, v_recv),
-            )
-        ]
-
-    def token_local(k):
-        at = pl.ds(pl.multiple_of(z * BLK, BLK), BLK)
-        return [
-            pltpu.make_async_copy(tok.at[k], rows_out.at[:, at], local.at[2]),
-            pltpu.make_async_copy(vec, vec_out.at[:, at], local.at[3]),
-        ]
-
-    def stays(k):
-        return jnp.logical_and(2 * c + k // 2 == z, c == k % 2)
-
-    def from_right(j):
-        return z <= 2 - j
-
-    def from_left(j):
-        return z >= j + 1
-
-    pl.when(z < 3)(lambda: start(z_copies(True, 0)))
-    pl.when(z > 0)(lambda: start(z_copies(False, 0)))
-    keep = [
-        pltpu.make_async_copy(mine.at[:, pl.ds(0, wide)], wq.at[:, pl.ds(pl.multiple_of(z * wide, half), wide)], local.at[0]),
-        pltpu.make_async_copy(mine.at[:, pl.ds(wide, half)], wo.at[:, pl.ds(pl.multiple_of(z * half, half), half)], local.at[1]),
-        pltpu.make_async_copy(later, wt.at[:, pl.ds(pl.multiple_of(z * span, span), span)], local.at[4]),
-    ]
-    start(keep)
-
-    def forward(j, left):
-        r = 3 - j if left else j + 1
-        landed(copies(piece(0, 0, r), piece(0, 0, r), z_send.at[0, 0], z_recv.at[r], near_y))
-        if j < 2:
-            pl.when(z < 3 if left else z > 0)(lambda: start(z_copies(left, j + 1)))
-        start(y_copies(r))
-        start(x_copies(r))
-
-    def corners(j, left):
-        r = 3 - j if left else j + 1
-        landed(copies(piece(1, 0, r), piece(1, 0, r), y_send.at[r], y_recv.at[r], near_y))
-        start(corner_x(r))
-        landed(copies(piece(0, 1, r), piece(0, 1, r), x_send.at[r], x_recv.at[r], near_x))
-        start(corner_y(r))
-
-    for j in range(3):
-        for left in (True, False):
-            pl.when(from_left(j) if left else from_right(j))(lambda j=j, left=left: forward(j, left))
-        if j == 0:
-            for k in range(4):
-                pl.when(stays(k))(lambda k=k: start(token_local(k)))
-                pl.when(jnp.logical_not(stays(k)))(lambda k=k: start(token_copies(k)))
-            pl.when(z < 3)(lambda: start(time_z(True, 0)))
-            pl.when(z > 0)(lambda: start(time_z(False, 0)))
-        else:
-            for left in (True, False):
-                pl.when(from_left(j - 1) if left else from_right(j - 1))(lambda j=j, left=left: corners(j - 1, left))
-    for left in (True, False):
-        pl.when(from_left(2) if left else from_right(2))(lambda left=left: corners(2, left))
-    for j in range(3):
-        for left in (True, False):
-            pl.when(from_left(j) if left else from_right(j))(lambda j=j, left=left: time_forward(j, left))
-
-    for copy in keep:
-        copy.wait()
-    for r in (1, 2, 3):
-        part = piece(1, 1, r, split=True)
-        landed(copies(part[:1], part[:1], p_send.at[r], p_recv.at[r], near_x))
-        landed(copies(part[1:], part[1:], q_send.at[r], q_recv.at[r], near_y))
-        for group in (y_copies(r), x_copies(r), corner_x(r), corner_y(r), time_x(0, r)):
-            sent(group)
-        landed(time_x(1, r))
-    for step in range(3):
-        pl.when(jnp.logical_and(z >= step, z < 3))(lambda step=step: sent(z_copies(True, step) + time_z(True, step)))
-        pl.when(jnp.logical_and(z + step <= 3, z > 0))(lambda step=step: sent(z_copies(False, step) + time_z(False, step)))
-    for k in range(4):
-        def finish_local(k=k):
-            for copy in token_local(k):
-                copy.wait()
-
-        pl.when(stays(k))(finish_local)
-        pl.when(jnp.logical_not(stays(k)))(lambda k=k: sent(token_copies(k)))
-    for s in range(4):
-        at = pl.ds(s * BLK, BLK)
-        away = jnp.logical_not(jnp.logical_and(z == s, z // 2 == c))
-
-        def arrived(s=s, at=at):
-            for src, dst, send, recv in (
-                (tok.at[0], rows_out.at[:, at], t_send, t_recv),
-                (vec, vec_out.at[:, at], v_send, v_recv),
-            ):
-                pltpu.make_async_remote_copy(
-                    src_ref=src, dst_ref=dst, send_sem=send.at[0], recv_sem=recv.at[s], device_id=near_y, device_id_type=MESH
-                ).wait_recv()
-
-        pl.when(away)(arrived)
-
-
-def arrive(tok, vec, mine, later):
-    own, width, half = tok.shape[1], 4 * tok.shape[2], mine.shape[1] // 4
-    dma = pltpu.SemaphoreType.DMA
-    anywhere = pl.BlockSpec(memory_space=pl.ANY)
-    return pl.pallas_call(
-        arrive_kernel,
-        in_specs=[anywhere] * 4,
-        out_specs=[anywhere] * 5,
-        out_shape=[
-            jax.ShapeDtypeStruct((own, width), BF16),
-            jax.ShapeDtypeStruct((vec.shape[0], width), BF16),
-            jax.ShapeDtypeStruct((width, 12 * half), BF16),
-            jax.ShapeDtypeStruct((width, 4 * half), BF16),
-            jax.ShapeDtypeStruct((width, 4 * later.shape[1]), BF16),
-        ],
-        scratch_shapes=[
-            dma((2, 3, 2)), dma((4, 2)), dma((4, 2)), dma((4, 2)), dma((4, 2)), dma((4, 2)),
-            dma((4, 1)), dma((4, 1)), dma((4, 2)), dma((4, 2)),
-            dma((4,)), dma((4,)), dma((4,)), dma((4,)),
-            dma((2, 3)), dma((4,)), dma((4,)), dma((4,)), dma((5,)),
-        ],
-        compiler_params=pltpu.CompilerParams(collective_id=0, has_side_effects=True),
-        name="arrive",
-    )(tok, vec, mine, later)
-
-
 def dot_nn(a, b):
     return lax.dot_general(a, b, (((1,), (0,)), ((), ())), preferred_element_type=F32)
 
@@ -747,15 +496,6 @@
 PAIR = 2 * HEAD_DIM
 
 
-def space_attend_kernel(scale, qkv_ref, out_ref, total_ref):
-    for i in range(out_ref.shape[1] // PAIR):
-        q, k, v = (qkv_ref[:, (3 * i + part) * PAIR : (3 * i + part + 1) * PAIR] for part in range(3))
-        mixed, totals = attend_pair(q, k, v, None, scale)
-        out_ref[:, i * PAIR : (i + 1) * PAIR] = mixed.astype(BF16)
-        for h in range(2):
-            total_ref[0, 2 * i + h : 2 * i + h + 1, :] = totals[h]
-
-
 def space_attend_back_kernel(scale, qkv_ref, grad_ref, total_ref, out_ref):
     for i in range(grad_ref.shape[1] // PAIR):
         q, k, v = (qkv_ref[:, (3 * i + part) * PAIR : (3 * i + part + 1) * PAIR] for part in range(3))
@@ -771,25 +511,6 @@
         transcendentals=groups * heads * rows * rows,
         bytes_accessed=2 * groups * rows * heads * HEAD_DIM * 2 * products,
     )
-
-
-def space_attend(qkv, frames, patches, heads, scale):
-    width = heads * HEAD_DIM
-    return pl.pallas_call(
-        functools.partial(space_attend_kernel, scale),
-        grid=(frames,),
-        in_specs=[pl.BlockSpec((patches, 3 * width), lambda i: (i, 0))],
-        out_specs=[
-            pl.BlockSpec((patches, width), lambda i: (i, 0)),
-            pl.BlockSpec((1, heads, patches), lambda i: (i, 0, 0)),
-        ],
-        out_shape=[
-            jax.ShapeDtypeStruct((frames * patches, width), BF16),
-            jax.ShapeDtypeStruct((frames, heads, patches), F32),
-        ],
-        cost_estimate=attention_cost(frames, patches, heads, 2),
-        name="space_attend",
-    )(qkv)
 
 
 def space_attend_back(qkv, grad, total, frames, patches, heads, scale):
@@ -809,6 +530,363 @@
     )(qkv, grad, total)
 
 
+def enter_kernel(
+    scale,
+    tok, vec, qkv_hbm, out_hbm, later, feed_hbm, masked,
+    wq_out, wo_out, wt, wf, joined_out, turned_out, std_out,
+    mixed, total_out, inverse, resid, std_next, inverse_next, low_next, vec_out,
+    rows_in, vec_in, wq, wo, normed, joined, turned, std, base, part, part_out, part_in,
+    z_send, z_recv, y_send, y_recv, x_send, x_recv, p_send, p_recv, q_send, q_recv,
+    t_send, t_recv, v_send, v_recv, u_send, u_recv, w_send, w_recv,
+    f_send, f_recv, g_send, g_recv, n_send, n_recv, local, saved,
+):
+    y, x, c, z = (lax.axis_index(name) for name in AXES)
+    half = wo.shape[0] // 4
+    wide = 3 * half
+    span = wt.shape[1] // 4
+    size = wf.shape[1] // 4
+    own = rows_in.shape[0]
+    near_y, near_x, pair = (1 - y, x, c, z), (y, 1 - x, c, z), (y, x, 1 - c, z)
+    right_z, left_z = (y, x, c, (z + 1) % 4), (y, x, c, (z + 3) % 4)
+
+    def at(i, length):
+        return pl.ds(pl.multiple_of(i * length, length), length)
+
+    def remote(src, dst, send, recv, peer):
+        return pltpu.make_async_remote_copy(
+            src_ref=src, dst_ref=dst, send_sem=send, recv_sem=recv, device_id=peer, device_id_type=MESH
+        )
+
+    def start(all_copies):
+        for copy in all_copies:
+            copy.start()
+
+    def landed(all_copies):
+        for copy in all_copies:
+            copy.wait_recv()
+
+    def sent(all_copies):
+        for copy in all_copies:
+            copy.wait_send()
+
+    core = at(c, half)
+    keep = [
+        pltpu.make_async_copy(
+            qkv_hbm.at[j, :, core], wq.at[:, pl.ds(pl.multiple_of(z * wide + j * half, half), half)], local.at[j]
+        )
+        for j in range(3)
+    ] + [pltpu.make_async_copy(out_hbm.at[core], wo.at[at(z, half)], local.at[3])]
+    keep_later = [
+        pltpu.make_async_copy(later, wt.at[:, at(z, span)], local.at[4]),
+        pltpu.make_async_copy(feed_hbm.at[at(c, 4 * size)], wf.at[z], local.at[5]),
+    ]
+    start(keep + keep_later)
+
+    barrier = pltpu.get_barrier_semaphore()
+    for dc in range(2):
+        for dz in range(4):
+            if dc or dz:
+                peer = (y, x, (c + dc) % 2, (z + dz) % 4)
+                pl.semaphore_signal(barrier, inc=1, device_id=peer, device_id_type=MESH)
+    for peer in (near_y, near_x):
+        pl.semaphore_signal(barrier, inc=1, device_id=peer, device_id_type=MESH)
+    pl.semaphore_wait(barrier, 9)
+
+    def spot(dy, dx):
+        return 2 * ((y + dy) % 2) + (x + dx) % 2
+
+    def piece(dy, dx, r, split=False):
+        s = (z + r) % 4
+        rows = at(spot(dy, dx), BLK)
+        first = pl.multiple_of(s * wide, half)
+        out = wo.at[at(s, half), at(spot(dy, dx), BLK)]
+        if split:
+            last = pl.multiple_of(s * wide + 2 * half, half)
+            return (wq.at[rows, pl.ds(first, 2 * half)], wq.at[rows, pl.ds(last, half)], out)
+        return (wq.at[rows, pl.ds(first, wide)], out)
+
+    def time_piece(dx, r):
+        return wt.at[at((x + dx) % 2, 2 * BLK), at((z + r) % 4, span)]
+
+    def feed_piece(dy, r):
+        return wf.at[(z + r) % 4, at(spot(dy, 0), size)]
+
+    def copies(parts, send, recv, peer):
+        return [remote(ref, ref, send.at[i], recv.at[i], peer) for i, ref in enumerate(parts)]
+
+    def leg(right, step):
+        if right:
+            return (0 if step == 0 else 4 - step), right_z, 3 - step
+        return step, left_z, step + 1
+
+    def z_copies(right, step):
+        r, peer, lands = leg(right, step)
+        return copies(piece(0, 0, r), z_send.at[int(right), step], z_recv.at[lands], peer)
+
+    def time_z(right, step):
+        r, peer, lands = leg(right, step)
+        source = later.at[at(x, 2 * BLK)] if step == 0 else time_piece(0, r)
+        return [remote(source, time_piece(0, r), u_send.at[int(right), step], u_recv.at[lands], peer)]
+
+    def feed_z(right, step):
+        r, peer, lands = leg(right, step)
+        source = feed_hbm.at[at(4 * c + spot(0, 0), size)] if step == 0 else feed_piece(0, r)
+        return [remote(source, feed_piece(0, r), f_send.at[int(right), step], f_recv.at[lands], peer)]
+
+    def y_copies(r, dy=0):
+        return copies(piece(dy, 0, r), y_send.at[r], y_recv.at[r], near_y)
+
+    def x_copies(r, dx=0):
+        return copies(piece(0, dx, r), x_send.at[r], x_recv.at[r], near_x)
+
+    def corner_x(r, dx=0):
+        return copies(piece(1, dx, r, split=True)[:1], p_send.at[r], p_recv.at[r], near_x)
+
+    def corner_y(r, dy=0):
+        return copies(piece(dy, 1, r, split=True)[1:], q_send.at[r], q_recv.at[r], near_y)
+
+    def time_x(r, dx=0):
+        return [remote(time_piece(dx, r), time_piece(dx, r), w_send.at[r], w_recv.at[r], near_x)]
+
+    def feed_y(r, dy=0):
+        return [remote(feed_piece(dy, r), feed_piece(dy, r), g_send.at[r], g_recv.at[r], near_y)]
+
+    def token_copies(k):
+        peer = (y, x, k % 2, 2 * c + k // 2)
+        return [
+            remote(tok.at[k], rows_in.at[:, at(z, BLK)], t_send.at[k], t_recv.at[z], peer),
+            remote(vec, vec_in.at[:, at(z, BLK)], v_send.at[k], v_recv.at[z], peer),
+        ]
+
+    def token_local(k):
+        return [
+            pltpu.make_async_copy(tok.at[k], rows_in.at[:, at(z, BLK)], local.at[6]),
+            pltpu.make_async_copy(vec, vec_in.at[:, at(z, BLK)], local.at[7]),
+        ]
+
+    def stays(k):
+        return jnp.logical_and(2 * c + k // 2 == z, c == k % 2)
+
+    def start_tokens(ks):
+        for k in ks:
+            pl.when(stays(k))(lambda k=k: start(token_local(k)))
+            pl.when(jnp.logical_not(stays(k)))(lambda k=k: start(token_copies(k)))
+
+    def each_side(j, act):
+        pl.when(z >= j + 1)(lambda: act(3 - j, True))
+        pl.when(z <= 2 - j)(lambda: act(j + 1, False))
+
+    def begin(make):
+        pl.when(z < 3)(lambda: start(make(True, 0)))
+        pl.when(z > 0)(lambda: start(make(False, 0)))
+
+    def onward(j, make, right):
+        if j < 2:
+            pl.when(z < 3 if right else z > 0)(lambda: start(make(right, j + 1)))
+
+    def forward(j):
+        def act(r, right):
+            landed(copies(piece(0, 0, r), z_send.at[0, 0], z_recv.at[r], near_y))
+            onward(j, z_copies, right)
+            start(y_copies(r))
+            start(x_copies(r))
+
+        each_side(j, act)
+
+    def corners(j):
+        def act(r, right):
+            landed(y_copies(r, 1))
+            start(corner_x(r))
+            landed(x_copies(r, 1))
+            start(corner_y(r))
+
+        each_side(j, act)
+
+    def time_forward_step(j):
+        def act(r, right):
+            landed([remote(time_piece(0, r), time_piece(0, r), u_send.at[0, 0], u_recv.at[r], near_x)])
+            onward(j, time_z, right)
+            start(time_x(r))
+
+        each_side(j, act)
+
+    def feed_forward_step(j):
+        def act(r, right):
+            landed([remote(feed_piece(0, r), feed_piece(0, r), f_send.at[0, 0], f_recv.at[r], near_y)])
+            onward(j, feed_z, right)
+            start(feed_y(r))
+
+        each_side(j, act)
+
+    for copy in keep:
+        copy.wait()
+    begin(z_copies)
+    forward(0)
+    start_tokens((0, 1))
+    forward(1)
+    start_tokens((2, 3))
+    begin(time_z)
+    corners(0)
+    forward(2)
+    corners(1)
+    for k in range(4):
+        def finish_local(k=k):
+            for copy in token_local(k):
+                copy.wait()
+
+        pl.when(stays(k))(finish_local)
+    for s in range(4):
+        def arrived(s=s):
+            landed([
+                remote(tok.at[0], rows_in.at[:, at(s, BLK)], t_send.at[0], t_recv.at[s], near_y),
+                remote(vec, vec_in.at[:, at(s, BLK)], v_send.at[0], v_recv.at[s], near_y),
+            ])
+
+        pl.when(jnp.logical_not(jnp.logical_and(z == s, z // 2 == c)))(arrived)
+
+    step = own // 2
+    slab = 128
+    vec_out[...] = vec_in[...].astype(F32)
+
+    def first_norm(i, carry):
+        rows = at(i, step)
+        value = jnp.where(masked[rows] > 0.0, vec_out[0:1], rows_in[rows].astype(F32))
+        base[rows] = value
+        standard, inv = norm_rows(value)
+        std[rows] = standard
+        inverse[rows] = inv
+        normed[rows] = (standard * vec_out[1:2]).astype(BF16)
+        return carry
+
+    lax.fori_loop(0, 2, first_norm, 0)
+    give_normed = remote(normed.at[pl.ds(0, own)], normed.at[pl.ds(own, own)], n_send.at[0], n_recv.at[0], pair)
+    give_normed.start()
+    corners(2)
+
+    def turn(i, carry):
+        turned[:, at(i, slab)] = normed[at(i, slab)].T
+        return carry
+
+    lax.fori_loop(0, own // slab, turn, 0)
+    for r in (1, 2, 3):
+        landed(corner_x(r, 1))
+        landed(corner_y(r, 1))
+    saves = [
+        pltpu.make_async_copy(wq, wq_out, saved.at[0]),
+        pltpu.make_async_copy(wo, wo_out, saved.at[1]),
+        pltpu.make_async_copy(std, std_out, saved.at[2]),
+    ]
+    start(saves)
+    time_forward_step(0)
+
+    def attend(i, carry):
+        rows = at(i, slab)
+        for h in range(wo.shape[0] // PAIR):
+            q, k, v = (joined[rows, (3 * h + j) * PAIR : (3 * h + j + 1) * PAIR] for j in range(3))
+            out, totals = attend_pair(q, k, v, None, scale)
+            mixed[rows, h * PAIR : (h + 1) * PAIR] = out.astype(BF16)
+            for j in range(2):
+                total_out[i, 2 * h + j : 2 * h + j + 1, :] = totals[j]
+        return carry
+
+    def project(t):
+        rows = pl.ds(t * own, own)
+        joined[rows] = dot_nn(normed[rows], wq[...]).astype(BF16)
+
+    frames = own // slab
+    project(0)
+    time_forward_step(1)
+    begin(feed_z)
+    lax.fori_loop(0, frames, attend, 0)
+    part[...] = dot_nn(mixed[pl.ds(0, own)], wo[...])
+    time_forward_step(2)
+    give_normed.wait_recv()
+    project(1)
+    saves.append(pltpu.make_async_copy(joined, joined_out, saved.at[3]))
+    saves[3].start()
+    lax.fori_loop(frames, 2 * frames, attend, 0)
+    part_out[...] = dot_nn(mixed[pl.ds(own, own)], wo[...]).astype(BF16)
+    give_part = remote(part_out, part_in, n_send.at[1], n_recv.at[1], pair)
+    give_part.start()
+    feed_forward_step(0)
+    lax.fori_loop(own // slab, 2 * own // slab, turn, 0)
+    saves.append(pltpu.make_async_copy(turned, turned_out, saved.at[4]))
+    saves[4].start()
+    give_part.wait_recv()
+    feed_forward_step(1)
+
+    def second_norm(i, carry):
+        rows = at(i, step)
+        value = base[rows] + part[rows] + part_in[rows].astype(F32)
+        resid[rows] = value
+        standard, inv = norm_rows(value)
+        std_next[rows] = standard
+        inverse_next[rows] = inv
+        low_next[rows] = (standard * vec_out[2:3]).astype(BF16)
+        return carry
+
+    lax.fori_loop(0, 2, second_norm, 0)
+    feed_forward_step(2)
+
+    for copy in keep_later + saves:
+        copy.wait()
+    give_normed.wait_send()
+    give_part.wait_send()
+    for r in (1, 2, 3):
+        landed(time_x(r, 1))
+        landed(feed_y(r, 1))
+        for group in (y_copies(r), x_copies(r), corner_x(r), corner_y(r), time_x(r), feed_y(r)):
+            sent(group)
+    for step_z in range(3):
+        for make in (z_copies, time_z, feed_z):
+            pl.when(jnp.logical_and(z >= step_z, z < 3))(lambda step_z=step_z, make=make: sent(make(True, step_z)))
+            pl.when(jnp.logical_and(z + step_z <= 3, z > 0))(lambda step_z=step_z, make=make: sent(make(False, step_z)))
+    for k in range(4):
+        pl.when(jnp.logical_not(stays(k)))(lambda k=k: sent(token_copies(k)))
+
+
+def enter(tok, vec, qkv, out, later, feed_weight, masked, scale):
+    own, width, half = tok.shape[1], 4 * tok.shape[2], out.shape[0] // 2
+    size = feed_weight.shape[0] // 2
+    dma = pltpu.SemaphoreType.DMA
+    anywhere = pl.BlockSpec(memory_space=pl.ANY)
+    whole = pl.BlockSpec(memory_space=pltpu.VMEM)
+    heads = 4 * half // HEAD_DIM
+
+    def low(*shape):
+        return pltpu.VMEM(shape, BF16)
+
+    def high(*shape):
+        return pltpu.VMEM(shape, F32)
+
+    shapes = [
+        ((width, 12 * half), BF16), ((4 * half, width), BF16), ((width, 4 * later.shape[1]), BF16),
+        ((4, size, width), BF16), ((2 * own, 12 * half), BF16), ((width, 2 * own), BF16), ((own, width), F32),
+        ((2 * own, 4 * half), BF16), ((2 * own // 128, heads, 128), F32), ((own, 1), F32), ((own, width), F32),
+        ((own, width), F32), ((own, 1), F32), ((own, width), BF16), ((vec.shape[0], width), F32),
+    ]
+    return pl.pallas_call(
+        functools.partial(enter_kernel, scale),
+        in_specs=[anywhere] * 6 + [whole],
+        out_specs=[anywhere] * 7 + [whole] * 8,
+        out_shape=[jax.ShapeDtypeStruct(shape, kind) for shape, kind in shapes],
+        scratch_shapes=[
+            low(own, width), low(vec.shape[0], width), low(width, 12 * half), low(4 * half, width),
+            low(2 * own, width), low(2 * own, 12 * half), low(width, 2 * own), high(own, width), high(own, width),
+            high(own, width), low(own, width), low(own, width),
+            dma((2, 3, 2)), dma((4, 2)), dma((4, 2)), dma((4, 2)), dma((4, 2)), dma((4, 2)),
+            dma((4, 1)), dma((4, 1)), dma((4, 2)), dma((4, 2)),
+            dma((4,)), dma((4,)), dma((4,)), dma((4,)), dma((2, 3)), dma((4,)), dma((4,)), dma((4,)),
+            dma((2, 3)), dma((4,)), dma((4,)), dma((4,)), dma((2,)), dma((2,)), dma((8,)), dma((5,)),
+        ],
+        compiler_params=pltpu.CompilerParams(
+            collective_id=0, has_side_effects=True, vmem_limit_bytes=56 * 1024 * 1024
+        ),
+        cost_estimate=pl.CostEstimate(flops=10**10, transcendentals=10**6, bytes_accessed=10**8),
+        name="enter",
+    )(tok, vec, qkv, out, later, feed_weight, masked)
+
+
 GROUP = 8
 CHUNK = 32
 
@@ -816,17 +894,17 @@
 def time_kernel(back, scale, heads, *refs):
     if back:
         (own_ref, rider_ref, joined_ref, total_ref, wide_ref, wq_ref, wo_ref, bias_ref) = refs[:8]
-        (all_ref, out_ref, delta_ref, halved_ref, rider_out) = refs[8:13]
-        (halved_in, halved_own, half_send, half_recv, half_local) = refs[-5:]
-        refs = refs[13:-5]
+        (all_ref, out_ref, delta_ref, reduced_ref, rider_out) = refs[8:13]
+        (half_in, half_own, line_out, line_in, half_send, half_recv, half_local, line_send, line_recv) = refs[-9:]
+        refs = refs[13:-9]
     else:
-        (own_ref, rider_ref, far_ref, near_ref, wq_ref, wo_ref, bias_ref) = refs[:7]
-        (all_ref, out_ref, mixed_ref, total_ref, delta_ref, rider_out, spread_out) = refs[7:14]
-        refs = refs[14:]
+        (own_ref, rider_ref, far_ref, wq_ref, wo_ref, bias_ref) = refs[:6]
+        (all_ref, out_ref, mixed_ref, total_ref, delta_ref, rider_out, spread_out) = refs[6:13]
+        refs = refs[13:]
     (
         held, wide, narrow, kept, core_out, core_in, near_out, near_in,
         gy_send, gy_recv, gc_send, gc_recv, gd_send, gd_recv, sc_send, sc_recv, sy_send, sy_recv,
-        r_send, r_recv, r_local, out_sem, wy_send, wy_recv, wx_send, wx_recv, wd_send, wd_recv, w_local,
+        r_send, r_recv, r_local, out_sem, wx_send, wx_recv,
     ) = refs
     y, x, c, z = (lax.axis_index(name) for name in AXES)
     near, pair, near_x = (1 - y, x, c, z), (y, x, 1 - c, z), (y, 1 - x, c, z)
@@ -910,59 +988,47 @@
             return jnp.logical_and(2 * c + k // 2 == z, c == k % 2)
         return jnp.logical_and(z == k, z // 2 == c)
 
-    def place(dy, dx, r):
-        size = far_ref.shape[1]
-        at = pl.multiple_of(size * (2 * ((y + dy) % 2) + (x + dx) % 2), size)
-        return spread_out.at[(z + r) % 4, pl.ds(at, size)]
-
-    def spread_y(r, dy=0):
-        src = far_ref.at[r - 1] if dy == 0 else place(1, 0, r)
-        return remote(src, place(dy, 0, r), wy_send.at[r], wy_recv.at[r], near)
-
-    def spread_x(r, dx=0):
-        src = far_ref.at[r - 1] if dx == 0 else place(0, 1, r)
-        return remote(src, place(0, dx, r), wx_send.at[r], wx_recv.at[r], near_x)
-
-    def spread_d(r, dx=0):
-        return remote(place(1, dx, r), place(1, dx, r), wd_send.at[r], wd_recv.at[r], near_x)
-
-    def spread_keep(r):
-        if r == 0:
-            size = 4 * far_ref.shape[1]
-            here = near_ref.at[pl.ds(pl.multiple_of(c * size, size), size)]
-            return pltpu.make_async_copy(here, spread_out.at[z], w_local.at[0])
-        return pltpu.make_async_copy(far_ref.at[r - 1], place(0, 0, r), w_local.at[r])
-
-    def spread_on(r):
-        spread_y(r, 1).wait_recv()
-        spread_d(r).start()
+    def spread_x(i, dx=0):
+        r, yb = i // 2 + 1, i % 2
+        size = far_ref.shape[1] // 4
+        at = pl.multiple_of(size * (2 * yb + (x + dx) % 2), size)
+        src = far_ref.at[(z + r) % 4, pl.ds(at, size)]
+        return remote(src, spread_out.at[(z + r) % 4, pl.ds(at, size)], wx_send.at[i], wx_recv.at[i], near_x)
 
     gather_y(0).start()
     for k in range(chunks):
         if k > 0:
             gather_y(k).start()
         gather_c(k).start()
-    def half_rows(yb, xb):
-        return pl.ds(pl.multiple_of(BLK * (2 * yb + xb), BLK), BLK)
-
-    def half_away(i):
-        src = wide_ref.at[i % 4, half_rows(i // 4, 1 - x)]
-        return remote(src, halved_in.at[i // 4, i % 4], half_send.at[i], half_recv.at[i], near_x)
-
-    def half_here(i):
-        src = wide_ref.at[i % 4, half_rows(i // 4, x)]
-        return pltpu.make_async_copy(src, halved_own.at[i // 4, i % 4], half_local.at[i])
+    def half_away(s):
+        return remote(wide_ref.at[1 - x, s], half_in.at[s], half_send.at[s], half_recv.at[s], near_x)
+
+    def half_here(s):
+        return pltpu.make_async_copy(wide_ref.at[x, s], half_own.at[s], half_local.at[s])
+
+    def line_away(r):
+        return remote(line_out.at[r], line_in.at[r], line_send.at[r], line_recv.at[r], (y, x, c, (z + r) % 4))
+
+    def halve():
+        for s in range(4):
+            half_away(s).wait_recv()
+            half_here(s).wait()
+        for r in range(4):
+            s = (z + r) % 4
+            whole = half_own[s].astype(F32) + half_in[s].astype(F32)
+            if r == 0:
+                reduced_ref[...] = whole
+            else:
+                line_out[r] = whole.astype(BF16)
+                line_away(r).start()
 
     if back:
-        for i in range(8):
-            half_away(i).start()
-            half_here(i).start()
+        for s in range(4):
+            half_away(s).start()
+            half_here(s).start()
     else:
-        for r in (1, 2, 3):
-            spread_x(r).start()
-            spread_y(r).start()
-        for r in range(4):
-            spread_keep(r).start()
+        for i in range(6):
+            spread_x(i).start()
     for k in range(4):
         pl.when(stays(k))(lambda k=k: ride_local(k).start())
         pl.when(jnp.logical_not(stays(k)))(lambda k=k: ride_remote(k).start())
@@ -1031,36 +1097,32 @@
         core_out[k] = partial[2 * frames :].astype(BF16)
         scatter_c(k).start()
         pl.when(k > 0)(lambda: finish(k - 1))
-        if not back:
-            for r in (1, 2, 3):
-                pl.when(k == r)(lambda r=r: spread_on(r))
+        if back:
+            pl.when(k == 1)(halve)
         return carry
 
     pass_on(0)
     lax.fori_loop(0, chunks, one_chunk, 0)
     finish(chunks - 1)
-    if back:
-        for i in range(8):
-            half_away(i).wait_recv()
-            half_here(i).wait()
-            at = (i // 4, i % 4)
-            halved_ref[at] = (halved_own[at].astype(F32) + halved_in[at].astype(F32)).astype(BF16)
-            half_away(i).wait_send()
     for k in range(chunks):
         scatter_y(k).wait_recv()
         delta_ref[:, patches(k)] = delta_ref[:, patches(k)] + near_in[k].astype(F32)
+    if back:
+        for r in (1, 2, 3):
+            line_away(r).wait_recv()
+            reduced_ref[...] = reduced_ref[...] + line_in[r].astype(F32)
+        for r in (1, 2, 3):
+            line_away(r).wait_send()
+        for s in range(4):
+            half_away(s).wait_send()
     for k in range(chunks):
         for copy in (gather_y(k), gather_c(k), gather_d(k), scatter_c(k), scatter_y(k)):
             copy.wait_send()
         save(k).wait()
     if not back:
-        for r in (1, 2, 3):
-            spread_x(r, 1).wait_recv()
-            spread_d(r, 1).wait_recv()
-            for copy in (spread_x(r), spread_y(r), spread_d(r)):
-                copy.wait_send()
-        for r in range(4):
-            spread_keep(r).wait()
+        for i in range(6):
+            spread_x(i, 1).wait_recv()
+            spread_x(i).wait_send()
     for k in range(4):
         pl.when(stays(k))(lambda k=k: ride_local(k).wait())
         pl.when(jnp.logical_not(stays(k)))(lambda k=k: ride_remote(k).wait_send())
@@ -1091,15 +1153,15 @@
         jax.ShapeDtypeStruct(rider_shape, BF16),
     ]
     held = 2
-    halves = (2, 4, BLK, saved[2].shape[2]) if back else None
+    half = saved[2].shape[1:] if back else None
     if back:
-        out_shape.insert(-1, jax.ShapeDtypeStruct(halves, BF16))
+        out_shape.insert(-1, jax.ShapeDtypeStruct(half[1:], F32))
     else:
-        out_shape.append(jax.ShapeDtypeStruct((4, 4 * saved[0].shape[1], features), BF16))
+        out_shape.append(jax.ShapeDtypeStruct(saved[0].shape, BF16))
         held = 3
     return pl.pallas_call(
         functools.partial(time_kernel, back, scale, heads),
-        in_specs=[whole, anywhere] + ([whole, whole, anywhere] if back else [anywhere] * 2) + [whole] * 3,
+        in_specs=[whole, anywhere] + ([whole, whole, anywhere] if back else [anywhere]) + [whole] * 3,
         out_specs=[anywhere] + [whole] * (len(out_shape) - held) + [anywhere] * (held - 1),
         out_shape=out_shape,
         scratch_shapes=[
@@ -1114,8 +1176,8 @@
         ]
         + [dma((chunks,))] * 10
         + [dma((4,)), dma((4,)), dma((1,)), dma((chunks,))]
-        + [dma((4,))] * 7
-        + ([pltpu.VMEM(halves, BF16), pltpu.VMEM(halves, BF16), dma((8,)), dma((8,)), dma((8,))] if back else []),
+        + [dma((6,))] * 2
+        + ([pltpu.VMEM(half, BF16)] * 4 + [dma((4,))] * 5 if back else []),
         compiler_params=pltpu.CompilerParams(
             collective_id=2 if back else 1, has_side_effects=True, vmem_limit_bytes=48 * 1024 * 1024
         ),
@@ -1125,34 +1187,66 @@
 
 
 def feed_kernel(
-    resid, delta, upstream, masked, gain, w_in_hbm, w_out_hbm,
-    g_in_hbm, g_out_hbm, grad_out, low_out, rows_out, gain_out,
+    resid, delta, upstream, masked, gain, w_in_hbm, w_out_hbm, w_far_hbm,
+    half_in_hbm, half_out_hbm, grad_out, low_out, rows_out, gain_out,
     w_in, w_out, standard, inverse, normed, grads, normed_t, grads_t, hidden, pulled, g_in, g_out, back, ahead,
-    back_out, back_in, ahead_out, ahead_in,
-    w_sem, g_sem, n_send, n_recv, b_send, b_recv,
+    back_out, back_in, ahead_out, ahead_in, from_x, from_y,
+    w_sem, g_sem, n_send, n_recv, b_send, b_recv, hx_send, hx_recv, hy_send, hy_recv,
 ):
     y, x, c, z = (lax.axis_index(name) for name in AXES)
-    pair = (y, x, 1 - c, z)
+    pair, near_y, near_x = (y, x, 1 - c, z), (1 - y, x, c, z), (y, 1 - x, c, z)
     own = resid.shape[0]
     step = own // 2
     slab = 128
 
-    def fetch(s):
+    def fetch(s, far):
+        size = w_out.shape[1] // 4
+        copies = [pltpu.make_async_copy(w_in_hbm.at[s], w_in.at[s], w_sem.at[0, s])]
+        for i in range(4):
+            rows = pl.ds(pl.multiple_of(size * (2 * (i // 2) + (x + i % 2) % 2), size), size)
+            source = w_far_hbm if far and i % 2 else w_out_hbm
+            copies.append(pltpu.make_async_copy(source.at[s, rows], w_out.at[s, rows], w_sem.at[1 + i, s]))
+        return copies
+
+    def fetch_now(s, far):
+        for copy in fetch(s, far):
+            copy.start()
+
+    for s in range(4):
+        pl.when(z == s)(lambda s=s: fetch_now(s, False))
+        pl.when(z != s)(lambda s=s: fetch_now(s, True))
+    barrier = pltpu.get_barrier_semaphore()
+    for peer in (pair, near_y, near_x):
+        pl.semaphore_signal(barrier, inc=1, device_id=peer, device_id_type=MESH)
+
+    def remote(src, dst, send, recv, peer=pair):
+        return pltpu.make_async_remote_copy(
+            src_ref=src, dst_ref=dst, send_sem=send, recv_sem=recv, device_id=peer, device_id_type=MESH
+        )
+
+    def block(yb, xb):
+        return pl.ds(pl.multiple_of(BLK * (2 * yb + xb), BLK), BLK)
+
+    def away_x(s, i):
+        return remote(g_out.at[s, block(i, 1 - x)], from_x.at[i, s], hx_send.at[i, s], hx_recv.at[i, s], near_x)
+
+    def away_y(s, i):
+        return remote(g_in.at[s, block(1 - y, i)], from_y.at[i, s], hy_send.at[i, s], hy_recv.at[i, s], near_y)
+
+    def keep(s, i):
         return (
-            pltpu.make_async_copy(w_in_hbm.at[s], w_in.at[s], w_sem.at[0, s]),
-            pltpu.make_async_copy(w_out_hbm.at[s], w_out.at[s], w_sem.at[1, s]),
-        )
-
-    for s in range(4):
-        for copy in fetch(s):
-            copy.start()
-    barrier = pltpu.get_barrier_semaphore()
-    pl.semaphore_signal(barrier, inc=1, device_id=pair, device_id_type=MESH)
-
-    def remote(src, dst, send, recv):
-        return pltpu.make_async_remote_copy(
-            src_ref=src, dst_ref=dst, send_sem=send, recv_sem=recv, device_id=pair, device_id_type=MESH
-        )
+            pltpu.make_async_copy(g_out.at[s, block(i, x)], half_out_hbm.at[i, s], g_sem.at[0, i, s]),
+            pltpu.make_async_copy(g_in.at[s, block(y, i)], half_in_hbm.at[i, s], g_sem.at[1, i, s]),
+        )
+
+    def combine(s):
+        for i in range(2):
+            away_x(s, i).wait_recv()
+            g_out[s, block(i, x)] = (g_out[s, block(i, x)].astype(F32) + from_x[i, s].astype(F32)).astype(BF16)
+            away_y(s, i).wait_recv()
+            g_in[s, block(y, i)] = (g_in[s, block(y, i)].astype(F32) + from_y[i, s].astype(F32)).astype(BF16)
+            for copy in keep(s, i):
+                copy.start()
 
     def at(i, size):
         return pl.ds(pl.multiple_of(i * size, size), size)
@@ -1167,7 +1261,7 @@
         return carry
 
     lax.fori_loop(0, 2, prepare, 0)
-    pl.semaphore_wait(barrier, 1)
+    pl.semaphore_wait(barrier, 3)
     mine, theirs = pl.ds(0, own), pl.ds(own, own)
     give_grads = remote(grads.at[mine], grads.at[theirs], n_send.at[0], n_recv.at[0])
     give_normed = remote(normed.at[mine], normed.at[theirs], n_send.at[1], n_recv.at[1])
@@ -1195,19 +1289,13 @@
         ahead[rows] = ahead[rows] + dot_nn(hidden[rows], w_out[s])
         back[rows] = back[rows] + dot_nt(pulled[rows], w_in[s])
 
-    def keep(s):
-        return (
-            pltpu.make_async_copy(g_in.at[s], g_in_hbm.at[s], g_sem.at[0, s]),
-            pltpu.make_async_copy(g_out.at[s], g_out_hbm.at[s], g_sem.at[1, s]),
-        )
-
     def meet():
         give_normed.wait_recv()
         give_grads.wait_recv()
         lax.fori_loop(own // slab, 2 * own // slab, turn, 0)
 
     def one_piece(s, carry):
-        for copy in fetch(s):
+        for copy in fetch(s, False):
             copy.wait()
 
         def one_half(t, carry):
@@ -1218,8 +1306,9 @@
         lax.fori_loop(0, 2, one_half, 0)
         g_out[s] = dot_nn(grads_t[...], hidden[...]).astype(BF16)
         g_in[s] = dot_nn(normed_t[...], pulled[...]).astype(BF16)
-        for copy in keep(s):
-            copy.start()
+        for i in range(2):
+            away_x(s, i).start()
+            away_y(s, i).start()
         return carry
 
     lax.fori_loop(0, 4, one_piece, 0)
@@ -1252,14 +1341,18 @@
         return carry
 
     lax.fori_loop(0, 2, emit, 0)
+    lax.fori_loop(0, 4, lambda s, carry: (combine(s), carry)[1], 0)
     for copy in (give_normed, give_grads, give_back, give_ahead):
         copy.wait_send()
     for s in range(4):
-        for copy in keep(s):
-            copy.wait()
-
-
-def feed(resid, delta, upstream, masked, gain, w_in, w_out):
+        for i in range(2):
+            away_x(s, i).wait_send()
+            away_y(s, i).wait_send()
+            for copy in keep(s, i):
+                copy.wait()
+
+
+def feed(resid, delta, upstream, masked, gain, w_in, w_out, w_far):
     own, features = resid.shape
     units = w_in.shape[2]
     dma = pltpu.SemaphoreType.DMA
@@ -1274,11 +1367,11 @@
 
     return pl.pallas_call(
         feed_kernel,
-        in_specs=[whole] * 5 + [anywhere] * 2,
+        in_specs=[whole] * 5 + [anywhere] * 3,
         out_specs=[anywhere] * 2 + [whole] * 4,
         out_shape=[
-            jax.ShapeDtypeStruct((4, features, units), BF16),
-            jax.ShapeDtypeStruct((4, features, units), BF16),
+            jax.ShapeDtypeStruct((2, 4, BLK, units), BF16),
+            jax.ShapeDtypeStruct((2, 4, BLK, units), BF16),
             jax.ShapeDtypeStruct((own, features), F32),
             jax.ShapeDtypeStruct((own, features), BF16),
             jax.ShapeDtypeStruct((own, features), BF16),
@@ -1290,14 +1383,16 @@
             low(2 * own, units), low(2 * own, units), low(4, features, units), low(4, features, units),
             high(2 * own, features), high(2 * own, features),
             low(own, features), low(own, features), low(own, features), low(own, features),
-            dma((2, 4)), dma((2, 4)), dma((2,)), dma((2,)), dma((2,)), dma((2,)),
+            low(2, 4, BLK, units), low(2, 4, BLK, units),
+            dma((5, 4)), dma((2, 2, 4)), dma((2,)), dma((2,)), dma((2,)), dma((2,)),
+            dma((2, 4)), dma((2, 4)), dma((2, 4)), dma((2, 4)),
         ],
         compiler_params=pltpu.CompilerParams(
             collective_id=4, has_side_effects=True, vmem_limit_bytes=60 * 1024 * 1024
         ),
         cost_estimate=pl.CostEstimate(flops=26 * 10**9, transcendentals=2 * 10**6, bytes_accessed=10**8),
         name="feed",
-    )(resid, delta, upstream, masked, gain, w_in, w_out)
+    )(resid, delta, upstream, masked, gain, w_in, w_out, w_far)
 
 
 def settle_kernel(
@@ -1628,13 +1723,6 @@
     visible = (order[:, None] <= order[None, :]) & (patch[:, None] == patch[None, :])
     bias = jnp.where(visible, 0.0, -1e30).astype(F32)
 
-    half = qkv_space.shape[2] // 2
-    sp_own = cols(
-        [
-            lax.dynamic_slice_in_dim(qkv_space, c * half, half, 2).reshape(width, -1),
-            lax.dynamic_slice_in_dim(out_space, c * half, half, 0).T,
-        ]
-    )
     vectors = rows_of([mask_embed[None], gains, jnp.zeros((4, BLK), BF16)])
     head = (2 * y + c) * HEAD_DIM
     ti_own = cols(
@@ -1643,19 +1731,26 @@
             lax.dynamic_slice_in_dim(out_time, head, HEAD_DIM, 0).T,
         ]
     )
-    arrived, vectors, ws_qkv, ws_out, wt_all = arrive(tokens.reshape(4, own, BLK), vectors, sp_own, ti_own)
+    (
+        ws_qkv, ws_out, wt_all, wf_out, joined0, turned0, std0,
+        mixed0, total0, inv0, resid1, std1, inv1, normed1, vectors,
+    ) = enter(
+        tokens.reshape(4, own, BLK),
+        vectors,
+        jnp.swapaxes(qkv_space, 0, 1),
+        out_space,
+        ti_own,
+        w_out,
+        masked.astype(F32),
+        scale,
+    )
+    gain = [vectors[1 + i : 2 + i] for i in range(3)]
     wt_all = wt_all.reshape(width, 4, 4, HEAD_DIM)
     wt_qkv = jnp.swapaxes(wt_all[:, :, :3], 1, 2).reshape(width, 12 * HEAD_DIM)
     wt_out = wt_all[:, :, 3].reshape(width, 4 * HEAD_DIM)
-    source = arrived.astype(F32)
-    embed_row = vectors[:1].astype(F32)
-    gain = [vectors[1 + i : 2 + i].astype(F32) for i in range(3)]
 
     ff_in = lax.dynamic_slice(w_in, (plane * BLK, c * hidden_own), (BLK, hidden_own))
-    arrived, ff_in, w_out = tie(arrived, ff_in, w_out)
-    out_size = hidden_own // 4
-    out_slice = lax.dynamic_slice_in_dim(w_out, c * hidden_own + plane * out_size, out_size, 0)
-    out_far = [hop_z(out_slice, -r) for r in (1, 2, 3)]
+    ff_in, normed1 = tie(ff_in, normed1)
     wf_in = lax.all_gather(ff_in, ("mp", "tm", "x")).reshape(4, width, hidden_own)
 
     def pair_gather(v):
@@ -1664,21 +1759,14 @@
     def pair_scatter(v):
         return v[:own] + hop_c(v[own:].astype(BF16)).astype(F32)
 
+    half = qkv_space.shape[2] // 2
     heads_s = 4 * half // HEAD_DIM
     frames_pair = 2 * frames_own
-    resid0 = jnp.where(masked, embed_row, source)
-    std0, inv0 = norm_rows(resid0)
-    normed0 = pair_gather((std0 * gain[0]).astype(BF16))
-    joined0 = dot_nn(normed0, ws_qkv).astype(BF16)
-    mixed0, total0 = space_attend(joined0, frames_pair, patches, heads_s, scale)
-    mixed0, out_far = tie(mixed0, out_far)
-    resid1 = resid0 + pair_scatter(dot_nt(mixed0, ws_out))
-    std1, inv1 = norm_rows(resid1)
-    normed1, joined1, mixed1, total1, delta, upstream, wf_out = time_call(
+    normed1, joined1, mixed1, total1, delta, upstream, wf_far = time_call(
         False,
-        (std1 * gain[1]).astype(BF16).reshape(frames_own, patches, width),
+        normed1.reshape(frames_own, patches, width),
         cotangent.reshape(4, own, BLK),
-        [jnp.stack(out_far), w_out],
+        [wf_out],
         wt_qkv,
         wt_out,
         bias,
@@ -1686,15 +1774,9 @@
     )
     normed1 = normed1.reshape(4 * own, width)
     mixed1 = mixed1.reshape(4 * own, -1)
-    g_w_in, g_w_out, grad2, grad2_low, block_rows, gain_grad2 = feed(
-        resid1, delta.reshape(own, width), upstream, masked.astype(F32), gain[2], wf_in, wf_out
-    )
-
-    def line_scatter(parts):
-        return lax.psum_scatter(parts, "mp", scatter_dimension=0)
-
-    def plane_scatter(v):
-        return lax.psum_scatter(v, ("tm", "x"), scatter_dimension=0, tiled=True).astype(F32)
+    w_in_half, w_out_half, grad2, grad2_low, block_rows, gain_grad2 = feed(
+        resid1, delta.reshape(own, width), upstream, masked.astype(F32), gain[2], wf_in, wf_out, wf_far
+    )
 
     def send_x(lhs, rhs):
         there = jnp.where(x == 0, cols([lhs[:, BLK : 2 * BLK], lhs[:, 3 * BLK :]]), cols([lhs[:, :BLK], lhs[:, 2 * BLK : 3 * BLK]]))
@@ -1725,12 +1807,11 @@
     def by_core(kept, landed):
         return jnp.where(c == 0, jnp.concatenate([kept, landed], -1), jnp.concatenate([landed, kept], -1))
 
-    w_in_part = line_scatter(g_w_in)
-    gb2, djoined1, part1, w_out_part, block_out = time_call(
+    gb2, djoined1, part1, g_w_in, block_out = time_call(
         True,
         grad2_low.reshape(frames_own, patches, width),
         block_rows,
-        [joined1, total1, g_w_out],
+        [joined1, total1, w_in_half],
         wt_qkv,
         wt_out,
         bias,
@@ -1739,17 +1820,15 @@
     block_out = block_out.reshape(tokens.shape)
     gb2 = gb2.reshape(4 * own, width)
     djoined1 = djoined1.reshape(4 * own, -1)
-    part1 = part1.reshape(own, width)
+    part1, w_out_half = tie(part1.reshape(own, width), w_out_half)
+    g_w_out = lax.psum_scatter(w_out_half, "tm", scatter_dimension=0)
+    g_w_out = lax.psum_scatter(g_w_out, "mp", scatter_dimension=0).astype(F32)
     back1, gain_grad1 = norm_rows_back(part1, std1, inv1, gain[1])
     grad1 = grad2 + back1
-    w_out_part, w_in_part = tie(w_out_part, w_in_part)
     gb1 = pair_gather(grad1.astype(BF16))
-    w_out_part = lax.psum_scatter(w_out_part, "tm", scatter_dimension=0)
-    g_w_out = lax.psum_scatter(w_out_part, "mp", scatter_dimension=0).astype(F32)
     t_out_x = send_x(gb2, mixed1)
     t_qkv_x = send_x(normed1, djoined1)
-    dmixed0 = dot_nn(gb1, ws_out).astype(BF16)
-    g_w_in = plane_scatter(w_in_part)
+    dmixed0 = dot_nt(gb1, ws_out).astype(BF16)
     go = dot_tn(gb1, mixed0).astype(BF16)
     djoined0 = space_attend_back(joined0, dmixed0, total0, frames_pair, patches, heads_s, scale)
     djoined0, t_out_x, t_qkv_x, go = tie(djoined0, t_out_x, t_qkv_x, go)
@@ -1768,7 +1847,7 @@
     )
     small = rows_of([jnp.zeros((1, width), F32), gain_grad1[None], gain_grad2, jnp.zeros((5, width), F32)])
     kept, landed, grad_tokens, small = settle(
-        djoined0, go, normed0.T, ws_qkv, std0, grad1, inv0, masked.astype(F32), gain[0], small
+        djoined0, go, turned0, ws_qkv, std0, grad1, inv0, masked.astype(F32), gain[0], small
     )
     grad_tokens = grad_tokens.reshape(tokens.shape).astype(F32)
 

time: 556 us -> 530 us (0.953)
  waiting for transfers between devices: 34.4 us -> 55.4 us
  matrix products: 26.8 us -> 12.7 us
  starting transfers between devices: 23.4 us -> 9.58 us
  local copies, waits for them, and re-layouts: 53.4 us -> 41.4 us
  other arithmetic: 31.1 us -> 22 us
    pallas_call x3 -> x2, Pallas kernels: 120 us -> 157 us  [the longest x1 91.4 us: enter(): pl.pallas_call(functools.partial(enter_kernel, scale), in_specs=[anywhere...]
    ppermute x6 -> x3, waiting for transfers between devices: 0.02 us -> 31.2 us  [hop_z(): lax.ppermute(v, AXES, device_pairs(lambda y, x, c, z: (y, x, c, (z + shif...]
    reduce_scatter x4 -> x2, waiting for transfers between devices: 29.7 us -> 0.02 us  [the longest x1 0.02 us: token_parallel(): g_w_out = lax.psum_scatter(w_out_half, 'tm', scatter_dimension=0)]
    pallas_call x2, Pallas kernels: 141 us -> 122 us  [time_call(): pl.pallas_call(functools.partial(time_kernel, back, scale, heads), in_spe...]
    all_gather x1, waiting for transfers between devices: 0.01 us -> 18.4 us  [token_parallel(): lax.all_gather(ff_in, ('mp', 'tm', 'x')).reshape(4, width, hidden_own)]
    pallas_call x1, Pallas kernels: 86.2 us -> 68.3 us  [settle(): pl.pallas_call(settle_kernel, in_specs=[whole] * 3 + [anywhere] * 3 + [wh...]
    ppermute x6 -> x3, starting transfers between devices: 17 us -> 2.84 us  [hop_z(): lax.ppermute(v, AXES, device_pairs(lambda y, x, c, z: (y, x, c, (z + shif...]
    dot_general x2 -> x0, matrix products: 10.8 us -> none  [dot_nn(): lax.dot_general(a, b, (((1,), (0,)), ((), ())), preferred_element_type=F32)]
  transfers between devices with their start and end apart: 20 -> 13, of which waited for: 3 -> 6; matrix products, arithmetic and copies ran while one was open for 16% -> 12% of each run, Pallas kernels for 48% -> 29%
where the time goes in v6:
time: 530 us; the launch traced here: 521 us
  Pallas kernels  365 us (69%)
  waiting for transfers between devices  55.4 us (10%)
  local copies, waits for them, and re-layouts  41.4 us (8%)
  other arithmetic  22 us (4%)
  between operations  14.9 us (3%)
  matrix products  12.7 us (2%)
  starting transfers between devices  9.58 us (2%)
    pallas_call x2, Pallas kernels, time_call(): pl.pallas_call(functools.partial(time_kernel, back, scale, heads), in_spe...  122 us
    pallas_call x1, Pallas kernels, enter(): pl.pallas_call(functools.partial(enter_kernel, scale), in_specs=[anywhere...  91.4 us
    pallas_call x1, Pallas kernels, settle(): pl.pallas_call(settle_kernel, in_specs=[whole] * 3 + [anywhere] * 3 + [wh...  68.3 us
    pallas_call x1, Pallas kernels, feed(): pl.pallas_call(feed_kernel, in_specs=[whole] * 5 + [anywhere] * 3, out_sp...  65.3 us
    ppermute x3, waiting for transfers between devices, hop_z(): lax.ppermute(v, AXES, device_pairs(lambda y, x, c, z: (y, x, c, (z + shif...  31.2 us
    all_gather x1, waiting for transfers between devices, token_parallel(): lax.all_gather(ff_in, ('mp', 'tm', 'x')).reshape(4, width, hidden_own)  18.4 us
    pallas_call x1, Pallas kernels, space_attend_back(): pl.pallas_call(functools.partial(space_attend_back_kernel, scale), grid=(...  18.1 us
    unnamed x64, local copies, waits for them, and re-layouts  11.7 us
  transfers between devices with their start and end apart: 13, of which 6 were waited for; matrix products, arithmetic and copies ran while one was open for 12% of the time, Pallas kernels for 29%

profile of v6, /device:TPU:9, one launch (start us, length us, event | category | flops | bytes accessed | tf_op | source)
XLA Modules:
  0.0 521.1 jit_solution(10746132365666333972)
XLA Ops:
  12.8 1.0 pad_maximum_fusion.15.later
  13.8 1.7 dynamic_slice.79
  16.4 91.4 %enter.1 = (bf16[1024,1536]{1,0:T(8,128)(2,1)}, bf16[512,1024]{1,0:T(8,128)(2,1)}, bf16[1024,1024]{1,0:T(8,128)(2,1)}, bf16[4,512,1024]{2,1,0:T(8,128)(2,1)}, bf...) custom-call(bf16[4,512,256]{2,1,0:T(8,128)(2,1)} %bitcast.89, ...), custom_call_target="tpu_custom_call" | custom-call | flops 10000000000 | bytes 100000000 | tf_op jit(solution)/shard_map/enter/pallas_call | solution.py:868
  108.6 2.9 copy.63
  111.6 1.3 copy.64
  112.9 2.7 copy.66.refs_3_.refs_5_
  116.0 1.5 fusion.41
  117.6 66.8 %time_forward.1 = (bf16[16,128,1024]{2,1,0:T(8,128)(2,1)}, bf16[16,128,768]{2,1,0:T(8,128)(2,1)}, bf16[16,128,256]{2,1,0:T(8,128)(2,1)S(1)}, f32[16,4,128]{2,1,0...) custom-call(bf16[4,128,1024]{2,1,0:T(8,128)(2,1)S(1)} %bitcast.61, ...), custom_call_target="tpu_custom_call" | custom-call | flops 10000000000 | bytes 100000000 | tf_op jit(solution)/shard_map/time_forward/pallas_call | solution.py:1162
  184.5 1.0 copy-done.7
  185.5 1.0 copy-done.11
  186.4 4.4 fusion.37
  190.8 18.4 %all-gather.3.cloned.1.call-done = bf16[4096,512]{1,0:T(8,128)(2,1)} async-done(((bf16[256,512]{1,0:T(8,128)(2,1)}), bf16[4096,512]{1,0:T(8,128)(2,1)}) %all-gather.3.cloned.1.call-update) | async-done | bytes 4194320 | tf_op jit(solution)/shard_map/all_gather | solution.py:1754
  209.2 65.3 %feed.1 = (bf16[2,4,256,512]{3,2,1,0:T(8,128)(2,1)}, bf16[2,4,256,512]{3,2,1,0:T(8,128)(2,1)}, f32[512,1024]{1,0:T(8,128)}, bf16[512,1024]{1,0:T(8,128)(2,1)}, b...) custom-call(f32[512,1024]{1,0:T(8,128)} %get-tuple-element.55.resid, f32[512,1024]{1,0:T(8,128)} %bitcast.92, ...), custom_call_target="tpu_custom_call" | custom-call | flops 25999998976 | bytes 100000000 | tf_op jit(solution)/shard_map/feed/pallas_call | solution.py:1368
  274.6 1.2 copy-done.9
  275.8 1.2 copy-done.10
  277.1 55.1 %time_back.1 = (bf16[16,128,1024]{2,1,0:T(8,128)(2,1)}, bf16[16,128,768]{2,1,0:T(8,128)(2,1)}, f32[4,128,1024]{2,1,0:T(8,128)}, f32[256,512]{1,0:T(8,128)S(1)}, bf16[4,512,256]{2,1,0:T(8,128)(2,1)S(1)}) custom-call(bf16[4,128,1024]{2,1,0:T(8,128)(2,1)S(1)} %bitcast.64, bf16[512,1024]{1,0:T(8,128)(2,1)S(1)} %copy-done.10, ...), custom_call_target="tpu_custom_call" | custom-call | flops 10000000000 | bytes 100000000 | tf_op jit(solution)/shard_map/time_back/pallas_call | solution.py:1162
  332.3 3.0 multiply_reduce_fusion
  335.7 3.6 fusion.36
  339.4 2.2 collective-permute-start.1
  341.8 0.9 copy-done.8
  342.8 1.5 fusion.15
  344.3 1.0 collective-permute-start.2
  346.0 2.9 fusion.12
  348.9 1.0 collective-permute-start.3
  351.4 3.0 fusion.2
  354.4 2.3 convolution_convert_fusion.go
  356.7 2.3 convolution_convert_fusion.1.grad_ref
  358.9 18.1 %space_attend_back.1.dj = bf16[1024,1536]{1,0:T(8,128)(2,1)} custom-call(bf16[1024,1536]{1,0:T(8,128)(2,1)} %get-tuple-element.71.qkv_ref, bf16[1024,512]{1,0:T(8,128)(2,1)} %convolution_convert_fusion.1.grad_ref, f32[8,8,128]{2,1,0:T(8,128)} %get-tuple-element.79.total_ref), custom_call_target="tpu_custom_call" | custom-call | flops 2684354560 | bytes 10485760 | tf_op jit(solution)/shard_map/space_attend_back/pallas_call | solution.py:518
  377.1 68.3 %settle.1 = (f32[128,512]{1,0:T(8,128)}, f32[128,512]{1,0:T(8,128)}, bf16[4,512,256]{2,1,0:T(8,128)(2,1)}, f32[8,256]{1,0:T(8,128)}) custom-call(bf16[1024,1536]{1,0:T(8,128)(2,1)} %space_attend_back.1.dj, bf16[1024,512]{1,0:T(8,128)(2,1)} %convolution_convert_fusion.go, bf16[1024,1024]{1,0:T(8,128)(2,1)} %get-tuple-element.87.lhs, ...), custom_call_target="tpu_custom_call" | custom-call | flops 10000000000 | bytes 100000000 | tf_op jit(solution)/shard_map/settle/pallas_call | solution.py:1631
  445.4 0.9 slice.111
  447.2 0.9 slice.112
  449.8 1.3 dynamic-slice_convert_fusion.8
  451.1 1.8 convert_add_fusion
  454.1 1.4 collective-permute-start.5
  457.3 1.5 collective-permute-start.4
  458.8 1.1 constant_dynamic-slice_fusion
  461.9 15.4 %collective-permute-done.5 = bf16[512,256]{1,0:T(8,128)(2,1)} collective-permute-done((bf16[512,256]{1,0:T(8,128)(2,1)}, bf16[512,256]{1,0:T(8,128)(2,1)}, u32[]{:S(2)}, u32[]{:S(2)}) %collective-permute-start.5) | collective-permute-done | bytes 262176 | tf_op jit(solution)/shard_map/ppermute | solution.py:438
  477.3 6.5 %collective-permute-done.6 = bf16[512,256]{1,0:T(8,128)(2,1)} collective-permute-done((bf16[512,256]{1,0:T(8,128)(2,1)}, bf16[512,256]{1,0:T(8,128)(2,1)}, u32[]{:S(2)}, u32[]{:S(2)}) %collective-permute-start.6) | collective-permute-done | bytes 262176 | tf_op jit(solution)/shard_map/ppermute | solution.py:438
  483.8 9.3 %collective-permute-done.4 = bf16[512,256]{1,0:T(8,128)(2,1)} collective-permute-done((bf16[512,256]{1,0:T(8,128)(2,1)}, bf16[512,256]{1,0:T(8,128)(2,1)}, u32[]{:S(2)}, u32[]{:S(2)}) %collective-permute-start.4) | collective-permute-done | bytes 262176 | tf_op jit(solution)/shard_map/ppermute | solution.py:438
  493.1 1.4 fusion.23
  494.9 4.3 collective-permute-done.7
  499.2 1.5 collective-permute-start.8
  503.6 2.8 convert.53
  508.4 1.0 bitcast_convert_fusion
  509.7 1.4 collective-permute-done.9
  511.2 1.0 maximum_select_fusion
  512.1 1.0 copy.81
  513.1 1.0 copy.89
  (139 shorter events, 23.9 us)
Async XLA Ops:
  7.2 4.1 copy-start
  7.2 202.1 %all-gather.3.cloned.1.call-start = ((), (), s32[]{:S(2)}) async-start(), calls=%async_computation.4 | async-start | bytes 4456448 | tf_op jit(solution)/shard_map/all_gather | solution.py:1754
  8.8 6.6 %collective-permute-start = (s32[2,1040]{1,0:T(2,128)S(1)}, s32[2,1040]{1,0:T(2,128)S(1)}, u32[]{:S(2)}, u32[]{:S(2)}) collective-permute-start(s32[2,1040]{1,0:T(2,128)S(1)} %constant_dynamic-update-slice_fusion), channel_id=1, source_target_pairs={{0,4},{1,5},{2,6},{3,7},{4,0},{5,1},{6,2},{7,3},{8,12},{9,13},{10,... | collective-permute-start | bytes 24968 | tf_op jit(solution)/shard_map/ppermute | solution.py:434
  11.1 1.1 copy-start.24
  107.8 351.0 %reduce-scatter.3.cloned.1.call-start = ((), (), s32[]{:S(2)}) async-start(), calls=%async_computation.2 | async-start | bytes 3145728 | tf_op jit(solution)/shard_map/reduce_scatter | solution.py:1824
  112.9 3.0 copy-start.21
  112.9 4.7 copy-start.5
  112.9 4.7 copy-start.6
  115.9 68.6 %copy-start.3 = (bf16[1024,256]{1,0:T(8,128)(2,1)}, bf16[1024,256]{1,0:T(8,128)(2,1)S(1)}, u32[]{:S(2)}) copy-start(bf16[1024,256]{1,0:T(8,128)(2,1)S(1)} %copy.67.refs_4_.refs_6_) | copy-start | bytes 1572868
  184.4 1.0 copy-start.7
  185.5 1.0 copy-start.11
  209.2 65.4 %copy-start.2 = (bf16[1024,768]{1,0:T(8,128)(2,1)S(1)}, bf16[1024,768]{1,0:T(8,128)(2,1)}, u32[]{:S(2)}) copy-start(bf16[1024,768]{1,0:T(8,128)(2,1)} %copy.66.refs_3_.refs_5_) | copy-start | bytes 4718596
  209.2 65.4 %copy-start.4 = (bf16[1024,256]{1,0:T(8,128)(2,1)S(1)}, bf16[1024,256]{1,0:T(8,128)(2,1)}, u32[]{:S(2)}) copy-start(bf16[1024,256]{1,0:T(8,128)(2,1)} %copy-done.3) | copy-start | bytes 1572868
  274.6 1.2 copy-start.9
  275.8 1.2 copy-start.10
  332.2 176.2 %reduce-scatter.5.cloned.1.call-start = ((), (), s32[]{:S(2)}) async-start(), calls=%async_computation.3 | async-start | bytes 1310720 | tf_op jit(solution)/shard_map/reduce_scatter | solution.py:1825
  332.2 3.0 copy-start.12
  332.3 3.5 copy-start.13
  335.7 5.8 %copy-start.14 = (bf16[16,128,1024]{2,1,0:T(8,128)(2,1)S(1)}, bf16[16,128,1024]{2,1,0:T(8,128)(2,1)}, u32[]{:S(2)}) copy-start(bf16[16,128,1024]{2,1,0:T(8,128)(2,1)} %get-tuple-element.80) | copy-start | bytes 12582916
  339.4 15.1 %collective-permute-start.1 = (bf16[512,1024]{1,0:T(8,128)(2,1)S(1)}, bf16[512,1024]{1,0:T(8,128)(2,1)S(1)}, u32[]{:S(2)}, u32[]{:S(2)}) collective-permute-start(bf16[512,1024]{1,0:T(8,128)(2,1)S(1)} %get-tuple-element.133), channel_id=1, source_target_pairs={{0,4},{1,5},{2,6},{3,7},{4,0},{5,1},{6,2},{7,3},{8,12},{9,13},{10,... | collective-permute-start | bytes 3145736 | tf_op jit(solution)/shard_map/ppermute | solution.py:434
  341.5 1.2 copy-start.8
  342.7 2.5 copy-start.15
  342.7 2.5 copy-start.16
  342.7 2.5 copy-start.17
  342.8 2.5 copy-start.18
  342.8 3.3 copy-start.25
  344.3 32.8 %collective-permute-start.2 = (bf16[512,256]{1,0:T(8,128)(2,1)}, bf16[512,256]{1,0:T(8,128)(2,1)S(1)}, u32[]{:S(2)}, u32[]{:S(2)}) collective-permute-start(bf16[512,256]{1,0:T(8,128)(2,1)} %fusion.15), channel_id=1, source_target_pairs={{0,8},{1,9},{2,10},{3,11},{4,12},{5,13},{6,14},{7,15},{8,0},{9,1},... | collective-permute-start | bytes 786440 | tf_op jit(solution)/shard_map/ppermute | solution.py:430
  346.0 3.9 copy-start.22
  348.9 28.2 %collective-permute-start.3 = (bf16[512,768]{1,0:T(8,128)(2,1)}, bf16[512,768]{1,0:T(8,128)(2,1)}, u32[]{:S(2)}, u32[]{:S(2)}) collective-permute-start(bf16[512,768]{1,0:T(8,128)(2,1)} %fusion.12), channel_id=1, source_target_pairs={{0,8},{1,9},{2,10},{3,11},{4,12},{5,13},{6,14},{7,15},{8,0},{9,1},... | collective-permute-start | bytes 2359304 | tf_op jit(solution)/shard_map/ppermute | solution.py:430
  351.3 3.1 copy-start.27
  354.4 2.3 copy-start.26
  452.8 5.9 %copy-start.19 = (f32[128,384]{0,1:T(8,128)S(1)}, f32[128,384]{0,1:T(8,128)}, u32[]{:S(2)}) copy-start(f32[128,384]{0,1:T(8,128)} %copy.72) | copy-start | bytes 589828
  452.8 5.9 %copy-start.20 = (f32[128,384]{0,1:T(8,128)S(1)}, f32[128,384]{0,1:T(8,128)}, u32[]{:S(2)}) copy-start(f32[128,384]{0,1:T(8,128)} %copy.73) | copy-start | bytes 589828
  454.1 23.1 %collective-permute-start.5 = (bf16[512,256]{1,0:T(8,128)(2,1)}, bf16[512,256]{1,0:T(8,128)(2,1)}, u32[]{:S(2)}, u32[]{:S(2)}) collective-permute-start(bf16[512,256]{1,0:T(8,128)(2,1)} %pad_maximum_fusion.18), channel_id=1, source_target_pairs={{0,2},{1,3},{2,0},{3,1},{4,6},{5,7},{6,4},{7,5},{8,10},{9,11},{10,... | collective-permute-start | bytes 786440 | tf_op jit(solution)/shard_map/ppermute | solution.py:438
  456.4 27.4 %collective-permute-start.6 = (bf16[512,256]{1,0:T(8,128)(2,1)}, bf16[512,256]{1,0:T(8,128)(2,1)}, u32[]{:S(2)}, u32[]{:S(2)}) collective-permute-start(bf16[512,256]{1,0:T(8,128)(2,1)} %pad_maximum_fusion.19), channel_id=1, source_target_pairs={{0,3},{1,0},{2,1},{3,2},{4,7},{5,4},{6,5},{7,6},{8,11},{9,8},{10,9... | collective-permute-start | bytes 786440 | tf_op jit(solution)/shard_map/ppermute | solution.py:438
  457.3 35.8 %collective-permute-start.4 = (bf16[512,256]{1,0:T(8,128)(2,1)}, bf16[512,256]{1,0:T(8,128)(2,1)}, u32[]{:S(2)}, u32[]{:S(2)}) collective-permute-start(bf16[512,256]{1,0:T(8,128)(2,1)} %pad_maximum_fusion.17), channel_id=1, source_target_pairs={{0,1},{1,2},{2,3},{3,0},{4,5},{5,6},{6,7},{7,4},{8,9},{9,10},{10,1... | collective-permute-start | bytes 786440 | tf_op jit(solution)/shard_map/ppermute | solution.py:438
  493.1 7.6 %copy-start.23 = (f32[8,256]{1,0:T(8,128)S(1)}, f32[8,256]{1,0:T(8,128)}, u32[]{:S(2)}) copy-start(f32[8,256]{1,0:T(8,128)} %get-tuple-element.93) | copy-start | bytes 24580
  494.6 4.5 collective-permute-start.7
  499.2 7.3 %collective-permute-start.8 = (bf16[128,512]{1,0:T(8,128)(2,1)S(1)}, bf16[128,512]{1,0:T(8,128)(2,1)S(1)}, u32[]{:S(2)}, u32[]{:S(2)}) collective-permute-start(bf16[128,512]{1,0:T(8,128)(2,1)S(1)} %fusion.26), channel_id=1, source_target_pairs={{0,4},{1,5},{2,6},{3,7},{4,0},{5,1},{6,2},{7,3},{8,12},{9,13},{10,... | collective-permute-start | bytes 393224 | tf_op jit(solution)/shard_map/ppermute | solution.py:434
  509.5 1.6 collective-permute-start.9
  511.1 3.0 copy-start.1
Sparse Core Ops, SparseCore 0:
  107.9 101.2 all-gather.2
  332.3 32.9 reduce-scatter.2
  459.0 37.1 reduce-scatter.4

commit v7 on v6

--- a/solution.py
+++ b/solution.py
@@ -494,40 +494,6 @@
 
 
 PAIR = 2 * HEAD_DIM
-
-
-def space_attend_back_kernel(scale, qkv_ref, grad_ref, total_ref, out_ref):
-    for i in range(grad_ref.shape[1] // PAIR):
-        q, k, v = (qkv_ref[:, (3 * i + part) * PAIR : (3 * i + part + 1) * PAIR] for part in range(3))
-        totals = [total_ref[0, 2 * i + h : 2 * i + h + 1, :] for h in range(2)]
-        grads = attend_pair_back(q, k, v, grad_ref[:, i * PAIR : (i + 1) * PAIR], totals, None, scale)
-        for part in range(3):
-            out_ref[:, (3 * i + part) * PAIR : (3 * i + part + 1) * PAIR] = grads[part].astype(BF16)
-
-
-def attention_cost(groups, rows, heads, products):
-    return pl.CostEstimate(
-        flops=8 * products * groups * heads * rows * rows * HEAD_DIM,
-        transcendentals=groups * heads * rows * rows,
-        bytes_accessed=2 * groups * rows * heads * HEAD_DIM * 2 * products,
-    )
-
-
-def space_attend_back(qkv, grad, total, frames, patches, heads, scale):
-    width = heads * HEAD_DIM
-    return pl.pallas_call(
-        functools.partial(space_attend_back_kernel, scale),
-        grid=(frames,),
-        in_specs=[
-            pl.BlockSpec((patches, 3 * width), lambda i: (i, 0)),
-            pl.BlockSpec((patches, width), lambda i: (i, 0)),
-            pl.BlockSpec((1, heads, patches), lambda i: (i, 0, 0)),
-        ],
-        out_specs=pl.BlockSpec((patches, 3 * width), lambda i: (i, 0)),
-        out_shape=jax.ShapeDtypeStruct((frames * patches, 3 * width), BF16),
-        cost_estimate=attention_cost(frames, patches, heads, 5),
-        name="space_attend_back",
-    )(qkv, grad, total)
 
 
 def enter_kernel(
@@ -1395,13 +1361,19 @@
     )(resid, delta, upstream, masked, gain, w_in, w_out, w_far)
 
 
-def settle_kernel(
-    dj, go, lhs, weight_hbm, std_hbm, base_hbm, inverse, masked, gain, small_in,
-    kept_out, landed_out, rows_out, small_out,
-    weight, std, base, grads, a1_out, a1_in, b1_out, b1_in, a2_out, a2_in, b2_out, b2_in, z_out, z_in,
+def leave_kernel(
+    scale,
+    part_hbm, next_hbm, grad_hbm, out_hbm, joined_hbm, mixed_hbm, lhs_hbm, weight_hbm, std_hbm, time_hbm, feed_hbm, feed_in_hbm,
+    totals, inverse_next, inverse, masked, gain_next, gain, small_in,
+    kept_out, landed_out, feed_kept, feed_landed, time_out, rows_out, small_out,
+    part, std, base, w_out, dj, mixed, lhs, weight, low_grads, turned, dmixed, go,
+    t_own, t_in, tz_out, tz_in, t_total, ty_out, ty_in, tc_out, tc_in,
+    f_own, f_in, fz_out, fz_in, f_total, f_other, fc_out, fc_in,
+    grads, a1_out, a1_in, b1_out, b1_in, a2_out, a2_in, b2_out, b2_in, z_out, z_in,
     half_out, half_in, ready, core_out, core_in, sums, sum_out, sum_in, share_in,
     a1_send, a1_recv, b1_send, b1_recv, a2_send, a2_recv, b2_send, b2_recv, z_send, z_recv,
     h_send, h_recv, r_send, r_recv, c_send, c_recv, s_send, s_recv, p_send, p_recv, local,
+    g_send, g_recv, tx_send, tx_recv, tz_send, tz_recv, ty_send, ty_recv, fy_send, fy_recv, fz_send, fz_recv, t_local, f_local, fetched,
 ):
     y, x, c, z = (lax.axis_index(name) for name in AXES)
     near_y, near_x, pair = (1 - y, x, c, z), (y, 1 - x, c, z), (y, x, 1 - c, z)
@@ -1409,14 +1381,18 @@
     third = go.shape[1] // 4
     wide = 3 * third
     two = 2 * third
+    slab = 128
 
     fetches = [
-        pltpu.make_async_copy(weight_hbm, weight, local.at[0]),
-        pltpu.make_async_copy(std_hbm, std, local.at[1]),
-        pltpu.make_async_copy(base_hbm, base, local.at[2]),
+        pltpu.make_async_copy(src, dst, fetched.at[i])
+        for i, (src, dst) in enumerate((
+            (part_hbm, part), (next_hbm, std), (grad_hbm, base), (out_hbm, w_out), (joined_hbm, dj), (mixed_hbm, mixed),
+            (lhs_hbm, lhs), (weight_hbm, weight), (feed_in_hbm, f_other),
+        ))
     ]
     for copy in fetches:
         copy.start()
+    fetch_std = pltpu.make_async_copy(std_hbm, std, fetched.at[9])
 
     barrier = pltpu.get_barrier_semaphore()
     for dc in range(2):
@@ -1432,6 +1408,122 @@
             src_ref=src, dst_ref=dst, send_sem=send, recv_sem=recv, device_id=peer, device_id_type=MESH
         )
 
+    def at(i, length):
+        return pl.ds(pl.multiple_of(i * length, length), length)
+
+    def along(r):
+        return (y, x, c, (z + r) % 4)
+
+    def time_x(yb):
+        return remote(time_hbm.at[at(2 * yb + 1 - x, BLK)], t_in.at[yb], tx_send.at[yb], tx_recv.at[yb], near_x)
+
+    def time_keep(yb):
+        return pltpu.make_async_copy(time_hbm.at[at(2 * yb + x, BLK)], t_own.at[yb], t_local.at[yb])
+
+    def time_z(r):
+        return remote(tz_out.at[r], tz_in.at[r], tz_send.at[r], tz_recv.at[r], along(r))
+
+    def feed_y(r):
+        s = (z + r) % 4
+        return remote(feed_hbm.at[1 - y, s], f_in.at[r], fy_send.at[r], fy_recv.at[r], near_y)
+
+    def feed_keep(r):
+        return pltpu.make_async_copy(feed_hbm.at[y, (z + r) % 4], f_own.at[r], f_local.at[r])
+
+    def feed_z(r):
+        return remote(fz_out.at[r], fz_in.at[r], fz_send.at[r], fz_recv.at[r], along(r))
+
+    for r in (1, 2, 3, 0):
+        feed_y(r).start()
+        feed_keep(r).start()
+    for yb in range(2):
+        time_x(yb).start()
+        time_keep(yb).start()
+
+    def feed_step(r):
+        feed_y(r).wait_recv()
+        feed_keep(r).wait()
+        total = f_own[r].astype(F32) + f_in[r].astype(F32)
+        if r == 0:
+            f_total[...] = total
+        else:
+            fz_out[r] = total.astype(BF16)
+            feed_z(r).start()
+
+    def time_step():
+        for yb in range(2):
+            time_x(yb).wait_recv()
+            time_keep(yb).wait()
+        for r in (1, 2, 3, 0):
+            piece_at = at((z + r) % 4, BLK)
+            for yb in range(2):
+                total = t_own[yb, :, piece_at].astype(F32) + t_in[yb, :, piece_at].astype(F32)
+                if r == 0:
+                    t_total[yb] = total
+                else:
+                    tz_out[r, yb] = total.astype(BF16)
+            if r:
+                time_z(r).start()
+
+    step = own // 2
+    for copy in fetches[:3]:
+        copy.wait()
+
+    def norm_back(grad, standard, weights, inv):
+        inner = grad * weights
+        mean = jnp.mean(inner, axis=-1, keepdims=True)
+        slope = jnp.mean(inner * standard, axis=-1, keepdims=True)
+        return (inner - mean - standard * slope) * inv
+
+    def after_time(i, total):
+        rows = at(i, step)
+        grad, standard = part[rows], std[rows]
+        full = base[rows] + norm_back(grad, standard, gain_next[...], inverse_next[rows])
+        base[rows] = full
+        low_grads[rows] = full.astype(BF16)
+        return total + jnp.sum(grad * standard, axis=0, keepdims=True)
+
+    zero = jnp.zeros((1, std.shape[1]), F32)
+    next_grad = lax.fori_loop(0, 2, after_time, zero)
+    give = remote(low_grads.at[pl.ds(0, own)], low_grads.at[pl.ds(own, own)], g_send.at[0], g_recv.at[0], pair)
+    give.start()
+    fetch_std.start()
+    for copy in fetches[3:6]:
+        copy.wait()
+
+    def attend(i, carry):
+        rows = at(i, slab)
+        for h in range(mixed.shape[1] // PAIR):
+            places = [pl.ds((3 * h + j) * PAIR, PAIR) for j in range(3)]
+            q, k, v = (dj[rows, place] for place in places)
+            lines = [totals[i, 2 * h + j : 2 * h + j + 1, :] for j in range(2)]
+            found = attend_pair_back(q, k, v, dmixed[rows, h * PAIR : (h + 1) * PAIR], lines, None, scale)
+            for place, value in zip(places, found):
+                dj[rows, place] = value.astype(BF16)
+        return carry
+
+    def turn(i, carry):
+        turned[:, at(i, slab)] = low_grads[at(i, slab)].T
+        return carry
+
+    def attend_half(t):
+        rows = pl.ds(t * own, own)
+        dmixed[rows] = dot_nt(low_grads[rows], w_out[...]).astype(BF16)
+        lax.fori_loop(t * own // slab, (t + 1) * own // slab, attend, 0)
+        lax.fori_loop(t * own // slab, (t + 1) * own // slab, turn, 0)
+
+    attend_half(0)
+    feed_step(1)
+    feed_step(2)
+    give.wait_recv()
+    attend_half(1)
+    feed_step(3)
+    time_step()
+    feed_step(0)
+    for copy in fetches[6:]:
+        copy.wait()
+    go[...] = dot_nn(turned[...], mixed[...]).astype(BF16)
+
     def block(yb, xb):
         return pl.ds(pl.multiple_of(BLK * (2 * yb + xb), BLK), BLK)
 
@@ -1448,7 +1540,7 @@
         return remote(b2_out.at[i], b2_in.at[i], b2_send.at[i], b2_recv.at[i], near_x)
 
     def to_z(r):
-        return remote(z_out.at[r], z_in.at[r], z_send.at[r], z_recv.at[r], (y, x, c, (z + r) % 4))
+        return remote(z_out.at[r], z_in.at[r], z_send.at[r], z_recv.at[r], along(r))
 
     def piece(i, carry):
         s = (z + i + 1) % 4
@@ -1483,9 +1575,6 @@
             z_out[i + 1] = grads[i, block(y, x), :].astype(BF16)
             to_z(i + 1).start()
 
-    step = own // 2
-    fetches[0].wait()
-
     def away(i, carry):
         rows = pl.ds(pl.multiple_of(own + i * step, step), step)
         half_out[pl.ds(pl.multiple_of(i * step, step), step)] = dot_nt(dj[rows], weight[...]).astype(BF16)
@@ -1495,19 +1584,16 @@
     swap = remote(half_out, half_in, h_send.at[0], h_recv.at[0], pair)
     swap.start()
     second(0)
-    for copy in fetches[1:]:
-        copy.wait()
+    fetch_std.wait()
     sums[...] = small_in[...]
+    sums[1:2] = next_grad
     swap.wait_recv()
 
     def home(i, totals):
         rows = pl.ds(pl.multiple_of(i * step, step), step)
         grad = dot_nt(dj[rows], weight[...]) + half_in[rows].astype(F32)
         standard = std[rows]
-        inner = grad * gain[...]
-        mean = jnp.mean(inner, axis=-1, keepdims=True)
-        along = jnp.mean(inner * standard, axis=-1, keepdims=True)
-        full = base[rows] + (inner - mean - standard * along) * inverse[rows]
+        full = base[rows] + norm_back(grad, standard, gain[...], inverse[rows])
         hide = masked[rows] > 0.0
         ready[rows] = jnp.where(hide, 0.0, full).astype(BF16)
         return (
@@ -1515,7 +1601,6 @@
             totals[1] + jnp.sum(jnp.where(hide, full, 0.0), axis=0, keepdims=True),
         )
 
-    zero = jnp.zeros((1, std.shape[1]), F32)
     gain_grad, embed_grad = lax.fori_loop(0, 2, home, (zero, zero))
     sums[0:1] = gain_grad
     sums[3:4] = embed_grad
@@ -1570,6 +1655,30 @@
     for r in (1, 2, 3):
         deal(r).start()
     third_step(3)
+    parity = BLK // 2
+
+    for r in (1, 2, 3):
+        time_z(r).wait_recv()
+        t_total[...] = t_total[...] + tz_in[r].astype(F32)
+    ty_out[...] = t_total[1 - y].astype(BF16)
+    swap_y = remote(ty_out, ty_in, ty_send.at[0], ty_recv.at[0], near_y)
+    swap_y.start()
+    for r in (1, 2, 3):
+        feed_z(r).wait_recv()
+        f_total[...] = f_total[...] + fz_in[r].astype(F32)
+    fc_out[0] = f_other[at(1 - c, parity)].astype(BF16)
+    fc_out[1] = f_total[at(1 - c, parity)].astype(BF16)
+    swap_feed = remote(fc_out, fc_in, c_send.at[1], c_recv.at[1], pair)
+    swap_feed.start()
+    feed_kept[0] = f_other[at(c, parity)]
+    feed_kept[1] = f_total[at(c, parity)]
+    swap_y.wait_recv()
+    tc_out[0] = t_total[y, at(1 - c, parity)].astype(BF16)
+    tc_out[1] = ty_in[at(1 - c, parity)]
+    swap_time = remote(tc_out, tc_in, c_send.at[2], c_recv.at[2], pair)
+    swap_time.start()
+    time_out[0, 0] = t_total[y, at(c, parity)]
+    time_out[0, 1] = ty_in[at(c, parity)].astype(F32)
     for r in (1, 2, 3):
         to_z(r).wait_recv()
     total = grads[3, block(y, x), :]
@@ -1590,11 +1699,22 @@
         deal(r).wait_recv()
         result = result + share_in[r]
     small_out[...] = result
+    swap_feed.wait_recv()
+    feed_landed[...] = fc_in[...].astype(F32)
+    swap_time.wait_recv()
+    time_out[1] = tc_in[...].astype(F32)
     last.wait_recv()
     landed_out[...] = core_in[...].astype(F32)
 
-    last.wait_send()
-    swap.wait_send()
+    for copy in (last, swap, give, swap_y, swap_feed, swap_time):
+        copy.wait_send()
+    for yb in range(2):
+        time_x(yb).wait_send()
+    for r in range(4):
+        feed_y(r).wait_send()
+    for r in (1, 2, 3):
+        time_z(r).wait_send()
+        feed_z(r).wait_send()
     for i in range(4):
         for copy in (a1(i), b1(i), a2(i), b2(i)):
             copy.wait_send()
@@ -1614,13 +1734,18 @@
         pl.when(jnp.logical_not(from_self))(landed)
 
 
-def settle(dj, go, lhs, weight, std, base, inverse, masked, gain, small):
+def leave(
+    part, std_next, grad, w_out, joined, mixed, lhs, weight, std, g_time, g_out, g_in,
+    totals, inverse_next, inverse, masked, gain_next, gain, small, scale,
+):
     own, features = std.shape
-    cols4 = go.shape[1]
+    cols4 = mixed.shape[1]
     quarter = cols4 // 4
+    units = g_in.shape[1]
     dma = pltpu.SemaphoreType.DMA
     anywhere = pl.BlockSpec(memory_space=pl.ANY)
     whole = pl.BlockSpec(memory_space=pltpu.VMEM)
+    parity = BLK // 2
 
     def low(*shape):
         return pltpu.VMEM(shape, BF16)
@@ -1629,32 +1754,47 @@
         return pltpu.VMEM(shape, F32)
 
     return pl.pallas_call(
-        settle_kernel,
-        in_specs=[whole] * 3 + [anywhere] * 3 + [whole] * 4,
-        out_specs=[whole, whole, anywhere, whole],
+        functools.partial(leave_kernel, scale),
+        in_specs=[anywhere] * 12 + [whole] * 7,
+        out_specs=[whole] * 5 + [anywhere, whole],
         out_shape=[
-            jax.ShapeDtypeStruct((BLK // 2, cols4), F32),
-            jax.ShapeDtypeStruct((BLK // 2, cols4), F32),
+            jax.ShapeDtypeStruct((parity, cols4), F32),
+            jax.ShapeDtypeStruct((parity, cols4), F32),
+            jax.ShapeDtypeStruct((2, parity, units), F32),
+            jax.ShapeDtypeStruct((2, parity, units), F32),
+            jax.ShapeDtypeStruct((2, 2, parity, BLK), F32),
             jax.ShapeDtypeStruct((4, own, BLK), BF16),
             jax.ShapeDtypeStruct((8, BLK), F32),
         ],
         scratch_shapes=[
-            low(*weight.shape), high(own, features), high(own, features), high(4, features, cols4),
+            high(own, features), high(own, features), high(own, features), low(*w_out.shape), low(*joined.shape),
+            low(*mixed.shape), low(*lhs.shape), low(*weight.shape), low(2 * own, features), low(features, 2 * own),
+            low(*mixed.shape), low(features, cols4),
+            low(2, BLK, features), low(2, BLK, features), low(4, 2, BLK, BLK), low(4, 2, BLK, BLK), high(2, BLK, BLK),
+            low(BLK, BLK), low(BLK, BLK), low(2, parity, BLK), low(2, parity, BLK),
+            low(4, BLK, units), low(4, BLK, units), low(4, BLK, units), low(4, BLK, units),
+            high(BLK, units), high(BLK, units), low(2, parity, units), low(2, parity, units),
+            high(4, features, cols4),
             low(4, 2, BLK, 2 * quarter), low(4, 2, BLK, 2 * quarter), low(4, 2, BLK, 2 * quarter), low(4, 2, BLK, 2 * quarter),
             low(4, BLK, 2 * quarter), low(4, BLK, 2 * quarter), low(4, BLK, 2 * quarter), low(4, BLK, 2 * quarter),
             low(4, BLK, cols4), low(4, BLK, cols4),
             low(own, features), low(own, features), low(own, features),
-            low(BLK // 2, cols4), low(BLK // 2, cols4),
+            low(parity, cols4), low(parity, cols4),
             high(8, features), high(4, 8, features), high(3, 8, features), high(4, 8, BLK),
         ]
         + [dma((4,))] * 10
-        + [dma((1,)), dma((1,)), dma((4,)), dma((4,)), dma((1,)), dma((1,)), dma((3,)), dma((3,)), dma((4,)), dma((4,)), dma((4,))],
+        + [dma((1,)), dma((1,)), dma((4,)), dma((4,)), dma((3,)), dma((3,)), dma((3,)), dma((3,)), dma((4,)), dma((4,)), dma((4,))]
+        + [dma((1,)), dma((1,)), dma((2,)), dma((2,)), dma((4,)), dma((4,)), dma((1,)), dma((1,))]
+        + [dma((4,)), dma((4,)), dma((4,)), dma((4,)), dma((2,)), dma((4,)), dma((10,))],
         compiler_params=pltpu.CompilerParams(
-            collective_id=3, has_side_effects=True, vmem_limit_bytes=56 * 1024 * 1024
+            collective_id=3, has_side_effects=True, vmem_limit_bytes=62 * 1024 * 1024
         ),
-        cost_estimate=pl.CostEstimate(flops=10**10, transcendentals=10**6, bytes_accessed=10**8),
-        name="settle",
-    )(dj, go, lhs, weight, std, base, inverse, masked, gain, small)
+        cost_estimate=pl.CostEstimate(flops=2 * 10**10, transcendentals=10**6, bytes_accessed=10**8),
+        name="leave",
+    )(
+        part, std_next, grad, w_out, joined, mixed, lhs, weight, std, g_time, g_out, g_in,
+        totals, inverse_next, inverse, masked, gain_next, gain, small,
+    )
 
 
 def tie(*values):
@@ -1760,8 +1900,6 @@
         return v[:own] + hop_c(v[own:].astype(BF16)).astype(F32)
 
     half = qkv_space.shape[2] // 2
-    heads_s = 4 * half // HEAD_DIM
-    frames_pair = 2 * frames_own
     normed1, joined1, mixed1, total1, delta, upstream, wf_far = time_call(
         False,
         normed1.reshape(frames_own, patches, width),
@@ -1778,32 +1916,6 @@
         resid1, delta.reshape(own, width), upstream, masked.astype(F32), gain[2], wf_in, wf_out, wf_far
     )
 
-    def send_x(lhs, rhs):
-        there = jnp.where(x == 0, cols([lhs[:, BLK : 2 * BLK], lhs[:, 3 * BLK :]]), cols([lhs[:, :BLK], lhs[:, 2 * BLK : 3 * BLK]]))
-        return hop_x(dot_tn(there, rhs).astype(BF16))
-
-    def keep_x(lhs, rhs, landed):
-        here = jnp.where(x == 1, cols([lhs[:, BLK : 2 * BLK], lhs[:, 3 * BLK :]]), cols([lhs[:, :BLK], lhs[:, 2 * BLK : 3 * BLK]]))
-        return dot_tn(here, rhs) + landed.astype(F32)
-
-    def mine_y(v):
-        return jnp.where(y == 0, v[:BLK], v[BLK:])
-
-    def other_y(v):
-        return jnp.where(y == 1, v[:BLK], v[BLK:])
-
-    def reduce_z(pieces):
-        total = pieces[0]
-        for r in (1, 2, 3):
-            total = total + hop_z(pieces[r].astype(BF16), r).astype(F32)
-        return total
-
-    def swap_c(total):
-        rows = BLK // 2
-        kept = lax.dynamic_slice_in_dim(total, c * rows, rows, 0)
-        sent = hop_c(lax.dynamic_slice_in_dim(total, (1 - c) * rows, rows, 0).astype(BF16))
-        return (kept, sent.astype(F32))
-
     def by_core(kept, landed):
         return jnp.where(c == 0, jnp.concatenate([kept, landed], -1), jnp.concatenate([landed, kept], -1))
 
@@ -1820,34 +1932,13 @@
     block_out = block_out.reshape(tokens.shape)
     gb2 = gb2.reshape(4 * own, width)
     djoined1 = djoined1.reshape(4 * own, -1)
-    part1, w_out_half = tie(part1.reshape(own, width), w_out_half)
-    g_w_out = lax.psum_scatter(w_out_half, "tm", scatter_dimension=0)
-    g_w_out = lax.psum_scatter(g_w_out, "mp", scatter_dimension=0).astype(F32)
-    back1, gain_grad1 = norm_rows_back(part1, std1, inv1, gain[1])
-    grad1 = grad2 + back1
-    gb1 = pair_gather(grad1.astype(BF16))
-    t_out_x = send_x(gb2, mixed1)
-    t_qkv_x = send_x(normed1, djoined1)
-    dmixed0 = dot_nt(gb1, ws_out).astype(BF16)
-    go = dot_tn(gb1, mixed0).astype(BF16)
-    djoined0 = space_attend_back(joined0, dmixed0, total0, frames_pair, patches, heads_s, scale)
-    djoined0, t_out_x, t_qkv_x, go = tie(djoined0, t_out_x, t_qkv_x, go)
-    g_t_out = keep_x(gb2, mixed1, t_out_x)
-    g_t_qkv = keep_x(normed1, djoined1, t_qkv_x)
-    z_at = [(z + r) % 4 for r in range(4)]
-    span = 4 * HEAD_DIM
-    g_time = reduce_z(
-        [
-            cols(
-                [lax.dynamic_slice_in_dim(g_t_qkv, j * span + s * HEAD_DIM, HEAD_DIM, 1) for j in range(3)]
-                + [lax.dynamic_slice_in_dim(g_t_out, s * HEAD_DIM, HEAD_DIM, 1)]
-            )
-            for s in z_at
-        ]
-    )
-    small = rows_of([jnp.zeros((1, width), F32), gain_grad1[None], gain_grad2, jnp.zeros((5, width), F32)])
-    kept, landed, grad_tokens, small = settle(
-        djoined0, go, turned0, ws_qkv, std0, grad1, inv0, masked.astype(F32), gain[0], small
+    g_t_qkv = dot_tn(normed1, djoined1).astype(BF16).reshape(width, 3, 4, HEAD_DIM)
+    g_t_out = dot_tn(gb2, mixed1).astype(BF16).reshape(width, 1, 4, HEAD_DIM)
+    g_time = jnp.swapaxes(jnp.concatenate([g_t_qkv, g_t_out], axis=1), 1, 2).reshape(width, width)
+    small = rows_of([jnp.zeros((2, width), F32), gain_grad2, jnp.zeros((5, width), F32)])
+    kept, landed, feed_kept, feed_landed, quad, grad_tokens, small = leave(
+        part1.reshape(own, width), std1, grad2, ws_out, joined0, mixed0, turned0, ws_qkv, std0, g_time, w_out_half, g_w_in,
+        total0, inv1, inv0, masked.astype(F32), gain[1], gain[0], small, scale,
     )
     grad_tokens = grad_tokens.reshape(tokens.shape).astype(F32)
 
@@ -1856,12 +1947,9 @@
         kept[:, : 3 * half].reshape(rows, 3, half), landed[:, : 3 * half].reshape(rows, 3, half)
     )
     grad_out_space = by_core(kept[:, 3 * half :], landed[:, 3 * half :]).T
-    kept, landed = swap_c(cols([g_w_in, g_w_out]))
-    grad_w_in = by_core(kept[:, :hidden_own], landed[:, :hidden_own])
-    grad_w_out = by_core(kept[:, hidden_own:], landed[:, hidden_own:]).T
-    both = cols([mine_y(g_time), hop_y(other_y(g_time).astype(BF16)).astype(F32)])
-    kept, landed = swap_c(both)
-    quad = jnp.stack([kept, landed], 1).reshape(rows, 2, 2, 4, HEAD_DIM)
+    grad_w_in = by_core(feed_kept[0], feed_landed[0])
+    grad_w_out = by_core(feed_kept[1], feed_landed[1]).T
+    quad = jnp.transpose(quad, (2, 0, 1, 3)).reshape(rows, 2, 2, 4, HEAD_DIM)
     quad = jnp.where(c == 1, quad[:, ::-1], quad)
     quad = jnp.where(y == 1, quad[:, :, ::-1], quad)
     quad = jnp.transpose(quad, (0, 3, 2, 1, 4)).reshape(rows, 4, 4 * HEAD_DIM)

time: 530 us -> 486 us (0.917)
  waiting for transfers between devices: 55.4 us -> 22.9 us
  Pallas kernels: 365 us -> 392 us
  other arithmetic: 22 us -> 7.61 us
  local copies, waits for them, and re-layouts: 41.4 us -> 32 us
  starting transfers between devices: 9.58 us -> 0.71 us
  matrix products: 12.7 us -> 7.24 us
    ppermute x6 -> x0, waiting for transfers between devices: 35.5 us -> none  [the longest x3 31.2 us: hop_z(): lax.ppermute(v, AXES, device_pairs(lambda y, x, c, z: (y, x, c, (z + shif...]
    pallas_call x2 -> x1, Pallas kernels: 86.4 us -> 113 us  [leave(): pl.pallas_call(functools.partial(leave_kernel, scale), in_specs=[anywhere...]
    unnamed x64 -> x50, local copies, waits for them, and re-layouts: 11.7 us -> 10.7 us
  transfers between devices with their start and end apart: 13 -> 2, of which waited for: 6 -> 1; matrix products, arithmetic and copies ran while one was open for 12% -> 3% of each run, Pallas kernels for 29% -> 14%
where the time goes in v7:
time: 486 us; the launch traced here: 477 us
  Pallas kernels  392 us (81%)
  local copies, waits for them, and re-layouts  32 us (7%)
  waiting for transfers between devices  22.9 us (5%)
  between operations  14.9 us (3%)
  other arithmetic  7.61 us (2%)
  matrix products  7.24 us (1%)
    pallas_call x2, Pallas kernels, time_call(): pl.pallas_call(functools.partial(time_kernel, back, scale, heads), in_spe...  123 us
    pallas_call x1, Pallas kernels, leave(): pl.pallas_call(functools.partial(leave_kernel, scale), in_specs=[anywhere...  113 us
    pallas_call x1, Pallas kernels, enter(): pl.pallas_call(functools.partial(enter_kernel, scale), in_specs=[anywhere...  91.4 us
    pallas_call x1, Pallas kernels, feed(): pl.pallas_call(feed_kernel, in_specs=[whole] * 5 + [anywhere] * 3, out_sp...  65.2 us
    all_gather x1, waiting for transfers between devices, token_parallel(): lax.all_gather(ff_in, ('mp', 'tm', 'x')).reshape(4, width, hidden_own)  22.9 us
    unnamed x50, local copies, waits for them, and re-layouts  10.7 us
  transfers between devices with their start and end apart: 2, of which 1 were waited for; matrix products, arithmetic and copies ran while one was open for 3% of the time, Pallas kernels for 14%

profile of v7, /device:TPU:9, one launch (start us, length us, event | category | flops | bytes accessed | tf_op | source)
XLA Modules:
  0.0 477.2 jit_solution(11977497454893077480)
XLA Ops:
  7.2 0.9 convert_bitcast_fusion
  8.1 0.7 constant_dynamic-update-slice_fusion
  8.8 0.7 collective-permute-start
  9.5 0.3 constant_dynamic-slice_fusion.1
  9.8 0.3 copy.93
  10.1 0.2 copy.67
  10.3 0.9 constant_dynamic-slice_fusion
  11.2 0.2 copy.94
  11.5 0.7 maximum_maximum_fusion.1.vec
  12.1 1.0 pad_maximum_fusion.1.later
  13.1 1.7 dynamic_slice.19
  14.9 0.9 copy.68.masked
  15.7 91.4 %enter.1 = (bf16[1024,1536]{1,0:T(8,128)(2,1)}, bf16[512,1024]{1,0:T(8,128)(2,1)}, bf16[1024,1024]{1,0:T(8,128)(2,1)}, bf16[4,512,1024]{2,1,0:T(8,128)(2,1)}, bf...) custom-call(bf16[4,512,256]{2,1,0:T(8,128)(2,1)} %bitcast.90, ...), custom_call_target="tpu_custom_call" | custom-call | flops 10000000000 | bytes 100000000 | tf_op jit(solution)/shard_map/enter/pallas_call | solution.py:834
  107.3 2.9 copy.69
  110.4 0.2 copy.70
  110.5 1.6 copy.72.refs_3_.refs_5_
  112.1 0.2 copy.73.refs_4_.refs_6_
  112.8 1.5 fusion.5
  114.4 1.2 copy-done.6
  115.6 67.2 %time_forward.1 = (bf16[16,128,1024]{2,1,0:T(8,128)(2,1)}, bf16[16,128,768]{2,1,0:T(8,128)(2,1)}, bf16[16,128,256]{2,1,0:T(8,128)(2,1)S(1)}, f32[16,4,128]{2,1,0...) custom-call(bf16[4,128,1024]{2,1,0:T(8,128)(2,1)S(1)} %bitcast.69, ...), custom_call_target="tpu_custom_call" | custom-call | flops 10000000000 | bytes 100000000 | tf_op jit(solution)/shard_map/time_forward/pallas_call | solution.py:1128
  182.9 1.0 copy-done.8
  183.8 1.0 copy-done.11
  184.8 22.9 %all-gather.3.cloned.1.call-done = bf16[4096,512]{1,0:T(8,128)(2,1)} async-done(((bf16[256,512]{1,0:T(8,128)(2,1)}), bf16[4096,512]{1,0:T(8,128)(2,1)}) %all-gather.3.cloned.1.call-update) | async-done | bytes 4194320 | tf_op jit(solution)/shard_map/all_gather | solution.py:1894
  207.7 65.2 %feed.1 = (bf16[2,4,256,512]{3,2,1,0:T(8,128)(2,1)}, bf16[2,4,256,512]{3,2,1,0:T(8,128)(2,1)}, f32[512,1024]{1,0:T(8,128)}, bf16[512,1024]{1,0:T(8,128)(2,1)}, b...) custom-call(f32[512,1024]{1,0:T(8,128)} %get-tuple-element.52.resid, f32[512,1024]{1,0:T(8,128)} %bitcast.92, ...), custom_call_target="tpu_custom_call" | custom-call | flops 25999998976 | bytes 100000000 | tf_op jit(solution)/shard_map/feed/pallas_call | solution.py:1334
  273.0 1.2 copy-done.7
  274.2 1.2 copy-done.10
  275.4 55.4 %time_back.1 = (bf16[16,128,1024]{2,1,0:T(8,128)(2,1)}, bf16[16,128,768]{2,1,0:T(8,128)(2,1)}, f32[4,128,1024]{2,1,0:T(8,128)}, f32[256,512]{1,0:T(8,128)S(1)}, bf16[4,512,256]{2,1,0:T(8,128)(2,1)S(1)}) custom-call(bf16[4,128,1024]{2,1,0:T(8,128)(2,1)S(1)} %bitcast.70, bf16[512,1024]{1,0:T(8,128)(2,1)S(1)} %copy-done.10, ...), custom_call_target="tpu_custom_call" | custom-call | flops 10000000000 | bytes 100000000 | tf_op jit(solution)/shard_map/time_back/pallas_call | solution.py:1128
  330.9 5.9 %bitcast_convert_fusion = bf16[1024,768]{0,1:T(8,128)(2,1)S(1)} fusion(bf16[16,128,1024]{2,1,0:T(8,128)(2,1)S(1)} %copy-done.20, bf16[16,128,768]{2,1,0:T(8,128)(2,1)} %get-tuple-element.78), kind=kOutput, calls=%fused_computation | convolution fusion | flops 3222011904 | bytes 8912896 | tf_op jit(solution)/shard_map/dot_general | solution.py:458
  336.8 1.3 fusion
  338.1 0.3 pad_maximum_fusion
  338.4 2.6 copy.81.time_hbm
  341.0 0.7 maximum_maximum_fusion.small_in
  341.7 112.6 %leave.1 = (f32[128,512]{1,0:T(8,128)}, f32[128,512]{1,0:T(8,128)}, f32[2,128,512]{2,1,0:T(8,128)}, f32[2,128,512]{2,1,0:T(8,128)}, f32[2,2,128,256]{3,2,1,0:T(8...) custom-call(f32[512,1024]{1,0:T(8,128)} %bitcast.91, f32[512,1024]{1,0:T(8,128)} %get-tuple-element.69.next_hbm, ...), custom_call_target="tpu_custom_call" | custom-call | flops 20000000000 | bytes 100000000 | tf_op jit(solution)/shard_map/leave/pallas_call | solution.py:1756
  454.3 0.8 slice.65
  455.1 0.9 slice.63
  456.1 0.8 slice.66
  456.9 0.9 slice.64
  457.9 1.2 copy.85
  459.3 0.7 slice_bitcast_fusion.5
  460.0 0.6 slice.62
  460.6 0.6 slice.61
  461.3 1.0 copy.90
  462.3 0.8 copy.88
  463.4 0.9 copy.87
  464.3 0.9 copy.89
  465.2 2.9 convert.3
  468.1 0.8 maximum_select_fusion
  469.0 1.0 copy.101
  (73 shorter events, 1.8 us)
Async XLA Ops:
  7.2 2.3 copy-start
  7.2 200.5 %all-gather.3.cloned.1.call-start = ((), (), s32[]{:S(2)}) async-start(), calls=%async_computation | async-start | bytes 4456448 | tf_op jit(solution)/shard_map/all_gather | solution.py:1894
  8.8 6.0 %collective-permute-start = (s32[2,1040]{1,0:T(2,128)S(1)}, s32[2,1040]{1,0:T(2,128)S(1)}, u32[]{:S(2)}, u32[]{:S(2)}) collective-permute-start(s32[2,1040]{1,0:T(2,128)S(1)} %constant_dynamic-update-slice_fusion), channel_id=1, source_target_pairs={{0,4},{1,5},{2,6},{3,7},{4,0},{5,1},{6,2},{7,3},{8,12},{9,13},{10,... | collective-permute-start | bytes 24968 | tf_op jit(solution)/shard_map/ppermute | solution.py:434
  9.5 1.9 copy-start.18
  9.5 2.0 copy-start.17
  110.5 3.9 copy-start.5
  114.4 1.2 copy-start.6
  182.9 1.0 copy-start.8
  183.8 1.0 copy-start.11
  207.7 65.3 %copy-start.2 = (bf16[1024,768]{1,0:T(8,128)(2,1)S(1)}, bf16[1024,768]{1,0:T(8,128)(2,1)}, u32[]{:S(2)}) copy-start(bf16[1024,768]{1,0:T(8,128)(2,1)} %copy.72.refs_3_.refs_5_) | copy-start | bytes 4718596
  272.9 1.2 copy-start.7
  274.2 1.2 copy-start.10
  275.4 55.4 %copy-start.20 = (bf16[16,128,1024]{2,1,0:T(8,128)(2,1)S(1)}, bf16[16,128,1024]{2,1,0:T(8,128)(2,1)}, u32[]{:S(2)}) copy-start(bf16[16,128,1024]{2,1,0:T(8,128)(2,1)} %get-tuple-element.77) | copy-start | bytes 12582916
  330.8 6.0 %copy-start.3 = (bf16[4,512,256]{2,1,0:T(8,128)(2,1)}, bf16[4,512,256]{2,1,0:T(8,128)(2,1)S(1)}, u32[]{:S(2)}) copy-start(bf16[4,512,256]{2,1,0:T(8,128)(2,1)S(1)} %get-tuple-element.67) | copy-start | bytes 3145732
  330.8 6.0 %copy-start.12 = (f32[256,512]{1,0:T(8,128)}, f32[256,512]{1,0:T(8,128)S(1)}, u32[]{:S(2)}) copy-start(f32[256,512]{1,0:T(8,128)S(1)} %get-tuple-element.82.feed_in_hbm) | copy-start | bytes 1572868
  330.8 6.0 %copy-start.9 = (bf16[16,128,256]{2,1,0:T(8,128)(2,1)S(1)}, bf16[16,128,256]{2,1,0:T(8,128)(2,1)}, u32[]{:S(2)}) copy-start(bf16[16,128,256]{2,1,0:T(8,128)(2,1)} %copy-done.8) | copy-start | bytes 3145732
  330.8 6.0 %copy-start.19 = (bf16[16,128,1024]{2,1,0:T(8,128)(2,1)S(1)}, bf16[16,128,1024]{2,1,0:T(8,128)(2,1)}, u32[]{:S(2)}) copy-start(bf16[16,128,1024]{2,1,0:T(8,128)(2,1)} %get-tuple-element.79) | copy-start | bytes 12582916
  338.4 2.6 copy-start.15
  459.1 0.9 copy-start.16
  459.1 2.0 copy-start.13
  459.1 2.0 copy-start.14
  465.2 3.8 copy-start.4
  465.2 4.7 copy-start.1
Sparse Core Ops, SparseCore 0:
  107.3 100.3 all-gather.2

commit v8 on v7

--- a/solution.py
+++ b/solution.py
@@ -498,13 +498,14 @@
 
 def enter_kernel(
     scale,
-    tok, vec, qkv_hbm, out_hbm, later, feed_hbm, masked,
-    wq_out, wo_out, wt, wf, joined_out, turned_out, std_out,
+    tok, vec, qkv_hbm, out_hbm, later, feed_hbm, first_hbm, masked,
+    wq_out, wo_out, wt, wf, wi, joined_out, turned_out, std_out,
     mixed, total_out, inverse, resid, std_next, inverse_next, low_next, vec_out,
     rows_in, vec_in, wq, wo, normed, joined, turned, std, base, part, part_out, part_in,
     z_send, z_recv, y_send, y_recv, x_send, x_recv, p_send, p_recv, q_send, q_recv,
     t_send, t_recv, v_send, v_recv, u_send, u_recv, w_send, w_recv,
     f_send, f_recv, g_send, g_recv, n_send, n_recv, local, saved,
+    i_send, i_recv, j_send, j_recv, k_send, k_recv,
 ):
     y, x, c, z = (lax.axis_index(name) for name in AXES)
     half = wo.shape[0] // 4
@@ -545,6 +546,7 @@
     keep_later = [
         pltpu.make_async_copy(later, wt.at[:, at(z, span)], local.at[4]),
         pltpu.make_async_copy(feed_hbm.at[at(c, 4 * size)], wf.at[z], local.at[5]),
+        pltpu.make_async_copy(first_hbm.at[:, at(c, 4 * size)], wi.at[z], local.at[8]),
     ]
     start(keep + keep_later)
 
@@ -599,6 +601,20 @@
         source = feed_hbm.at[at(4 * c + spot(0, 0), size)] if step == 0 else feed_piece(0, r)
         return [remote(source, feed_piece(0, r), f_send.at[int(right), step], f_recv.at[lands], peer)]
 
+    def first_piece(dy, dx, r):
+        return wi.at[(z + r) % 4, at(spot(dy, dx), BLK)]
+
+    def first_z(right, step):
+        r, peer, lands = leg(right, step)
+        source = first_hbm.at[at(spot(0, 0), BLK), at(c, 4 * size)] if step == 0 else first_piece(0, 0, r)
+        return [remote(source, first_piece(0, 0, r), i_send.at[int(right), step], i_recv.at[lands], peer)]
+
+    def first_y(r, dy=0):
+        return [remote(first_piece(dy, 0, r), first_piece(dy, 0, r), j_send.at[r], j_recv.at[r], near_y)]
+
+    def first_x(r, dx=0):
+        return [remote(first_piece(0, dx, r), first_piece(0, dx, r), k_send.at[r], k_recv.at[r], near_x)]
+
     def y_copies(r, dy=0):
         return copies(piece(dy, 0, r), y_send.at[r], y_recv.at[r], near_y)
 
@@ -681,6 +697,15 @@
             landed([remote(feed_piece(0, r), feed_piece(0, r), f_send.at[0, 0], f_recv.at[r], near_y)])
             onward(j, feed_z, right)
             start(feed_y(r))
+
+        each_side(j, act)
+
+    def first_forward_step(j):
+        def act(r, right):
+            landed([remote(first_piece(0, 0, r), first_piece(0, 0, r), i_send.at[0, 0], i_recv.at[r], near_y)])
+            onward(j, first_z, right)
+            start(first_y(r))
+            start(first_x(r))
 
         each_side(j, act)
 
@@ -762,7 +787,7 @@
     frames = own // slab
     project(0)
     time_forward_step(1)
-    begin(feed_z)
+    begin(first_z)
     lax.fori_loop(0, frames, attend, 0)
     part[...] = dot_nn(mixed[pl.ds(0, own)], wo[...])
     time_forward_step(2)
@@ -770,16 +795,18 @@
     project(1)
     saves.append(pltpu.make_async_copy(joined, joined_out, saved.at[3]))
     saves[3].start()
+    first_forward_step(0)
     lax.fori_loop(frames, 2 * frames, attend, 0)
     part_out[...] = dot_nn(mixed[pl.ds(own, own)], wo[...]).astype(BF16)
     give_part = remote(part_out, part_in, n_send.at[1], n_recv.at[1], pair)
     give_part.start()
-    feed_forward_step(0)
+    first_forward_step(1)
+    begin(feed_z)
     lax.fori_loop(own // slab, 2 * own // slab, turn, 0)
     saves.append(pltpu.make_async_copy(turned, turned_out, saved.at[4]))
     saves[4].start()
     give_part.wait_recv()
-    feed_forward_step(1)
+    first_forward_step(2)
 
     def second_norm(i, carry):
         rows = at(i, step)
@@ -792,7 +819,8 @@
         return carry
 
     lax.fori_loop(0, 2, second_norm, 0)
-    feed_forward_step(2)
+    for j in range(3):
+        feed_forward_step(j)
 
     for copy in keep_later + saves:
         copy.wait()
@@ -801,17 +829,19 @@
     for r in (1, 2, 3):
         landed(time_x(r, 1))
         landed(feed_y(r, 1))
-        for group in (y_copies(r), x_copies(r), corner_x(r), corner_y(r), time_x(r), feed_y(r)):
+        landed(first_y(r, 1))
+        landed(first_x(r, 1))
+        for group in (y_copies(r), x_copies(r), corner_x(r), corner_y(r), time_x(r), feed_y(r), first_y(r), first_x(r)):
             sent(group)
     for step_z in range(3):
-        for make in (z_copies, time_z, feed_z):
+        for make in (z_copies, time_z, first_z, feed_z):
             pl.when(jnp.logical_and(z >= step_z, z < 3))(lambda step_z=step_z, make=make: sent(make(True, step_z)))
             pl.when(jnp.logical_and(z + step_z <= 3, z > 0))(lambda step_z=step_z, make=make: sent(make(False, step_z)))
     for k in range(4):
         pl.when(jnp.logical_not(stays(k)))(lambda k=k: sent(token_copies(k)))
 
 
-def enter(tok, vec, qkv, out, later, feed_weight, masked, scale):
+def enter(tok, vec, qkv, out, later, feed_weight, first_weight, masked, scale):
     own, width, half = tok.shape[1], 4 * tok.shape[2], out.shape[0] // 2
     size = feed_weight.shape[0] // 2
     dma = pltpu.SemaphoreType.DMA
@@ -827,14 +857,14 @@
 
     shapes = [
         ((width, 12 * half), BF16), ((4 * half, width), BF16), ((width, 4 * later.shape[1]), BF16),
-        ((4, size, width), BF16), ((2 * own, 12 * half), BF16), ((width, 2 * own), BF16), ((own, width), F32),
+        ((4, size, width), BF16), ((4, width, size), BF16), ((2 * own, 12 * half), BF16), ((width, 2 * own), BF16), ((own, width), F32),
         ((2 * own, 4 * half), BF16), ((2 * own // 128, heads, 128), F32), ((own, 1), F32), ((own, width), F32),
         ((own, width), F32), ((own, 1), F32), ((own, width), BF16), ((vec.shape[0], width), F32),
     ]
     return pl.pallas_call(
         functools.partial(enter_kernel, scale),
-        in_specs=[anywhere] * 6 + [whole],
-        out_specs=[anywhere] * 7 + [whole] * 8,
+        in_specs=[anywhere] * 7 + [whole],
+        out_specs=[anywhere] * 8 + [whole] * 8,
         out_shape=[jax.ShapeDtypeStruct(shape, kind) for shape, kind in shapes],
         scratch_shapes=[
             low(own, width), low(vec.shape[0], width), low(width, 12 * half), low(4 * half, width),
@@ -843,14 +873,15 @@
             dma((2, 3, 2)), dma((4, 2)), dma((4, 2)), dma((4, 2)), dma((4, 2)), dma((4, 2)),
             dma((4, 1)), dma((4, 1)), dma((4, 2)), dma((4, 2)),
             dma((4,)), dma((4,)), dma((4,)), dma((4,)), dma((2, 3)), dma((4,)), dma((4,)), dma((4,)),
-            dma((2, 3)), dma((4,)), dma((4,)), dma((4,)), dma((2,)), dma((2,)), dma((8,)), dma((5,)),
+            dma((2, 3)), dma((4,)), dma((4,)), dma((4,)), dma((2,)), dma((2,)), dma((9,)), dma((5,)),
+            dma((2, 3)), dma((4,)), dma((4,)), dma((4,)), dma((4,)), dma((4,)),
         ],
         compiler_params=pltpu.CompilerParams(
             collective_id=0, has_side_effects=True, vmem_limit_bytes=56 * 1024 * 1024
         ),
         cost_estimate=pl.CostEstimate(flops=10**10, transcendentals=10**6, bytes_accessed=10**8),
         name="enter",
-    )(tok, vec, qkv, out, later, feed_weight, masked)
+    )(tok, vec, qkv, out, later, feed_weight, first_weight, masked)
 
 
 GROUP = 8
@@ -859,16 +890,16 @@
 
 def time_kernel(back, scale, heads, *refs):
     if back:
-        (own_ref, rider_ref, joined_ref, total_ref, wide_ref, wq_ref, wo_ref, bias_ref) = refs[:8]
-        (all_ref, out_ref, delta_ref, reduced_ref, rider_out) = refs[8:13]
+        (own_ref, rider_ref, joined_ref, total_ref, wide_ref, wt_ref, bias_ref) = refs[:7]
+        (all_ref, out_ref, delta_ref, reduced_ref, rider_out) = refs[7:12]
         (half_in, half_own, line_out, line_in, half_send, half_recv, half_local, line_send, line_recv) = refs[-9:]
-        refs = refs[13:-9]
+        refs = refs[12:-9]
     else:
-        (own_ref, rider_ref, far_ref, wq_ref, wo_ref, bias_ref) = refs[:6]
-        (all_ref, out_ref, mixed_ref, total_ref, delta_ref, rider_out, spread_out) = refs[6:13]
-        refs = refs[13:]
+        (own_ref, rider_ref, far_ref, in_ref, wt_ref, bias_ref) = refs[:6]
+        (all_ref, out_ref, mixed_ref, total_ref, delta_ref, rider_out, spread_out, in_out) = refs[6:14]
+        refs = refs[14:]
     (
-        held, wide, narrow, kept, core_out, core_in, near_out, near_in,
+        wq_ref, wo_ref, held, wide, narrow, kept, core_out, core_in, near_out, near_in,
         gy_send, gy_recv, gc_send, gc_recv, gd_send, gd_recv, sc_send, sc_recv, sy_send, sy_recv,
         r_send, r_recv, r_local, out_sem, wx_send, wx_recv,
     ) = refs
@@ -966,6 +997,11 @@
         if k > 0:
             gather_y(k).start()
         gather_c(k).start()
+    def spread_in(r, dx=0):
+        at = pl.multiple_of(BLK * (2 * (1 - y) + (x + dx) % 2), BLK)
+        there = in_out.at[(z + r) % 4, pl.ds(at, BLK)]
+        return remote(in_ref.at[(z + r) % 4, pl.ds(at, BLK)], there, wx_send.at[5 + r], wx_recv.at[5 + r], near_x)
+
     def half_away(s):
         return remote(wide_ref.at[1 - x, s], half_in.at[s], half_send.at[s], half_recv.at[s], near_x)
 
@@ -993,12 +1029,31 @@
             half_away(s).start()
             half_here(s).start()
     else:
+        for r in (1, 2, 3):
+            spread_in(r).start()
         for i in range(6):
             spread_x(i).start()
     for k in range(4):
         pl.when(stays(k))(lambda k=k: ride_local(k).start())
         pl.when(jnp.logical_not(stays(k)))(lambda k=k: ride_remote(k).start())
     held[:frames] = own_ref[...]
+
+    def assemble(i, carry):
+        rows = pl.ds(pl.multiple_of(i * BLK, BLK), BLK)
+        for s in range(0, heads, 2):
+            for part in range(4):
+                both = [
+                    wt_ref[rows, (s + j) * 4 * HEAD_DIM + part * HEAD_DIM : (s + j) * 4 * HEAD_DIM + (part + 1) * HEAD_DIM]
+                    for j in range(2)
+                ]
+                both = jnp.concatenate(both, axis=1)
+                if part < 3:
+                    wq_ref[rows, part * width + s * HEAD_DIM : part * width + s * HEAD_DIM + PAIR] = both
+                else:
+                    wo_ref[rows, s * HEAD_DIM : s * HEAD_DIM + PAIR] = both
+        return carry
+
+    lax.fori_loop(0, wt_ref.shape[0] // BLK, assemble, 0)
 
     def finish(k):
         scatter_c(k).wait_recv()
@@ -1089,15 +1144,18 @@
         for i in range(6):
             spread_x(i, 1).wait_recv()
             spread_x(i).wait_send()
+        for r in (1, 2, 3):
+            spread_in(r, 1).wait_recv()
+            spread_in(r).wait_send()
     for k in range(4):
         pl.when(stays(k))(lambda k=k: ride_local(k).wait())
         pl.when(jnp.logical_not(stays(k)))(lambda k=k: ride_remote(k).wait_send())
         pl.when(jnp.logical_not(from_self(k)))(lambda k=k: ride_landed(k).wait_recv())
 
 
-def time_call(back, own, rider, saved, wq, wo, bias, scale):
+def time_call(back, own, rider, saved, weights, bias, scale):
     frames, patches, features = own.shape
-    width = wo.shape[1]
+    width = weights.shape[1] // 4
     heads = width // HEAD_DIM
     chunks = patches // CHUNK
     rows = 4 * frames * GROUP
@@ -1123,14 +1181,16 @@
     if back:
         out_shape.insert(-1, jax.ShapeDtypeStruct(half[1:], F32))
     else:
-        out_shape.append(jax.ShapeDtypeStruct(saved[0].shape, BF16))
-        held = 3
+        out_shape += [jax.ShapeDtypeStruct(w.shape, BF16) for w in saved]
+        held = 4
     return pl.pallas_call(
         functools.partial(time_kernel, back, scale, heads),
-        in_specs=[whole, anywhere] + ([whole, whole, anywhere] if back else [anywhere]) + [whole] * 3,
+        in_specs=[whole, anywhere] + ([whole, whole, anywhere] if back else [anywhere] * 2) + [whole] * 2,
         out_specs=[anywhere] + [whole] * (len(out_shape) - held) + [anywhere] * (held - 1),
         out_shape=out_shape,
         scratch_shapes=[
+            pltpu.VMEM((features, 3 * width), BF16),
+            pltpu.VMEM((features, width), BF16),
             pltpu.VMEM((4 * frames, patches, features), BF16),
             pltpu.VMEM((4 * frames, CHUNK, 3 * width), F32),
             pltpu.VMEM((4 * frames, CHUNK, width), F32),
@@ -1142,18 +1202,18 @@
         ]
         + [dma((chunks,))] * 10
         + [dma((4,)), dma((4,)), dma((1,)), dma((chunks,))]
-        + [dma((6,))] * 2
+        + [dma((9,))] * 2
         + ([pltpu.VMEM(half, BF16)] * 4 + [dma((4,))] * 5 if back else []),
         compiler_params=pltpu.CompilerParams(
             collective_id=2 if back else 1, has_side_effects=True, vmem_limit_bytes=48 * 1024 * 1024
         ),
         cost_estimate=pl.CostEstimate(flops=10**10, transcendentals=10**6, bytes_accessed=10**8),
         name="time_back" if back else "time_forward",
-    )(own, rider, *saved, wq, wo, bias)
+    )(own, rider, *saved, weights, bias)
 
 
 def feed_kernel(
-    resid, delta, upstream, masked, gain, w_in_hbm, w_out_hbm, w_far_hbm,
+    resid, delta, upstream, masked, gain, w_in_hbm, w_in_far_hbm, w_out_hbm, w_far_hbm,
     half_in_hbm, half_out_hbm, grad_out, low_out, rows_out, gain_out,
     w_in, w_out, standard, inverse, normed, grads, normed_t, grads_t, hidden, pulled, g_in, g_out, back, ahead,
     back_out, back_in, ahead_out, ahead_in, from_x, from_y,
@@ -1167,11 +1227,15 @@
 
     def fetch(s, far):
         size = w_out.shape[1] // 4
-        copies = [pltpu.make_async_copy(w_in_hbm.at[s], w_in.at[s], w_sem.at[0, s])]
+        copies = []
+        for i in range(4):
+            rows = pl.ds(pl.multiple_of(BLK * (2 * ((y + i // 2) % 2) + (x + i % 2) % 2), BLK), BLK)
+            source = w_in_far_hbm if far and i == 3 else w_in_hbm
+            copies.append(pltpu.make_async_copy(source.at[s, rows], w_in.at[s, rows], w_sem.at[5 + i, s]))
         for i in range(4):
             rows = pl.ds(pl.multiple_of(size * (2 * (i // 2) + (x + i % 2) % 2), size), size)
             source = w_far_hbm if far and i % 2 else w_out_hbm
-            copies.append(pltpu.make_async_copy(source.at[s, rows], w_out.at[s, rows], w_sem.at[1 + i, s]))
+            copies.append(pltpu.make_async_copy(source.at[s, rows], w_out.at[s, rows], w_sem.at[i, s]))
         return copies
 
     def fetch_now(s, far):
@@ -1318,7 +1382,7 @@
                 copy.wait()
 
 
-def feed(resid, delta, upstream, masked, gain, w_in, w_out, w_far):
+def feed(resid, delta, upstream, masked, gain, w_in, w_in_far, w_out, w_far):
     own, features = resid.shape
     units = w_in.shape[2]
     dma = pltpu.SemaphoreType.DMA
@@ -1333,7 +1397,7 @@
 
     return pl.pallas_call(
         feed_kernel,
-        in_specs=[whole] * 5 + [anywhere] * 3,
+        in_specs=[whole] * 5 + [anywhere] * 4,
         out_specs=[anywhere] * 2 + [whole] * 4,
         out_shape=[
             jax.ShapeDtypeStruct((2, 4, BLK, units), BF16),
@@ -1350,7 +1414,7 @@
             high(2 * own, features), high(2 * own, features),
             low(own, features), low(own, features), low(own, features), low(own, features),
             low(2, 4, BLK, units), low(2, 4, BLK, units),
-            dma((5, 4)), dma((2, 2, 4)), dma((2,)), dma((2,)), dma((2,)), dma((2,)),
+            dma((9, 4)), dma((2, 2, 4)), dma((2,)), dma((2,)), dma((2,)), dma((2,)),
             dma((2, 4)), dma((2, 4)), dma((2, 4)), dma((2, 4)),
         ],
         compiler_params=pltpu.CompilerParams(
@@ -1358,7 +1422,7 @@
         ),
         cost_estimate=pl.CostEstimate(flops=26 * 10**9, transcendentals=2 * 10**6, bytes_accessed=10**8),
         name="feed",
-    )(resid, delta, upstream, masked, gain, w_in, w_out, w_far)
+    )(resid, delta, upstream, masked, gain, w_in, w_in_far, w_out, w_far)
 
 
 def leave_kernel(
@@ -1872,7 +1936,7 @@
         ]
     )
     (
-        ws_qkv, ws_out, wt_all, wf_out, joined0, turned0, std0,
+        ws_qkv, ws_out, wt_all, wf_out, wf_in, joined0, turned0, std0,
         mixed0, total0, inv0, resid1, std1, inv1, normed1, vectors,
     ) = enter(
         tokens.reshape(4, own, BLK),
@@ -1881,39 +1945,26 @@
         out_space,
         ti_own,
         w_out,
+        w_in,
         masked.astype(F32),
         scale,
     )
     gain = [vectors[1 + i : 2 + i] for i in range(3)]
-    wt_all = wt_all.reshape(width, 4, 4, HEAD_DIM)
-    wt_qkv = jnp.swapaxes(wt_all[:, :, :3], 1, 2).reshape(width, 12 * HEAD_DIM)
-    wt_out = wt_all[:, :, 3].reshape(width, 4 * HEAD_DIM)
-
-    ff_in = lax.dynamic_slice(w_in, (plane * BLK, c * hidden_own), (BLK, hidden_own))
-    ff_in, normed1 = tie(ff_in, normed1)
-    wf_in = lax.all_gather(ff_in, ("mp", "tm", "x")).reshape(4, width, hidden_own)
-
-    def pair_gather(v):
-        return rows_of([v, hop_c(v)])
-
-    def pair_scatter(v):
-        return v[:own] + hop_c(v[own:].astype(BF16)).astype(F32)
 
     half = qkv_space.shape[2] // 2
-    normed1, joined1, mixed1, total1, delta, upstream, wf_far = time_call(
+    normed1, joined1, mixed1, total1, delta, upstream, wf_far, wf_in_far = time_call(
         False,
         normed1.reshape(frames_own, patches, width),
         cotangent.reshape(4, own, BLK),
-        [wf_out],
-        wt_qkv,
-        wt_out,
+        [wf_out, wf_in],
+        wt_all,
         bias,
         scale,
     )
     normed1 = normed1.reshape(4 * own, width)
     mixed1 = mixed1.reshape(4 * own, -1)
     w_in_half, w_out_half, grad2, grad2_low, block_rows, gain_grad2 = feed(
-        resid1, delta.reshape(own, width), upstream, masked.astype(F32), gain[2], wf_in, wf_out, wf_far
+        resid1, delta.reshape(own, width), upstream, masked.astype(F32), gain[2], wf_in, wf_in_far, wf_out, wf_far
     )
 
     def by_core(kept, landed):
@@ -1924,8 +1975,7 @@
         grad2_low.reshape(frames_own, patches, width),
         block_rows,
         [joined1, total1, w_in_half],
-        wt_qkv,
-        wt_out,
+        wt_all,
         bias,
         scale,
     )

time: 486 us -> 459 us (0.944)
  the two profiles are of different devices: /device:TPU:9 before, /device:TPU:0 now
where the time goes in v8:
time: 459 us; the launch traced here: 450 us
  Pallas kernels  406 us (88%)
  local copies, waits for them, and re-layouts  24.4 us (5%)
  matrix products  9.26 us (2%)
  other arithmetic  7.61 us (2%)
    pallas_call x2, Pallas kernels, time_call(): pl.pallas_call(functools.partial(time_kernel, back, scale, heads), in_spe...  119 us
    pallas_call x1, Pallas kernels, enter(): pl.pallas_call(functools.partial(enter_kernel, scale), in_specs=[anywhere...  112 us
    pallas_call x1, Pallas kernels, leave(): pl.pallas_call(functools.partial(leave_kernel, scale), in_specs=[anywhere...  111 us
    pallas_call x1, Pallas kernels, feed(): pl.pallas_call(feed_kernel, in_specs=[whole] * 5 + [anywhere] * 4, out_sp...  64.2 us
    unnamed x44, local copies, waits for them, and re-layouts  9.69 us
    dot_general x2, matrix products, dot_tn(): lax.dot_general(a, b, (((0,), (0,)), ((), ())), preferred_element_type=F32)  9.26 us
  transfers between devices with their start and end apart: 1, of which 0 were waited for; matrix products, arithmetic and copies ran while one was open for 1% of the time, Pallas kernels for 0%

profile of v8, /device:TPU:0, one launch (start us, length us, event | category | flops | bytes accessed | tf_op | source)
XLA Modules:
  0.0 449.6 jit_solution(17728486508227901140)
XLA Ops:
  0.7 0.9 convert_bitcast_fusion
  1.6 0.7 constant_dynamic-update-slice_fusion
  2.2 0.5 collective-permute-start
  2.7 0.3 constant_dynamic-slice_fusion.1
  3.0 0.3 copy.79
  3.3 0.2 copy.59
  3.5 0.9 constant_dynamic-slice_fusion
  4.4 0.2 copy.80
  4.6 1.0 pad_maximum_fusion.1.later
  5.6 0.7 maximum_maximum_fusion.1.vec
  6.5 0.9 copy.60.masked
  7.4 0.1 dynamic-slice_reduce_fusion
  7.6 0.1 reshape.136
  7.8 0.1 le.15
  7.9 112.3 %enter.1 = (bf16[1024,1536]{1,0:T(8,128)(2,1)}, bf16[512,1024]{1,0:T(8,128)(2,1)}, bf16[1024,1024]{1,0:T(8,128)(2,1)}, bf16[4,512,1024]{2,1,0:T(8,128)(2,1)}, bf...) custom-call(bf16[4,512,256]{2,1,0:T(8,128)(2,1)} %bitcast.80, ...), custom_call_target="tpu_custom_call" | custom-call | flops 10000000000 | bytes 100000000 | tf_op jit(solution)/shard_map/enter/pallas_call | solution.py:864
  120.1 1.5 fusion.5
  121.6 0.1 and_select_fusion.refs_5_.refs_6_
  121.7 1.2 copy-done.6
  123.0 63.3 %time_forward.1 = (bf16[16,128,1024]{2,1,0:T(8,128)(2,1)}, bf16[16,128,768]{2,1,0:T(8,128)(2,1)}, bf16[16,128,256]{2,1,0:T(8,128)(2,1)S(1)}, f32[16,4,128]{2,1,0...) custom-call(bf16[4,128,1024]{2,1,0:T(8,128)(2,1)S(1)} %bitcast.64, ...), custom_call_target="tpu_custom_call" | custom-call | flops 10000000000 | bytes 100000000 | tf_op jit(solution)/shard_map/time_forward/pallas_call | solution.py:1186
  186.2 1.0 copy-done.8
  187.2 64.2 %feed.1 = (bf16[2,4,256,512]{3,2,1,0:T(8,128)(2,1)}, bf16[2,4,256,512]{3,2,1,0:T(8,128)(2,1)}, f32[512,1024]{1,0:T(8,128)}, bf16[512,1024]{1,0:T(8,128)(2,1)}, b...) custom-call(f32[512,1024]{1,0:T(8,128)} %get-tuple-element.52.resid, f32[512,1024]{1,0:T(8,128)} %bitcast.81, ...), custom_call_target="tpu_custom_call" | custom-call | flops 25999998976 | bytes 100000000 | tf_op jit(solution)/shard_map/feed/pallas_call | solution.py:1398
  251.4 1.2 copy-done.7
  252.6 1.2 copy-done.9
  253.8 56.1 %time_back.1 = (bf16[16,128,1024]{2,1,0:T(8,128)(2,1)}, bf16[16,128,768]{2,1,0:T(8,128)(2,1)}, f32[4,128,1024]{2,1,0:T(8,128)S(1)}, f32[256,512]{1,0:T(8,128)S(1)}, bf16[4,512,256]{2,1,0:T(8,128)(2,1)S(1)}) custom-call(bf16[4,128,1024]{2,1,0:T(8,128)(2,1)S(1)} %bitcast.65, bf16[512,1024]{1,0:T(8,128)(2,1)S(1)} %copy-done.9, ...), custom_call_target="tpu_custom_call" | custom-call | flops 10000000000 | bytes 100000000 | tf_op jit(solution)/shard_map/time_back/pallas_call | solution.py:1186
  309.9 8.0 %bitcast_convert_fusion = bf16[1024,768]{0,1:T(8,128)(2,1)S(1)} fusion(bf16[16,128,1024]{2,1,0:T(8,128)(2,1)} %get-tuple-element.77, bf16[16,128,768]{2,1,0:T(8,128)(2,1)} %get-tuple-element.78), kind=kOutput, calls=%fused_computation | convolution fusion | flops 3222011904 | bytes 8912896 | tf_op jit(solution)/shard_map/dot_general | solution.py:458
  317.9 1.3 fusion
  319.2 0.3 pad_maximum_fusion
  319.5 2.6 copy.67.time_hbm
  322.1 0.7 maximum_maximum_fusion.small_in
  322.8 110.7 %leave.1 = (f32[128,512]{1,0:T(8,128)}, f32[128,512]{1,0:T(8,128)}, f32[2,128,512]{2,1,0:T(8,128)}, f32[2,128,512]{2,1,0:T(8,128)}, f32[2,2,128,256]{3,2,1,0:T(8...) custom-call(f32[512,1024]{1,0:T(8,128)} %bitcast.63, f32[512,1024]{1,0:T(8,128)} %get-tuple-element.69.next_hbm, ...), custom_call_target="tpu_custom_call" | custom-call | flops 20000000000 | bytes 100000000 | tf_op jit(solution)/shard_map/leave/pallas_call | solution.py:1820
  433.5 0.8 slice.57
  434.4 0.9 slice.55
  435.3 0.8 slice.58
  436.2 0.9 slice.56
  437.1 1.2 copy.71
  438.6 0.7 slice_bitcast_fusion.4
  439.2 0.6 slice.54
  439.8 0.6 slice.53
  440.4 0.1 slice_bitcast_fusion
  440.6 1.0 copy.76
  441.6 0.8 copy.74
  442.3 0.1 copy.69
  442.5 0.1 copy.70
  442.6 0.9 copy.73
  443.5 0.9 copy.75
  444.5 2.9 convert.3
  447.4 0.8 maximum_select_fusion
  448.2 1.0 copy.87
  (57 shorter events, 0.8 us)
Async XLA Ops:
  0.6 2.1 copy-start
  2.2 4.2 collective-permute-start
  2.7 1.9 copy-start.16
  3.0 2.7 copy-start.15
  7.8 113.9 %copy-start.4 = (bf16[2,8,128,256]{3,2,1,0:T(8,128)(2,1)S(1)}, bf16[2,8,128,256]{3,2,1,0:T(8,128)(2,1)}, u32[]{:S(2)}) copy-start(bf16[2,8,128,256]{3,2,1,0:T(8,128)(2,1)} %param.14) | copy-start | bytes 3145732
  121.7 1.2 copy-start.6
  186.2 1.0 copy-start.8
  251.4 1.2 copy-start.7
  252.6 1.2 copy-start.9
  309.9 8.0 %copy-start.2 = (bf16[4,512,256]{2,1,0:T(8,128)(2,1)}, bf16[4,512,256]{2,1,0:T(8,128)(2,1)S(1)}, u32[]{:S(2)}) copy-start(bf16[4,512,256]{2,1,0:T(8,128)(2,1)S(1)} %get-tuple-element.67) | copy-start | bytes 3145732
  309.9 8.0 %copy-start.5 = (f32[4,128,1024]{2,1,0:T(8,128)}, f32[4,128,1024]{2,1,0:T(8,128)S(1)}, u32[]{:S(2)}) copy-start(f32[4,128,1024]{2,1,0:T(8,128)S(1)} %get-tuple-element.68) | copy-start | bytes 6291460
  309.9 8.0 %copy-start.10 = (f32[256,512]{1,0:T(8,128)}, f32[256,512]{1,0:T(8,128)S(1)}, u32[]{:S(2)}) copy-start(f32[256,512]{1,0:T(8,128)S(1)} %get-tuple-element.82.feed_in_hbm) | copy-start | bytes 1572868
  309.9 8.0 %copy-start.17 = (bf16[16,128,1024]{2,1,0:T(8,128)(2,1)S(1)}, bf16[16,128,1024]{2,1,0:T(8,128)(2,1)}, u32[]{:S(2)}) copy-start(bf16[16,128,1024]{2,1,0:T(8,128)(2,1)} %get-tuple-element.79) | copy-start | bytes 12582916
  319.5 2.6 copy-start.13
  438.3 0.9 copy-start.14
  438.3 2.0 copy-start.11
  438.4 2.0 copy-start.12
  444.5 3.8 copy-start.3
  444.5 4.7 %copy-start.1 = (bf16[1024,3,256]{2,0,1:T(8,128)(2,1)S(1)}, bf16[1024,3,256]{2,0,1:T(8,128)(2,1)}, u32[]{:S(2)}) copy-start(bf16[1024,3,256]{2,0,1:T(8,128)(2,1)} %param.22) | copy-start | bytes 4718596

commit v9 on v8

--- a/solution.py
+++ b/solution.py
@@ -890,14 +890,16 @@
 
 def time_kernel(back, scale, heads, *refs):
     if back:
-        (own_ref, rider_ref, joined_ref, total_ref, wide_ref, wt_ref, bias_ref) = refs[:7]
-        (all_ref, out_ref, delta_ref, reduced_ref, rider_out) = refs[7:12]
-        (half_in, half_own, line_out, line_in, half_send, half_recv, half_local, line_send, line_recv) = refs[-9:]
-        refs = refs[12:-9]
+        (own_ref, rider_ref, joined_ref, total_ref, wide_ref, turned_ref, mixed_ref, wt_ref, bias_ref) = refs[:9]
+        (delta_ref, grad_ref, reduced_ref, rider_out) = refs[9:13]
+        (half_in, half_own, line_out, line_in, half_send, half_recv, half_local, line_send, line_recv) = refs[-13:-4]
+        (out_ref, turned, grad_qkv, grad_out) = refs[-4:]
+        refs = refs[13:-13]
     else:
         (own_ref, rider_ref, far_ref, in_ref, wt_ref, bias_ref) = refs[:6]
-        (all_ref, out_ref, mixed_ref, total_ref, delta_ref, rider_out, spread_out, in_out) = refs[6:14]
-        refs = refs[14:]
+        (turned_ref, out_ref, mixed_ref, total_ref, delta_ref, rider_out, spread_out, in_out) = refs[6:14]
+        turned = refs[-1]
+        refs = refs[14:-1]
     (
         wq_ref, wo_ref, held, wide, narrow, kept, core_out, core_in, near_out, near_in,
         gy_send, gy_recv, gc_send, gc_recv, gd_send, gd_recv, sc_send, sc_recv, sy_send, sy_recv,
@@ -946,7 +948,8 @@
         return remote(near_out.at[k], near_in.at[k], sy_send.at[k], sy_recv.at[k], near)
 
     def save(k):
-        return pltpu.make_async_copy(held.at[:, patches(k)], all_ref.at[:, patches(k)], out_sem.at[k])
+        there = (turned_ref.at[k], turned.at[k]) if back else (turned.at[k], turned_ref.at[k])
+        return pltpu.make_async_copy(*there, out_sem.at[k])
 
     def columns(s):
         return pl.ds(pl.multiple_of(s * BLK, BLK), BLK)
@@ -1037,6 +1040,9 @@
         pl.when(stays(k))(lambda k=k: ride_local(k).start())
         pl.when(jnp.logical_not(stays(k)))(lambda k=k: ride_remote(k).start())
     held[:frames] = own_ref[...]
+    if back:
+        for k in range(chunks):
+            save(k).start()
 
     def assemble(i, carry):
         rows = pl.ds(pl.multiple_of(i * BLK, BLK), BLK)
@@ -1103,7 +1109,6 @@
             joined = dot_nn(lhs, wq_ref[...]).astype(BF16)
             out_ref[:, patches(k)] = joined.reshape(wide.shape)
             wide[...] = joined.astype(F32).reshape(wide.shape)
-        save(k).start()
         lax.fori_loop(0, groups, lambda i, carry: (one_group(i, k), carry)[1], 0)
         if back:
             grads = wide[...].astype(BF16)
@@ -1118,6 +1123,11 @@
         core_out[k] = partial[2 * frames :].astype(BF16)
         scatter_c(k).start()
         pl.when(k > 0)(lambda: finish(k - 1))
+        if not back:
+            for b in range(4):
+                slab = held[b * frames : (b + 1) * frames, patches(k)].reshape(frames * CHUNK, held.shape[2])
+                turned[k, :, b * frames * CHUNK : (b + 1) * frames * CHUNK] = slab.T
+            save(k).start()
         if back:
             pl.when(k == 1)(halve)
         return carry
@@ -1125,6 +1135,31 @@
     pass_on(0)
     lax.fori_loop(0, chunks, one_chunk, 0)
     finish(chunks - 1)
+
+    def weigh(k, carry):
+        count = 4 * frames * CHUNK
+        save(k).wait()
+        grad_qkv[...] = grad_qkv[...] + dot_nn(turned[k], out_ref[:, patches(k)].reshape(count, 3 * width))
+        grad_out[...] = grad_out[...] + dot_tn(
+            mixed_ref[:, patches(k)].reshape(count, width), held[:, patches(k)].reshape(count, held.shape[2])
+        )
+        return carry
+
+    def arrange(i, carry):
+        rows = pl.ds(pl.multiple_of(i * BLK, BLK), BLK)
+        last = grad_out[:, rows].T
+        for s in range(heads):
+            mine = slice(s * HEAD_DIM, (s + 1) * HEAD_DIM)
+            parts = [grad_qkv[rows, j * width : (j + 1) * width][:, mine] for j in range(3)] + [last[:, mine]]
+            grad_ref[rows, 2 * s * PAIR : (2 * s + 1) * PAIR] = jnp.concatenate(parts[:2], axis=1).astype(BF16)
+            grad_ref[rows, (2 * s + 1) * PAIR : (2 * s + 2) * PAIR] = jnp.concatenate(parts[2:], axis=1).astype(BF16)
+        return carry
+
+    if back:
+        grad_qkv[...] = jnp.zeros_like(grad_qkv)
+        grad_out[...] = jnp.zeros_like(grad_out)
+        lax.fori_loop(0, chunks, weigh, 0)
+        lax.fori_loop(0, grad_ref.shape[0] // BLK, arrange, 0)
     for k in range(chunks):
         scatter_y(k).wait_recv()
         delta_ref[:, patches(k)] = delta_ref[:, patches(k)] + near_in[k].astype(F32)
@@ -1139,7 +1174,8 @@
     for k in range(chunks):
         for copy in (gather_y(k), gather_c(k), gather_d(k), scatter_c(k), scatter_y(k)):
             copy.wait_send()
-        save(k).wait()
+        if not back:
+            save(k).wait()
     if not back:
         for i in range(6):
             spread_x(i, 1).wait_recv()
@@ -1162,12 +1198,13 @@
     dma = pltpu.SemaphoreType.DMA
     anywhere = pl.BlockSpec(memory_space=pl.ANY)
     whole = pl.BlockSpec(memory_space=pltpu.VMEM)
-    out_shape = [
-        jax.ShapeDtypeStruct((4 * frames, patches, features), BF16),
-        jax.ShapeDtypeStruct((4 * frames, patches, 3 * width), BF16),
-    ]
-    if not back:
-        out_shape += [
+    turned = (chunks, features, 4 * frames * CHUNK)
+    if back:
+        out_shape = []
+    else:
+        out_shape = [
+            jax.ShapeDtypeStruct(turned, BF16),
+            jax.ShapeDtypeStruct((4 * frames, patches, 3 * width), BF16),
             jax.ShapeDtypeStruct((4 * frames, patches, width), BF16),
             jax.ShapeDtypeStruct((patches // GROUP, heads, rows), F32),
         ]
@@ -1179,14 +1216,15 @@
     held = 2
     half = saved[2].shape[1:] if back else None
     if back:
+        out_shape.insert(-1, jax.ShapeDtypeStruct((features, features), BF16))
         out_shape.insert(-1, jax.ShapeDtypeStruct(half[1:], F32))
     else:
         out_shape += [jax.ShapeDtypeStruct(w.shape, BF16) for w in saved]
         held = 4
     return pl.pallas_call(
         functools.partial(time_kernel, back, scale, heads),
-        in_specs=[whole, anywhere] + ([whole, whole, anywhere] if back else [anywhere] * 2) + [whole] * 2,
-        out_specs=[anywhere] + [whole] * (len(out_shape) - held) + [anywhere] * (held - 1),
+        in_specs=[whole, anywhere] + ([whole, whole, anywhere, anywhere, whole] if back else [anywhere] * 2) + [whole] * 2,
+        out_specs=([] if back else [anywhere]) + [whole] * (len(out_shape) - held + back) + [anywhere] * (held - 1),
         out_shape=out_shape,
         scratch_shapes=[
             pltpu.VMEM((features, 3 * width), BF16),
@@ -1203,9 +1241,12 @@
         + [dma((chunks,))] * 10
         + [dma((4,)), dma((4,)), dma((1,)), dma((chunks,))]
         + [dma((9,))] * 2
-        + ([pltpu.VMEM(half, BF16)] * 4 + [dma((4,))] * 5 if back else []),
+        + ([pltpu.VMEM(half, BF16)] * 4 + [dma((4,))] * 5 if back else [])
+        + ([pltpu.VMEM((4 * frames, patches, 3 * width), BF16)] if back else [])
+        + [pltpu.VMEM(turned, BF16)]
+        + ([pltpu.VMEM((features, 3 * width), F32), pltpu.VMEM((width, features), F32)] if back else []),
         compiler_params=pltpu.CompilerParams(
-            collective_id=2 if back else 1, has_side_effects=True, vmem_limit_bytes=48 * 1024 * 1024
+            collective_id=2 if back else 1, has_side_effects=True, vmem_limit_bytes=60 * 1024 * 1024
         ),
         cost_estimate=pl.CostEstimate(flops=10**10, transcendentals=10**6, bytes_accessed=10**8),
         name="time_back" if back else "time_forward",
@@ -1429,7 +1470,8 @@
     scale,
     part_hbm, next_hbm, grad_hbm, out_hbm, joined_hbm, mixed_hbm, lhs_hbm, weight_hbm, std_hbm, time_hbm, feed_hbm, feed_in_hbm,
     totals, inverse_next, inverse, masked, gain_next, gain, small_in,
-    kept_out, landed_out, feed_kept, feed_landed, time_out, rows_out, small_out,
+    space_qkv, space_out, feed_in_out, feed_out_out, time_qkv, time_out, rows_out, small_out,
+    rows_in,
     part, std, base, w_out, dj, mixed, lhs, weight, low_grads, turned, dmixed, go,
     t_own, t_in, tz_out, tz_in, t_total, ty_out, ty_in, tc_out, tc_in,
     f_own, f_in, fz_out, fz_in, f_total, f_other, fc_out, fc_in,
@@ -1570,20 +1612,23 @@
         turned[:, at(i, slab)] = low_grads[at(i, slab)].T
         return carry
 
-    def attend_half(t):
+    def attend_half(t, *between):
         rows = pl.ds(t * own, own)
+        first, count = t * own // slab, own // slab
         dmixed[rows] = dot_nt(low_grads[rows], w_out[...]).astype(BF16)
-        lax.fori_loop(t * own // slab, (t + 1) * own // slab, attend, 0)
-        lax.fori_loop(t * own // slab, (t + 1) * own // slab, turn, 0)
-
-    attend_half(0)
-    feed_step(1)
-    feed_step(2)
+        between[0]()
+        lax.fori_loop(first, first + count // 2, attend, 0)
+        between[1]()
+        lax.fori_loop(first + count // 2, first + count, attend, 0)
+        between[2]()
+        lax.fori_loop(first, first + count, turn, 0)
+
+    def nothing():
+        pass
+
+    attend_half(0, lambda: feed_step(1), lambda: feed_step(2), lambda: feed_step(3))
     give.wait_recv()
-    attend_half(1)
-    feed_step(3)
-    time_step()
-    feed_step(0)
+    attend_half(1, nothing, time_step, lambda: feed_step(0))
     for copy in fetches[6:]:
         copy.wait()
     go[...] = dot_nn(turned[...], mixed[...]).astype(BF16)
@@ -1677,10 +1722,10 @@
 
     def ride(k):
         slot = 2 * (z % 2) + c
-        return remote(ready.at[:, columns(k)], rows_out.at[slot], r_send.at[k], r_recv.at[slot], (y, x, z // 2, k))
+        return remote(ready.at[:, columns(k)], rows_in.at[slot], r_send.at[k], r_recv.at[slot], (y, x, z // 2, k))
 
     def ride_local(k):
-        return pltpu.make_async_copy(ready.at[:, columns(k)], rows_out.at[2 * (z % 2) + c], local.at[3])
+        return pltpu.make_async_copy(ready.at[:, columns(k)], rows_in.at[2 * (z % 2) + c], local.at[3])
 
     for k in range(4):
         pl.when(stays(k))(lambda k=k: ride_local(k).start())
@@ -1734,15 +1779,23 @@
     fc_out[1] = f_total[at(1 - c, parity)].astype(BF16)
     swap_feed = remote(fc_out, fc_in, c_send.at[1], c_recv.at[1], pair)
     swap_feed.start()
-    feed_kept[0] = f_other[at(c, parity)]
-    feed_kept[1] = f_total[at(c, parity)]
+    units = f_total.shape[1]
+    feed_in_out[:, at(c, units)] = f_other[at(c, parity)]
+    feed_out_out[at(c, units)] = f_total[at(c, parity)].T
     swap_y.wait_recv()
     tc_out[0] = t_total[y, at(1 - c, parity)].astype(BF16)
     tc_out[1] = ty_in[at(1 - c, parity)]
     swap_time = remote(tc_out, tc_in, c_send.at[2], c_recv.at[2], pair)
     swap_time.start()
-    time_out[0, 0] = t_total[y, at(c, parity)]
-    time_out[0, 1] = ty_in[at(c, parity)].astype(F32)
+    for k in range(4):
+        pl.when(stays(k))(lambda k=k: ride_local(k).wait())
+        from_self = jnp.logical_and(2 * c + k // 2 == z, c == k % 2)
+
+        def landed(k=k):
+            remote(ready.at[:, columns(k)], rows_in.at[k], r_send.at[k], r_recv.at[k], near_y).wait_recv()
+
+        pl.when(jnp.logical_not(from_self))(landed)
+    rows_out[...] = rows_in[...].astype(F32)
     for r in (1, 2, 3):
         to_z(r).wait_recv()
     total = grads[3, block(y, x), :]
@@ -1757,18 +1810,41 @@
     core_out[...] = grads[3, core_rows(1 - c), :].astype(BF16)
     last = remote(core_out, core_in, c_send.at[0], c_recv.at[0], pair)
     last.start()
-    kept_out[...] = grads[3, core_rows(c), :]
+    def place(core, value):
+        for j in range(3):
+            space_qkv[j, :, at(core, third)] = value[:, j * third : (j + 1) * third]
+        space_out[at(core, third)] = value[:, 3 * third :].T
+
+    place(c, grads[3, core_rows(c), :])
     result = sums[:, columns(z)]
     for r in (1, 2, 3):
         deal(r).wait_recv()
         result = result + share_in[r]
     small_out[...] = result
     swap_feed.wait_recv()
-    feed_landed[...] = fc_in[...].astype(F32)
+    feed_in_out[:, at(1 - c, units)] = fc_in[0].astype(F32)
+    feed_out_out[at(1 - c, units)] = fc_in[1].astype(F32).T
     swap_time.wait_recv()
-    time_out[1] = tc_in[...].astype(F32)
+    mine = (t_total[y, at(c, parity)], ty_in[at(c, parity)].astype(F32))
+    other = (tc_in[0].astype(F32), tc_in[1].astype(F32))
+    by_head = []
+    for yb in range(2):
+        for cb in range(2):
+            by_head.append(
+                jnp.where(
+                    c == cb,
+                    jnp.where(y == yb, mine[0], mine[1]),
+                    jnp.where(y == yb, other[0], other[1]),
+                )
+            )
+    for j in range(4):
+        made = jnp.concatenate([v[:, j * HEAD_DIM : (j + 1) * HEAD_DIM] for v in by_head], axis=1)
+        if j < 3:
+            time_qkv[j] = made
+        else:
+            time_out[...] = made.T
     last.wait_recv()
-    landed_out[...] = core_in[...].astype(F32)
+    place(1 - c, core_in[...].astype(F32))
 
     for copy in (last, swap, give, swap_y, swap_feed, swap_time):
         copy.wait_send()
@@ -1788,14 +1864,7 @@
     for h in range(3):
         share(h).wait_send()
     for k in range(4):
-        pl.when(stays(k))(lambda k=k: ride_local(k).wait())
         pl.when(jnp.logical_not(stays(k)))(lambda k=k: ride(k).wait_send())
-        from_self = jnp.logical_and(2 * c + k // 2 == z, c == k % 2)
-
-        def landed(k=k):
-            remote(ready.at[:, columns(k)], rows_out.at[k], r_send.at[k], r_recv.at[k], near_y).wait_recv()
-
-        pl.when(jnp.logical_not(from_self))(landed)
 
 
 def leave(
@@ -1820,17 +1889,16 @@
     return pl.pallas_call(
         functools.partial(leave_kernel, scale),
         in_specs=[anywhere] * 12 + [whole] * 7,
-        out_specs=[whole] * 5 + [anywhere, whole],
+        out_specs=[whole] * 8,
         out_shape=[
-            jax.ShapeDtypeStruct((parity, cols4), F32),
-            jax.ShapeDtypeStruct((parity, cols4), F32),
-            jax.ShapeDtypeStruct((2, parity, units), F32),
-            jax.ShapeDtypeStruct((2, parity, units), F32),
-            jax.ShapeDtypeStruct((2, 2, parity, BLK), F32),
-            jax.ShapeDtypeStruct((4, own, BLK), BF16),
-            jax.ShapeDtypeStruct((8, BLK), F32),
+            jax.ShapeDtypeStruct(shape, F32)
+            for shape in (
+                (3, parity, 2 * quarter), (2 * quarter, parity), (parity, 2 * units), (2 * units, parity),
+                (3, parity, BLK), (BLK, parity), (4, own, BLK), (8, BLK),
+            )
         ],
         scratch_shapes=[
+            low(4, own, BLK),
             high(own, features), high(own, features), high(own, features), low(*w_out.shape), low(*joined.shape),
             low(*mixed.shape), low(*lhs.shape), low(*weight.shape), low(2 * own, features), low(features, 2 * own),
             low(*mixed.shape), low(features, cols4),
@@ -1952,7 +2020,7 @@
     gain = [vectors[1 + i : 2 + i] for i in range(3)]
 
     half = qkv_space.shape[2] // 2
-    normed1, joined1, mixed1, total1, delta, upstream, wf_far, wf_in_far = time_call(
+    turned1, joined1, mixed1, total1, delta, upstream, wf_far, wf_in_far = time_call(
         False,
         normed1.reshape(frames_own, patches, width),
         cotangent.reshape(4, own, BLK),
@@ -1961,58 +2029,34 @@
         bias,
         scale,
     )
-    normed1 = normed1.reshape(4 * own, width)
-    mixed1 = mixed1.reshape(4 * own, -1)
     w_in_half, w_out_half, grad2, grad2_low, block_rows, gain_grad2 = feed(
         resid1, delta.reshape(own, width), upstream, masked.astype(F32), gain[2], wf_in, wf_in_far, wf_out, wf_far
     )
 
-    def by_core(kept, landed):
-        return jnp.where(c == 0, jnp.concatenate([kept, landed], -1), jnp.concatenate([landed, kept], -1))
-
-    gb2, djoined1, part1, g_w_in, block_out = time_call(
+    part1, g_time, g_w_in, block_out = time_call(
         True,
         grad2_low.reshape(frames_own, patches, width),
         block_rows,
-        [joined1, total1, w_in_half],
+        [joined1, total1, w_in_half, turned1, mixed1],
         wt_all,
         bias,
         scale,
     )
     block_out = block_out.reshape(tokens.shape)
-    gb2 = gb2.reshape(4 * own, width)
-    djoined1 = djoined1.reshape(4 * own, -1)
-    g_t_qkv = dot_tn(normed1, djoined1).astype(BF16).reshape(width, 3, 4, HEAD_DIM)
-    g_t_out = dot_tn(gb2, mixed1).astype(BF16).reshape(width, 1, 4, HEAD_DIM)
-    g_time = jnp.swapaxes(jnp.concatenate([g_t_qkv, g_t_out], axis=1), 1, 2).reshape(width, width)
     small = rows_of([jnp.zeros((2, width), F32), gain_grad2, jnp.zeros((5, width), F32)])
-    kept, landed, feed_kept, feed_landed, quad, grad_tokens, small = leave(
+    grad_qkv_space, grad_out_space, grad_w_in, grad_w_out, grad_qkv_time, grad_out_time, grad_tokens, small = leave(
         part1.reshape(own, width), std1, grad2, ws_out, joined0, mixed0, turned0, ws_qkv, std0, g_time, w_out_half, g_w_in,
         total0, inv1, inv0, masked.astype(F32), gain[1], gain[0], small, scale,
     )
-    grad_tokens = grad_tokens.reshape(tokens.shape).astype(F32)
-
-    rows = BLK // 2
-    grad_qkv_space = by_core(
-        kept[:, : 3 * half].reshape(rows, 3, half), landed[:, : 3 * half].reshape(rows, 3, half)
-    )
-    grad_out_space = by_core(kept[:, 3 * half :], landed[:, 3 * half :]).T
-    grad_w_in = by_core(feed_kept[0], feed_landed[0])
-    grad_w_out = by_core(feed_kept[1], feed_landed[1]).T
-    quad = jnp.transpose(quad, (2, 0, 1, 3)).reshape(rows, 2, 2, 4, HEAD_DIM)
-    quad = jnp.where(c == 1, quad[:, ::-1], quad)
-    quad = jnp.where(y == 1, quad[:, :, ::-1], quad)
-    quad = jnp.transpose(quad, (0, 3, 2, 1, 4)).reshape(rows, 4, 4 * HEAD_DIM)
-    grad_qkv_time = quad[:, :3]
-    grad_out_time = quad[:, 3].T
+    small = small[:4]
     return (
         block_out,
-        grad_tokens,
+        grad_tokens.reshape(tokens.shape),
         small[3],
         small[:3],
-        grad_qkv_space,
+        jnp.swapaxes(grad_qkv_space, 0, 1),
         grad_out_space,
-        grad_qkv_time,
+        jnp.swapaxes(grad_qkv_time, 0, 1),
         grad_out_time,
         grad_w_in,
         grad_w_out,

time: 459 us -> 430 us (0.937)
  the two profiles are of different devices: /device:TPU:0 before, /device:TPU:9 now
where the time goes in v9:
time: 430 us; the launch traced here: 425 us
  Pallas kernels  404 us (94%)
  local copies, waits for them, and re-layouts  14.9 us (3%)
  other arithmetic  4.71 us (1%)
    pallas_call x2, Pallas kernels, time_call(): pl.pallas_call(functools.partial(time_kernel, back, scale, heads), in_spe...  126 us
    pallas_call x1, Pallas kernels, leave(): pl.pallas_call(functools.partial(leave_kernel, scale), in_specs=[anywhere...  109 us
    pallas_call x1, Pallas kernels, enter(): pl.pallas_call(functools.partial(enter_kernel, scale), in_specs=[anywhere...  105 us
    pallas_call x1, Pallas kernels, feed(): pl.pallas_call(feed_kernel, in_specs=[whole] * 5 + [anywhere] * 4, out_sp...  64.2 us
  transfers between devices with their start and end apart: 1, of which 0 were waited for; matrix products, arithmetic and copies ran while one was open for 1% of the time, Pallas kernels for 0%

profile of v9, /device:TPU:9, one launch (start us, length us, event | category | flops | bytes accessed | tf_op | source)
XLA Modules:
  0.0 425.4 jit_solution(17297513985077818892)
XLA Ops:
  0.6 0.0 copy-start
  0.7 0.9 convert_bitcast_fusion
  1.6 0.7 constant_dynamic-update-slice_fusion
  2.2 0.7 collective-permute-start
  2.9 0.0 copy-done
  2.9 0.3 constant_dynamic-slice_fusion.1
  3.2 0.0 copy-start.10
  3.2 0.3 copy.33
  3.5 0.2 copy.28
  3.7 0.9 constant_dynamic-slice_fusion
  4.6 0.2 copy.34
  4.8 0.0 copy-done.11
  4.8 1.0 pad_maximum_fusion.later
  5.8 0.1 pad.7.clone
  5.9 0.0 copy-done.10
  5.9 0.7 maximum_maximum_fusion.1.vec
  6.5 0.1 pad.2.clone
  6.6 0.0 collective-permute-done
  6.6 0.1 fusion
  6.7 0.9 copy.29.masked
  7.6 0.1 dynamic-slice_reduce_fusion
  7.7 0.1 reshape.110
  7.8 0.1 reshape.111
  7.9 0.1 broadcast_in_dim.29
  8.0 0.1 le.15
  8.1 104.6 %enter.1 = (bf16[1024,1536]{1,0:T(8,128)(2,1)}, bf16[512,1024]{1,0:T(8,128)(2,1)}, bf16[1024,1024]{1,0:T(8,128)(2,1)}, bf16[4,512,1024]{2,1,0:T(8,128)(2,1)}, bf...) custom-call(bf16[4,512,256]{2,1,0:T(8,128)(2,1)} %bitcast.30, ...), custom_call_target="tpu_custom_call" | custom-call | flops 10000000000 | bytes 100000000 | tf_op jit(solution)/shard_map/enter/pallas_call | solution.py:864
  112.7 1.5 fusion.1
  114.2 0.7 and_select_fusion.refs_5_.refs_8_
  114.9 69.1 %time_forward.1 = (bf16[4,1024,512]{2,1,0:T(8,128)(2,1)}, bf16[16,128,768]{2,1,0:T(8,128)(2,1)}, bf16[16,128,256]{2,1,0:T(8,128)(2,1)}, f32[16,4,128]{2,1,0:T(4,...) custom-call(bf16[4,128,1024]{2,1,0:T(8,128)(2,1)} %bitcast.34, ...), custom_call_target="tpu_custom_call" | custom-call | flops 10000000000 | bytes 100000000 | tf_op jit(solution)/shard_map/time_forward/pallas_call | solution.py:1224
  184.1 64.2 %feed.1 = (bf16[2,4,256,512]{3,2,1,0:T(8,128)(2,1)}, bf16[2,4,256,512]{3,2,1,0:T(8,128)(2,1)}, f32[512,1024]{1,0:T(8,128)}, bf16[512,1024]{1,0:T(8,128)(2,1)}, b...) custom-call(f32[512,1024]{1,0:T(8,128)} %get-tuple-element.52.resid, f32[512,1024]{1,0:T(8,128)} %bitcast.33, ...), custom_call_target="tpu_custom_call" | custom-call | flops 25999998976 | bytes 100000000 | tf_op jit(solution)/shard_map/feed/pallas_call | solution.py:1439
  248.3 1.4 maximum_maximum_fusion.small_in
  249.7 57.1 %time_back.1 = (f32[4,128,1024]{2,1,0:T(8,128)}, bf16[1024,1024]{1,0:T(8,128)(2,1)}, f32[256,512]{1,0:T(8,128)}, bf16[4,512,256]{2,1,0:T(8,128)(2,1)}) custom-call(bf16[4,128,1024]{2,1,0:T(8,128)(2,1)} %bitcast.35, bf16[512,1024]{1,0:T(8,128)(2,1)} %get-tuple-element.63.refs_1_, bf16[16,128,768]{2,1,0:T(8,128)(2,1)} %get-tuple-element.64.refs_2_, ...), custom_call_target="tpu_custom_call" | custom-call | flops 10000000000 | bytes 100000000 | tf_op jit(solution)/shard_map/time_back/pallas_call | solution.py:1224
  306.7 0.0 copy-start.3
  306.8 108.9 %leave.1 = (f32[3,128,256]{2,1,0:T(8,128)}, f32[256,128]{1,0:T(8,128)}, f32[128,1024]{1,0:T(8,128)}, f32[1024,128]{1,0:T(8,128)}, f32[3,128,256]{2,1,0:T(8,128)}...) custom-call(f32[512,1024]{1,0:T(8,128)} %bitcast.32, f32[512,1024]{1,0:T(8,128)} %get-tuple-element.71.next_hbm, ...), custom_call_target="tpu_custom_call" | custom-call | flops 20000000000 | bytes 100000000 | tf_op jit(solution)/shard_map/leave/pallas_call | solution.py:1889
  415.7 1.4 slice.27
  417.2 1.3 slice.26
  418.4 1.0 copy.46
  419.4 0.0 copy-start.1
  419.4 1.3 copy.47
  420.8 0.0 copy-done.7
  420.8 0.7 copy.48
  421.5 0.7 copy.49
  422.2 0.7 copy.50
  422.9 0.0 copy-done.8
  422.9 0.7 copy.51
  423.6 0.0 copy-done.5
  423.6 0.8 copy.52
  424.4 0.8 copy.53
  (26 shorter events, 0.1 us)
Async XLA Ops:
  0.6 2.3 copy-start
  2.2 4.4 %collective-permute-start = (s32[2,1040]{1,0:T(2,128)S(1)}, s32[2,1040]{1,0:T(2,128)S(1)}, u32[]{:S(2)}, u32[]{:S(2)}) collective-permute-start(s32[2,1040]{1,0:T(2,128)S(1)} %constant_dynamic-update-slice_fusion), channel_id=1, source_target_pairs={{0,4},{1,5},{2,6},{3,7},{4,0},{5,1},{6,2},{7,3},{8,12},{9,13},{10,... | collective-permute-start | bytes 24968 | tf_op jit(solution)/shard_map/ppermute | solution.py:434
  2.9 1.9 copy-start.11
  3.2 2.7 copy-start.10
  306.7 111.7 %copy-start.3 = (bf16[4,512,256]{2,1,0:T(8,128)(2,1)S(1)}, bf16[4,512,256]{2,1,0:T(8,128)(2,1)}, u32[]{:S(2)}) copy-start(bf16[4,512,256]{2,1,0:T(8,128)(2,1)} %get-tuple-element.69) | copy-start | bytes 3145732
  415.7 3.7 copy-start.2
  419.4 1.4 copy-start.7
  419.4 2.1 copy-start.9
  419.4 2.8 copy-start.6
  419.4 3.5 copy-start.8
  419.4 4.2 copy-start.5
  419.4 5.7 %copy-start.1 = (bf16[1024,3,256]{2,0,1:T(8,128)(2,1)S(1)}, bf16[1024,3,256]{2,0,1:T(8,128)(2,1)}, u32[]{:S(2)}) copy-start(bf16[1024,3,256]{2,0,1:T(8,128)(2,1)} %param.22) | copy-start | bytes 4718596
  420.8 3.6 copy-start.4
